TPU v7x, 32 devices: a whole 2x2x4 slice. The times are simulated.
32 devices in a mesh: grp: 2 (over y), row: 8 (over z, core), col: 2 (over x).
Axes of the slice: x: 2, y: 2, z: 4, core: 2. Of those that a mesh axis runs over, the one named last changes fastest.
Arguments:
- single: float32 [2, 512, 384], P(None, ('grp', 'row')), parts along dimension 1, may hold values from -6 to 6
- frames: float32 [2, 12, 512], P(None, None, ('grp', 'row')), parts along dimension 2, may hold values from -4 to 4, as said below
- saved_probs: bfloat16 [2, 12, 512, 256], P(None, None, ('grp', 'row'), 'col'), parts along dimension 2, may hold values from 0.0009994507 to 100
- pair: bfloat16 [512, 256, 128], P(('grp', 'row'), 'col'), parts along dimension 0, may hold values from -6 to 6
- cotangent: float32 [512, 384], P(('grp', 'row')), parts along dimension 0, may hold values from -12 to 12
- chains: int32 [512], P(('grp', 'row')), parts along dimension 0, may hold values from 0 to 15, never falling along the last dimension, each value on 1 to 64 neighbouring positions
- links: int32 [32, 16], P('grp'), parts along dimension 0, may hold values 0 or 1
- w_query: bfloat16 [384, 192], replicated, may hold values from -0.3125 to 0.3125
- w_key: bfloat16 [384, 192], replicated, may hold values from -0.3125 to 0.3125
- w_value: bfloat16 [384, 192], replicated, may hold values from -0.3125 to 0.3125
- w_query_points: bfloat16 [384, 144], replicated, may hold values from -0.3125 to 0.3125
- w_key_points: bfloat16 [384, 144], replicated, may hold values from -0.3125 to 0.3125
- w_value_points: bfloat16 [384, 288], replicated, may hold values from -0.3125 to 0.3125
- w_bias: bfloat16 [128, 12], replicated, may hold values from -0.5 to 0.5
- w_out: bfloat16 [2112, 384], replicated, may hold values from -0.125 to 0.125
- head_weights: float32 [12], replicated, may hold values from -1 to 1
Outputs:
- d_single: float32 [512, 384], P(('grp', 'row')), parts along dimension 0
- d_frames: float32 [2, 12, 512], P(None, None, ('grp', 'row')), parts along dimension 2
- d_pair: bfloat16 [512, 256, 128], P(('grp', 'row'), 'col'), parts along dimension 0
There are 2 independent parts, one for each index of `grp`. A program takes and returns all parts, laid end to end along the dimension named above; an argument that names none is the same for every part. Nothing has to cross between parts.
Inputs may be any that keep to these rules, and one draw needn't show every extreme that they name: `chains`: chain numbers never fall along the residues; each chain holds 1 to 64 residues and one holds exactly 64. `frames`: rows 0 to 8 of each residue hold a rotation matrix in row-major order, rows 9 to 11 a translation.
All inputs are finite; a program needn't handle non-finite values.
Results may differ from a plain program's by a relative error of at most 0.0055.
Values sent between devices are 32-bit elements; how exact they have to be, the bound alone decides.
No kernel may reach another device: no remote copies, remote signals or barrier semaphores. Data moves between devices by JAX's collectives and lax.ppermute only.
A program may use at most 64 MiB of HBM per device.

v0:
```python
import functools
import math

import jax
import jax.numpy as jnp
from jax import lax
from jax.experimental import pallas as pl
from jax.experimental.pallas import tpu as pltpu
from jax.sharding import PartitionSpec as P

C = 384
H = 12
HD = 16
CZ = 128
PQ = 4
PV = 8
NCHAIN = 16
NORM_EPS = 1e-08
LOGIT_SCALE = math.sqrt(1.0 / 3.0)
PLAIN_SCALE = 1.0 / math.sqrt(HD)
POINT_SCALE = math.sqrt(2.0 / (9.0 * PQ))

LANES = 640
PACK = 896
FRAME_LANE = 768
CHAIN_LANE = 792
STAT = 96

F32 = jnp.float32
BF16 = jnp.bfloat16
NN = (((1,), (0,)), ((), ()))
NT = (((1,), (1,)), ((), ()))
TN = (((0,), (0,)), ((), ()))


def mm(a, b, dims=NN):
    return lax.dot_general(a, b, dims, preferred_element_type=F32)


def split(x):
    hi = x.astype(BF16)
    return hi, (x - hi.astype(F32)).astype(BF16)


def mm2(x, w, dims=NN):
    hi, lo = split(x)
    rows = x.shape[0]
    both = mm(jnp.concatenate([hi, lo], axis=0), w, dims)
    return both[:rows] + both[rows:]


def mm3(ah, al, bh, bl, dims=NN):
    return mm(ah, bh, dims) + mm(ah, bl, dims) + mm(al, bh, dims)


def iota(shape, axis):
    return lax.broadcasted_iota(jnp.int32, shape, axis)


def key_heads(rows):
    lane = iota((rows, LANES), 1)
    return jnp.where(lane < 256, lane >> 4, (lane & 127) >> 2)


def value_heads(rows):
    lane = iota((rows, LANES), 1)
    inner = lane & 127
    points = jnp.where(inner < STAT, inner >> 3, inner - STAT)
    return jnp.where(lane < 256, lane >> 4, points)


def pick(full, heads, rows):
    out = None
    for h in range(H):
        part = jnp.where(heads == h, full[h * rows : (h + 1) * rows], 0.0)
        out = part if out is None else out + part
    return out


def spread(x, heads):
    return jnp.concatenate([jnp.where(heads == h, x, 0.0) for h in range(H)], axis=0)


def spread2(x, heads):
    hi, lo = split(x)
    hi32, lo32 = hi.astype(F32), lo.astype(F32)
    return spread(hi32, heads).astype(BF16), spread(lo32, heads).astype(BF16)


def columns(frames_block, first):
    cols = [frames_block[:, first + n : first + n + 1] for n in range(12)]
    return [[cols[3 * a + b] for b in range(3)] for a in range(3)], cols[9:]


def block(x, a):
    return x[:, 256 + 128 * a : 384 + 128 * a]


def rotate(rot, pts):
    return [sum(rot[a][b] * pts[b] for b in range(3)) for a in range(3)]


def unrotate(rot, pts):
    return [sum(rot[a][b] * pts[a] for a in range(3)) for b in range(3)]


def place(rot, shift, flat):
    local_pts = [block(flat, a) for a in range(3)]
    turned = rotate(rot, local_pts)
    return jnp.concatenate(
        [flat[:, :256]] + [turned[a] + shift[a] for a in range(3)], axis=1
    )


def lane_matrix(rows, fn):
    r = iota((rows, 128), 0)
    c = iota((rows, 128), 1)
    return (fn(r) == c).astype(F32).astype(BF16)


def upstream_parts(g, w_out_ref, gp_ref, pu_ref, rows):
    hi, lo = split(g)
    both = jnp.concatenate([hi, lo], axis=0)

    def part(first, count):
        r = mm(both, w_out_ref[first : first + count, :], NT)
        return r[:rows] + r[rows:]

    gp_ref[...] = jnp.zeros(gp_ref.shape, F32)
    gp_ref[:, 0:192] = part(0, 192)
    for a in range(4):
        gp_ref[:, 256 + 128 * a : 352 + 128 * a] = part(192 + 96 * a, 96)
    wide = part(576, H * CZ)
    for h in range(H):
        pu_ref[h * rows : (h + 1) * rows, :] = (
            wide[:, h * CZ : (h + 1) * CZ].astype(BF16).astype(F32)
        )


def pair_products(pu_ref, pair_ref, d_ref, rows):
    for i in range(rows):
        lhs = pu_ref[pl.ds(i, H, stride=rows), :].astype(BF16)
        d_ref[pl.ds(i, H, stride=rows), :] = mm(lhs, pair_ref[i], NT)


def prep_body(
    hw_ref, pack_ref, cot_ref, wq_ref, wk_ref, wv_ref, wqp_ref, wkp_ref, wvp_ref, w_out_ref, pair_ref,
    wk_out, wq_out, gp_ref, q1_ref, q0_ref, pu_ref, d_ref, sc_ref,
):
    rows = pack_ref.shape[0]
    upstream_parts(cot_ref[...], w_out_ref, gp_ref, pu_ref, rows)
    pair_products(pu_ref, pair_ref, d_ref, rows)
    wq_out[...] = jnp.zeros(wq_out.shape, BF16)
    wk_out[...] = jnp.zeros(wk_out.shape, BF16)
    wq_out[:, 0:192] = wq_ref[...]
    wk_out[:, 0:192] = wk_ref[...]
    wk_out[:, 640:832] = wv_ref[...]
    for a in range(3):
        wq_out[:, 256 + 128 * a : 304 + 128 * a] = wqp_ref[:, 48 * a : 48 * a + 48]
        wk_out[:, 256 + 128 * a : 304 + 128 * a] = wkp_ref[:, 48 * a : 48 * a + 48]
        wk_out[:, 896 + 128 * a : 992 + 128 * a] = wvp_ref[:, 96 * a : 96 * a + 96]
    lane = iota((8, 128), 1)
    raw = jnp.zeros((8, 128), F32)
    for h in range(H):
        raw = jnp.where((lane >> 2) == h, hw_ref[h], raw)
    soft = jnp.maximum(raw, 0.0) + jnp.log(1.0 + jnp.exp(-jnp.abs(raw)))
    sc_ref[...] = soft * POINT_SCALE
    fr = pack_ref[:, FRAME_LANE : FRAME_LANE + 128]
    for out, first, fcol in ((q1_ref, 0, 0), (q0_ref, C, 12)):
        flat = mm2(pack_ref[:, first : first + C], wq_out[...])
        rot, shift = columns(fr, fcol)
        out[:, :LANES] = place(rot, shift, flat)
        out[:, LANES:] = flat[:, 256:]


def project_keys(x, fr, fcol, wk_ref, kv_ref):
    flat = mm2(x, wk_ref[...])
    rot, shift = columns(fr, fcol)
    kv_ref[:, 0:640] = place(rot, shift, flat[:, :640])
    kv_ref[:, 640:1280] = place(rot, shift, flat[:, 640:])
    kv_ref[:, 1280:1664] = flat[:, 256:640]
    kv_ref[:, 1664:2048] = flat[:, 896:1280]


def value_sums(probs, kv_ref, rows):
    values = kv_ref[:, 640:1280]
    lane = iota(values.shape, 1)
    values = jnp.where((lane >= 256 + STAT) & (lane < 256 + STAT + H), 1.0, values)
    hi, lo = split(values)
    return pick(mm(probs, hi) + mm(probs, lo), value_heads(rows), rows)


def head_dots(prod, rows):
    return mm2(prod, lane_matrix(256, lambda r: STAT + (r >> 4)))


def first_body(
    flag_ref, own_ref, ownx_ref, p1_ref, p1x_ref, p2_ref, p2x_ref, wk_ref, links_ref, probs_ref, gp_ref, d_ref,
    keys_ref, kv_ref, pm_ref, e_ref,
):
    rows = own_ref.shape[0]
    home = flag_ref[0] == 1
    zb = flag_ref[1]
    core = flag_ref[2]

    def put(z, k, value):
        keys_ref[pl.ds(pl.multiple_of((2 * z + k) * rows, rows), rows), :] = value

    put(zb, core, jnp.where(home, own_ref[...], p1_ref[...]))
    put(zb, 1 - core, jnp.where(home, ownx_ref[...], p1x_ref[...]))
    put(1 - zb, core, jnp.where(home, p1_ref[...], p2_ref[...]))
    put(1 - zb, 1 - core, jnp.where(home, p1x_ref[...], p2x_ref[...]))
    fr = keys_ref[:, FRAME_LANE : FRAME_LANE + 128]
    keys = fr.shape[0]
    at = CHAIN_LANE - FRAME_LANE
    key_chain = fr[:, at : at + 1]
    own_chain = own_ref[:, FRAME_LANE : FRAME_LANE + 128][:, at : at + 1]
    key_hot = (iota((keys, NCHAIN), 1).astype(F32) == key_chain).astype(F32).astype(BF16)
    own_hot = (iota((rows, NCHAIN), 1).astype(F32) == own_chain).astype(F32).astype(BF16)
    eye = iota((NCHAIN, NCHAIN), 0) == iota((NCHAIN, NCHAIN), 1)
    allowed = jnp.where(eye, 1.0, links_ref[...].astype(F32)).astype(BF16)
    mask = mm(mm(own_hot, allowed).astype(BF16), key_hot, NT)
    mask_all = jnp.concatenate([mask] * H, axis=0)
    for l in range(2):
        pm_ref[l] = (probs_ref[l].astype(F32) * mask_all).astype(BF16)
    project_keys(keys_ref[:, 0:C], fr, 0, wk_ref, kv_ref)
    probs = pm_ref[1]
    sums = value_sums(probs, kv_ref, rows)
    weighted = mm2(probs.astype(F32) * d_ref[...], jnp.ones((keys, 128), BF16))
    lane = iota((rows, 128), 1)
    dots = pick(weighted, lane - STAT, rows) + head_dots(gp_ref[:, 0:256] * sums[:, 0:256], rows)
    e_ref[:, 0:128] = block(sums, 0)
    e_ref[:, 128:256] = jnp.where(lane < STAT, block(sums, 1), dots)
    e_ref[:, 256:384] = block(sums, 2)


def second_body(keys_ref, wk_ref, pm_ref, pair_ref, kv_ref, e_ref, p32_ref, op_ref):
    rows = pair_ref.shape[0]
    fr = keys_ref[:, FRAME_LANE : FRAME_LANE + 128]
    project_keys(keys_ref[:, C : 2 * C], fr, 12, wk_ref, kv_ref)
    probs = pm_ref[0]
    sums = value_sums(probs, kv_ref, rows)
    for a in range(3):
        e_ref[:, 128 * a : 128 * a + 128] = block(sums, a)
    e_ref[:, 384:640] = sums[:, 0:256]
    p32_ref[...] = probs.astype(F32)
    for i in range(rows):
        lhs = p32_ref[pl.ds(i, H, stride=rows), :].astype(BF16)
        op_ref[pl.ds(i, H, stride=rows), :] = mm(lhs, pair_ref[i])
    for h in range(H):
        e_ref[:, 640 + CZ * h : 640 + CZ * (h + 1)] = op_ref[h * rows : (h + 1) * rows, :]


def backward(
    flag_ref, e, dots, probs, kv_ref, key_fr, own_fr, fcol, q_ref, gp, d_ref, wk_ref, wq_ref, sc, shift_lane,
    share, z_ref, keys_out_ref,
):
    rows = e.shape[0]
    lane = iota((rows, 128), 1)
    stat = (lane >= STAT) & (lane < STAT + H)
    inv = jnp.where(stat, 1.0 / jnp.where(stat, e[:, 0:128], 1.0), 0.0)
    r128 = iota((128, LANES), 0)
    grow = (r128 - STAT == value_heads(128)) & ((iota((128, LANES), 1) & 127) < STAT)
    grow = grow | ((r128 - STAT == (iota((128, LANES), 1) >> 4)) & (iota((128, LANES), 1) < 256))
    inv_lanes = mm2(inv, grow.astype(F32).astype(BF16))
    rot, shift = columns(own_fr, fcol)
    inv_pts = block(inv_lanes, 0)
    ptg = [e[:, 128 * a : 128 * a + 128] * inv_pts for a in range(3)]
    off = [jnp.where(lane < STAT, ptg[a] - shift[a], 0.0) for a in range(3)]
    opt = unrotate(rot, off)
    length = jnp.sqrt(opt[0] * opt[0] + opt[1] * opt[1] + opt[2] * opt[2] + NORM_EPS)
    scale = gp[:, 640:768] / length
    gpt = [block(gp, a) + scale * opt[a] for a in range(3)]
    gptg = rotate(rot, gpt)
    upper = jnp.concatenate([gp[:, 0:256]] + gptg, axis=1)
    point_dots = gptg[0] * ptg[0] + gptg[1] * ptg[1] + gptg[2] * ptg[2]
    rd = dots * inv + mm2(point_dots, lane_matrix(128, lambda r: STAT + (r >> 3)))
    both = jnp.concatenate([spread(rd, lane - STAT), spread(inv, lane - STAT)], axis=0)
    wide = mm2(both, jnp.ones((128, 128), BF16))
    rd_all, inv_all = wide[: H * rows], wide[H * rows :]
    heads_v = value_heads(rows)
    heads_k = key_heads(rows)
    uh, ul = spread2(upper, heads_v)
    vh, vl = split(kv_ref[:, 640:1280])
    d_att = d_ref[...] + mm3(uh, ul, vh, vl, NT)
    p32 = probs.astype(F32)
    att = p32 * inv_all
    dl = LOGIT_SCALE * att * (d_att - rd_all)
    z_ref[0 : H * rows, :] = att
    z_ref[H * rows :, :] = dl
    dh, dlo = split(dl)
    kh, klo = split(kv_ref[:, 0:640])
    qr = pick(mm3(dh, dlo, kh, klo), heads_k, rows)
    d_qg = [sc * block(qr, a) for a in range(3)]
    d_ql = unrotate(rot, d_qg)
    query_grad = mm2(jnp.concatenate([PLAIN_SCALE * qr[:, 0:256]] + d_ql, axis=1), wq_ref[...], NT)
    q_local = [q_ref[:, 640 + 128 * b : 768 + 128 * b] for b in range(3)]
    prods = [d_qg[a] * q_local[b] + share * off[a] * gpt[b] for a in range(3) for b in range(3)]
    prods = prods + [d_qg[a] - share * gptg[a] for a in range(3)]
    gather12 = lane_matrix(12 * 128, lambda r: shift_lane + (r >> 7))
    query_frames = mm2(jnp.concatenate(prods, axis=1), gather12)
    dt = jnp.transpose(dl)
    th, tl = split(dt)
    qh, qlo = spread2(q_ref[:, 0:640], heads_k)
    kr = mm3(th, tl, qh, qlo)
    head_rows = iota((H * rows, 128), 0) // rows
    hot = ((iota((H * rows, 128), 1) >> 2) == head_rows).astype(F32).astype(BF16)
    cs = mm(th, hot) + mm(tl, hot)
    pt = jnp.transpose(p32).astype(BF16)
    sh, sl = spread2(upper * inv_lanes, heads_v)
    vr = mm(pt, sh) + mm(pt, sl)
    krot, _ = columns(key_fr, fcol)
    d_kg = [sc * (block(kr, a) - cs * kv_ref[:, 256 + 128 * a : 384 + 128 * a]) for a in range(3)]
    d_vg = [block(vr, a) for a in range(3)]
    d_kl = unrotate(krot, d_kg)
    d_vl = unrotate(krot, d_vg)
    flat = jnp.concatenate([PLAIN_SCALE * kr[:, 0:256]] + d_kl + [vr[:, 0:256]] + d_vl, axis=1)
    keys_out_ref[:, 0:C] = mm2(flat, wk_ref[...], NT)
    k_local = [kv_ref[:, 1280 + 128 * b : 1408 + 128 * b] for b in range(3)]
    v_local = [kv_ref[:, 1664 + 128 * b : 1792 + 128 * b] for b in range(3)]
    kprods = [d_kg[a] * k_local[b] + d_vg[a] * v_local[b] for a in range(3) for b in range(3)]
    kprods = kprods + [d_kg[a] + d_vg[a] for a in range(3)]
    key_frames = mm2(jnp.concatenate(kprods, axis=1), gather12)
    return query_grad, query_frames, key_frames


def send_blocks(flag_ref, src_ref, mine_a, mine_b, theirs, rows):
    zb = flag_ref[1]
    core = flag_ref[2]

    def get(z, k):
        return src_ref[pl.ds(pl.multiple_of((2 * z + k) * rows, rows), rows), :]

    mine_a[...] = get(zb, core)
    mine_b[...] = get(1 - zb, core)
    theirs[0:rows, :] = get(zb, 1 - core)
    theirs[rows:, :] = get(1 - zb, 1 - core)


def back_one_body(
    share, flag_ref, e_mine, e_other, pm_ref, kv_ref, keys_ref, own_ref, q_ref, gp_ref, d_ref, wk_ref, wq_ref, sc_ref,
    z_ref, mine_a, mine_b, theirs, query_out, frk_ref, frq_ref, work_ref,
):
    rows = own_ref.shape[0]
    e = e_mine[...] + e_other[...]
    query_grad, query_frames, key_frames = backward(
        flag_ref, e, e[:, 128:256], pm_ref[1], kv_ref, keys_ref[:, FRAME_LANE : FRAME_LANE + 128],
        own_ref[:, FRAME_LANE : FRAME_LANE + 128], 0, q_ref, gp_ref[...], d_ref, wk_ref, wq_ref, sc_ref[0:1, :], 12,
        share, z_ref, work_ref,
    )
    query_out[...] = query_grad
    frq_ref[...] = query_frames
    frk_ref[...] = key_frames
    send_blocks(flag_ref, work_ref, mine_a, mine_b, theirs, rows)


def back_zero_body(
    share, flag_ref, cot_ref, r0, r1, r2, r3, r4, r5, e_mine, e_other, pm_ref, kv_ref, keys_ref, own_ref, q_ref, pair_ref,
    w_out_ref, wk_ref, wq_ref, sc_ref, frk_ref, frq_ref,
    z_ref, mine_a, mine_b, theirs, query_out, sum_ref, pu_ref, work_ref, gp_ref, d_ref,
):
    rows = own_ref.shape[0]
    total = (r0[...] + r1[...]) + (r2[...] + r3[...]) + (r4[...] + r5[...])
    sum_ref[...] = total
    upstream_parts(cot_ref[...] + total, w_out_ref, gp_ref, pu_ref, rows)
    pair_products(pu_ref, pair_ref, d_ref, rows)
    gp = gp_ref[...]
    e = e_mine[:, 0:384] + e_other[:, 0:384]
    plain = e_mine[:, 384:640] + e_other[:, 384:640]
    dots = head_dots(gp[:, 0:256] * plain, rows)
    wide = jnp.concatenate(
        [
            pu_ref[h * rows : (h + 1) * rows, :]
            * (e_mine[:, 640 + CZ * h : 640 + CZ * (h + 1)] + e_other[:, 640 + CZ * h : 640 + CZ * (h + 1)])
            for h in range(H)
        ],
        axis=1,
    )
    dots = dots + mm2(wide, lane_matrix(H * CZ, lambda r: STAT + (r >> 7)))
    query_grad, query_frames, key_frames = backward(
        flag_ref, e, dots, pm_ref[0], kv_ref, keys_ref[:, FRAME_LANE : FRAME_LANE + 128],
        own_ref[:, FRAME_LANE : FRAME_LANE + 128], 12, q_ref, gp, d_ref, wk_ref, wq_ref, sc_ref[0:1, :], 0,
        share, z_ref, work_ref,
    )
    query_out[:, 0:C] = query_grad
    query_out[:, C:] = query_frames + frq_ref[...]
    work_ref[:, C:] = key_frames + frk_ref[...]
    send_blocks(flag_ref, work_ref, mine_a, mine_b, theirs, rows)


def pair_body(z1_ref, z0_ref, pu1_ref, pu0_ref, wbt_ref, out_ref):
    rows = out_ref.shape[0]
    wbt = wbt_ref[...].astype(F32)
    for i in range(rows):
        left = jnp.concatenate(
            [z1_ref[pl.ds(i, 2 * H, stride=rows), :], z0_ref[pl.ds(i, 2 * H, stride=rows), :]], axis=0
        )
        right = jnp.concatenate(
            [pu1_ref[pl.ds(i, H, stride=rows), :], wbt, pu0_ref[pl.ds(i, H, stride=rows), :], wbt], axis=0
        ).astype(BF16)
        out_ref[i] = mm(left.astype(BF16), right, TN).astype(BF16)


VMEM = pl.BlockSpec(memory_space=pltpu.VMEM)
SMEM = pl.BlockSpec(memory_space=pltpu.SMEM)


def call(body, name, in_specs, outs, args, scratch=()):
    return pl.pallas_call(
        body,
        name=name,
        in_specs=in_specs,
        out_specs=tuple(VMEM for _ in outs),
        out_shape=tuple(jax.ShapeDtypeStruct(s, d) for s, d in outs),
        scratch_shapes=list(scratch),
        compiler_params=pltpu.CompilerParams(vmem_limit_bytes=32 * 1024 * 1024),
    )(*args)


def joint(pairs):
    return [
        ((a * 2 + k) * 2 + x, (b * 2 + k) * 2 + y) for (x, a), (y, b) in pairs for k in range(2)
    ]


BOTH = ("row", "col")
FETCH_ONE = joint([((0, 0), (0, 1)), ((0, 1), (0, 0)), ((1, 0), (0, 2)), ((1, 1), (0, 3)), ((1, 2), (1, 3)), ((1, 3), (1, 2)), ((0, 2), (1, 0)), ((0, 3), (1, 1))])
FETCH_TWO = joint([((0, 0), (0, 3)), ((0, 1), (0, 2)), ((1, 2), (1, 1)), ((1, 3), (1, 0))])
SCATTER = [
    joint([((x, z), (((s ^ z) >> 1) & 1, 2 * x + ((s ^ z) & 1))) for x in range(2) for z in range(4)])
    for s in range(4)
]
CORE_SWAP = [(i, i ^ 1) for i in range(8)]
COL_SWAP = [(0, 1), (1, 0)]


def local(
    single, frames, saved_probs, pair, cotangent, chains, links, w_query, w_key, w_value, w_query_points,
    w_key_points, w_value_points, w_bias, w_out, head_weights,
):
    rows = single.shape[1]
    keys = pair.shape[1]
    row_total = lax.axis_size("row")
    col_total = lax.axis_size("col")
    fast = row_total == 8 and col_total == 2 and keys == 4 * rows
    small = jnp.concatenate([frames[1], frames[0], chains[None].astype(F32)], axis=0)
    pack = jnp.concatenate(
        [single[1], single[0], small.T, jnp.zeros((rows, PACK - CHAIN_LANE - 1), F32)], axis=1
    )
    col = lax.axis_index("col")
    row = lax.axis_index("row")
    if fast:
        home = (row // 4 == col).astype(jnp.int32)
        flags = jnp.stack([home, (row // 2) % 2, row % 2])
        ownx = lax.ppermute(pack, "row", CORE_SWAP)
        one = lax.ppermute(pack, BOTH, FETCH_ONE)
        two = lax.ppermute(pack, BOTH, FETCH_TWO)
        blocks = (pack, ownx, one, lax.ppermute(one, "row", CORE_SWAP), two, lax.ppermute(two, "row", CORE_SWAP))
        own = pack
    else:
        flags = jnp.array([1, 0, 0], jnp.int32)
        whole = lax.all_gather(pack, "row", axis=0, tiled=True)
        mine = lax.dynamic_slice_in_dim(whole, col * keys, keys, 0)
        quarter = keys // 4
        blocks = tuple(mine[quarter * n : quarter * (n + 1)] for n in (0, 1, 2, 3, 0, 0))
        own = pack

    def col_other(x):
        if col_total == 2:
            return lax.ppermute(x, "col", COL_SWAP)
        return lax.psum(x, "col") - x

    def reduce(mine_a, mine_b, theirs, query):
        if fast:
            query_other = lax.ppermute(query, "col", COL_SWAP)
            got = lax.ppermute(theirs, "row", CORE_SWAP)
            part = (mine_a + got[:rows], mine_b + got[rows:])
            return [query, query_other] + [lax.ppermute(part[s & 1], BOTH, SCATTER[s]) for s in range(4)]
        parts = jnp.concatenate([mine_a, theirs[:rows], mine_b, theirs[rows:]], axis=0)
        summed = lax.all_gather(lax.psum(parts, "row"), "col", axis=0, tiled=True)
        zero = jnp.zeros_like(query)
        back = lax.dynamic_slice_in_dim(summed, row * rows, rows, 0)
        return [lax.psum(query, "col"), back, zero, zero, zero, zero]

    probs = saved_probs.reshape(2, H * rows, keys)
    hr = H * rows
    wk, wq, gp1, q1, q0, pu1, d1, sc = call(
        prep_body, "prep", [SMEM] + [VMEM] * 10,
        [((C, 1280), BF16), ((C, LANES), BF16), ((rows, 768), F32), ((rows, 1024), F32), ((rows, 1024), F32),
         ((hr, CZ), F32), ((hr, keys), F32), ((8, 128), F32)],
        (head_weights, own, cotangent, w_query, w_key, w_value, w_query_points, w_key_points, w_value_points, w_out, pair),
    )
    key_pack, kv1, pm, e1 = call(
        first_body, "first", [SMEM] + [VMEM] * 11,
        [((keys, PACK), F32), ((keys, 2048), F32), ((2, hr, keys), BF16), ((rows, 384), F32)],
        (flags, *blocks, wk, links, probs, gp1, d1),
    )
    e1_other = col_other(e1)
    kv0, e0 = call(
        second_body, "second", [VMEM] * 4,
        [((keys, 2048), F32), ((rows, 640 + H * CZ), F32)],
        (key_pack, wk, pm, pair),
        [pltpu.VMEM((hr, keys), F32), pltpu.VMEM((hr, CZ), F32)],
    )
    e0_other = col_other(e0)
    z1, mine_a, mine_b, theirs, query, frk, frq = call(
        functools.partial(back_one_body, 1.0 / col_total), "back_one", [SMEM] + [VMEM] * 12,
        [((2 * hr, keys), F32), ((rows, C), F32), ((rows, C), F32), ((2 * rows, C), F32), ((rows, C), F32),
         ((keys, 128), F32), ((rows, 128), F32)],
        (flags, e1, e1_other, pm, kv1, key_pack, own, q1, gp1, d1, wk, wq, sc),
        [pltpu.VMEM((keys, C), F32)],
    )
    pieces = reduce(mine_a, mine_b, theirs, query)
    z0, mine_a, mine_b, theirs, query, single_one, pu0 = call(
        functools.partial(back_zero_body, 1.0 / col_total), "back_zero", [SMEM] + [VMEM] * 21,
        [((2 * hr, keys), F32), ((rows, 512), F32), ((rows, 512), F32), ((2 * rows, 512), F32), ((rows, 512), F32),
         ((rows, C), F32), ((hr, CZ), F32)],
        (flags, cotangent, *pieces, e0, e0_other, pm, kv0, key_pack, own, q0, pair, w_out, wk, wq, sc, frk, frq),
        [pltpu.VMEM((keys, 512), F32), pltpu.VMEM((rows, 768), F32), pltpu.VMEM((hr, keys), F32)],
    )
    pieces = reduce(mine_a, mine_b, theirs, query)
    (d_pair,) = call(
        pair_body, "pair_grad", [VMEM] * 5, [((rows, keys, CZ), BF16)], (z1, z0, pu1, pu0, w_bias.T)
    )
    total = sum(pieces)
    d_frames = total[:, C : C + 24].T.reshape(2, 12, rows)
    return (single_one + total[:, :C], d_frames, d_pair)


def solution(mesh):
    return jax.shard_map(
        local,
        mesh=mesh,
        in_specs=(
            P(None, ("grp", "row"), None),
            P(None, None, ("grp", "row")),
            P(None, None, ("grp", "row"), "col"),
            P(("grp", "row"), "col", None),
            P(("grp", "row"), None),
            P(("grp", "row")),
            P("grp", None),
            P(),
            P(),
            P(),
            P(),
            P(),
            P(),
            P(),
            P(),
            P(),
        ),
        out_specs=(
            P(("grp", "row"), None),
            P(None, None, ("grp", "row")),
            P(("grp", "row"), "col", None),
        ),
        check_vma=False,
    )
```

profile of v0, /device:TPU:0, one launch (start us, length us, event | category | flops | bytes accessed | tf_op | source)
XLA Modules:
  0.0 83.3 jit_solution(11939763981638428793)
XLA Ops:
  0.7 0.8 convert_bitcast_fusion
  1.5 0.8 fusion
  2.3 0.1 copy.42
  2.4 0.1 copy.31
  2.5 0.1 copy.43
  2.5 0.8 slice_bitcast_fusion.1
  3.4 0.1 pad.3.clone
  3.5 0.1 maximum_bitcast_fusion
  3.6 7.6 %collective-permute-start.3 = (f32[32,896]{1,0:T(8,128)S(1)}, f32[32,896]{1,0:T(8,128)}, u32[]{:S(2)}, u32[]{:S(2)}) collective-permute-start(f32[32,896]{1,0:T(8,128)S(1)} %maximum_maximum_fusion.pack_ref.own_ref), channel_id=1, source_target_pairs={{0,12},{2,14},{4,8},{6,10},{9,5},{11,7},{13,1},{15,3},{16,28},{18,... | collective-permute-start | bytes 344072 | tf_op jit(solution)/shard_map/ppermute | solution.py:457
  11.2 0.0 collective-permute-start.1
  11.2 0.0 collective-permute-start
  11.2 2.9 %collective-permute-done.3.p2_ref = f32[32,896]{1,0:T(8,128)} collective-permute-done((f32[32,896]{1,0:T(8,128)S(1)}, f32[32,896]{1,0:T(8,128)}, u32[]{:S(2)}, u32[]{:S(2)}) %collective-permute-start.3) | collective-permute-done | bytes 114720 | tf_op jit(solution)/shard_map/ppermute | solution.py:457
  14.1 0.0 collective-permute-start.4
  14.1 3.2 %collective-permute-done.1.p1_ref = f32[32,896]{1,0:T(8,128)} collective-permute-done((f32[32,896]{1,0:T(8,128)S(1)}, f32[32,896]{1,0:T(8,128)}, u32[]{:S(2)}, u32[]{:S(2)}) %collective-permute-start.1) | collective-permute-done | bytes 114720 | tf_op jit(solution)/shard_map/ppermute | solution.py:456
  17.2 0.0 collective-permute-start.2
  17.2 1.7 %copy.32.wq_ref = bf16[384,192]{1,0:T(8,128)(2,1)} copy(bf16[384,192]{0,1:T(8,128)(2,1)} %param.23) | data formatting | bytes 294912 | tf_op args[7]
  18.9 1.7 %copy.33.wk_ref = bf16[384,192]{1,0:T(8,128)(2,1)} copy(bf16[384,192]{0,1:T(8,128)(2,1)} %param.24) | data formatting | bytes 294912 | tf_op args[8]
  20.7 1.7 %copy.34.wv_ref = bf16[384,192]{1,0:T(8,128)(2,1)} copy(bf16[384,192]{0,1:T(8,128)(2,1)} %param.25) | data formatting | bytes 294912 | tf_op args[9]
  22.4 0.1 copy.35.wqp_ref
  22.6 1.0 %copy.36.wkp_ref = bf16[384,144]{1,0:T(8,128)(2,1)S(1)} copy(bf16[384,144]{0,1:T(8,128)(2,1)} %param.27) | data formatting | bytes 221184 | tf_op args[11]
  23.6 1.1 %copy.37.wvp_ref = bf16[384,288]{1,0:T(8,128)(2,1)S(1)} copy(bf16[384,288]{0,1:T(8,128)(2,1)} %param.28) | data formatting | bytes 442368 | tf_op args[12]
  24.8 0.0 copy-start.2
  24.8 0.9 %copy-done.2 = bf16[384,192]{1,0:T(8,128)(2,1)S(1)} copy-done((bf16[384,192]{1,0:T(8,128)(2,1)S(1)}, bf16[384,192]{1,0:T(8,128)(2,1)}, u32[]{:S(2)}) %copy-start.2) | copy-done | bytes 147480
  25.7 0.9 %copy-done.3 = bf16[384,192]{1,0:T(8,128)(2,1)S(1)} copy-done((bf16[384,192]{1,0:T(8,128)(2,1)S(1)}, bf16[384,192]{1,0:T(8,128)(2,1)}, u32[]{:S(2)}) %copy-start.3) | copy-done | bytes 147480
  26.7 0.9 %copy-done.4 = bf16[384,192]{1,0:T(8,128)(2,1)S(1)} copy-done((bf16[384,192]{1,0:T(8,128)(2,1)S(1)}, bf16[384,192]{1,0:T(8,128)(2,1)}, u32[]{:S(2)}) %copy-start.4) | copy-done | bytes 147480
  27.6 2.2 %prep.1 = (bf16[384,1280]{1,0:T(8,128)(2,1)S(1)}, bf16[384,640]{1,0:T(8,128)(2,1)S(1)}, f32[32,768]{1,0:T(8,128)S(1)}, f32[32,1024]{1,0:T(8,128)S(1)}, f32[32,10...) custom-call(f32[12]{0:T(128)S(1)} %copy-done.9, ...), custom_call_target="tpu_custom_call" | custom-call | tf_op jit(solution)/shard_map/prep/pallas_call | solution.py:409
  29.8 0.1 pad_add_fusion.flag_ref
  29.8 0.0 collective-permute-done.ownx_ref
  29.8 0.0 collective-permute-done.4.p2x_ref
  29.9 0.0 collective-permute-done.2.p1x_ref
  29.9 2.3 %first.1 = (f32[128,896]{1,0:T(8,128)S(1)}, f32[128,2048]{1,0:T(8,128)S(1)}, bf16[2,384,128]{2,1,0:T(8,128)(2,1)S(1)}, f32[32,384]{1,0:T(8,128)S(1)}) custom-call(s32[3]{0:T(128)S(1)} %pad_add_fusion.flag_ref, f32[32,896]{1,0:T(8,128)S(1)} %maximum_maximum_fusion.pack_ref.own_ref, f32[32,896]{1,0:T(8,128)} %collective-permute-done.ownx_ref, ...), custom_call_target="tpu_custom_call" | custom-call | tf_op jit(solution)/shard_map/first/pallas_call | solution.py:409
  32.2 0.1 collective-permute-start.5
  32.3 4.1 %collective-permute-done.5.e_other = f32[32,384]{1,0:T(8,128)S(1)} collective-permute-done((f32[32,384]{1,0:T(8,128)S(1)}, f32[32,384]{1,0:T(8,128)S(1)}, u32[]{:S(2)}, u32[]{:S(2)}) %collective-permute-start.5) | collective-permute-done | bytes 49184 | tf_op jit(solution)/shard_map/ppermute | solution.py:470
  36.4 3.6 %back_one.1 = (f32[768,128]{1,0:T(8,128)S(1)}, f32[32,384]{1,0:T(8,128)S(1)}, f32[32,384]{1,0:T(8,128)S(1)}, f32[64,384]{1,0:T(8,128)S(1)}, f32[32,384]{1,0:T(8,...) custom-call(s32[3]{0:T(128)S(1)} %pad_add_fusion.flag_ref, f32[32,384]{1,0:T(8,128)S(1)} %get-tuple-element.34.e_mine, ...), custom_call_target="tpu_custom_call" | custom-call | tf_op jit(solution)/shard_map/back_one/pallas_call | solution.py:409
  40.1 0.1 collective-permute-start.7
  40.2 1.3 %second.1 = (f32[128,2048]{1,0:T(8,128)S(1)}, f32[32,2176]{1,0:T(8,128)S(1)}) custom-call(f32[128,896]{1,0:T(8,128)S(1)} %get-tuple-element.37.keys_ref, bf16[384,1280]{1,0:T(8,128)(2,1)S(1)} %get-tuple-element.31.wk_ref, bf16[2,384,128]{2,1,0:T(8,128)(2,1)S(1)} %get-tuple-element.35.pm_ref, bf16[32,128,128]{2,1,0:T(8,128)(2,1)S(1)} %copy-done), custom_call_target="tpu_custom_call" | custom-call | tf_op jit(solution)/shard_map/second/pallas_call | solution.py:409
  41.4 0.3 collective-permute-start.12
  41.8 1.7 %collective-permute-start.6 = (f32[32,384]{1,0:T(8,128)S(1)}, f32[32,384]{1,0:T(8,128)S(1)}, u32[]{:S(2)}, u32[]{:S(2)}) collective-permute-start(f32[32,384]{1,0:T(8,128)S(1)} %get-tuple-element.41.r0), channel_id=1, source_target_pairs={{0,1},{1,0},{2,3},{3,2},{4,5},{5,4},{6,7},{7,6},{8,9},{9,8},{10,11... | collective-permute-start | bytes 147464 | tf_op jit(solution)/shard_map/ppermute | solution.py:475
  43.5 0.0 collective-permute-done.7
  43.6 0.5 collective-permute-start.11
  44.1 1.3 %collective-permute-start.9 = (f32[32,384]{1,0:T(8,128)S(1)}, f32[32,384]{1,0:T(8,128)S(1)}, u32[]{:S(2)}, u32[]{:S(2)}) collective-permute-start(f32[32,384]{1,0:T(8,128)S(1)} %get-tuple-element.67), channel_id=1, source_target_pairs={{0,4},{2,6},{4,0},{6,2},{8,5},{10,7},{12,1},{14,3},{1,12},{3,14},{... | collective-permute-start | bytes 147464 | tf_op jit(solution)/shard_map/ppermute | solution.py:478
  45.4 3.5 %collective-permute-start.10 = (f32[32,384]{1,0:T(8,128)S(1)}, f32[32,384]{1,0:T(8,128)S(1)}, u32[]{:S(2)}, u32[]{:S(2)}) collective-permute-start(f32[32,384]{1,0:T(8,128)S(1)} %get-tuple-element.68), channel_id=1, source_target_pairs={{0,1},{2,3},{4,5},{6,7},{8,0},{10,2},{12,4},{14,6},{1,9},{3,11},{5... | collective-permute-start | bytes 147464 | tf_op jit(solution)/shard_map/ppermute | solution.py:478
  48.9 3.0 %collective-permute-done.6.r1 = f32[32,384]{1,0:T(8,128)S(1)} collective-permute-done((f32[32,384]{1,0:T(8,128)S(1)}, f32[32,384]{1,0:T(8,128)S(1)}, u32[]{:S(2)}, u32[]{:S(2)}) %collective-permute-start.6) | collective-permute-done | bytes 49184 | tf_op jit(solution)/shard_map/ppermute | solution.py:475
  51.9 0.7 collective-permute-start.8
  52.6 0.0 collective-permute-done.11.r5
  52.6 0.0 collective-permute-done.9.r3
  52.6 0.1 collective-permute-done.10.r4
  52.7 0.0 collective-permute-done.8.r2
  52.7 5.0 %back_zero.1 = (f32[768,128]{1,0:T(8,128)S(1)}, f32[32,512]{1,0:T(8,128)S(1)}, f32[32,512]{1,0:T(8,128)S(1)}, f32[64,512]{1,0:T(8,128)S(1)}, f32[32,512]{1,0:T(8...) custom-call(s32[3]{0:T(128)S(1)} %pad_add_fusion.flag_ref, f32[32,384]{1,0:T(8,128)S(1)} %copy-done.5, ...), custom_call_target="tpu_custom_call" | custom-call | tf_op jit(solution)/shard_map/back_zero/pallas_call | solution.py:409
  57.7 0.1 collective-permute-start.14
  57.8 10.1 %collective-permute-start.13 = (f32[32,512]{1,0:T(8,128)S(1)}, f32[32,512]{1,0:T(8,128)S(1)}, u32[]{:S(2)}, u32[]{:S(2)}) collective-permute-start(f32[32,512]{1,0:T(8,128)S(1)} %get-tuple-element.51), channel_id=1, source_target_pairs={{0,1},{1,0},{2,3},{3,2},{4,5},{5,4},{6,7},{7,6},{8,9},{9,8},{10,11... | collective-permute-start | bytes 196616 | tf_op jit(solution)/shard_map/ppermute | solution.py:475
  67.9 1.3 %collective-permute-start.17 = (f32[32,512]{1,0:T(8,128)S(1)}, f32[32,512]{1,0:T(8,128)S(1)}, u32[]{:S(2)}, u32[]{:S(2)}) collective-permute-start(f32[32,512]{1,0:T(8,128)S(1)} %get-tuple-element.65), channel_id=1, source_target_pairs={{0,1},{2,3},{4,5},{6,7},{8,0},{10,2},{12,4},{14,6},{1,9},{3,11},{5... | collective-permute-start | bytes 196616 | tf_op jit(solution)/shard_map/ppermute | solution.py:478
  69.2 0.7 collective-permute-start.15
  69.9 4.2 %collective-permute-start.18 = (f32[32,512]{1,0:T(8,128)S(1)}, f32[32,512]{1,0:T(8,128)S(1)}, u32[]{:S(2)}, u32[]{:S(2)}) collective-permute-start(f32[32,512]{1,0:T(8,128)S(1)} %get-tuple-element.66), channel_id=1, source_target_pairs={{0,5},{2,7},{4,1},{6,3},{8,4},{10,6},{12,0},{14,2},{1,13},{3,15},{... | collective-permute-start | bytes 196616 | tf_op jit(solution)/shard_map/ppermute | solution.py:478
  74.1 1.7 %collective-permute-start.16 = (f32[32,512]{1,0:T(8,128)S(1)}, f32[32,512]{1,0:T(8,128)S(1)}, u32[]{:S(2)}, u32[]{:S(2)}) collective-permute-start(f32[32,512]{1,0:T(8,128)S(1)} %get-tuple-element.66), channel_id=1, source_target_pairs={{0,4},{2,6},{4,0},{6,2},{8,5},{10,7},{12,1},{14,3},{1,12},{3,14},{... | collective-permute-start | bytes 196616 | tf_op jit(solution)/shard_map/ppermute | solution.py:478
  75.8 1.9 %pair_grad.1 = bf16[32,128,128]{2,1,0:T(8,128)(2,1)} custom-call(f32[768,128]{1,0:T(8,128)S(1)} %get-tuple-element.55.z1_ref, f32[768,128]{1,0:T(8,128)S(1)} %get-tuple-element.56.z0_ref, f32[384,128]{1,0:T(8,128)S(1)} %get-tuple-element.57.pu1_ref, f32[384,128]{1,0:T(8,128)S(1)} %get-tuple-element.58.pu0_ref, bf16[12,128]{1,0:T(8,128)(2,1)S(1)} %bitcast.20), custom_call_target="tpu_custom_call" | custom-call | tf_op jit(solution)/shard_map/pair_grad/pallas_call | solution.py:409
  77.7 0.0 collective-permute-done.13
  77.7 0.0 collective-permute-done.17
  77.7 0.0 collective-permute-done.15
  77.7 1.8 %collective-permute-done.18 = f32[32,512]{1,0:T(8,128)S(1)} collective-permute-done((f32[32,512]{1,0:T(8,128)S(1)}, f32[32,512]{1,0:T(8,128)S(1)}, u32[]{:S(2)}, u32[]{:S(2)}) %collective-permute-start.18) | collective-permute-done | bytes 65568 | tf_op jit(solution)/shard_map/ppermute | solution.py:478
  79.5 2.3 %collective-permute-done.16 = f32[32,512]{1,0:T(8,128)S(1)} collective-permute-done((f32[32,512]{1,0:T(8,128)S(1)}, f32[32,512]{1,0:T(8,128)S(1)}, u32[]{:S(2)}, u32[]{:S(2)}) %collective-permute-start.16) | collective-permute-done | bytes 65568 | tf_op jit(solution)/shard_map/ppermute | solution.py:478
  81.9 0.6 slice_add_fusion.2
  82.5 0.1 reshape.16
  82.6 0.7 copy.39
  (26 shorter events, 0.1 us)
Async XLA Ops:
  0.6 21.8 %copy-start.10 = (bf16[384,144]{0,1:T(8,128)(2,1)S(1)}, bf16[384,144]{0,1:T(8,128)(2,1)}, u32[]{:S(2)}) copy-start(bf16[384,144]{0,1:T(8,128)(2,1)} %param.26) | copy-start | bytes 331780
  0.6 24.1 %copy-start = (bf16[32,128,128]{2,1,0:T(8,128)(2,1)S(1)}, bf16[32,128,128]{2,1,0:T(8,128)(2,1)}, u32[]{:S(2)}) copy-start(bf16[32,128,128]{2,1,0:T(8,128)(2,1)} %pair_ref.5) | copy-start | bytes 3145732
  0.7 24.1 %copy-start.1 = (bf16[2112,384]{1,0:T(8,128)(2,1)S(1)}, bf16[2112,384]{1,0:T(8,128)(2,1)}, u32[]{:S(2)}) copy-start(bf16[2112,384]{1,0:T(8,128)(2,1)} %w_out_ref.3) | copy-start | bytes 4866052
  0.7 24.1 %copy-start.5 = (f32[32,384]{1,0:T(8,128)S(1)}, f32[32,384]{1,0:T(8,128)}, u32[]{:S(2)}) copy-start(f32[32,384]{1,0:T(8,128)} %cot_ref.3) | copy-start | bytes 147460
  0.7 24.1 %copy-start.9 = (f32[12]{0:T(128)S(1)}, f32[12]{0:T(128)}, u32[]{:S(2)}) copy-start(f32[12]{0:T(128)} %hw_ref.1) | copy-start | bytes 148
  3.6 10.5 %collective-permute-start.3 = (f32[32,896]{1,0:T(8,128)S(1)}, f32[32,896]{1,0:T(8,128)}, u32[]{:S(2)}, u32[]{:S(2)}) collective-permute-start(f32[32,896]{1,0:T(8,128)S(1)} %maximum_maximum_fusion.pack_ref.own_ref), channel_id=1, source_target_pairs={{0,12},{2,14},{4,8},{6,10},{9,5},{11,7},{13,1},{15,3},{16,28},{18,... | collective-permute-start | bytes 344072 | tf_op jit(solution)/shard_map/ppermute | solution.py:457
  11.2 6.1 %collective-permute-start.1 = (f32[32,896]{1,0:T(8,128)S(1)}, f32[32,896]{1,0:T(8,128)}, u32[]{:S(2)}, u32[]{:S(2)}) collective-permute-start(f32[32,896]{1,0:T(8,128)S(1)} %maximum_maximum_fusion.pack_ref.own_ref), channel_id=1, source_target_pairs={{0,4},{2,6},{4,0},{6,2},{1,8},{3,10},{5,12},{7,14},{9,13},{11,15},... | collective-permute-start | bytes 344072 | tf_op jit(solution)/shard_map/ppermute | solution.py:456
  11.2 18.7 %collective-permute-start = (f32[32,896]{1,0:T(8,128)S(1)}, f32[32,896]{1,0:T(8,128)}, u32[]{:S(2)}, u32[]{:S(2)}) collective-permute-start(f32[32,896]{1,0:T(8,128)S(1)} %maximum_maximum_fusion.pack_ref.own_ref), channel_id=1, source_target_pairs={{0,2},{2,0},{4,6},{6,4},{8,10},{10,8},{12,14},{14,12},{1,3},{3,1},... | collective-permute-start | bytes 344072 | tf_op jit(solution)/shard_map/ppermute | solution.py:455
  14.1 15.8 %collective-permute-start.4 = (f32[32,896]{1,0:T(8,128)}, f32[32,896]{1,0:T(8,128)}, u32[]{:S(2)}, u32[]{:S(2)}) collective-permute-start(f32[32,896]{1,0:T(8,128)} %collective-permute-done.3.p2_ref), channel_id=1, source_target_pairs={{0,2},{2,0},{4,6},{6,4},{8,10},{10,8},{12,14},{14,12},{1,3},{3,1},... | collective-permute-start | bytes 344072 | tf_op jit(solution)/shard_map/ppermute | solution.py:458
  17.2 12.6 %collective-permute-start.2 = (f32[32,896]{1,0:T(8,128)}, f32[32,896]{1,0:T(8,128)}, u32[]{:S(2)}, u32[]{:S(2)}) collective-permute-start(f32[32,896]{1,0:T(8,128)} %collective-permute-done.1.p1_ref), channel_id=1, source_target_pairs={{0,2},{2,0},{4,6},{6,4},{8,10},{10,8},{12,14},{14,12},{1,3},{3,1},... | collective-permute-start | bytes 344072 | tf_op jit(solution)/shard_map/ppermute | solution.py:458
  24.8 0.9 %copy-start.2 = (bf16[384,192]{1,0:T(8,128)(2,1)S(1)}, bf16[384,192]{1,0:T(8,128)(2,1)}, u32[]{:S(2)}) copy-start(bf16[384,192]{1,0:T(8,128)(2,1)} %copy.32.wq_ref) | copy-start | bytes 442372
  25.7 0.9 %copy-start.3 = (bf16[384,192]{1,0:T(8,128)(2,1)S(1)}, bf16[384,192]{1,0:T(8,128)(2,1)}, u32[]{:S(2)}) copy-start(bf16[384,192]{1,0:T(8,128)(2,1)} %copy.33.wk_ref) | copy-start | bytes 442372
  26.7 0.9 %copy-start.4 = (bf16[384,192]{1,0:T(8,128)(2,1)S(1)}, bf16[384,192]{1,0:T(8,128)(2,1)}, u32[]{:S(2)}) copy-start(bf16[384,192]{1,0:T(8,128)(2,1)} %copy.34.wv_ref) | copy-start | bytes 442372
  27.6 2.3 %copy-start.6 = (bf16[2,12,32,128]{3,2,1,0:T(8,128)(2,1)S(1)}, bf16[2,12,32,128]{3,2,1,0:T(8,128)(2,1)}, u32[]{:S(2)}) copy-start(bf16[2,12,32,128]{3,2,1,0:T(8,128)(2,1)} %param.18) | copy-start | bytes 589828
  27.6 2.3 %copy-start.7 = (s32[16,16]{1,0:T(8,128)S(1)}, s32[16,16]{1,0:T(8,128)}, u32[]{:S(2)}) copy-start(s32[16,16]{1,0:T(8,128)} %links_ref.1) | copy-start | bytes 3076
  32.2 4.2 %collective-permute-start.5 = (f32[32,384]{1,0:T(8,128)S(1)}, f32[32,384]{1,0:T(8,128)S(1)}, u32[]{:S(2)}, u32[]{:S(2)}) collective-permute-start(f32[32,384]{1,0:T(8,128)S(1)} %get-tuple-element.34.e_mine), channel_id=1, source_target_pairs={{0,1},{1,0},{2,3},{3,2},{4,5},{5,4},{6,7},{7,6},{8,9},{9,8},{10,11... | collective-permute-start | bytes 147464 | tf_op jit(solution)/shard_map/ppermute | solution.py:470
  40.1 3.4 %collective-permute-start.7 = (f32[64,384]{1,0:T(8,128)S(1)}, f32[64,384]{1,0:T(8,128)S(1)}, u32[]{:S(2)}, u32[]{:S(2)}) collective-permute-start(f32[64,384]{1,0:T(8,128)S(1)} %get-tuple-element.43), channel_id=1, source_target_pairs={{0,2},{2,0},{4,6},{6,4},{8,10},{10,8},{12,14},{14,12},{1,3},{3,1},... | collective-permute-start | bytes 294920 | tf_op jit(solution)/shard_map/ppermute | solution.py:476
  41.4 11.2 %collective-permute-start.12 = (f32[32,2176]{1,0:T(8,128)S(1)}, f32[32,2176]{1,0:T(8,128)S(1)}, u32[]{:S(2)}, u32[]{:S(2)}) collective-permute-start(f32[32,2176]{1,0:T(8,128)S(1)} %get-tuple-element.45.e_mine), channel_id=1, source_target_pairs={{0,1},{1,0},{2,3},{3,2},{4,5},{5,4},{6,7},{7,6},{8,9},{9,8},{10,11... | collective-permute-start | bytes 835592 | tf_op jit(solution)/shard_map/ppermute | solution.py:470
  41.8 10.1 %collective-permute-start.6 = (f32[32,384]{1,0:T(8,128)S(1)}, f32[32,384]{1,0:T(8,128)S(1)}, u32[]{:S(2)}, u32[]{:S(2)}) collective-permute-start(f32[32,384]{1,0:T(8,128)S(1)} %get-tuple-element.41.r0), channel_id=1, source_target_pairs={{0,1},{1,0},{2,3},{3,2},{4,5},{5,4},{6,7},{7,6},{8,9},{9,8},{10,11... | collective-permute-start | bytes 147464 | tf_op jit(solution)/shard_map/ppermute | solution.py:475
  43.6 9.0 %collective-permute-start.11 = (f32[32,384]{1,0:T(8,128)S(1)}, f32[32,384]{1,0:T(8,128)S(1)}, u32[]{:S(2)}, u32[]{:S(2)}) collective-permute-start(f32[32,384]{1,0:T(8,128)S(1)} %get-tuple-element.67), channel_id=1, source_target_pairs={{0,5},{2,7},{4,1},{6,3},{8,4},{10,6},{12,0},{14,2},{1,13},{3,15},{... | collective-permute-start | bytes 147464 | tf_op jit(solution)/shard_map/ppermute | solution.py:478
  44.1 8.5 %collective-permute-start.9 = (f32[32,384]{1,0:T(8,128)S(1)}, f32[32,384]{1,0:T(8,128)S(1)}, u32[]{:S(2)}, u32[]{:S(2)}) collective-permute-start(f32[32,384]{1,0:T(8,128)S(1)} %get-tuple-element.67), channel_id=1, source_target_pairs={{0,4},{2,6},{4,0},{6,2},{8,5},{10,7},{12,1},{14,3},{1,12},{3,14},{... | collective-permute-start | bytes 147464 | tf_op jit(solution)/shard_map/ppermute | solution.py:478
  45.4 7.3 %collective-permute-start.10 = (f32[32,384]{1,0:T(8,128)S(1)}, f32[32,384]{1,0:T(8,128)S(1)}, u32[]{:S(2)}, u32[]{:S(2)}) collective-permute-start(f32[32,384]{1,0:T(8,128)S(1)} %get-tuple-element.68), channel_id=1, source_target_pairs={{0,1},{2,3},{4,5},{6,7},{8,0},{10,2},{12,4},{14,6},{1,9},{3,11},{5... | collective-permute-start | bytes 147464 | tf_op jit(solution)/shard_map/ppermute | solution.py:478
  51.9 0.7 collective-permute-start.8
  52.7 23.1 %copy-start.8 = (bf16[128,12]{0,1:T(8,128)(2,1)S(1)}, bf16[128,12]{0,1:T(8,128)(2,1)}, u32[]{:S(2)}) copy-start(bf16[128,12]{0,1:T(8,128)(2,1)} %param.29) | copy-start | bytes 9220
  57.7 10.2 %collective-permute-start.14 = (f32[64,512]{1,0:T(8,128)S(1)}, f32[64,512]{1,0:T(8,128)S(1)}, u32[]{:S(2)}, u32[]{:S(2)}) collective-permute-start(f32[64,512]{1,0:T(8,128)S(1)} %get-tuple-element.53), channel_id=1, source_target_pairs={{0,2},{2,0},{4,6},{6,4},{8,10},{10,8},{12,14},{14,12},{1,3},{3,1},... | collective-permute-start | bytes 393224 | tf_op jit(solution)/shard_map/ppermute | solution.py:476
  57.8 19.9 %collective-permute-start.13 = (f32[32,512]{1,0:T(8,128)S(1)}, f32[32,512]{1,0:T(8,128)S(1)}, u32[]{:S(2)}, u32[]{:S(2)}) collective-permute-start(f32[32,512]{1,0:T(8,128)S(1)} %get-tuple-element.51), channel_id=1, source_target_pairs={{0,1},{1,0},{2,3},{3,2},{4,5},{5,4},{6,7},{7,6},{8,9},{9,8},{10,11... | collective-permute-start | bytes 196616 | tf_op jit(solution)/shard_map/ppermute | solution.py:475
  67.9 9.8 %collective-permute-start.17 = (f32[32,512]{1,0:T(8,128)S(1)}, f32[32,512]{1,0:T(8,128)S(1)}, u32[]{:S(2)}, u32[]{:S(2)}) collective-permute-start(f32[32,512]{1,0:T(8,128)S(1)} %get-tuple-element.65), channel_id=1, source_target_pairs={{0,1},{2,3},{4,5},{6,7},{8,0},{10,2},{12,4},{14,6},{1,9},{3,11},{5... | collective-permute-start | bytes 196616 | tf_op jit(solution)/shard_map/ppermute | solution.py:478
  69.2 8.5 %collective-permute-start.15 = (f32[32,512]{1,0:T(8,128)S(1)}, f32[32,512]{1,0:T(8,128)S(1)}, u32[]{:S(2)}, u32[]{:S(2)}) collective-permute-start(f32[32,512]{1,0:T(8,128)S(1)} %get-tuple-element.65), channel_id=1, source_target_pairs={{0,0},{2,2},{4,4},{6,6},{8,1},{10,3},{12,5},{14,7},{1,8},{3,10},{5... | collective-permute-start | bytes 196616 | tf_op jit(solution)/shard_map/ppermute | solution.py:478
  69.9 9.6 %collective-permute-start.18 = (f32[32,512]{1,0:T(8,128)S(1)}, f32[32,512]{1,0:T(8,128)S(1)}, u32[]{:S(2)}, u32[]{:S(2)}) collective-permute-start(f32[32,512]{1,0:T(8,128)S(1)} %get-tuple-element.66), channel_id=1, source_target_pairs={{0,5},{2,7},{4,1},{6,3},{8,4},{10,6},{12,0},{14,2},{1,13},{3,15},{... | collective-permute-start | bytes 196616 | tf_op jit(solution)/shard_map/ppermute | solution.py:478
  74.1 7.7 %collective-permute-start.16 = (f32[32,512]{1,0:T(8,128)S(1)}, f32[32,512]{1,0:T(8,128)S(1)}, u32[]{:S(2)}, u32[]{:S(2)}) collective-permute-start(f32[32,512]{1,0:T(8,128)S(1)} %get-tuple-element.66), channel_id=1, source_target_pairs={{0,4},{2,6},{4,0},{6,2},{8,5},{10,7},{12,1},{14,3},{1,12},{3,14},{... | collective-permute-start | bytes 196616 | tf_op jit(solution)/shard_map/ppermute | solution.py:478
where the time goes:
time: 83.7 us; the launch traced here: 83.3 us
  starting transfers between devices  33.9 us (41%)
  waiting for transfers between devices  17.4 us (21%)
  Pallas kernels  16.4 us (20%)
  local copies, waits for them, and re-layouts  13 us (16%)
  other arithmetic  1.67 us (2%)
  between operations  0.93 us (1%)
    pallas_call x6, Pallas kernels, call(): pl.pallas_call(body, name=name, in_specs=in_specs, out_specs=tuple((VMEM...  16.4 us
    ppermute x8, starting transfers between devices, reduce(): lax.ppermute(part[s & 1], BOTH, SCATTER[s])  13.8 us
    ppermute x2, starting transfers between devices, reduce(): query_other = lax.ppermute(query, 'col', COL_SWAP)  11.8 us
    unnamed x31, local copies, waits for them, and re-layouts  11.2 us
    ppermute x1, starting transfers between devices, local(): two = lax.ppermute(pack, BOTH, FETCH_TWO)  7.61 us
    ppermute x8, waiting for transfers between devices, reduce(): lax.ppermute(part[s & 1], BOTH, SCATTER[s])  4.15 us
    ppermute x2, waiting for transfers between devices, col_other(): return lax.ppermute(x, 'col', COL_SWAP)  4.15 us
    ppermute x1, waiting for transfers between devices, local(): one = lax.ppermute(pack, BOTH, FETCH_ONE)  3.17 us
  transfers between devices with their start and end apart: 19, of which 7 were waited for; matrix products, arithmetic and copies ran while one was open for 9% of the time, Pallas kernels for 6%

commit v1 on v0

--- a/solution.py
+++ b/solution.py
@@ -143,22 +143,55 @@
         d_ref[pl.ds(i, H, stride=rows), :] = mm(lhs, pair_ref[i], NT)
 
 
+def split3(x):
+    hi, _ = split(x)
+    rest = x - hi.astype(F32)
+    mid, lo = split(rest)
+    return hi, mid, lo
+
+
+def pack_body(single_ref, frames_ref, chains_ref, pack_ref):
+    rows = pack_ref.shape[0]
+    pack_ref[:, 0:C] = single_ref[1]
+    pack_ref[:, C : 2 * C] = single_ref[0]
+    out = jnp.zeros((rows, 128), F32)
+    for slot, l in ((0, 1), (12, 0)):
+        hot = (iota((12, 128), 1) == iota((12, 128), 0) + slot).astype(F32).astype(BF16)
+        for part in split3(frames_ref[:, l, :]):
+            out = out + mm(part, hot, TN)
+    hot = (iota((1, 128), 1) == CHAIN_LANE - FRAME_LANE).astype(F32).astype(BF16)
+    pack_ref[:, 2 * C :] = out + mm(chains_ref[...].astype(F32).astype(BF16), hot, TN)
+
+
 def prep_body(
-    hw_ref, pack_ref, cot_ref, wq_ref, wk_ref, wv_ref, wqp_ref, wkp_ref, wvp_ref, w_out_ref, pair_ref,
+    hw_ref, pack_ref, cot_hbm, w_out_hbm, pair_hbm, wq_hbm, wk_hbm, wv_hbm, wqp_hbm, wkp_hbm, wvp_hbm,
     wk_out, wq_out, gp_ref, q1_ref, q0_ref, pu_ref, d_ref, sc_ref,
+    cot_ref, w_out_ref, pair_ref, wq_ref, wk_ref, wv_ref, wqp_ref, wkp_ref, wvp_ref, sems,
 ):
     rows = pack_ref.shape[0]
+    ends = (
+        (cot_hbm, cot_ref), (w_out_hbm, w_out_ref), (pair_hbm, pair_ref), (wq_hbm, wq_ref), (wk_hbm, wk_ref),
+        (wv_hbm, wv_ref), (wqp_hbm, wqp_ref), (wkp_hbm, wkp_ref), (wvp_hbm, wvp_ref),
+    )
+    copies = [pltpu.make_async_copy(src, dst, sems.at[n]) for n, (src, dst) in enumerate(ends)]
+    for copy in copies:
+        copy.start()
+    copies[0].wait()
+    copies[1].wait()
     upstream_parts(cot_ref[...], w_out_ref, gp_ref, pu_ref, rows)
+    copies[2].wait()
     pair_products(pu_ref, pair_ref, d_ref, rows)
+    for copy in copies[3:]:
+        copy.wait()
     wq_out[...] = jnp.zeros(wq_out.shape, BF16)
     wk_out[...] = jnp.zeros(wk_out.shape, BF16)
-    wq_out[:, 0:192] = wq_ref[...]
-    wk_out[:, 0:192] = wk_ref[...]
-    wk_out[:, 640:832] = wv_ref[...]
+    wq_out[0:192, :] = wq_ref[...]
+    wk_out[0:192, :] = wk_ref[...]
+    wk_out[640:832, :] = wv_ref[...]
     for a in range(3):
-        wq_out[:, 256 + 128 * a : 304 + 128 * a] = wqp_ref[:, 48 * a : 48 * a + 48]
-        wk_out[:, 256 + 128 * a : 304 + 128 * a] = wkp_ref[:, 48 * a : 48 * a + 48]
-        wk_out[:, 896 + 128 * a : 992 + 128 * a] = wvp_ref[:, 96 * a : 96 * a + 96]
+        wq_out[256 + 128 * a : 304 + 128 * a, :] = wqp_ref[48 * a : 48 * a + 48, :]
+        wk_out[256 + 128 * a : 304 + 128 * a, :] = wkp_ref[48 * a : 48 * a + 48, :]
+        wk_out[896 + 128 * a : 992 + 128 * a, :] = wvp_ref[96 * a : 96 * a + 96, :]
     lane = iota((8, 128), 1)
     raw = jnp.zeros((8, 128), F32)
     for h in range(H):
@@ -167,14 +200,14 @@
     sc_ref[...] = soft * POINT_SCALE
     fr = pack_ref[:, FRAME_LANE : FRAME_LANE + 128]
     for out, first, fcol in ((q1_ref, 0, 0), (q0_ref, C, 12)):
-        flat = mm2(pack_ref[:, first : first + C], wq_out[...])
+        flat = mm2(pack_ref[:, first : first + C], wq_out[...], NT)
         rot, shift = columns(fr, fcol)
         out[:, :LANES] = place(rot, shift, flat)
         out[:, LANES:] = flat[:, 256:]
 
 
 def project_keys(x, fr, fcol, wk_ref, kv_ref):
-    flat = mm2(x, wk_ref[...])
+    flat = mm2(x, wk_ref[...], NT)
     rot, shift = columns(fr, fcol)
     kv_ref[:, 0:640] = place(rot, shift, flat[:, :640])
     kv_ref[:, 640:1280] = place(rot, shift, flat[:, 640:])
@@ -252,8 +285,8 @@
 
 
 def backward(
-    flag_ref, e, dots, probs, kv_ref, key_fr, own_fr, fcol, q_ref, gp, d_ref, wk_ref, wq_ref, sc, shift_lane,
-    share, z_ref, keys_out_ref,
+    flag_ref, e, dots, probs, kv_ref, key_fr, own_fr, fcol, q_ref, gp, d_ref, wk_ref, sc,
+    z_ref, keys_out_ref,
 ):
     rows = e.shape[0]
     lane = iota((rows, 128), 1)
@@ -288,17 +321,6 @@
     dl = LOGIT_SCALE * att * (d_att - rd_all)
     z_ref[0 : H * rows, :] = att
     z_ref[H * rows :, :] = dl
-    dh, dlo = split(dl)
-    kh, klo = split(kv_ref[:, 0:640])
-    qr = pick(mm3(dh, dlo, kh, klo), heads_k, rows)
-    d_qg = [sc * block(qr, a) for a in range(3)]
-    d_ql = unrotate(rot, d_qg)
-    query_grad = mm2(jnp.concatenate([PLAIN_SCALE * qr[:, 0:256]] + d_ql, axis=1), wq_ref[...], NT)
-    q_local = [q_ref[:, 640 + 128 * b : 768 + 128 * b] for b in range(3)]
-    prods = [d_qg[a] * q_local[b] + share * off[a] * gpt[b] for a in range(3) for b in range(3)]
-    prods = prods + [d_qg[a] - share * gptg[a] for a in range(3)]
-    gather12 = lane_matrix(12 * 128, lambda r: shift_lane + (r >> 7))
-    query_frames = mm2(jnp.concatenate(prods, axis=1), gather12)
     dt = jnp.transpose(dl)
     th, tl = split(dt)
     qh, qlo = spread2(q_ref[:, 0:640], heads_k)
@@ -315,13 +337,39 @@
     d_kl = unrotate(krot, d_kg)
     d_vl = unrotate(krot, d_vg)
     flat = jnp.concatenate([PLAIN_SCALE * kr[:, 0:256]] + d_kl + [vr[:, 0:256]] + d_vl, axis=1)
-    keys_out_ref[:, 0:C] = mm2(flat, wk_ref[...], NT)
+    keys_out_ref[:, 0:C] = mm2(flat, wk_ref[...])
+    return jnp.concatenate(off + gpt + gptg, axis=1), jnp.concatenate(d_kg + d_vg, axis=1)
+
+
+def frame_sums(prods, first_lane):
+    return mm2(jnp.concatenate(prods, axis=1), lane_matrix(12 * 128, lambda r: first_lane + (r >> 7)))
+
+
+def backward_frames(grads, kv_ref, first_lane):
+    d_kg = [grads[:, 128 * a : 128 * a + 128] for a in range(3)]
+    d_vg = [grads[:, 384 + 128 * a : 512 + 128 * a] for a in range(3)]
     k_local = [kv_ref[:, 1280 + 128 * b : 1408 + 128 * b] for b in range(3)]
     v_local = [kv_ref[:, 1664 + 128 * b : 1792 + 128 * b] for b in range(3)]
-    kprods = [d_kg[a] * k_local[b] + d_vg[a] * v_local[b] for a in range(3) for b in range(3)]
-    kprods = kprods + [d_kg[a] + d_vg[a] for a in range(3)]
-    key_frames = mm2(jnp.concatenate(kprods, axis=1), gather12)
-    return query_grad, query_frames, key_frames
+    prods = [d_kg[a] * k_local[b] + d_vg[a] * v_local[b] for a in range(3) for b in range(3)]
+    return frame_sums(prods + [d_kg[a] + d_vg[a] for a in range(3)], first_lane)
+
+
+def backward_query(dl, kv_ref, own_fr, fcol, q_ref, pts_ref, wq_ref, sc, first_lane, share):
+    rows = own_fr.shape[0]
+    dh, dlo = split(dl)
+    kh, klo = split(kv_ref[:, 0:640])
+    qr = pick(mm3(dh, dlo, kh, klo), key_heads(rows), rows)
+    rot, _ = columns(own_fr, fcol)
+    d_qg = [sc * block(qr, a) for a in range(3)]
+    d_ql = unrotate(rot, d_qg)
+    grad = mm2(jnp.concatenate([PLAIN_SCALE * qr[:, 0:256]] + d_ql, axis=1), wq_ref[...])
+    q_local = [q_ref[:, 640 + 128 * b : 768 + 128 * b] for b in range(3)]
+    off, gpt, gptg = [
+        [pts_ref[:, 384 * n + 128 * a : 384 * n + 128 * a + 128] for a in range(3)] for n in range(3)
+    ]
+    prods = [d_qg[a] * q_local[b] + share * off[a] * gpt[b] for a in range(3) for b in range(3)]
+    prods = prods + [d_qg[a] - share * gptg[a] for a in range(3)]
+    return grad, frame_sums(prods, first_lane)
 
 
 def send_blocks(flag_ref, src_ref, mine_a, mine_b, theirs, rows):
@@ -337,27 +385,44 @@
     theirs[rows:, :] = get(1 - zb, 1 - core)
 
 
+def final_body(r0, r1, r2, r3, r4, r5, one_ref, single_out, frames_out):
+    total = (r0[...] + r1[...]) + (r2[...] + r3[...]) + (r4[...] + r5[...])
+    single_out[...] = one_ref[...] + total[:, 0:C]
+    turned = jnp.transpose(total[:, C:])
+    for l in range(2):
+        frames_out[:, l, :] = turned[12 * l : 12 * l + 12, :]
+
+
+def frame_part(ref):
+    return ref[:, FRAME_LANE : FRAME_LANE + 128]
+
+
 def back_one_body(
-    share, flag_ref, e_mine, e_other, pm_ref, kv_ref, keys_ref, own_ref, q_ref, gp_ref, d_ref, wk_ref, wq_ref, sc_ref,
-    z_ref, mine_a, mine_b, theirs, query_out, frk_ref, frq_ref, work_ref,
+    flag_ref, e_mine, e_other, pm_ref, kv_ref, keys_ref, own_ref, q_ref, gp_ref, d_ref, wk_ref, sc_ref,
+    z_ref, mine_a, mine_b, theirs, pts_ref, grads_ref, work_ref,
 ):
-    rows = own_ref.shape[0]
     e = e_mine[...] + e_other[...]
-    query_grad, query_frames, key_frames = backward(
-        flag_ref, e, e[:, 128:256], pm_ref[1], kv_ref, keys_ref[:, FRAME_LANE : FRAME_LANE + 128],
-        own_ref[:, FRAME_LANE : FRAME_LANE + 128], 0, q_ref, gp_ref[...], d_ref, wk_ref, wq_ref, sc_ref[0:1, :], 12,
-        share, z_ref, work_ref,
-    )
-    query_out[...] = query_grad
-    frq_ref[...] = query_frames
-    frk_ref[...] = key_frames
-    send_blocks(flag_ref, work_ref, mine_a, mine_b, theirs, rows)
+    pts_ref[...], grads_ref[...] = backward(
+        flag_ref, e, e[:, 128:256], pm_ref[1], kv_ref, frame_part(keys_ref), frame_part(own_ref), 0, q_ref,
+        gp_ref[...], d_ref, wk_ref, sc_ref[0:1, :], z_ref, work_ref,
+    )
+    send_blocks(flag_ref, work_ref, mine_a, mine_b, theirs, own_ref.shape[0])
+
+
+def query_one_body(
+    share, z_ref, kv_ref, own_ref, q_ref, pts_ref, grads_ref, wq_ref, sc_ref, query_out, frq_ref, frk_ref
+):
+    half = z_ref.shape[0] // 2
+    query_out[...], frq_ref[...] = backward_query(
+        z_ref[half:, :], kv_ref, frame_part(own_ref), 0, q_ref, pts_ref, wq_ref, sc_ref[0:1, :], 12, share
+    )
+    frk_ref[...] = backward_frames(grads_ref[...], kv_ref, 12)
 
 
 def back_zero_body(
-    share, flag_ref, cot_ref, r0, r1, r2, r3, r4, r5, e_mine, e_other, pm_ref, kv_ref, keys_ref, own_ref, q_ref, pair_ref,
-    w_out_ref, wk_ref, wq_ref, sc_ref, frk_ref, frq_ref,
-    z_ref, mine_a, mine_b, theirs, query_out, sum_ref, pu_ref, work_ref, gp_ref, d_ref,
+    flag_ref, cot_ref, r0, r1, r2, r3, r4, r5, e_mine, e_other, pm_ref, kv_ref, keys_ref, own_ref, q_ref, pair_ref,
+    w_out_ref, wk_ref, sc_ref, frk_ref,
+    z_ref, mine_a, mine_b, theirs, pts_ref, sum_ref, pu_ref, work_ref, gp_ref, d_ref,
 ):
     rows = own_ref.shape[0]
     total = (r0[...] + r1[...]) + (r2[...] + r3[...]) + (r4[...] + r5[...])
@@ -377,15 +442,21 @@
         axis=1,
     )
     dots = dots + mm2(wide, lane_matrix(H * CZ, lambda r: STAT + (r >> 7)))
-    query_grad, query_frames, key_frames = backward(
-        flag_ref, e, dots, pm_ref[0], kv_ref, keys_ref[:, FRAME_LANE : FRAME_LANE + 128],
-        own_ref[:, FRAME_LANE : FRAME_LANE + 128], 12, q_ref, gp, d_ref, wk_ref, wq_ref, sc_ref[0:1, :], 0,
-        share, z_ref, work_ref,
-    )
-    query_out[:, 0:C] = query_grad
-    query_out[:, C:] = query_frames + frq_ref[...]
-    work_ref[:, C:] = key_frames + frk_ref[...]
+    pts_ref[...], grads = backward(
+        flag_ref, e, dots, pm_ref[0], kv_ref, frame_part(keys_ref), frame_part(own_ref), 12, q_ref, gp, d_ref, wk_ref,
+        sc_ref[0:1, :], z_ref, work_ref,
+    )
+    work_ref[:, C:] = backward_frames(grads, kv_ref, 0) + frk_ref[...]
     send_blocks(flag_ref, work_ref, mine_a, mine_b, theirs, rows)
+
+
+def query_zero_body(share, z_ref, kv_ref, own_ref, q_ref, pts_ref, wq_ref, sc_ref, frq_ref, query_out):
+    half = z_ref.shape[0] // 2
+    grad, frames = backward_query(
+        z_ref[half:, :], kv_ref, frame_part(own_ref), 12, q_ref, pts_ref, wq_ref, sc_ref[0:1, :], 0, share
+    )
+    query_out[:, 0:C] = grad
+    query_out[:, C:] = frames + frq_ref[...]
 
 
 def pair_body(z1_ref, z0_ref, pu1_ref, pu0_ref, wbt_ref, out_ref):
@@ -403,9 +474,10 @@
 
 VMEM = pl.BlockSpec(memory_space=pltpu.VMEM)
 SMEM = pl.BlockSpec(memory_space=pltpu.SMEM)
-
-
-def call(body, name, in_specs, outs, args, scratch=()):
+HBM = pl.BlockSpec(memory_space=pltpu.HBM)
+
+
+def call(body, name, in_specs, outs, args, scratch=(), micros=1.0):
     return pl.pallas_call(
         body,
         name=name,
@@ -413,7 +485,8 @@
         out_specs=tuple(VMEM for _ in outs),
         out_shape=tuple(jax.ShapeDtypeStruct(s, d) for s, d in outs),
         scratch_shapes=list(scratch),
-        compiler_params=pltpu.CompilerParams(vmem_limit_bytes=32 * 1024 * 1024),
+        compiler_params=pltpu.CompilerParams(vmem_limit_bytes=16 * 1024 * 1024),
+        cost_estimate=pl.CostEstimate(flops=int(micros * 1e9), transcendentals=0, bytes_accessed=int(micros * 3e6)),
     )(*args)
 
 
@@ -443,9 +516,9 @@
     row_total = lax.axis_size("row")
     col_total = lax.axis_size("col")
     fast = row_total == 8 and col_total == 2 and keys == 4 * rows
-    small = jnp.concatenate([frames[1], frames[0], chains[None].astype(F32)], axis=0)
-    pack = jnp.concatenate(
-        [single[1], single[0], small.T, jnp.zeros((rows, PACK - CHAIN_LANE - 1), F32)], axis=1
+    (pack,) = call(
+        pack_body, "pack", [VMEM] * 3, [((rows, PACK), F32)],
+        (single, frames.transpose(1, 0, 2), chains[None]),
     )
     col = lax.axis_index("col")
     row = lax.axis_index("row")
@@ -455,7 +528,6 @@
         ownx = lax.ppermute(pack, "row", CORE_SWAP)
         one = lax.ppermute(pack, BOTH, FETCH_ONE)
         two = lax.ppermute(pack, BOTH, FETCH_TWO)
-        blocks = (pack, ownx, one, lax.ppermute(one, "row", CORE_SWAP), two, lax.ppermute(two, "row", CORE_SWAP))
         own = pack
     else:
         flags = jnp.array([1, 0, 0], jnp.int32)
@@ -470,26 +542,38 @@
             return lax.ppermute(x, "col", COL_SWAP)
         return lax.psum(x, "col") - x
 
-    def reduce(mine_a, mine_b, theirs, query):
+    def reduce(mine_a, mine_b, theirs, late):
         if fast:
+            got = lax.ppermute(theirs, "row", CORE_SWAP)
+            query, *rest = late()
+            got, query = lax.optimization_barrier((got, query))
             query_other = lax.ppermute(query, "col", COL_SWAP)
-            got = lax.ppermute(theirs, "row", CORE_SWAP)
             part = (mine_a + got[:rows], mine_b + got[rows:])
-            return [query, query_other] + [lax.ppermute(part[s & 1], BOTH, SCATTER[s]) for s in range(4)]
+            return [query, query_other] + [lax.ppermute(part[s & 1], BOTH, SCATTER[s]) for s in range(4)], rest
+        query, *rest = late()
         parts = jnp.concatenate([mine_a, theirs[:rows], mine_b, theirs[rows:]], axis=0)
         summed = lax.all_gather(lax.psum(parts, "row"), "col", axis=0, tiled=True)
         zero = jnp.zeros_like(query)
         back = lax.dynamic_slice_in_dim(summed, row * rows, rows, 0)
-        return [lax.psum(query, "col"), back, zero, zero, zero, zero]
+        return [lax.psum(query, "col"), back, zero, zero, zero, zero], rest
 
     probs = saved_probs.reshape(2, H * rows, keys)
     hr = H * rows
+    loads = (
+        cotangent, w_out, pair, w_query.T, w_key.T, w_value.T, w_query_points.T, w_key_points.T, w_value_points.T,
+    )
     wk, wq, gp1, q1, q0, pu1, d1, sc = call(
-        prep_body, "prep", [SMEM] + [VMEM] * 10,
-        [((C, 1280), BF16), ((C, LANES), BF16), ((rows, 768), F32), ((rows, 1024), F32), ((rows, 1024), F32),
+        prep_body, "prep", [SMEM, VMEM] + [HBM] * 9,
+        [((1280, C), BF16), ((LANES, C), BF16), ((rows, 768), F32), ((rows, 1024), F32), ((rows, 1024), F32),
          ((hr, CZ), F32), ((hr, keys), F32), ((8, 128), F32)],
-        (head_weights, own, cotangent, w_query, w_key, w_value, w_query_points, w_key_points, w_value_points, w_out, pair),
-    )
+        (head_weights, own, *(pltpu.with_memory_space_constraint(x, pltpu.HBM) for x in loads)),
+        [pltpu.VMEM(x.shape, x.dtype) for x in loads] + [pltpu.SemaphoreType.DMA((len(loads),))],
+    )
+    if fast:
+        one, two, wk, wq, gp1, q1, q0, pu1, d1, sc = lax.optimization_barrier(
+            (one, two, wk, wq, gp1, q1, q0, pu1, d1, sc)
+        )
+        blocks = (pack, ownx, one, lax.ppermute(one, "row", CORE_SWAP), two, lax.ppermute(two, "row", CORE_SWAP))
     key_pack, kv1, pm, e1 = call(
         first_body, "first", [SMEM] + [VMEM] * 11,
         [((keys, PACK), F32), ((keys, 2048), F32), ((2, hr, keys), BF16), ((rows, 384), F32)],
@@ -503,28 +587,46 @@
         [pltpu.VMEM((hr, keys), F32), pltpu.VMEM((hr, CZ), F32)],
     )
     e0_other = col_other(e0)
-    z1, mine_a, mine_b, theirs, query, frk, frq = call(
-        functools.partial(back_one_body, 1.0 / col_total), "back_one", [SMEM] + [VMEM] * 12,
-        [((2 * hr, keys), F32), ((rows, C), F32), ((rows, C), F32), ((2 * rows, C), F32), ((rows, C), F32),
-         ((keys, 128), F32), ((rows, 128), F32)],
-        (flags, e1, e1_other, pm, kv1, key_pack, own, q1, gp1, d1, wk, wq, sc),
+    share = 1.0 / col_total
+    e1_other, e0 = lax.optimization_barrier((e1_other, e0))
+    z1, mine_a, mine_b, theirs, pts, grads = call(
+        back_one_body, "back_one", [SMEM] + [VMEM] * 11,
+        [((2 * hr, keys), F32), ((rows, C), F32), ((rows, C), F32), ((2 * rows, C), F32), ((rows, 1152), F32),
+         ((keys, 768), F32)],
+        (flags, e1, e1_other, pm, kv1, key_pack, own, q1, gp1, d1, wk, sc),
         [pltpu.VMEM((keys, C), F32)],
-    )
-    pieces = reduce(mine_a, mine_b, theirs, query)
-    z0, mine_a, mine_b, theirs, query, single_one, pu0 = call(
-        functools.partial(back_zero_body, 1.0 / col_total), "back_zero", [SMEM] + [VMEM] * 21,
-        [((2 * hr, keys), F32), ((rows, 512), F32), ((rows, 512), F32), ((2 * rows, 512), F32), ((rows, 512), F32),
+        6.0,
+    )
+    pts, e0_other = lax.optimization_barrier((pts, e0_other))
+    pieces, (frq, frk) = reduce(
+        mine_a, mine_b, theirs,
+        lambda: call(
+            functools.partial(query_one_body, share), "query_one", [VMEM] * 8,
+            [((rows, C), F32), ((rows, 128), F32), ((keys, 128), F32)],
+            (z1, kv1, own, q1, pts, grads, wq, sc),
+        ),
+    )
+    z0, mine_a, mine_b, theirs, pts, single_one, pu0 = call(
+        back_zero_body, "back_zero", [SMEM] + [VMEM] * 19,
+        [((2 * hr, keys), F32), ((rows, 512), F32), ((rows, 512), F32), ((2 * rows, 512), F32), ((rows, 1152), F32),
          ((rows, C), F32), ((hr, CZ), F32)],
-        (flags, cotangent, *pieces, e0, e0_other, pm, kv0, key_pack, own, q0, pair, w_out, wk, wq, sc, frk, frq),
+        (flags, cotangent, *pieces, e0, e0_other, pm, kv0, key_pack, own, q0, pair, w_out, wk, sc, frk),
         [pltpu.VMEM((keys, 512), F32), pltpu.VMEM((rows, 768), F32), pltpu.VMEM((hr, keys), F32)],
     )
-    pieces = reduce(mine_a, mine_b, theirs, query)
+    pieces, _ = reduce(
+        mine_a, mine_b, theirs,
+        lambda: call(
+            functools.partial(query_zero_body, share), "query_zero", [VMEM] * 8, [((rows, 512), F32)],
+            (z0, kv0, own, q0, pts, wq, sc, frq),
+        ),
+    )
     (d_pair,) = call(
         pair_body, "pair_grad", [VMEM] * 5, [((rows, keys, CZ), BF16)], (z1, z0, pu1, pu0, w_bias.T)
     )
-    total = sum(pieces)
-    d_frames = total[:, C : C + 24].T.reshape(2, 12, rows)
-    return (single_one + total[:, :C], d_frames, d_pair)
+    d_single, d_frames = call(
+        final_body, "final", [VMEM] * 7, [((rows, C), F32), ((12, 2, rows), F32)], (*pieces, single_one)
+    )
+    return (d_single, d_frames.transpose(1, 0, 2), d_pair)
 
 
 def solution(mesh):

time: 83.7 us -> 66.6 us (0.80)
  local copies, waits for them, and re-layouts: 13 us -> 2.28 us
  waiting for transfers between devices: 17.4 us -> 12.9 us
  starting transfers between devices: 33.9 us -> 31.1 us
  Pallas kernels: 16.4 us -> 19 us
  other arithmetic: 1.67 us -> 0.11 us
    unnamed x31 -> x20, local copies, waits for them, and re-layouts: 11.2 us -> 2.28 us
    ppermute x2, starting transfers between devices: 11.8 us -> 6.19 us  [reduce(): query_other = lax.ppermute(query, 'col', COL_SWAP)]
    ppermute x1, waiting for transfers between devices: 3.17 us -> 0.01 us  [local(): one = lax.ppermute(pack, BOTH, FETCH_ONE)]
    ppermute x1, starting transfers between devices: 0.01 us -> 3.03 us  [local(): one = lax.ppermute(pack, BOTH, FETCH_ONE)]
    ppermute x1, waiting for transfers between devices: 2.88 us -> 0.01 us  [local(): two = lax.ppermute(pack, BOTH, FETCH_TWO)]
    ppermute x2, waiting for transfers between devices: 3.03 us -> 0.17 us  [reduce(): query_other = lax.ppermute(query, 'col', COL_SWAP)]
    pallas_call x6 -> x10, Pallas kernels: 16.4 us -> 19 us  [call(): pl.pallas_call(body, name=name, in_specs=in_specs, out_specs=tuple((VMEM...]
    ppermute x1, starting transfers between devices: 7.61 us -> 5.19 us  [local(): two = lax.ppermute(pack, BOTH, FETCH_TWO)]
  transfers between devices with their start and end apart: 19 -> 19, of which waited for: 7 -> 8; matrix products, arithmetic and copies ran while one was open for 9% -> 0% of each run, Pallas kernels for 6% -> 18%
where the time goes in v1:
time: 66.6 us; the launch traced here: 66.3 us
  starting transfers between devices  31.1 us (47%)
  Pallas kernels  19 us (29%)
  waiting for transfers between devices  12.9 us (19%)
  local copies, waits for them, and re-layouts  2.28 us (3%)
  between operations  0.83 us (1%)
    pallas_call x10, Pallas kernels, call(): pl.pallas_call(body, name=name, in_specs=in_specs, out_specs=tuple((VMEM...  19 us
    ppermute x8, starting transfers between devices, reduce(): lax.ppermute(part[s & 1], BOTH, SCATTER[s])  13.8 us
    ppermute x2, starting transfers between devices, reduce(): query_other = lax.ppermute(query, 'col', COL_SWAP)  6.19 us
    ppermute x8, waiting for transfers between devices, reduce(): lax.ppermute(part[s & 1], BOTH, SCATTER[s])  6 us
    ppermute x1, starting transfers between devices, local(): two = lax.ppermute(pack, BOTH, FETCH_TWO)  5.19 us
    ppermute x2, waiting for transfers between devices, col_other(): return lax.ppermute(x, 'col', COL_SWAP)  5.17 us
    ppermute x1, starting transfers between devices, local(): one = lax.ppermute(pack, BOTH, FETCH_ONE)  3.03 us
    unnamed x20, local copies, waits for them, and re-layouts  2.28 us
  transfers between devices with their start and end apart: 19, of which 8 were waited for; matrix products, arithmetic and copies ran while one was open for 0% of the time, Pallas kernels for 18%

profile of v1, /device:TPU:0, one launch (start us, length us, event | category | flops | bytes accessed | tf_op | source)
XLA Modules:
  0.0 66.3 jit_solution(341160143082472828)
XLA Ops:
  0.6 0.0 copy-start.5
  0.6 0.9 %copy-done.5 = f32[2,32,384]{2,1,0:T(8,128)S(1)} copy-done((f32[2,32,384]{2,1,0:T(8,128)S(1)}, f32[2,32,384]{2,1,0:T(8,128)}, u32[]{:S(2)}) %copy-start.5) | copy-done | bytes 98328
  1.5 0.0 copy-start.6
  1.5 0.7 %copy-done.6 = f32[2,12,32]{2,0,1:T(2,128)S(1)} copy-done((f32[2,12,32]{2,0,1:T(2,128)S(1)}, f32[2,12,32]{2,0,1:T(2,128)}, u32[]{:S(2)}) %copy-start.6) | copy-done | bytes 3096
  2.2 0.7 copy-done.9
  2.9 0.2 pack.1.pack_ref.own_ref
  3.1 3.0 %collective-permute-start.1 = (f32[32,896]{1,0:T(8,128)S(1)}, f32[32,896]{1,0:T(8,128)S(1)}, u32[]{:S(2)}, u32[]{:S(2)}) collective-permute-start(f32[32,896]{1,0:T(8,128)S(1)} %pack.1.pack_ref.own_ref), channel_id=1, source_target_pairs={{0,4},{2,6},{4,0},{6,2},{1,8},{3,10},{5,12},{7,14},{9,13},{11,15},... | collective-permute-start | bytes 344072 | tf_op jit(solution)/shard_map/ppermute | solution.py:529
  6.1 5.2 %collective-permute-start.2 = (f32[32,896]{1,0:T(8,128)S(1)}, f32[32,896]{1,0:T(8,128)S(1)}, u32[]{:S(2)}, u32[]{:S(2)}) collective-permute-start(f32[32,896]{1,0:T(8,128)S(1)} %pack.1.pack_ref.own_ref), channel_id=1, source_target_pairs={{0,12},{2,14},{4,8},{6,10},{9,5},{11,7},{13,1},{15,3},{16,28},{18,... | collective-permute-start | bytes 344072 | tf_op jit(solution)/shard_map/ppermute | solution.py:530
  11.3 0.1 collective-permute-start
  11.4 0.0 copy-done.3
  11.4 0.0 copy-start.4
  11.4 0.0 copy-start.7
  11.5 4.0 %prep.1 = (bf16[1280,384]{1,0:T(8,128)(2,1)S(1)}, bf16[640,384]{1,0:T(8,128)(2,1)S(1)}, f32[32,768]{1,0:T(8,128)S(1)}, f32[32,1024]{1,0:T(8,128)S(1)}, f32[32,10...) custom-call(f32[12]{0:T(128)S(1)} %copy-done.3, ...), custom_call_target="tpu_custom_call" | custom-call | flops 1000000000 | bytes 3000000 | tf_op jit(solution)/shard_map/prep/pallas_call | solution.py:481
  15.5 0.0 collective-permute-done.1.p1_ref
  15.5 0.0 collective-permute-done.2.p2_ref
  15.5 0.5 collective-permute-start.3
  16.0 0.1 collective-permute-start.4
  16.1 0.1 pad_add_fusion.flag_ref
  16.2 0.0 collective-permute-done.ownx_ref
  16.2 0.8 %collective-permute-done.3.p1x_ref = f32[32,896]{1,0:T(8,128)S(1)} collective-permute-done((f32[32,896]{1,0:T(8,128)S(1)}, f32[32,896]{1,0:T(8,128)S(1)}, u32[]{:S(2)}, u32[]{:S(2)}) %collective-permute-start.3) | collective-permute-done | bytes 114720 | tf_op jit(solution)/shard_map/ppermute | solution.py:576
  17.0 0.4 collective-permute-done.4.p2x_ref
  17.4 0.0 copy-done.4
  17.4 0.0 copy-done.7
  17.4 1.8 %first.1 = (f32[128,896]{1,0:T(8,128)S(1)}, f32[128,2048]{1,0:T(8,128)S(1)}, bf16[2,384,128]{2,1,0:T(8,128)(2,1)S(1)}, f32[32,384]{1,0:T(8,128)S(1)}) custom-call(s32[3]{0:T(128)S(1)} %pad_add_fusion.flag_ref, f32[32,896]{1,0:T(8,128)S(1)} %pack.1.pack_ref.own_ref, f32[32,896]{1,0:T(8,128)S(1)} %collective-permute-done.ownx_ref, ...), custom_call_target="tpu_custom_call" | custom-call | flops 1000000000 | bytes 3000000 | tf_op jit(solution)/shard_map/first/pallas_call | solution.py:481
  19.1 1.3 %collective-permute-start.5 = (f32[32,384]{1,0:T(8,128)S(1)}, f32[32,384]{1,0:T(8,128)S(1)}, u32[]{:S(2)}, u32[]{:S(2)}) collective-permute-start(f32[32,384]{1,0:T(8,128)S(1)} %get-tuple-element.66.e_mine), channel_id=1, source_target_pairs={{0,1},{1,0},{2,3},{3,2},{4,5},{5,4},{6,7},{7,6},{8,9},{9,8},{10,11... | collective-permute-start | bytes 147464 | tf_op jit(solution)/shard_map/ppermute | solution.py:542
  20.5 0.0 copy-done.1
  20.5 1.3 %second.1 = (f32[128,2048]{1,0:T(8,128)S(1)}, f32[32,2176]{1,0:T(8,128)S(1)}) custom-call(f32[128,896]{1,0:T(8,128)S(1)} %get-tuple-element.67.keys_ref, bf16[1280,384]{1,0:T(8,128)(2,1)S(1)} %get-tuple-element.63.wk_ref, bf16[2,384,128]{2,1,0:T(8,128)(2,1)S(1)} %get-tuple-element.68.pm_ref, bf16[32,128,128]{2,1,0:T(8,128)(2,1)S(1)} %copy-done.1), custom_call_target="tpu_custom_call" | custom-call | flops 1000000000 | bytes 3000000 | tf_op jit(solution)/shard_map/second/pallas_call | solution.py:481
  21.8 0.8 %collective-permute-start.7 = (f32[32,2176]{1,0:T(8,128)S(1)}, f32[32,2176]{1,0:T(8,128)S(1)}, u32[]{:S(2)}, u32[]{:S(2)}) collective-permute-start(f32[32,2176]{1,0:T(8,128)S(1)} %get-tuple-element.85.e_mine), channel_id=1, source_target_pairs={{0,1},{1,0},{2,3},{3,2},{4,5},{5,4},{6,7},{7,6},{8,9},{9,8},{10,11... | collective-permute-start | bytes 835592 | tf_op jit(solution)/shard_map/ppermute | solution.py:542
  22.6 0.7 %collective-permute-done.5.e_other = f32[32,384]{1,0:T(8,128)S(1)} collective-permute-done((f32[32,384]{1,0:T(8,128)S(1)}, f32[32,384]{1,0:T(8,128)S(1)}, u32[]{:S(2)}, u32[]{:S(2)}) %collective-permute-start.5) | collective-permute-done | bytes 49184 | tf_op jit(solution)/shard_map/ppermute | solution.py:542
  23.3 2.6 %back_one.1 = (f32[768,128]{1,0:T(8,128)S(1)}, f32[32,384]{1,0:T(8,128)S(1)}, f32[32,384]{1,0:T(8,128)S(1)}, f32[64,384]{1,0:T(8,128)S(1)}, f32[32,1152]{1,0:T(8,128)S(1)}, /*index=5*/f32[128,768]{1,0:T(8,128)S(1)}) custom-call(s32[3]{0:T(128)S(1)} %pad_add_fusion.flag_ref, f32[32,384]{1,0:T(8,128)S(1)} %get-tuple-element.66.e_mine, ...), custom_call_target="tpu_custom_call" | custom-call | flops 6000000000 | bytes 18000000 | tf_op jit(solution)/shard_map/back_one/pallas_call | solution.py:481
  25.9 0.1 collective-permute-start.6
  26.0 4.5 %collective-permute-done.7.e_other = f32[32,2176]{1,0:T(8,128)S(1)} collective-permute-done((f32[32,2176]{1,0:T(8,128)S(1)}, f32[32,2176]{1,0:T(8,128)S(1)}, u32[]{:S(2)}, u32[]{:S(2)}) %collective-permute-start.7) | collective-permute-done | bytes 278560 | tf_op jit(solution)/shard_map/ppermute | solution.py:542
  30.5 1.2 %query_one.1 = (f32[32,384]{1,0:T(8,128)S(1)}, f32[32,128]{1,0:T(8,128)S(1)}, f32[128,128]{1,0:T(8,128)S(1)}) custom-call(f32[768,128]{1,0:T(8,128)S(1)} %get-tuple-element.75.z_ref.z1_ref, f32[128,2048]{1,0:T(8,128)S(1)} %get-tuple-element.71.kv_ref, f32[32,896]{1,0:T(8,128)S(1)} %pack.1.pack_ref.own_ref, f32[32,1024]{1,0:T(8,128)S(1)} %get-tuple-element.72.q_ref, ...), custom_call_target="tpu_custom_call" | custom-call | flops 1000000000 | bytes 3000000 | tf_op jit(solution)/shard_map/query_one/pallas_call | solution.py:481
  31.7 0.0 collective-permute-done.6
  31.8 2.1 %collective-permute-start.10 = (f32[32,384]{1,0:T(8,128)S(1)}, f32[32,384]{1,0:T(8,128)S(1)}, u32[]{:S(2)}, u32[]{:S(2)}) collective-permute-start(f32[32,384]{1,0:T(8,128)S(1)} %get-tuple-element.105), channel_id=1, source_target_pairs={{0,4},{2,6},{4,0},{6,2},{8,5},{10,7},{12,1},{14,3},{1,12},{3,14},{... | collective-permute-start | bytes 147464 | tf_op jit(solution)/shard_map/ppermute | solution.py:552
  33.8 0.4 collective-permute-start.12
  34.3 1.5 %collective-permute-start.11 = (f32[32,384]{1,0:T(8,128)S(1)}, f32[32,384]{1,0:T(8,128)S(1)}, u32[]{:S(2)}, u32[]{:S(2)}) collective-permute-start(f32[32,384]{1,0:T(8,128)S(1)} %get-tuple-element.106), channel_id=1, source_target_pairs={{0,1},{2,3},{4,5},{6,7},{8,0},{10,2},{12,4},{14,6},{1,9},{3,11},{5... | collective-permute-start | bytes 147464 | tf_op jit(solution)/shard_map/ppermute | solution.py:552
  35.7 0.7 collective-permute-start.9
  36.4 4.2 %collective-permute-start.8 = (f32[32,384]{1,0:T(8,128)S(1)}, f32[32,384]{1,0:T(8,128)S(1)}, u32[]{:S(2)}, u32[]{:S(2)}) collective-permute-start(f32[32,384]{1,0:T(8,128)S(1)} %get-tuple-element.81.r0), channel_id=1, source_target_pairs={{0,1},{1,0},{2,3},{3,2},{4,5},{5,4},{6,7},{7,6},{8,9},{9,8},{10,11... | collective-permute-start | bytes 147464 | tf_op jit(solution)/shard_map/ppermute | solution.py:550
  40.6 0.0 collective-permute-done.10.r3
  40.6 1.9 %collective-permute-done.11.r4 = f32[32,384]{1,0:T(8,128)S(1)} collective-permute-done((f32[32,384]{1,0:T(8,128)S(1)}, f32[32,384]{1,0:T(8,128)S(1)}, u32[]{:S(2)}, u32[]{:S(2)}) %collective-permute-start.11) | collective-permute-done | bytes 49184 | tf_op jit(solution)/shard_map/ppermute | solution.py:552
  42.5 0.0 collective-permute-done.12.r5
  42.5 0.0 collective-permute-done.9.r2
  42.5 0.2 collective-permute-done.8.r1
  42.7 0.0 copy-done
  42.7 0.0 copy-done.2
  42.7 4.3 %back_zero.1 = (f32[768,128]{1,0:T(8,128)S(1)}, f32[32,512]{1,0:T(8,128)S(1)}, f32[32,512]{1,0:T(8,128)S(1)}, f32[64,512]{1,0:T(8,128)S(1)}, f32[32,1152]{1,0:T(...) custom-call(s32[3]{0:T(128)S(1)} %pad_add_fusion.flag_ref, f32[32,384]{1,0:T(8,128)S(1)} %copy-done.2, ...), custom_call_target="tpu_custom_call" | custom-call | flops 1000000000 | bytes 3000000 | tf_op jit(solution)/shard_map/back_zero/pallas_call | solution.py:481
  47.0 0.1 collective-permute-start.13
  47.1 0.0 copy-start.8
  47.1 0.9 %query_zero.1.r0 = f32[32,512]{1,0:T(8,128)S(1)} custom-call(f32[768,128]{1,0:T(8,128)S(1)} %get-tuple-element.91.z_ref.z0_ref, f32[128,2048]{1,0:T(8,128)S(1)} %get-tuple-element.87.kv_ref, f32[32,896]{1,0:T(8,128)S(1)} %pack.1.pack_ref.own_ref, f32[32,1024]{1,0:T(8,128)S(1)} %get-tuple-element.88.q_ref, f32[32,1152]{1,0:T(8,128)S(1)} %get-tuple-element.92.pts_ref, ...), custom_call_target="tpu_custom_call" | custom-call | flops 1000000000 | bytes 3000000 | tf_op jit(solution)/shard_map/query_zero/pallas_call | solution.py:481
  48.0 0.4 collective-permute-done.13
  48.4 0.7 %collective-permute-start.15 = (f32[32,512]{1,0:T(8,128)S(1)}, f32[32,512]{1,0:T(8,128)S(1)}, u32[]{:S(2)}, u32[]{:S(2)}) collective-permute-start(f32[32,512]{1,0:T(8,128)S(1)} %get-tuple-element.104), channel_id=1, source_target_pairs={{0,0},{2,2},{4,4},{6,6},{8,1},{10,3},{12,5},{14,7},{1,8},{3,10},{5... | collective-permute-start | bytes 196616 | tf_op jit(solution)/shard_map/ppermute | solution.py:552
  49.1 6.2 %collective-permute-start.17 = (f32[32,512]{1,0:T(8,128)S(1)}, f32[32,512]{1,0:T(8,128)S(1)}, u32[]{:S(2)}, u32[]{:S(2)}) collective-permute-start(f32[32,512]{1,0:T(8,128)S(1)} %get-tuple-element.104), channel_id=1, source_target_pairs={{0,1},{2,3},{4,5},{6,7},{8,0},{10,2},{12,4},{14,6},{1,9},{3,11},{5... | collective-permute-start | bytes 196616 | tf_op jit(solution)/shard_map/ppermute | solution.py:552
  55.3 1.4 %collective-permute-start.16 = (f32[32,512]{1,0:T(8,128)S(1)}, f32[32,512]{1,0:T(8,128)S(1)}, u32[]{:S(2)}, u32[]{:S(2)}) collective-permute-start(f32[32,512]{1,0:T(8,128)S(1)} %get-tuple-element.103), channel_id=1, source_target_pairs={{0,4},{2,6},{4,0},{6,2},{8,5},{10,7},{12,1},{14,3},{1,12},{3,14},{... | collective-permute-start | bytes 196616 | tf_op jit(solution)/shard_map/ppermute | solution.py:552
  56.6 1.0 %collective-permute-start.18 = (f32[32,512]{1,0:T(8,128)S(1)}, f32[32,512]{1,0:T(8,128)S(1)}, u32[]{:S(2)}, u32[]{:S(2)}) collective-permute-start(f32[32,512]{1,0:T(8,128)S(1)} %get-tuple-element.103), channel_id=1, source_target_pairs={{0,5},{2,7},{4,1},{6,3},{8,4},{10,6},{12,0},{14,2},{1,13},{3,15},{... | collective-permute-start | bytes 196616 | tf_op jit(solution)/shard_map/ppermute | solution.py:552
  57.6 1.9 %collective-permute-start.14 = (f32[32,512]{1,0:T(8,128)S(1)}, f32[32,512]{1,0:T(8,128)S(1)}, u32[]{:S(2)}, u32[]{:S(2)}) collective-permute-start(f32[32,512]{1,0:T(8,128)S(1)} %query_zero.1.r0), channel_id=1, source_target_pairs={{0,1},{1,0},{2,3},{3,2},{4,5},{5,4},{6,7},{7,6},{8,9},{9,8},{10,11... | collective-permute-start | bytes 196616 | tf_op jit(solution)/shard_map/ppermute | solution.py:550
  59.6 0.0 copy-done.8
  59.6 1.9 %pair_grad.1 = bf16[32,128,128]{2,1,0:T(8,128)(2,1)} custom-call(f32[768,128]{1,0:T(8,128)S(1)} %get-tuple-element.75.z_ref.z1_ref, f32[768,128]{1,0:T(8,128)S(1)} %get-tuple-element.91.z_ref.z0_ref, f32[384,128]{1,0:T(8,128)S(1)} %get-tuple-element.101.pu1_ref, f32[384,128]{1,0:T(8,128)S(1)} %get-tuple-element.102.pu0_ref, bf16[12,128]{1,0:T(8,128)(2,1)S(1)} %bitcast.16), custom_call_target="tpu_custom_call" | custom-call | flops 1000000000 | bytes 3000000 | tf_op jit(solution)/shard_map/pair_grad/pallas_call | solution.py:481
  61.5 0.0 collective-permute-done.15.r2
  61.5 0.0 collective-permute-done.16.r3
  61.5 4.1 %collective-permute-done.17.r4 = f32[32,512]{1,0:T(8,128)S(1)} collective-permute-done((f32[32,512]{1,0:T(8,128)S(1)}, f32[32,512]{1,0:T(8,128)S(1)}, u32[]{:S(2)}, u32[]{:S(2)}) %collective-permute-start.17) | collective-permute-done | bytes 65568 | tf_op jit(solution)/shard_map/ppermute | solution.py:552
  65.6 0.0 collective-permute-done.18.r5
  65.6 0.0 collective-permute-done.14.r1
  65.6 0.7 %final.1 = (f32[32,384]{1,0:T(8,128)}, f32[12,2,32]{2,1,0:T(2,128)}) custom-call(f32[32,512]{1,0:T(8,128)S(1)} %query_zero.1.r0, f32[32,512]{1,0:T(8,128)S(1)} %collective-permute-done.14.r1, f32[32,512]{1,0:T(8,128)S(1)} %collective-permute-done.15.r2, f32[32,512]{1,0:T(8,128)S(1)} %collective-permute-done.16.r3, f32[32,512]{1,0:T(8,128)S(1)} %collective-permute-done.17.r4, ...), custom_call_target="tpu_custom_call" | custom-call | flops 1000000000 | bytes 3000000 | tf_op jit(solution)/shard_map/final/pallas_call | solution.py:481
  (7 shorter events, 0.0 us)
Async XLA Ops:
  0.6 0.9 %copy-start.5 = (f32[2,32,384]{2,1,0:T(8,128)S(1)}, f32[2,32,384]{2,1,0:T(8,128)}, u32[]{:S(2)}) copy-start(f32[2,32,384]{2,1,0:T(8,128)} %single_ref.1) | copy-start | bytes 294916
  1.5 0.7 %copy-start.6 = (f32[2,12,32]{2,0,1:T(2,128)S(1)}, f32[2,12,32]{2,0,1:T(2,128)}, u32[]{:S(2)}) copy-start(f32[2,12,32]{2,0,1:T(2,128)} %param.17) | copy-start | bytes 9220
  2.2 0.7 copy-start.9
  2.9 8.5 %copy-start.3 = (f32[12]{0:T(128)S(1)}, f32[12]{0:T(128)}, u32[]{:S(2)}) copy-start(f32[12]{0:T(128)} %hw_ref.1) | copy-start | bytes 148
  3.1 12.4 %collective-permute-start.1 = (f32[32,896]{1,0:T(8,128)S(1)}, f32[32,896]{1,0:T(8,128)S(1)}, u32[]{:S(2)}, u32[]{:S(2)}) collective-permute-start(f32[32,896]{1,0:T(8,128)S(1)} %pack.1.pack_ref.own_ref), channel_id=1, source_target_pairs={{0,4},{2,6},{4,0},{6,2},{1,8},{3,10},{5,12},{7,14},{9,13},{11,15},... | collective-permute-start | bytes 344072 | tf_op jit(solution)/shard_map/ppermute | solution.py:529
  6.1 9.4 %collective-permute-start.2 = (f32[32,896]{1,0:T(8,128)S(1)}, f32[32,896]{1,0:T(8,128)S(1)}, u32[]{:S(2)}, u32[]{:S(2)}) collective-permute-start(f32[32,896]{1,0:T(8,128)S(1)} %pack.1.pack_ref.own_ref), channel_id=1, source_target_pairs={{0,12},{2,14},{4,8},{6,10},{9,5},{11,7},{13,1},{15,3},{16,28},{18,... | collective-permute-start | bytes 344072 | tf_op jit(solution)/shard_map/ppermute | solution.py:530
  11.3 4.9 %collective-permute-start = (f32[32,896]{1,0:T(8,128)S(1)}, f32[32,896]{1,0:T(8,128)S(1)}, u32[]{:S(2)}, u32[]{:S(2)}) collective-permute-start(f32[32,896]{1,0:T(8,128)S(1)} %pack.1.pack_ref.own_ref), channel_id=1, source_target_pairs={{0,2},{2,0},{4,6},{6,4},{8,10},{10,8},{12,14},{14,12},{1,3},{3,1},... | collective-permute-start | bytes 344072 | tf_op jit(solution)/shard_map/ppermute | solution.py:528
  11.4 5.9 %copy-start.4 = (bf16[2,12,32,128]{3,2,1,0:T(8,128)(2,1)S(1)}, bf16[2,12,32,128]{3,2,1,0:T(8,128)(2,1)}, u32[]{:S(2)}) copy-start(bf16[2,12,32,128]{3,2,1,0:T(8,128)(2,1)} %param.18) | copy-start | bytes 589828
  11.4 5.9 %copy-start.7 = (s32[16,16]{1,0:T(8,128)S(1)}, s32[16,16]{1,0:T(8,128)}, u32[]{:S(2)}) copy-start(s32[16,16]{1,0:T(8,128)} %links_ref.1) | copy-start | bytes 3076
  15.5 1.5 %collective-permute-start.3 = (f32[32,896]{1,0:T(8,128)S(1)}, f32[32,896]{1,0:T(8,128)S(1)}, u32[]{:S(2)}, u32[]{:S(2)}) collective-permute-start(f32[32,896]{1,0:T(8,128)S(1)} %collective-permute-done.1.p1_ref), channel_id=1, source_target_pairs={{0,2},{2,0},{4,6},{6,4},{8,10},{10,8},{12,14},{14,12},{1,3},{3,1},... | collective-permute-start | bytes 344072 | tf_op jit(solution)/shard_map/ppermute | solution.py:576
  16.0 1.3 %collective-permute-start.4 = (f32[32,896]{1,0:T(8,128)S(1)}, f32[32,896]{1,0:T(8,128)S(1)}, u32[]{:S(2)}, u32[]{:S(2)}) collective-permute-start(f32[32,896]{1,0:T(8,128)S(1)} %collective-permute-done.2.p2_ref), channel_id=1, source_target_pairs={{0,2},{2,0},{4,6},{6,4},{8,10},{10,8},{12,14},{14,12},{1,3},{3,1},... | collective-permute-start | bytes 344072 | tf_op jit(solution)/shard_map/ppermute | solution.py:576
  17.4 3.1 %copy-start.1 = (bf16[32,128,128]{2,1,0:T(8,128)(2,1)S(1)}, bf16[32,128,128]{2,1,0:T(8,128)(2,1)}, u32[]{:S(2)}) copy-start(bf16[32,128,128]{2,1,0:T(8,128)(2,1)} %pair_ref.3) | copy-start | bytes 3145732
  19.1 4.2 %collective-permute-start.5 = (f32[32,384]{1,0:T(8,128)S(1)}, f32[32,384]{1,0:T(8,128)S(1)}, u32[]{:S(2)}, u32[]{:S(2)}) collective-permute-start(f32[32,384]{1,0:T(8,128)S(1)} %get-tuple-element.66.e_mine), channel_id=1, source_target_pairs={{0,1},{1,0},{2,3},{3,2},{4,5},{5,4},{6,7},{7,6},{8,9},{9,8},{10,11... | collective-permute-start | bytes 147464 | tf_op jit(solution)/shard_map/ppermute | solution.py:542
  21.8 8.7 %collective-permute-start.7 = (f32[32,2176]{1,0:T(8,128)S(1)}, f32[32,2176]{1,0:T(8,128)S(1)}, u32[]{:S(2)}, u32[]{:S(2)}) collective-permute-start(f32[32,2176]{1,0:T(8,128)S(1)} %get-tuple-element.85.e_mine), channel_id=1, source_target_pairs={{0,1},{1,0},{2,3},{3,2},{4,5},{5,4},{6,7},{7,6},{8,9},{9,8},{10,11... | collective-permute-start | bytes 835592 | tf_op jit(solution)/shard_map/ppermute | solution.py:542
  25.9 5.8 %collective-permute-start.6 = (f32[64,384]{1,0:T(8,128)S(1)}, f32[64,384]{1,0:T(8,128)S(1)}, u32[]{:S(2)}, u32[]{:S(2)}) collective-permute-start(f32[64,384]{1,0:T(8,128)S(1)} %get-tuple-element.74), channel_id=1, source_target_pairs={{0,2},{2,0},{4,6},{6,4},{8,10},{10,8},{12,14},{14,12},{1,3},{3,1},... | collective-permute-start | bytes 294920 | tf_op jit(solution)/shard_map/ppermute | solution.py:547
  30.5 12.2 %copy-start = (bf16[2112,384]{1,0:T(8,128)(2,1)S(1)}, bf16[2112,384]{1,0:T(8,128)(2,1)}, u32[]{:S(2)}) copy-start(bf16[2112,384]{1,0:T(8,128)(2,1)} %w_out_ref.1) | copy-start | bytes 4866052
  30.5 12.2 %copy-start.2 = (f32[32,384]{1,0:T(8,128)S(1)}, f32[32,384]{1,0:T(8,128)}, u32[]{:S(2)}) copy-start(f32[32,384]{1,0:T(8,128)} %cot_ref.1) | copy-start | bytes 147460
  31.8 8.9 %collective-permute-start.10 = (f32[32,384]{1,0:T(8,128)S(1)}, f32[32,384]{1,0:T(8,128)S(1)}, u32[]{:S(2)}, u32[]{:S(2)}) collective-permute-start(f32[32,384]{1,0:T(8,128)S(1)} %get-tuple-element.105), channel_id=1, source_target_pairs={{0,4},{2,6},{4,0},{6,2},{8,5},{10,7},{12,1},{14,3},{1,12},{3,14},{... | collective-permute-start | bytes 147464 | tf_op jit(solution)/shard_map/ppermute | solution.py:552
  33.8 8.7 %collective-permute-start.12 = (f32[32,384]{1,0:T(8,128)S(1)}, f32[32,384]{1,0:T(8,128)S(1)}, u32[]{:S(2)}, u32[]{:S(2)}) collective-permute-start(f32[32,384]{1,0:T(8,128)S(1)} %get-tuple-element.105), channel_id=1, source_target_pairs={{0,5},{2,7},{4,1},{6,3},{8,4},{10,6},{12,0},{14,2},{1,13},{3,15},{... | collective-permute-start | bytes 147464 | tf_op jit(solution)/shard_map/ppermute | solution.py:552
  34.3 8.2 %collective-permute-start.11 = (f32[32,384]{1,0:T(8,128)S(1)}, f32[32,384]{1,0:T(8,128)S(1)}, u32[]{:S(2)}, u32[]{:S(2)}) collective-permute-start(f32[32,384]{1,0:T(8,128)S(1)} %get-tuple-element.106), channel_id=1, source_target_pairs={{0,1},{2,3},{4,5},{6,7},{8,0},{10,2},{12,4},{14,6},{1,9},{3,11},{5... | collective-permute-start | bytes 147464 | tf_op jit(solution)/shard_map/ppermute | solution.py:552
  35.7 6.8 %collective-permute-start.9 = (f32[32,384]{1,0:T(8,128)S(1)}, f32[32,384]{1,0:T(8,128)S(1)}, u32[]{:S(2)}, u32[]{:S(2)}) collective-permute-start(f32[32,384]{1,0:T(8,128)S(1)} %get-tuple-element.106), channel_id=1, source_target_pairs={{0,0},{2,2},{4,4},{6,6},{8,1},{10,3},{12,5},{14,7},{1,8},{3,10},{5... | collective-permute-start | bytes 147464 | tf_op jit(solution)/shard_map/ppermute | solution.py:552
  36.4 6.3 %collective-permute-start.8 = (f32[32,384]{1,0:T(8,128)S(1)}, f32[32,384]{1,0:T(8,128)S(1)}, u32[]{:S(2)}, u32[]{:S(2)}) collective-permute-start(f32[32,384]{1,0:T(8,128)S(1)} %get-tuple-element.81.r0), channel_id=1, source_target_pairs={{0,1},{1,0},{2,3},{3,2},{4,5},{5,4},{6,7},{7,6},{8,9},{9,8},{10,11... | collective-permute-start | bytes 147464 | tf_op jit(solution)/shard_map/ppermute | solution.py:550
  47.0 1.4 %collective-permute-start.13 = (f32[64,512]{1,0:T(8,128)S(1)}, f32[64,512]{1,0:T(8,128)S(1)}, u32[]{:S(2)}, u32[]{:S(2)}) collective-permute-start(f32[64,512]{1,0:T(8,128)S(1)} %get-tuple-element.90), channel_id=1, source_target_pairs={{0,2},{2,0},{4,6},{6,4},{8,10},{10,8},{12,14},{14,12},{1,3},{3,1},... | collective-permute-start | bytes 393224 | tf_op jit(solution)/shard_map/ppermute | solution.py:547
  47.1 12.5 %copy-start.8 = (bf16[128,12]{0,1:T(8,128)(2,1)S(1)}, bf16[128,12]{0,1:T(8,128)(2,1)}, u32[]{:S(2)}) copy-start(bf16[128,12]{0,1:T(8,128)(2,1)} %param.29) | copy-start | bytes 9220
  48.4 13.1 %collective-permute-start.15 = (f32[32,512]{1,0:T(8,128)S(1)}, f32[32,512]{1,0:T(8,128)S(1)}, u32[]{:S(2)}, u32[]{:S(2)}) collective-permute-start(f32[32,512]{1,0:T(8,128)S(1)} %get-tuple-element.104), channel_id=1, source_target_pairs={{0,0},{2,2},{4,4},{6,6},{8,1},{10,3},{12,5},{14,7},{1,8},{3,10},{5... | collective-permute-start | bytes 196616 | tf_op jit(solution)/shard_map/ppermute | solution.py:552
  49.1 16.5 %collective-permute-start.17 = (f32[32,512]{1,0:T(8,128)S(1)}, f32[32,512]{1,0:T(8,128)S(1)}, u32[]{:S(2)}, u32[]{:S(2)}) collective-permute-start(f32[32,512]{1,0:T(8,128)S(1)} %get-tuple-element.104), channel_id=1, source_target_pairs={{0,1},{2,3},{4,5},{6,7},{8,0},{10,2},{12,4},{14,6},{1,9},{3,11},{5... | collective-permute-start | bytes 196616 | tf_op jit(solution)/shard_map/ppermute | solution.py:552
  55.3 6.2 %collective-permute-start.16 = (f32[32,512]{1,0:T(8,128)S(1)}, f32[32,512]{1,0:T(8,128)S(1)}, u32[]{:S(2)}, u32[]{:S(2)}) collective-permute-start(f32[32,512]{1,0:T(8,128)S(1)} %get-tuple-element.103), channel_id=1, source_target_pairs={{0,4},{2,6},{4,0},{6,2},{8,5},{10,7},{12,1},{14,3},{1,12},{3,14},{... | collective-permute-start | bytes 196616 | tf_op jit(solution)/shard_map/ppermute | solution.py:552
  56.6 9.0 %collective-permute-start.18 = (f32[32,512]{1,0:T(8,128)S(1)}, f32[32,512]{1,0:T(8,128)S(1)}, u32[]{:S(2)}, u32[]{:S(2)}) collective-permute-start(f32[32,512]{1,0:T(8,128)S(1)} %get-tuple-element.103), channel_id=1, source_target_pairs={{0,5},{2,7},{4,1},{6,3},{8,4},{10,6},{12,0},{14,2},{1,13},{3,15},{... | collective-permute-start | bytes 196616 | tf_op jit(solution)/shard_map/ppermute | solution.py:552
  57.6 8.0 %collective-permute-start.14 = (f32[32,512]{1,0:T(8,128)S(1)}, f32[32,512]{1,0:T(8,128)S(1)}, u32[]{:S(2)}, u32[]{:S(2)}) collective-permute-start(f32[32,512]{1,0:T(8,128)S(1)} %query_zero.1.r0), channel_id=1, source_target_pairs={{0,1},{1,0},{2,3},{3,2},{4,5},{5,4},{6,7},{7,6},{8,9},{9,8},{10,11... | collective-permute-start | bytes 196616 | tf_op jit(solution)/shard_map/ppermute | solution.py:550

commit v2 on v1

--- a/solution.py
+++ b/solution.py
@@ -150,10 +150,17 @@
     return hi, mid, lo
 
 
-def pack_body(single_ref, frames_ref, chains_ref, pack_ref):
+def pack_body(single_hbm, frames_hbm, chains_hbm, pack_ref, frames_ref, chains_ref, sems):
     rows = pack_ref.shape[0]
-    pack_ref[:, 0:C] = single_ref[1]
-    pack_ref[:, C : 2 * C] = single_ref[0]
+    ends = (
+        (frames_hbm, frames_ref), (chains_hbm, chains_ref), (single_hbm.at[1], pack_ref.at[:, 0:C]),
+        (single_hbm.at[0], pack_ref.at[:, C : 2 * C]),
+    )
+    copies = [pltpu.make_async_copy(src, dst, sems.at[n]) for n, (src, dst) in enumerate(ends)]
+    for copy in copies:
+        copy.start()
+    copies[0].wait()
+    copies[1].wait()
     out = jnp.zeros((rows, 128), F32)
     for slot, l in ((0, 1), (12, 0)):
         hot = (iota((12, 128), 1) == iota((12, 128), 0) + slot).astype(F32).astype(BF16)
@@ -161,6 +168,8 @@
             out = out + mm(part, hot, TN)
     hot = (iota((1, 128), 1) == CHAIN_LANE - FRAME_LANE).astype(F32).astype(BF16)
     pack_ref[:, 2 * C :] = out + mm(chains_ref[...].astype(F32).astype(BF16), hot, TN)
+    copies[2].wait()
+    copies[3].wait()
 
 
 def prep_body(
@@ -385,8 +394,12 @@
     theirs[rows:, :] = get(1 - zb, 1 - core)
 
 
-def final_body(r0, r1, r2, r3, r4, r5, one_ref, single_out, frames_out):
-    total = (r0[...] + r1[...]) + (r2[...] + r3[...]) + (r4[...] + r5[...])
+def add_pieces(flag_ref, query, query_other, part, one, two):
+    return (query[...] + query_other[...]) + (one[...] + jnp.where(flag_ref[0] == 1, part[...], two[...]))
+
+
+def final_body(flag_ref, r0, r1, r2, r3, r4, one_ref, single_out, frames_out):
+    total = add_pieces(flag_ref, r0, r1, r2, r3, r4)
     single_out[...] = one_ref[...] + total[:, 0:C]
     turned = jnp.transpose(total[:, C:])
     for l in range(2):
@@ -420,12 +433,12 @@
 
 
 def back_zero_body(
-    flag_ref, cot_ref, r0, r1, r2, r3, r4, r5, e_mine, e_other, pm_ref, kv_ref, keys_ref, own_ref, q_ref, pair_ref,
+    flag_ref, cot_ref, r0, r1, r2, r3, r4, e_mine, e_other, pm_ref, kv_ref, keys_ref, own_ref, q_ref, pair_ref,
     w_out_ref, wk_ref, sc_ref, frk_ref,
     z_ref, mine_a, mine_b, theirs, pts_ref, sum_ref, pu_ref, work_ref, gp_ref, d_ref,
 ):
     rows = own_ref.shape[0]
-    total = (r0[...] + r1[...]) + (r2[...] + r3[...]) + (r4[...] + r5[...])
+    total = add_pieces(flag_ref, r0, r1, r2, r3, r4)
     sum_ref[...] = total
     upstream_parts(cot_ref[...] + total, w_out_ref, gp_ref, pu_ref, rows)
     pair_products(pu_ref, pair_ref, d_ref, rows)
@@ -490,6 +503,10 @@
     )(*args)
 
 
+def in_hbm(*arrays):
+    return tuple(pltpu.with_memory_space_constraint(x, pltpu.HBM) for x in arrays)
+
+
 def joint(pairs):
     return [
         ((a * 2 + k) * 2 + x, (b * 2 + k) * 2 + y) for (x, a), (y, b) in pairs for k in range(2)
@@ -498,12 +515,11 @@
 
 BOTH = ("row", "col")
 FETCH_ONE = joint([((0, 0), (0, 1)), ((0, 1), (0, 0)), ((1, 0), (0, 2)), ((1, 1), (0, 3)), ((1, 2), (1, 3)), ((1, 3), (1, 2)), ((0, 2), (1, 0)), ((0, 3), (1, 1))])
-FETCH_TWO = joint([((0, 0), (0, 3)), ((0, 1), (0, 2)), ((1, 2), (1, 1)), ((1, 3), (1, 0))])
-SCATTER = [
-    joint([((x, z), (((s ^ z) >> 1) & 1, 2 * x + ((s ^ z) & 1))) for x in range(2) for z in range(4)])
-    for s in range(4)
-]
+FETCH_TWO = joint([((0, 0), (0, 3)), ((0, 1), (0, 2)), ((1, 2), (1, 1)), ((1, 3), (1, 0)), ((1, 0), (0, 0)), ((1, 1), (0, 1)), ((0, 2), (1, 2)), ((0, 3), (1, 3))])
+SEND_ONE = joint([((0, 0), (1, 0)), ((0, 1), (1, 1)), ((0, 2), (0, 0)), ((0, 3), (0, 1)), ((1, 2), (0, 2)), ((1, 3), (0, 3)), ((1, 0), (1, 2)), ((1, 1), (1, 3))])
+SEND_TWO = joint([((0, 2), (1, 0)), ((0, 3), (1, 1)), ((1, 0), (0, 2)), ((1, 1), (0, 3)), ((0, 0), (0, 1)), ((0, 1), (0, 0)), ((1, 2), (1, 3)), ((1, 3), (1, 2))])
 CORE_SWAP = [(i, i ^ 1) for i in range(8)]
+Z_SWAP = [(i, i ^ 2) for i in range(8)]
 COL_SWAP = [(0, 1), (1, 0)]
 
 
@@ -517,8 +533,8 @@
     col_total = lax.axis_size("col")
     fast = row_total == 8 and col_total == 2 and keys == 4 * rows
     (pack,) = call(
-        pack_body, "pack", [VMEM] * 3, [((rows, PACK), F32)],
-        (single, frames.transpose(1, 0, 2), chains[None]),
+        pack_body, "pack", [HBM] * 3, [((rows, PACK), F32)], in_hbm(single, frames.transpose(1, 0, 2), chains[None]),
+        [pltpu.VMEM((12, 2, rows), F32), pltpu.VMEM((1, rows), jnp.int32), pltpu.SemaphoreType.DMA((4,))],
     )
     col = lax.axis_index("col")
     row = lax.axis_index("row")
@@ -542,20 +558,23 @@
             return lax.ppermute(x, "col", COL_SWAP)
         return lax.psum(x, "col") - x
 
-    def reduce(mine_a, mine_b, theirs, late):
+    def reduce(mine_a, mine_b, theirs, late, beside):
         if fast:
             got = lax.ppermute(theirs, "row", CORE_SWAP)
             query, *rest = late()
             got, query = lax.optimization_barrier((got, query))
             query_other = lax.ppermute(query, "col", COL_SWAP)
-            part = (mine_a + got[:rows], mine_b + got[rows:])
-            return [query, query_other] + [lax.ppermute(part[s & 1], BOTH, SCATTER[s]) for s in range(4)], rest
+            half = lax.ppermute(mine_b + got[rows:], "row", Z_SWAP)
+            half, beside = lax.optimization_barrier((half, beside))
+            part = mine_a + got[:rows] + half
+            sent = [lax.ppermute(part, BOTH, SEND_ONE), lax.ppermute(part, BOTH, SEND_TWO)]
+            return [query, query_other, part] + sent, rest, beside
         query, *rest = late()
         parts = jnp.concatenate([mine_a, theirs[:rows], mine_b, theirs[rows:]], axis=0)
         summed = lax.all_gather(lax.psum(parts, "row"), "col", axis=0, tiled=True)
+        back = lax.dynamic_slice_in_dim(summed, row * rows, rows, 0)
         zero = jnp.zeros_like(query)
-        back = lax.dynamic_slice_in_dim(summed, row * rows, rows, 0)
-        return [lax.psum(query, "col"), back, zero, zero, zero, zero], rest
+        return [lax.psum(query, "col"), zero, back, zero, zero], rest, beside
 
     probs = saved_probs.reshape(2, H * rows, keys)
     hr = H * rows
@@ -566,7 +585,7 @@
         prep_body, "prep", [SMEM, VMEM] + [HBM] * 9,
         [((1280, C), BF16), ((LANES, C), BF16), ((rows, 768), F32), ((rows, 1024), F32), ((rows, 1024), F32),
          ((hr, CZ), F32), ((hr, keys), F32), ((8, 128), F32)],
-        (head_weights, own, *(pltpu.with_memory_space_constraint(x, pltpu.HBM) for x in loads)),
+        (head_weights, own, *in_hbm(*loads)),
         [pltpu.VMEM(x.shape, x.dtype) for x in loads] + [pltpu.SemaphoreType.DMA((len(loads),))],
     )
     if fast:
@@ -597,34 +616,38 @@
         [pltpu.VMEM((keys, C), F32)],
         6.0,
     )
-    pts, e0_other = lax.optimization_barrier((pts, e0_other))
-    pieces, (frq, frk) = reduce(
+    pieces, (frq, frk), e0_other = reduce(
         mine_a, mine_b, theirs,
         lambda: call(
             functools.partial(query_one_body, share), "query_one", [VMEM] * 8,
             [((rows, C), F32), ((rows, 128), F32), ((keys, 128), F32)],
             (z1, kv1, own, q1, pts, grads, wq, sc),
+            (),
+            0.01,
         ),
+        e0_other,
     )
     z0, mine_a, mine_b, theirs, pts, single_one, pu0 = call(
-        back_zero_body, "back_zero", [SMEM] + [VMEM] * 19,
+        back_zero_body, "back_zero", [SMEM] + [VMEM] * 18,
         [((2 * hr, keys), F32), ((rows, 512), F32), ((rows, 512), F32), ((2 * rows, 512), F32), ((rows, 1152), F32),
          ((rows, C), F32), ((hr, CZ), F32)],
         (flags, cotangent, *pieces, e0, e0_other, pm, kv0, key_pack, own, q0, pair, w_out, wk, sc, frk),
         [pltpu.VMEM((keys, 512), F32), pltpu.VMEM((rows, 768), F32), pltpu.VMEM((hr, keys), F32)],
     )
-    pieces, _ = reduce(
+    (d_pair,) = call(
+        pair_body, "pair_grad", [VMEM] * 5, [((rows, keys, CZ), BF16)], (z1, z0, pu1, pu0, w_bias.T)
+    )
+    pieces, _, d_pair = reduce(
         mine_a, mine_b, theirs,
         lambda: call(
             functools.partial(query_zero_body, share), "query_zero", [VMEM] * 8, [((rows, 512), F32)],
             (z0, kv0, own, q0, pts, wq, sc, frq),
         ),
-    )
-    (d_pair,) = call(
-        pair_body, "pair_grad", [VMEM] * 5, [((rows, keys, CZ), BF16)], (z1, z0, pu1, pu0, w_bias.T)
+        d_pair,
     )
     d_single, d_frames = call(
-        final_body, "final", [VMEM] * 7, [((rows, C), F32), ((12, 2, rows), F32)], (*pieces, single_one)
+        final_body, "final", [SMEM] + [VMEM] * 6, [((rows, C), F32), ((12, 2, rows), F32)],
+        (flags, *pieces, single_one),
     )
     return (d_single, d_frames.transpose(1, 0, 2), d_pair)
 

time: 66.6 us -> 59.5 us (0.89)
  starting transfers between devices: 31.1 us -> 22.6 us
  waiting for transfers between devices: 12.9 us -> 15.5 us
  local copies, waits for them, and re-layouts: 2.28 us -> 0.03 us
  Pallas kernels: 19 us -> 20.3 us
    ppermute x8 -> x6, starting transfers between devices: 13.8 us -> 9.41 us  [the longest x2 3.43 us: reduce(): half = lax.ppermute(mine_b + got[rows:], 'row', Z_SWAP)]
    ppermute x8 -> x6, waiting for transfers between devices: 6 us -> 10.3 us  [the longest x2 7.65 us: reduce(): lax.ppermute(part, BOTH, SEND_ONE)]
    ppermute x2, starting transfers between devices: 6.19 us -> 2.68 us  [reduce(): query_other = lax.ppermute(query, 'col', COL_SWAP)]
    unnamed x20 -> x14, local copies, waits for them, and re-layouts: 2.28 us -> 0.03 us
    ppermute x1, starting transfers between devices: 5.19 us -> 3.29 us  [local(): two = lax.ppermute(pack, BOTH, FETCH_TWO)]
    ppermute x2, waiting for transfers between devices: 5.17 us -> 3.63 us  [col_other(): return lax.ppermute(x, 'col', COL_SWAP)]
    pallas_call x10, Pallas kernels: 19 us -> 20.3 us  [call(): pl.pallas_call(body, name=name, in_specs=in_specs, out_specs=tuple((VMEM...]
    ppermute x2, starting transfers between devices: 2.15 us -> 3.31 us  [col_other(): return lax.ppermute(x, 'col', COL_SWAP)]
  transfers between devices with their start and end apart: 19 -> 17, of which waited for: 8 -> 9; matrix products, arithmetic and copies ran while one was open for 0% -> 0% of each run, Pallas kernels for 18% -> 16%
where the time goes in v2:
time: 59.5 us; the launch traced here: 59.3 us
  starting transfers between devices  22.6 us (38%)
  Pallas kernels  20.3 us (34%)
  waiting for transfers between devices  15.5 us (26%)
  between operations  0.8 us (1%)
    pallas_call x10, Pallas kernels, call(): pl.pallas_call(body, name=name, in_specs=in_specs, out_specs=tuple((VMEM...  20.3 us
    ppermute x2, waiting for transfers between devices, reduce(): lax.ppermute(part, BOTH, SEND_ONE)  7.65 us
    ppermute x2, waiting for transfers between devices, col_other(): return lax.ppermute(x, 'col', COL_SWAP)  3.63 us
    ppermute x2, starting transfers between devices, reduce(): half = lax.ppermute(mine_b + got[rows:], 'row', Z_SWAP)  3.43 us
    ppermute x2, starting transfers between devices, col_other(): return lax.ppermute(x, 'col', COL_SWAP)  3.31 us
    ppermute x1, starting transfers between devices, local(): two = lax.ppermute(pack, BOTH, FETCH_TWO)  3.29 us
    ppermute x2, starting transfers between devices, reduce(): lax.ppermute(part, BOTH, SEND_TWO)  3.25 us
    ppermute x1, starting transfers between devices, local(): one = lax.ppermute(pack, BOTH, FETCH_ONE)  3.09 us
  transfers between devices with their start and end apart: 17, of which 9 were waited for; matrix products, arithmetic and copies ran while one was open for 0% of the time, Pallas kernels for 16%

profile of v2, /device:TPU:0, one launch (start us, length us, event | category | flops | bytes accessed | tf_op | source)
XLA Modules:
  0.0 59.3 jit_solution(14929678533298409085)
XLA Ops:
  0.6 0.0 copy-start.3
  0.6 1.0 %pack.1.pack_ref.own_ref = f32[32,896]{1,0:T(8,128)S(1)} custom-call(f32[2,32,384]{2,1,0:T(8,128)} %single_hbm.1, f32[12,2,32]{2,1,0:T(2,128)} %bitcast.22, s32[1,32]{1,0:T(1,128)} %bitcast.23), custom_call_target="tpu_custom_call" | custom-call | flops 1000000000 | bytes 3000000 | tf_op jit(solution)/shard_map/pack/pallas_call | solution.py:494
  1.6 3.1 %collective-permute-start.1 = (f32[32,896]{1,0:T(8,128)S(1)}, f32[32,896]{1,0:T(8,128)S(1)}, u32[]{:S(2)}, u32[]{:S(2)}) collective-permute-start(f32[32,896]{1,0:T(8,128)S(1)} %pack.1.pack_ref.own_ref), channel_id=1, source_target_pairs={{0,4},{2,6},{4,0},{6,2},{1,8},{3,10},{5,12},{7,14},{9,13},{11,15},... | collective-permute-start | bytes 344072 | tf_op jit(solution)/shard_map/ppermute | solution.py:545
  4.7 3.3 %collective-permute-start.2 = (f32[32,896]{1,0:T(8,128)S(1)}, f32[32,896]{1,0:T(8,128)S(1)}, u32[]{:S(2)}, u32[]{:S(2)}) collective-permute-start(f32[32,896]{1,0:T(8,128)S(1)} %pack.1.pack_ref.own_ref), channel_id=1, source_target_pairs={{0,12},{2,14},{4,8},{6,10},{9,5},{11,7},{13,1},{15,3},{1,0},{3,2},... | collective-permute-start | bytes 344072 | tf_op jit(solution)/shard_map/ppermute | solution.py:546
  8.0 0.0 collective-permute-start
  8.0 0.0 copy-done.3
  8.0 0.0 copy-start.4
  8.0 0.0 copy-start.5
  8.0 4.0 %prep.1 = (bf16[1280,384]{1,0:T(8,128)(2,1)S(1)}, bf16[640,384]{1,0:T(8,128)(2,1)S(1)}, f32[32,768]{1,0:T(8,128)S(1)}, f32[32,1024]{1,0:T(8,128)S(1)}, f32[32,10...) custom-call(f32[12]{0:T(128)S(1)} %copy-done.3, ...), custom_call_target="tpu_custom_call" | custom-call | flops 1000000000 | bytes 3000000 | tf_op jit(solution)/shard_map/prep/pallas_call | solution.py:494
  12.1 0.0 collective-permute-done.1.p1_ref
  12.1 0.0 collective-permute-done.2.p2_ref
  12.1 0.6 collective-permute-start.3
  12.6 0.1 collective-permute-start.4
  12.7 0.1 pad_add_fusion.flag_ref
  12.8 0.0 collective-permute-done.ownx_ref
  12.8 0.8 %collective-permute-done.3.p1x_ref = f32[32,896]{1,0:T(8,128)S(1)} collective-permute-done((f32[32,896]{1,0:T(8,128)S(1)}, f32[32,896]{1,0:T(8,128)S(1)}, u32[]{:S(2)}, u32[]{:S(2)}) %collective-permute-start.3) | collective-permute-done | bytes 114720 | tf_op jit(solution)/shard_map/ppermute | solution.py:595
  13.6 0.4 collective-permute-done.4.p2x_ref
  14.0 0.0 copy-done.4
  14.0 0.0 copy-done.5
  14.0 0.0 copy-start.1
  14.0 1.8 %first.1 = (f32[128,896]{1,0:T(8,128)S(1)}, f32[128,2048]{1,0:T(8,128)S(1)}, bf16[2,384,128]{2,1,0:T(8,128)(2,1)S(1)}, f32[32,384]{1,0:T(8,128)S(1)}) custom-call(s32[3]{0:T(128)S(1)} %pad_add_fusion.flag_ref, f32[32,896]{1,0:T(8,128)S(1)} %pack.1.pack_ref.own_ref, f32[32,896]{1,0:T(8,128)S(1)} %collective-permute-done.ownx_ref, ...), custom_call_target="tpu_custom_call" | custom-call | flops 1000000000 | bytes 3000000 | tf_op jit(solution)/shard_map/first/pallas_call | solution.py:494
  15.7 1.7 %collective-permute-start.5 = (f32[32,384]{1,0:T(8,128)S(1)}, f32[32,384]{1,0:T(8,128)S(1)}, u32[]{:S(2)}, u32[]{:S(2)}) collective-permute-start(f32[32,384]{1,0:T(8,128)S(1)} %get-tuple-element.68.e_mine), channel_id=1, source_target_pairs={{0,1},{1,0},{2,3},{3,2},{4,5},{5,4},{6,7},{7,6},{8,9},{9,8},{10,11... | collective-permute-start | bytes 147464 | tf_op jit(solution)/shard_map/ppermute | solution.py:558
  17.4 0.0 copy-done.1
  17.4 1.3 %second.1 = (f32[128,2048]{1,0:T(8,128)S(1)}, f32[32,2176]{1,0:T(8,128)S(1)}) custom-call(f32[128,896]{1,0:T(8,128)S(1)} %get-tuple-element.69.keys_ref, bf16[1280,384]{1,0:T(8,128)(2,1)S(1)} %get-tuple-element.65.wk_ref, bf16[2,384,128]{2,1,0:T(8,128)(2,1)S(1)} %get-tuple-element.70.pm_ref, bf16[32,128,128]{2,1,0:T(8,128)(2,1)S(1)} %copy-done.1), custom_call_target="tpu_custom_call" | custom-call | flops 1000000000 | bytes 3000000 | tf_op jit(solution)/shard_map/second/pallas_call | solution.py:494
  18.7 1.2 %collective-permute-done.5.e_other = f32[32,384]{1,0:T(8,128)S(1)} collective-permute-done((f32[32,384]{1,0:T(8,128)S(1)}, f32[32,384]{1,0:T(8,128)S(1)}, u32[]{:S(2)}, u32[]{:S(2)}) %collective-permute-start.5) | collective-permute-done | bytes 49184 | tf_op jit(solution)/shard_map/ppermute | solution.py:558
  19.9 2.6 %back_one.1 = (f32[768,128]{1,0:T(8,128)S(1)}, f32[32,384]{1,0:T(8,128)S(1)}, f32[32,384]{1,0:T(8,128)S(1)}, f32[64,384]{1,0:T(8,128)S(1)}, f32[32,1152]{1,0:T(8,128)S(1)}, /*index=5*/f32[128,768]{1,0:T(8,128)S(1)}) custom-call(s32[3]{0:T(128)S(1)} %pad_add_fusion.flag_ref, f32[32,384]{1,0:T(8,128)S(1)} %get-tuple-element.68.e_mine, ...), custom_call_target="tpu_custom_call" | custom-call | flops 6000000000 | bytes 18000000 | tf_op jit(solution)/shard_map/back_one/pallas_call | solution.py:494
  22.5 0.0 copy-start
  22.5 0.0 copy-start.2
  22.6 0.1 collective-permute-start.6
  22.6 1.7 %collective-permute-start.9 = (f32[32,2176]{1,0:T(8,128)S(1)}, f32[32,2176]{1,0:T(8,128)S(1)}, u32[]{:S(2)}, u32[]{:S(2)}) collective-permute-start(f32[32,2176]{1,0:T(8,128)S(1)} %get-tuple-element.87.e_mine), channel_id=1, source_target_pairs={{0,1},{1,0},{2,3},{3,2},{4,5},{5,4},{6,7},{7,6},{8,9},{9,8},{10,11... | collective-permute-start | bytes 835592 | tf_op jit(solution)/shard_map/ppermute | solution.py:558
  24.3 1.2 %query_one.1 = (f32[32,384]{1,0:T(8,128)S(1)}, f32[32,128]{1,0:T(8,128)S(1)}, f32[128,128]{1,0:T(8,128)S(1)}) custom-call(f32[768,128]{1,0:T(8,128)S(1)} %get-tuple-element.77.z_ref.z1_ref, f32[128,2048]{1,0:T(8,128)S(1)} %get-tuple-element.73.kv_ref, f32[32,896]{1,0:T(8,128)S(1)} %pack.1.pack_ref.own_ref, f32[32,1024]{1,0:T(8,128)S(1)} %get-tuple-element.74.q_ref, ...), custom_call_target="tpu_custom_call" | custom-call | flops 10000000 | bytes 30000 | tf_op jit(solution)/shard_map/query_one/pallas_call | solution.py:494
  25.5 0.0 collective-permute-done.6
  25.5 1.8 %collective-permute-start.8 = (f32[32,384]{1,0:T(8,128)S(1)}, f32[32,384]{1,0:T(8,128)S(1)}, u32[]{:S(2)}, u32[]{:S(2)}) collective-permute-start(f32[32,384]{1,0:T(8,128)S(1)} %slice_add_fusion.1), channel_id=1, source_target_pairs={{0,4},{2,6},{4,0},{6,2},{8,12},{10,14},{12,8},{14,10},{1,5},{3,7},... | collective-permute-start | bytes 147464 | tf_op jit(solution)/shard_map/ppermute | solution.py:567
  27.4 0.2 collective-permute-start.7
  27.6 2.1 %collective-permute-done.8 = f32[32,384]{1,0:T(8,128)S(1)} collective-permute-done((f32[32,384]{1,0:T(8,128)S(1)}, f32[32,384]{1,0:T(8,128)S(1)}, u32[]{:S(2)}, u32[]{:S(2)}) %collective-permute-start.8) | collective-permute-done | bytes 49184 | tf_op jit(solution)/shard_map/ppermute | solution.py:567
  29.7 2.5 %collective-permute-done.9.e_other = f32[32,2176]{1,0:T(8,128)S(1)} collective-permute-done((f32[32,2176]{1,0:T(8,128)S(1)}, f32[32,2176]{1,0:T(8,128)S(1)}, u32[]{:S(2)}, u32[]{:S(2)}) %collective-permute-start.9) | collective-permute-done | bytes 278560 | tf_op jit(solution)/shard_map/ppermute | solution.py:558
  32.2 1.8 %collective-permute-start.10 = (f32[32,384]{1,0:T(8,128)S(1)}, f32[32,384]{1,0:T(8,128)S(1)}, u32[]{:S(2)}, u32[]{:S(2)}) collective-permute-start(f32[32,384]{1,0:T(8,128)S(1)} %add_add_fusion.1.r2), channel_id=1, source_target_pairs={{0,1},{2,3},{4,5},{6,7},{8,0},{10,2},{12,4},{14,6},{9,8},{11,10},{... | collective-permute-start | bytes 147464 | tf_op jit(solution)/shard_map/ppermute | solution.py:570
  34.0 1.8 %collective-permute-start.11 = (f32[32,384]{1,0:T(8,128)S(1)}, f32[32,384]{1,0:T(8,128)S(1)}, u32[]{:S(2)}, u32[]{:S(2)}) collective-permute-start(f32[32,384]{1,0:T(8,128)S(1)} %add_add_fusion.1.r2), channel_id=1, source_target_pairs={{8,1},{10,3},{12,5},{14,7},{1,8},{3,10},{5,12},{7,14},{0,4},{2,6},... | collective-permute-start | bytes 147464 | tf_op jit(solution)/shard_map/ppermute | solution.py:570
  35.8 0.0 collective-permute-done.7.r1
  35.8 2.1 %collective-permute-done.10.r3 = f32[32,384]{1,0:T(8,128)S(1)} collective-permute-done((f32[32,384]{1,0:T(8,128)S(1)}, f32[32,384]{1,0:T(8,128)S(1)}, u32[]{:S(2)}, u32[]{:S(2)}) %collective-permute-start.10) | collective-permute-done | bytes 49184 | tf_op jit(solution)/shard_map/ppermute | solution.py:570
  37.8 0.5 collective-permute-done.11.r4
  38.3 0.0 copy-done
  38.3 0.0 copy-done.2
  38.3 4.3 %back_zero.1 = (f32[768,128]{1,0:T(8,128)S(1)}, f32[32,512]{1,0:T(8,128)S(1)}, f32[32,512]{1,0:T(8,128)S(1)}, f32[64,512]{1,0:T(8,128)S(1)}, f32[32,1152]{1,0:T(...) custom-call(s32[3]{0:T(128)S(1)} %pad_add_fusion.flag_ref, f32[32,384]{1,0:T(8,128)S(1)} %copy-done.2, ...), custom_call_target="tpu_custom_call" | custom-call | flops 1000000000 | bytes 3000000 | tf_op jit(solution)/shard_map/back_zero/pallas_call | solution.py:494
  42.7 0.1 collective-permute-start.12
  42.8 0.0 copy-start.6
  42.8 0.9 %query_zero.1.r0 = f32[32,512]{1,0:T(8,128)S(1)} custom-call(f32[768,128]{1,0:T(8,128)S(1)} %get-tuple-element.93.z_ref.z0_ref, f32[128,2048]{1,0:T(8,128)S(1)} %get-tuple-element.89.kv_ref, f32[32,896]{1,0:T(8,128)S(1)} %pack.1.pack_ref.own_ref, f32[32,1024]{1,0:T(8,128)S(1)} %get-tuple-element.90.q_ref, f32[32,1152]{1,0:T(8,128)S(1)} %get-tuple-element.94.pts_ref, ...), custom_call_target="tpu_custom_call" | custom-call | flops 1000000000 | bytes 3000000 | tf_op jit(solution)/shard_map/query_zero/pallas_call | solution.py:494
  43.7 0.4 collective-permute-done.12
  44.1 1.6 %collective-permute-start.14 = (f32[32,512]{1,0:T(8,128)S(1)}, f32[32,512]{1,0:T(8,128)S(1)}, u32[]{:S(2)}, u32[]{:S(2)}) collective-permute-start(f32[32,512]{1,0:T(8,128)S(1)} %slice_add_fusion), channel_id=1, source_target_pairs={{0,4},{2,6},{4,0},{6,2},{8,12},{10,14},{12,8},{14,10},{1,5},{3,7},... | collective-permute-start | bytes 196616 | tf_op jit(solution)/shard_map/ppermute | solution.py:567
  45.7 0.0 copy-done.6
  45.7 1.9 %pair_grad.1 = bf16[32,128,128]{2,1,0:T(8,128)(2,1)} custom-call(f32[768,128]{1,0:T(8,128)S(1)} %get-tuple-element.77.z_ref.z1_ref, f32[768,128]{1,0:T(8,128)S(1)} %get-tuple-element.93.z_ref.z0_ref, f32[384,128]{1,0:T(8,128)S(1)} %get-tuple-element.100.pu1_ref, f32[384,128]{1,0:T(8,128)S(1)} %get-tuple-element.101.pu0_ref, bf16[12,128]{1,0:T(8,128)(2,1)S(1)} %bitcast.15), custom_call_target="tpu_custom_call" | custom-call | flops 1000000000 | bytes 3000000 | tf_op jit(solution)/shard_map/pair_grad/pallas_call | solution.py:494
  47.6 2.5 %collective-permute-start.13 = (f32[32,512]{1,0:T(8,128)S(1)}, f32[32,512]{1,0:T(8,128)S(1)}, u32[]{:S(2)}, u32[]{:S(2)}) collective-permute-start(f32[32,512]{1,0:T(8,128)S(1)} %query_zero.1.r0), channel_id=1, source_target_pairs={{0,1},{1,0},{2,3},{3,2},{4,5},{5,4},{6,7},{7,6},{8,9},{9,8},{10,11... | collective-permute-start | bytes 196616 | tf_op jit(solution)/shard_map/ppermute | solution.py:566
  50.1 0.0 collective-permute-done.14
  50.1 0.9 %collective-permute-start.15 = (f32[32,512]{1,0:T(8,128)S(1)}, f32[32,512]{1,0:T(8,128)S(1)}, u32[]{:S(2)}, u32[]{:S(2)}) collective-permute-start(f32[32,512]{1,0:T(8,128)S(1)} %add_add_fusion.r2), channel_id=1, source_target_pairs={{0,1},{2,3},{4,5},{6,7},{8,0},{10,2},{12,4},{14,6},{9,8},{11,10},{... | collective-permute-start | bytes 196616 | tf_op jit(solution)/shard_map/ppermute | solution.py:570
  51.0 1.5 %collective-permute-start.16 = (f32[32,512]{1,0:T(8,128)S(1)}, f32[32,512]{1,0:T(8,128)S(1)}, u32[]{:S(2)}, u32[]{:S(2)}) collective-permute-start(f32[32,512]{1,0:T(8,128)S(1)} %add_add_fusion.r2), channel_id=1, source_target_pairs={{8,1},{10,3},{12,5},{14,7},{1,8},{3,10},{5,12},{7,14},{0,4},{2,6},... | collective-permute-start | bytes 196616 | tf_op jit(solution)/shard_map/ppermute | solution.py:570
  52.5 0.0 collective-permute-done.13.r1
  52.5 5.6 %collective-permute-done.15.r3 = f32[32,512]{1,0:T(8,128)S(1)} collective-permute-done((f32[32,512]{1,0:T(8,128)S(1)}, f32[32,512]{1,0:T(8,128)S(1)}, u32[]{:S(2)}, u32[]{:S(2)}) %collective-permute-start.15) | collective-permute-done | bytes 65568 | tf_op jit(solution)/shard_map/ppermute | solution.py:570
  58.1 0.0 collective-permute-done.16.r4
  58.1 1.2 %final.1 = (f32[32,384]{1,0:T(8,128)}, f32[12,2,32]{2,1,0:T(2,128)}) custom-call(s32[3]{0:T(128)S(1)} %pad_add_fusion.flag_ref, f32[32,512]{1,0:T(8,128)S(1)} %query_zero.1.r0, f32[32,512]{1,0:T(8,128)S(1)} %collective-permute-done.13.r1, f32[32,512]{1,0:T(8,128)S(1)} %add_add_fusion.r2, f32[32,512]{1,0:T(8,128)S(1)} %collective-permute-done.15.r3, ...), custom_call_target="tpu_custom_call" | custom-call | flops 1000000000 | bytes 3000000 | tf_op jit(solution)/shard_map/final/pallas_call | solution.py:494
  (4 shorter events, 0.0 us)
Async XLA Ops:
  0.6 7.4 %copy-start.3 = (f32[12]{0:T(128)S(1)}, f32[12]{0:T(128)}, u32[]{:S(2)}) copy-start(f32[12]{0:T(128)} %hw_ref.1) | copy-start | bytes 148
  1.6 10.4 %collective-permute-start.1 = (f32[32,896]{1,0:T(8,128)S(1)}, f32[32,896]{1,0:T(8,128)S(1)}, u32[]{:S(2)}, u32[]{:S(2)}) collective-permute-start(f32[32,896]{1,0:T(8,128)S(1)} %pack.1.pack_ref.own_ref), channel_id=1, source_target_pairs={{0,4},{2,6},{4,0},{6,2},{1,8},{3,10},{5,12},{7,14},{9,13},{11,15},... | collective-permute-start | bytes 344072 | tf_op jit(solution)/shard_map/ppermute | solution.py:545
  4.7 7.4 %collective-permute-start.2 = (f32[32,896]{1,0:T(8,128)S(1)}, f32[32,896]{1,0:T(8,128)S(1)}, u32[]{:S(2)}, u32[]{:S(2)}) collective-permute-start(f32[32,896]{1,0:T(8,128)S(1)} %pack.1.pack_ref.own_ref), channel_id=1, source_target_pairs={{0,12},{2,14},{4,8},{6,10},{9,5},{11,7},{13,1},{15,3},{1,0},{3,2},... | collective-permute-start | bytes 344072 | tf_op jit(solution)/shard_map/ppermute | solution.py:546
  8.0 4.8 %collective-permute-start = (f32[32,896]{1,0:T(8,128)S(1)}, f32[32,896]{1,0:T(8,128)S(1)}, u32[]{:S(2)}, u32[]{:S(2)}) collective-permute-start(f32[32,896]{1,0:T(8,128)S(1)} %pack.1.pack_ref.own_ref), channel_id=1, source_target_pairs={{0,2},{2,0},{4,6},{6,4},{8,10},{10,8},{12,14},{14,12},{1,3},{3,1},... | collective-permute-start | bytes 344072 | tf_op jit(solution)/shard_map/ppermute | solution.py:544
  8.0 5.9 %copy-start.4 = (bf16[2,12,32,128]{3,2,1,0:T(8,128)(2,1)S(1)}, bf16[2,12,32,128]{3,2,1,0:T(8,128)(2,1)}, u32[]{:S(2)}) copy-start(bf16[2,12,32,128]{3,2,1,0:T(8,128)(2,1)} %param.18) | copy-start | bytes 589828
  8.0 5.9 %copy-start.5 = (s32[16,16]{1,0:T(8,128)S(1)}, s32[16,16]{1,0:T(8,128)}, u32[]{:S(2)}) copy-start(s32[16,16]{1,0:T(8,128)} %links_ref.1) | copy-start | bytes 3076
  12.1 1.5 %collective-permute-start.3 = (f32[32,896]{1,0:T(8,128)S(1)}, f32[32,896]{1,0:T(8,128)S(1)}, u32[]{:S(2)}, u32[]{:S(2)}) collective-permute-start(f32[32,896]{1,0:T(8,128)S(1)} %collective-permute-done.1.p1_ref), channel_id=1, source_target_pairs={{0,2},{2,0},{4,6},{6,4},{8,10},{10,8},{12,14},{14,12},{1,3},{3,1},... | collective-permute-start | bytes 344072 | tf_op jit(solution)/shard_map/ppermute | solution.py:595
  12.6 1.3 %collective-permute-start.4 = (f32[32,896]{1,0:T(8,128)S(1)}, f32[32,896]{1,0:T(8,128)S(1)}, u32[]{:S(2)}, u32[]{:S(2)}) collective-permute-start(f32[32,896]{1,0:T(8,128)S(1)} %collective-permute-done.2.p2_ref), channel_id=1, source_target_pairs={{0,2},{2,0},{4,6},{6,4},{8,10},{10,8},{12,14},{14,12},{1,3},{3,1},... | collective-permute-start | bytes 344072 | tf_op jit(solution)/shard_map/ppermute | solution.py:595
  14.0 3.4 %copy-start.1 = (bf16[32,128,128]{2,1,0:T(8,128)(2,1)S(1)}, bf16[32,128,128]{2,1,0:T(8,128)(2,1)}, u32[]{:S(2)}) copy-start(bf16[32,128,128]{2,1,0:T(8,128)(2,1)} %pair_ref.3) | copy-start | bytes 3145732
  15.7 4.2 %collective-permute-start.5 = (f32[32,384]{1,0:T(8,128)S(1)}, f32[32,384]{1,0:T(8,128)S(1)}, u32[]{:S(2)}, u32[]{:S(2)}) collective-permute-start(f32[32,384]{1,0:T(8,128)S(1)} %get-tuple-element.68.e_mine), channel_id=1, source_target_pairs={{0,1},{1,0},{2,3},{3,2},{4,5},{5,4},{6,7},{7,6},{8,9},{9,8},{10,11... | collective-permute-start | bytes 147464 | tf_op jit(solution)/shard_map/ppermute | solution.py:558
  22.5 15.8 %copy-start = (bf16[2112,384]{1,0:T(8,128)(2,1)S(1)}, bf16[2112,384]{1,0:T(8,128)(2,1)}, u32[]{:S(2)}) copy-start(bf16[2112,384]{1,0:T(8,128)(2,1)} %w_out_ref.1) | copy-start | bytes 4866052
  22.5 15.8 %copy-start.2 = (f32[32,384]{1,0:T(8,128)S(1)}, f32[32,384]{1,0:T(8,128)}, u32[]{:S(2)}) copy-start(f32[32,384]{1,0:T(8,128)} %cot_ref.1) | copy-start | bytes 147460
  22.6 3.0 %collective-permute-start.6 = (f32[64,384]{1,0:T(8,128)S(1)}, f32[64,384]{1,0:T(8,128)S(1)}, u32[]{:S(2)}, u32[]{:S(2)}) collective-permute-start(f32[64,384]{1,0:T(8,128)S(1)} %get-tuple-element.76), channel_id=1, source_target_pairs={{0,2},{2,0},{4,6},{6,4},{8,10},{10,8},{12,14},{14,12},{1,3},{3,1},... | collective-permute-start | bytes 294920 | tf_op jit(solution)/shard_map/ppermute | solution.py:563
  22.6 9.5 %collective-permute-start.9 = (f32[32,2176]{1,0:T(8,128)S(1)}, f32[32,2176]{1,0:T(8,128)S(1)}, u32[]{:S(2)}, u32[]{:S(2)}) collective-permute-start(f32[32,2176]{1,0:T(8,128)S(1)} %get-tuple-element.87.e_mine), channel_id=1, source_target_pairs={{0,1},{1,0},{2,3},{3,2},{4,5},{5,4},{6,7},{7,6},{8,9},{9,8},{10,11... | collective-permute-start | bytes 835592 | tf_op jit(solution)/shard_map/ppermute | solution.py:558
  25.5 4.2 %collective-permute-start.8 = (f32[32,384]{1,0:T(8,128)S(1)}, f32[32,384]{1,0:T(8,128)S(1)}, u32[]{:S(2)}, u32[]{:S(2)}) collective-permute-start(f32[32,384]{1,0:T(8,128)S(1)} %slice_add_fusion.1), channel_id=1, source_target_pairs={{0,4},{2,6},{4,0},{6,2},{8,12},{10,14},{12,8},{14,10},{1,5},{3,7},... | collective-permute-start | bytes 147464 | tf_op jit(solution)/shard_map/ppermute | solution.py:567
  27.4 8.4 %collective-permute-start.7 = (f32[32,384]{1,0:T(8,128)S(1)}, f32[32,384]{1,0:T(8,128)S(1)}, u32[]{:S(2)}, u32[]{:S(2)}) collective-permute-start(f32[32,384]{1,0:T(8,128)S(1)} %get-tuple-element.82.r0), channel_id=1, source_target_pairs={{0,1},{1,0},{2,3},{3,2},{4,5},{5,4},{6,7},{7,6},{8,9},{9,8},{10,11... | collective-permute-start | bytes 147464 | tf_op jit(solution)/shard_map/ppermute | solution.py:566
  32.2 5.7 %collective-permute-start.10 = (f32[32,384]{1,0:T(8,128)S(1)}, f32[32,384]{1,0:T(8,128)S(1)}, u32[]{:S(2)}, u32[]{:S(2)}) collective-permute-start(f32[32,384]{1,0:T(8,128)S(1)} %add_add_fusion.1.r2), channel_id=1, source_target_pairs={{0,1},{2,3},{4,5},{6,7},{8,0},{10,2},{12,4},{14,6},{9,8},{11,10},{... | collective-permute-start | bytes 147464 | tf_op jit(solution)/shard_map/ppermute | solution.py:570
  34.0 4.3 %collective-permute-start.11 = (f32[32,384]{1,0:T(8,128)S(1)}, f32[32,384]{1,0:T(8,128)S(1)}, u32[]{:S(2)}, u32[]{:S(2)}) collective-permute-start(f32[32,384]{1,0:T(8,128)S(1)} %add_add_fusion.1.r2), channel_id=1, source_target_pairs={{8,1},{10,3},{12,5},{14,7},{1,8},{3,10},{5,12},{7,14},{0,4},{2,6},... | collective-permute-start | bytes 147464 | tf_op jit(solution)/shard_map/ppermute | solution.py:570
  42.7 1.4 %collective-permute-start.12 = (f32[64,512]{1,0:T(8,128)S(1)}, f32[64,512]{1,0:T(8,128)S(1)}, u32[]{:S(2)}, u32[]{:S(2)}) collective-permute-start(f32[64,512]{1,0:T(8,128)S(1)} %get-tuple-element.92), channel_id=1, source_target_pairs={{0,2},{2,0},{4,6},{6,4},{8,10},{10,8},{12,14},{14,12},{1,3},{3,1},... | collective-permute-start | bytes 393224 | tf_op jit(solution)/shard_map/ppermute | solution.py:563
  42.8 2.9 %copy-start.6 = (bf16[128,12]{0,1:T(8,128)(2,1)S(1)}, bf16[128,12]{0,1:T(8,128)(2,1)}, u32[]{:S(2)}) copy-start(bf16[128,12]{0,1:T(8,128)(2,1)} %param.29) | copy-start | bytes 9220
  44.1 6.0 %collective-permute-start.14 = (f32[32,512]{1,0:T(8,128)S(1)}, f32[32,512]{1,0:T(8,128)S(1)}, u32[]{:S(2)}, u32[]{:S(2)}) collective-permute-start(f32[32,512]{1,0:T(8,128)S(1)} %slice_add_fusion), channel_id=1, source_target_pairs={{0,4},{2,6},{4,0},{6,2},{8,12},{10,14},{12,8},{14,10},{1,5},{3,7},... | collective-permute-start | bytes 196616 | tf_op jit(solution)/shard_map/ppermute | solution.py:567
  47.6 4.9 %collective-permute-start.13 = (f32[32,512]{1,0:T(8,128)S(1)}, f32[32,512]{1,0:T(8,128)S(1)}, u32[]{:S(2)}, u32[]{:S(2)}) collective-permute-start(f32[32,512]{1,0:T(8,128)S(1)} %query_zero.1.r0), channel_id=1, source_target_pairs={{0,1},{1,0},{2,3},{3,2},{4,5},{5,4},{6,7},{7,6},{8,9},{9,8},{10,11... | collective-permute-start | bytes 196616 | tf_op jit(solution)/shard_map/ppermute | solution.py:566
  50.1 8.0 %collective-permute-start.15 = (f32[32,512]{1,0:T(8,128)S(1)}, f32[32,512]{1,0:T(8,128)S(1)}, u32[]{:S(2)}, u32[]{:S(2)}) collective-permute-start(f32[32,512]{1,0:T(8,128)S(1)} %add_add_fusion.r2), channel_id=1, source_target_pairs={{0,1},{2,3},{4,5},{6,7},{8,0},{10,2},{12,4},{14,6},{9,8},{11,10},{... | collective-permute-start | bytes 196616 | tf_op jit(solution)/shard_map/ppermute | solution.py:570
  51.0 7.1 %collective-permute-start.16 = (f32[32,512]{1,0:T(8,128)S(1)}, f32[32,512]{1,0:T(8,128)S(1)}, u32[]{:S(2)}, u32[]{:S(2)}) collective-permute-start(f32[32,512]{1,0:T(8,128)S(1)} %add_add_fusion.r2), channel_id=1, source_target_pairs={{8,1},{10,3},{12,5},{14,7},{1,8},{3,10},{5,12},{7,14},{0,4},{2,6},... | collective-permute-start | bytes 196616 | tf_op jit(solution)/shard_map/ppermute | solution.py:570

commit v3 on v2

--- a/solution.py
+++ b/solution.py
@@ -25,6 +25,7 @@
 FRAME_LANE = 768
 CHAIN_LANE = 792
 STAT = 96
+EARLY = 4
 
 F32 = jnp.float32
 BF16 = jnp.bfloat16
@@ -276,7 +277,7 @@
     e_ref[:, 256:384] = block(sums, 2)
 
 
-def second_body(keys_ref, wk_ref, pm_ref, pair_ref, kv_ref, e_ref, p32_ref, op_ref):
+def second_body(keys_ref, wk_ref, pm_ref, pair_ref, kv_ref, e_ref, tail_ref, p32_ref, op_ref):
     rows = pair_ref.shape[0]
     fr = keys_ref[:, FRAME_LANE : FRAME_LANE + 128]
     project_keys(keys_ref[:, C : 2 * C], fr, 12, wk_ref, kv_ref)
@@ -290,7 +291,8 @@
         lhs = p32_ref[pl.ds(i, H, stride=rows), :].astype(BF16)
         op_ref[pl.ds(i, H, stride=rows), :] = mm(lhs, pair_ref[i])
     for h in range(H):
-        e_ref[:, 640 + CZ * h : 640 + CZ * (h + 1)] = op_ref[h * rows : (h + 1) * rows, :]
+        ref, first = (e_ref, 640 + CZ * h) if h < EARLY else (tail_ref, CZ * (h - EARLY))
+        ref[:, first : first + CZ] = op_ref[h * rows : (h + 1) * rows, :]
 
 
 def backward(
@@ -433,7 +435,7 @@
 
 
 def back_zero_body(
-    flag_ref, cot_ref, r0, r1, r2, r3, r4, e_mine, e_other, pm_ref, kv_ref, keys_ref, own_ref, q_ref, pair_ref,
+    flag_ref, cot_ref, r0, r1, r2, r3, r4, e_mine, e_other, tail_mine, tail_other, pm_ref, kv_ref, keys_ref, own_ref, q_ref, pair_ref,
     w_out_ref, wk_ref, sc_ref, frk_ref,
     z_ref, mine_a, mine_b, theirs, pts_ref, sum_ref, pu_ref, work_ref, gp_ref, d_ref,
 ):
@@ -449,7 +451,12 @@
     wide = jnp.concatenate(
         [
             pu_ref[h * rows : (h + 1) * rows, :]
-            * (e_mine[:, 640 + CZ * h : 640 + CZ * (h + 1)] + e_other[:, 640 + CZ * h : 640 + CZ * (h + 1)])
+            * (
+                e_mine[:, 640 + CZ * h : 640 + CZ * (h + 1)] + e_other[:, 640 + CZ * h : 640 + CZ * (h + 1)]
+                if h < EARLY
+                else tail_mine[:, CZ * (h - EARLY) : CZ * (h - EARLY + 1)]
+                + tail_other[:, CZ * (h - EARLY) : CZ * (h - EARLY + 1)]
+            )
             for h in range(H)
         ],
         axis=1,
@@ -558,23 +565,23 @@
             return lax.ppermute(x, "col", COL_SWAP)
         return lax.psum(x, "col") - x
 
-    def reduce(mine_a, mine_b, theirs, late, beside):
+    def reduce(mine_a, mine_b, theirs, late, first_beside, beside):
         if fast:
             got = lax.ppermute(theirs, "row", CORE_SWAP)
             query, *rest = late()
-            got, query = lax.optimization_barrier((got, query))
+            got, query, first_beside = lax.optimization_barrier((got, query, first_beside))
             query_other = lax.ppermute(query, "col", COL_SWAP)
             half = lax.ppermute(mine_b + got[rows:], "row", Z_SWAP)
             half, beside = lax.optimization_barrier((half, beside))
             part = mine_a + got[:rows] + half
             sent = [lax.ppermute(part, BOTH, SEND_ONE), lax.ppermute(part, BOTH, SEND_TWO)]
-            return [query, query_other, part] + sent, rest, beside
+            return [query, query_other, part] + sent, rest, (first_beside, beside)
         query, *rest = late()
         parts = jnp.concatenate([mine_a, theirs[:rows], mine_b, theirs[rows:]], axis=0)
         summed = lax.all_gather(lax.psum(parts, "row"), "col", axis=0, tiled=True)
         back = lax.dynamic_slice_in_dim(summed, row * rows, rows, 0)
         zero = jnp.zeros_like(query)
-        return [lax.psum(query, "col"), zero, back, zero, zero], rest, beside
+        return [lax.psum(query, "col"), zero, back, zero, zero], rest, (first_beside, beside)
 
     probs = saved_probs.reshape(2, H * rows, keys)
     hr = H * rows
@@ -599,13 +606,14 @@
         (flags, *blocks, wk, links, probs, gp1, d1),
     )
     e1_other = col_other(e1)
-    kv0, e0 = call(
+    kv0, e0, tail = call(
         second_body, "second", [VMEM] * 4,
-        [((keys, 2048), F32), ((rows, 640 + H * CZ), F32)],
+        [((keys, 2048), F32), ((rows, 640 + EARLY * CZ), F32), ((rows, (H - EARLY) * CZ), F32)],
         (key_pack, wk, pm, pair),
         [pltpu.VMEM((hr, keys), F32), pltpu.VMEM((hr, CZ), F32)],
     )
     e0_other = col_other(e0)
+    tail_other = col_other(tail)
     share = 1.0 / col_total
     e1_other, e0 = lax.optimization_barrier((e1_other, e0))
     z1, mine_a, mine_b, theirs, pts, grads = call(
@@ -616,7 +624,7 @@
         [pltpu.VMEM((keys, C), F32)],
         6.0,
     )
-    pieces, (frq, frk), e0_other = reduce(
+    pieces, (frq, frk), (e0_other, tail_other) = reduce(
         mine_a, mine_b, theirs,
         lambda: call(
             functools.partial(query_one_body, share), "query_one", [VMEM] * 8,
@@ -626,23 +634,25 @@
             0.01,
         ),
         e0_other,
+        tail_other,
     )
     z0, mine_a, mine_b, theirs, pts, single_one, pu0 = call(
-        back_zero_body, "back_zero", [SMEM] + [VMEM] * 18,
+        back_zero_body, "back_zero", [SMEM] + [VMEM] * 20,
         [((2 * hr, keys), F32), ((rows, 512), F32), ((rows, 512), F32), ((2 * rows, 512), F32), ((rows, 1152), F32),
          ((rows, C), F32), ((hr, CZ), F32)],
-        (flags, cotangent, *pieces, e0, e0_other, pm, kv0, key_pack, own, q0, pair, w_out, wk, sc, frk),
+        (flags, cotangent, *pieces, e0, e0_other, tail, tail_other, pm, kv0, key_pack, own, q0, pair, w_out, wk, sc, frk),
         [pltpu.VMEM((keys, 512), F32), pltpu.VMEM((rows, 768), F32), pltpu.VMEM((hr, keys), F32)],
     )
     (d_pair,) = call(
         pair_body, "pair_grad", [VMEM] * 5, [((rows, keys, CZ), BF16)], (z1, z0, pu1, pu0, w_bias.T)
     )
-    pieces, _, d_pair = reduce(
+    pieces, _, (_, d_pair) = reduce(
         mine_a, mine_b, theirs,
         lambda: call(
             functools.partial(query_zero_body, share), "query_zero", [VMEM] * 8, [((rows, 512), F32)],
             (z0, kv0, own, q0, pts, wq, sc, frq),
         ),
+        (),
         d_pair,
     )
     d_single, d_frames = call(

time: 59.5 us -> 57.2 us (0.961)
  waiting for transfers between devices: 15.5 us -> 13 us
    ppermute x2 -> x3, waiting for transfers between devices: 3.63 us -> 1.65 us  [col_other(): return lax.ppermute(x, 'col', COL_SWAP)]
    ppermute x2, starting transfers between devices: 2.74 us -> 1.41 us  [reduce(): lax.ppermute(part, BOTH, SEND_ONE)]
    ppermute x2, waiting for transfers between devices: 2.12 us -> 1.16 us  [reduce(): half = lax.ppermute(mine_b + got[rows:], 'row', Z_SWAP)]
    ppermute x2, starting transfers between devices: 3.25 us -> 3.86 us  [reduce(): lax.ppermute(part, BOTH, SEND_TWO)]
    ppermute x2, waiting for transfers between devices: 7.65 us -> 8.25 us  [reduce(): lax.ppermute(part, BOTH, SEND_ONE)]
    ppermute x2 -> x3, starting transfers between devices: 3.31 us -> 3.81 us  [col_other(): return lax.ppermute(x, 'col', COL_SWAP)]
  transfers between devices with their start and end apart: 17 -> 18, of which waited for: 9 -> 9; matrix products, arithmetic and copies ran while one was open for 0% -> 0% of each run, Pallas kernels for 16% -> 21%
where the time goes in v3:
time: 57.2 us; the launch traced here: 57 us
  starting transfers between devices  22.7 us (40%)
  Pallas kernels  20.3 us (35%)
  waiting for transfers between devices  13 us (23%)
  between operations  0.81 us (1%)
    pallas_call x10, Pallas kernels, call(): pl.pallas_call(body, name=name, in_specs=in_specs, out_specs=tuple((VMEM...  20.3 us
    ppermute x2, waiting for transfers between devices, reduce(): lax.ppermute(part, BOTH, SEND_ONE)  8.25 us
    ppermute x2, starting transfers between devices, reduce(): lax.ppermute(part, BOTH, SEND_TWO)  3.86 us
    ppermute x3, starting transfers between devices, col_other(): return lax.ppermute(x, 'col', COL_SWAP)  3.81 us
    ppermute x1, starting transfers between devices, local(): two = lax.ppermute(pack, BOTH, FETCH_TWO)  3.29 us
    ppermute x2, starting transfers between devices, reduce(): half = lax.ppermute(mine_b + got[rows:], 'row', Z_SWAP)  3.28 us
    ppermute x2, starting transfers between devices, reduce(): query_other = lax.ppermute(query, 'col', COL_SWAP)  3.23 us
    ppermute x1, starting transfers between devices, local(): one = lax.ppermute(pack, BOTH, FETCH_ONE)  3.09 us
  transfers between devices with their start and end apart: 18, of which 9 were waited for; matrix products, arithmetic and copies ran while one was open for 0% of the time, Pallas kernels for 21%

profile of v3, /device:TPU:0, one launch (start us, length us, event | category | flops | bytes accessed | tf_op | source)
XLA Modules:
  0.0 57.0 jit_solution(18312077397274009562)
XLA Ops:
  0.6 0.0 copy-start.3
  0.6 1.0 %pack.1.pack_ref.own_ref = f32[32,896]{1,0:T(8,128)S(1)} custom-call(f32[2,32,384]{2,1,0:T(8,128)} %single_hbm.1, f32[12,2,32]{2,1,0:T(2,128)} %bitcast.22, s32[1,32]{1,0:T(1,128)} %bitcast.23), custom_call_target="tpu_custom_call" | custom-call | flops 1000000000 | bytes 3000000 | tf_op jit(solution)/shard_map/pack/pallas_call | solution.py:501
  1.6 3.1 %collective-permute-start.1 = (f32[32,896]{1,0:T(8,128)S(1)}, f32[32,896]{1,0:T(8,128)S(1)}, u32[]{:S(2)}, u32[]{:S(2)}) collective-permute-start(f32[32,896]{1,0:T(8,128)S(1)} %pack.1.pack_ref.own_ref), channel_id=1, source_target_pairs={{0,4},{2,6},{4,0},{6,2},{1,8},{3,10},{5,12},{7,14},{9,13},{11,15},... | collective-permute-start | bytes 344072 | tf_op jit(solution)/shard_map/ppermute | solution.py:552
  4.7 3.3 %collective-permute-start.2 = (f32[32,896]{1,0:T(8,128)S(1)}, f32[32,896]{1,0:T(8,128)S(1)}, u32[]{:S(2)}, u32[]{:S(2)}) collective-permute-start(f32[32,896]{1,0:T(8,128)S(1)} %pack.1.pack_ref.own_ref), channel_id=1, source_target_pairs={{0,12},{2,14},{4,8},{6,10},{9,5},{11,7},{13,1},{15,3},{1,0},{3,2},... | collective-permute-start | bytes 344072 | tf_op jit(solution)/shard_map/ppermute | solution.py:553
  8.0 0.0 collective-permute-start
  8.0 0.0 copy-done.3
  8.0 0.0 copy-start.4
  8.0 0.0 copy-start.5
  8.0 4.0 %prep.1 = (bf16[1280,384]{1,0:T(8,128)(2,1)S(1)}, bf16[640,384]{1,0:T(8,128)(2,1)S(1)}, f32[32,768]{1,0:T(8,128)S(1)}, f32[32,1024]{1,0:T(8,128)S(1)}, f32[32,10...) custom-call(f32[12]{0:T(128)S(1)} %copy-done.3, ...), custom_call_target="tpu_custom_call" | custom-call | flops 1000000000 | bytes 3000000 | tf_op jit(solution)/shard_map/prep/pallas_call | solution.py:501
  12.1 0.0 collective-permute-done.1.p1_ref
  12.1 0.0 collective-permute-done.2.p2_ref
  12.1 0.6 collective-permute-start.3
  12.6 0.1 collective-permute-start.4
  12.7 0.1 pad_add_fusion.flag_ref
  12.8 0.0 collective-permute-done.ownx_ref
  12.8 0.8 %collective-permute-done.3.p1x_ref = f32[32,896]{1,0:T(8,128)S(1)} collective-permute-done((f32[32,896]{1,0:T(8,128)S(1)}, f32[32,896]{1,0:T(8,128)S(1)}, u32[]{:S(2)}, u32[]{:S(2)}) %collective-permute-start.3) | collective-permute-done | bytes 114720 | tf_op jit(solution)/shard_map/ppermute | solution.py:602
  13.6 0.4 collective-permute-done.4.p2x_ref
  14.0 0.0 copy-done.4
  14.0 0.0 copy-done.5
  14.0 0.0 copy-start.1
  14.0 1.8 %first.1 = (f32[128,896]{1,0:T(8,128)S(1)}, f32[128,2048]{1,0:T(8,128)S(1)}, bf16[2,384,128]{2,1,0:T(8,128)(2,1)S(1)}, f32[32,384]{1,0:T(8,128)S(1)}) custom-call(s32[3]{0:T(128)S(1)} %pad_add_fusion.flag_ref, f32[32,896]{1,0:T(8,128)S(1)} %pack.1.pack_ref.own_ref, f32[32,896]{1,0:T(8,128)S(1)} %collective-permute-done.ownx_ref, ...), custom_call_target="tpu_custom_call" | custom-call | flops 1000000000 | bytes 3000000 | tf_op jit(solution)/shard_map/first/pallas_call | solution.py:501
  15.7 1.7 %collective-permute-start.5 = (f32[32,384]{1,0:T(8,128)S(1)}, f32[32,384]{1,0:T(8,128)S(1)}, u32[]{:S(2)}, u32[]{:S(2)}) collective-permute-start(f32[32,384]{1,0:T(8,128)S(1)} %get-tuple-element.70.e_mine), channel_id=1, source_target_pairs={{0,1},{1,0},{2,3},{3,2},{4,5},{5,4},{6,7},{7,6},{8,9},{9,8},{10,11... | collective-permute-start | bytes 147464 | tf_op jit(solution)/shard_map/ppermute | solution.py:565
  17.4 0.0 copy-done.1
  17.4 1.3 %second.1 = (f32[128,2048]{1,0:T(8,128)S(1)}, f32[32,1152]{1,0:T(8,128)S(1)}, f32[32,1024]{1,0:T(8,128)S(1)}) custom-call(f32[128,896]{1,0:T(8,128)S(1)} %get-tuple-element.71.keys_ref, bf16[1280,384]{1,0:T(8,128)(2,1)S(1)} %get-tuple-element.67.wk_ref, bf16[2,384,128]{2,1,0:T(8,128)(2,1)S(1)} %get-tuple-element.72.pm_ref, bf16[32,128,128]{2,1,0:T(8,128)(2,1)S(1)} %copy-done.1), custom_call_target="tpu_custom_call" | custom-call | flops 1000000000 | bytes 3000000 | tf_op jit(solution)/shard_map/second/pallas_call | solution.py:501
  18.7 0.5 collective-permute-start.7
  19.2 0.7 %collective-permute-done.5.e_other = f32[32,384]{1,0:T(8,128)S(1)} collective-permute-done((f32[32,384]{1,0:T(8,128)S(1)}, f32[32,384]{1,0:T(8,128)S(1)}, u32[]{:S(2)}, u32[]{:S(2)}) %collective-permute-start.5) | collective-permute-done | bytes 49184 | tf_op jit(solution)/shard_map/ppermute | solution.py:565
  19.9 2.6 %back_one.1 = (f32[768,128]{1,0:T(8,128)S(1)}, f32[32,384]{1,0:T(8,128)S(1)}, f32[32,384]{1,0:T(8,128)S(1)}, f32[64,384]{1,0:T(8,128)S(1)}, f32[32,1152]{1,0:T(8,128)S(1)}, /*index=5*/f32[128,768]{1,0:T(8,128)S(1)}) custom-call(s32[3]{0:T(128)S(1)} %pad_add_fusion.flag_ref, f32[32,384]{1,0:T(8,128)S(1)} %get-tuple-element.70.e_mine, ...), custom_call_target="tpu_custom_call" | custom-call | flops 6000000000 | bytes 18000000 | tf_op jit(solution)/shard_map/back_one/pallas_call | solution.py:501
  22.5 0.0 copy-start
  22.5 0.0 copy-start.2
  22.6 0.1 collective-permute-start.6
  22.6 1.7 %collective-permute-start.10 = (f32[32,1024]{1,0:T(8,128)S(1)}, f32[32,1024]{1,0:T(8,128)S(1)}, u32[]{:S(2)}, u32[]{:S(2)}) collective-permute-start(f32[32,1024]{1,0:T(8,128)S(1)} %get-tuple-element.88.tail_mine), channel_id=1, source_target_pairs={{0,1},{1,0},{2,3},{3,2},{4,5},{5,4},{6,7},{7,6},{8,9},{9,8},{10,11... | collective-permute-start | bytes 393224 | tf_op jit(solution)/shard_map/ppermute | solution.py:565
  24.3 1.2 %query_one.1 = (f32[32,384]{1,0:T(8,128)S(1)}, f32[32,128]{1,0:T(8,128)S(1)}, f32[128,128]{1,0:T(8,128)S(1)}) custom-call(f32[768,128]{1,0:T(8,128)S(1)} %get-tuple-element.79.z_ref.z1_ref, f32[128,2048]{1,0:T(8,128)S(1)} %get-tuple-element.75.kv_ref, f32[32,896]{1,0:T(8,128)S(1)} %pack.1.pack_ref.own_ref, f32[32,1024]{1,0:T(8,128)S(1)} %get-tuple-element.76.q_ref, ...), custom_call_target="tpu_custom_call" | custom-call | flops 10000000 | bytes 30000 | tf_op jit(solution)/shard_map/query_one/pallas_call | solution.py:501
  25.5 0.0 collective-permute-done.6
  25.5 0.0 collective-permute-done.7.e_other
  25.6 1.8 %collective-permute-start.9 = (f32[32,384]{1,0:T(8,128)S(1)}, f32[32,384]{1,0:T(8,128)S(1)}, u32[]{:S(2)}, u32[]{:S(2)}) collective-permute-start(f32[32,384]{1,0:T(8,128)S(1)} %slice_add_fusion.1), channel_id=1, source_target_pairs={{0,4},{2,6},{4,0},{6,2},{8,12},{10,14},{12,8},{14,10},{1,5},{3,7},... | collective-permute-start | bytes 147464 | tf_op jit(solution)/shard_map/ppermute | solution.py:574
  27.4 0.2 collective-permute-start.8
  27.6 1.0 %collective-permute-done.10.tail_other = f32[32,1024]{1,0:T(8,128)S(1)} collective-permute-done((f32[32,1024]{1,0:T(8,128)S(1)}, f32[32,1024]{1,0:T(8,128)S(1)}, u32[]{:S(2)}, u32[]{:S(2)}) %collective-permute-start.10) | collective-permute-done | bytes 131104 | tf_op jit(solution)/shard_map/ppermute | solution.py:565
  28.5 1.2 %collective-permute-done.9 = f32[32,384]{1,0:T(8,128)S(1)} collective-permute-done((f32[32,384]{1,0:T(8,128)S(1)}, f32[32,384]{1,0:T(8,128)S(1)}, u32[]{:S(2)}, u32[]{:S(2)}) %collective-permute-start.9) | collective-permute-done | bytes 49184 | tf_op jit(solution)/shard_map/ppermute | solution.py:574
  29.7 0.7 %collective-permute-start.11 = (f32[32,384]{1,0:T(8,128)S(1)}, f32[32,384]{1,0:T(8,128)S(1)}, u32[]{:S(2)}, u32[]{:S(2)}) collective-permute-start(f32[32,384]{1,0:T(8,128)S(1)} %add_add_fusion.1.r2), channel_id=1, source_target_pairs={{0,1},{2,3},{4,5},{6,7},{8,0},{10,2},{12,4},{14,6},{9,8},{11,10},{... | collective-permute-start | bytes 147464 | tf_op jit(solution)/shard_map/ppermute | solution.py:577
  30.4 2.2 %collective-permute-start.12 = (f32[32,384]{1,0:T(8,128)S(1)}, f32[32,384]{1,0:T(8,128)S(1)}, u32[]{:S(2)}, u32[]{:S(2)}) collective-permute-start(f32[32,384]{1,0:T(8,128)S(1)} %add_add_fusion.1.r2), channel_id=1, source_target_pairs={{8,1},{10,3},{12,5},{14,7},{1,8},{3,10},{5,12},{7,14},{0,4},{2,6},... | collective-permute-start | bytes 147464 | tf_op jit(solution)/shard_map/ppermute | solution.py:577
  32.6 0.0 collective-permute-done.8.r1
  32.6 2.8 %collective-permute-done.11.r3 = f32[32,384]{1,0:T(8,128)S(1)} collective-permute-done((f32[32,384]{1,0:T(8,128)S(1)}, f32[32,384]{1,0:T(8,128)S(1)}, u32[]{:S(2)}, u32[]{:S(2)}) %collective-permute-start.11) | collective-permute-done | bytes 49184 | tf_op jit(solution)/shard_map/ppermute | solution.py:577
  35.4 0.3 collective-permute-done.12.r4
  35.7 0.0 copy-done
  35.7 0.0 copy-done.2
  35.7 4.3 %back_zero.1 = (f32[768,128]{1,0:T(8,128)S(1)}, f32[32,512]{1,0:T(8,128)S(1)}, f32[32,512]{1,0:T(8,128)S(1)}, f32[64,512]{1,0:T(8,128)S(1)}, f32[32,1152]{1,0:T(...) custom-call(s32[3]{0:T(128)S(1)} %pad_add_fusion.flag_ref, f32[32,384]{1,0:T(8,128)S(1)} %copy-done.2, ...), custom_call_target="tpu_custom_call" | custom-call | flops 1000000000 | bytes 3000000 | tf_op jit(solution)/shard_map/back_zero/pallas_call | solution.py:501
  40.1 0.1 collective-permute-start.13
  40.2 0.0 copy-start.6
  40.2 0.9 %query_zero.1.r0 = f32[32,512]{1,0:T(8,128)S(1)} custom-call(f32[768,128]{1,0:T(8,128)S(1)} %get-tuple-element.97.z_ref.z0_ref, f32[128,2048]{1,0:T(8,128)S(1)} %get-tuple-element.93.kv_ref, f32[32,896]{1,0:T(8,128)S(1)} %pack.1.pack_ref.own_ref, f32[32,1024]{1,0:T(8,128)S(1)} %get-tuple-element.94.q_ref, f32[32,1152]{1,0:T(8,128)S(1)} %get-tuple-element.98.pts_ref, ...), custom_call_target="tpu_custom_call" | custom-call | flops 1000000000 | bytes 3000000 | tf_op jit(solution)/shard_map/query_zero/pallas_call | solution.py:501
  41.1 0.4 collective-permute-done.13
  41.5 1.4 %collective-permute-start.15 = (f32[32,512]{1,0:T(8,128)S(1)}, f32[32,512]{1,0:T(8,128)S(1)}, u32[]{:S(2)}, u32[]{:S(2)}) collective-permute-start(f32[32,512]{1,0:T(8,128)S(1)} %slice_add_fusion), channel_id=1, source_target_pairs={{0,4},{2,6},{4,0},{6,2},{8,12},{10,14},{12,8},{14,10},{1,5},{3,7},... | collective-permute-start | bytes 196616 | tf_op jit(solution)/shard_map/ppermute | solution.py:574
  42.9 0.0 copy-done.6
  42.9 1.9 %pair_grad.1 = bf16[32,128,128]{2,1,0:T(8,128)(2,1)} custom-call(f32[768,128]{1,0:T(8,128)S(1)} %get-tuple-element.79.z_ref.z1_ref, f32[768,128]{1,0:T(8,128)S(1)} %get-tuple-element.97.z_ref.z0_ref, f32[384,128]{1,0:T(8,128)S(1)} %get-tuple-element.104.pu1_ref, f32[384,128]{1,0:T(8,128)S(1)} %get-tuple-element.105.pu0_ref, bf16[12,128]{1,0:T(8,128)(2,1)S(1)} %bitcast.15), custom_call_target="tpu_custom_call" | custom-call | flops 1000000000 | bytes 3000000 | tf_op jit(solution)/shard_map/pair_grad/pallas_call | solution.py:501
  44.9 3.0 %collective-permute-start.14 = (f32[32,512]{1,0:T(8,128)S(1)}, f32[32,512]{1,0:T(8,128)S(1)}, u32[]{:S(2)}, u32[]{:S(2)}) collective-permute-start(f32[32,512]{1,0:T(8,128)S(1)} %query_zero.1.r0), channel_id=1, source_target_pairs={{0,1},{1,0},{2,3},{3,2},{4,5},{5,4},{6,7},{7,6},{8,9},{9,8},{10,11... | collective-permute-start | bytes 196616 | tf_op jit(solution)/shard_map/ppermute | solution.py:573
  47.9 0.0 collective-permute-done.15
  47.9 0.7 %collective-permute-start.16 = (f32[32,512]{1,0:T(8,128)S(1)}, f32[32,512]{1,0:T(8,128)S(1)}, u32[]{:S(2)}, u32[]{:S(2)}) collective-permute-start(f32[32,512]{1,0:T(8,128)S(1)} %add_add_fusion.r2), channel_id=1, source_target_pairs={{0,1},{2,3},{4,5},{6,7},{8,0},{10,2},{12,4},{14,6},{9,8},{11,10},{... | collective-permute-start | bytes 196616 | tf_op jit(solution)/shard_map/ppermute | solution.py:577
  48.7 1.6 %collective-permute-start.17 = (f32[32,512]{1,0:T(8,128)S(1)}, f32[32,512]{1,0:T(8,128)S(1)}, u32[]{:S(2)}, u32[]{:S(2)}) collective-permute-start(f32[32,512]{1,0:T(8,128)S(1)} %add_add_fusion.r2), channel_id=1, source_target_pairs={{8,1},{10,3},{12,5},{14,7},{1,8},{3,10},{5,12},{7,14},{0,4},{2,6},... | collective-permute-start | bytes 196616 | tf_op jit(solution)/shard_map/ppermute | solution.py:577
  50.3 0.0 collective-permute-done.14.r1
  50.3 5.4 %collective-permute-done.16.r3 = f32[32,512]{1,0:T(8,128)S(1)} collective-permute-done((f32[32,512]{1,0:T(8,128)S(1)}, f32[32,512]{1,0:T(8,128)S(1)}, u32[]{:S(2)}, u32[]{:S(2)}) %collective-permute-start.16) | collective-permute-done | bytes 65568 | tf_op jit(solution)/shard_map/ppermute | solution.py:577
  55.8 0.0 collective-permute-done.17.r4
  55.8 1.2 %final.1 = (f32[32,384]{1,0:T(8,128)}, f32[12,2,32]{2,1,0:T(2,128)}) custom-call(s32[3]{0:T(128)S(1)} %pad_add_fusion.flag_ref, f32[32,512]{1,0:T(8,128)S(1)} %query_zero.1.r0, f32[32,512]{1,0:T(8,128)S(1)} %collective-permute-done.14.r1, f32[32,512]{1,0:T(8,128)S(1)} %add_add_fusion.r2, f32[32,512]{1,0:T(8,128)S(1)} %collective-permute-done.16.r3, ...), custom_call_target="tpu_custom_call" | custom-call | flops 1000000000 | bytes 3000000 | tf_op jit(solution)/shard_map/final/pallas_call | solution.py:501
  (4 shorter events, 0.0 us)
Async XLA Ops:
  0.6 7.4 %copy-start.3 = (f32[12]{0:T(128)S(1)}, f32[12]{0:T(128)}, u32[]{:S(2)}) copy-start(f32[12]{0:T(128)} %hw_ref.1) | copy-start | bytes 148
  1.6 10.4 %collective-permute-start.1 = (f32[32,896]{1,0:T(8,128)S(1)}, f32[32,896]{1,0:T(8,128)S(1)}, u32[]{:S(2)}, u32[]{:S(2)}) collective-permute-start(f32[32,896]{1,0:T(8,128)S(1)} %pack.1.pack_ref.own_ref), channel_id=1, source_target_pairs={{0,4},{2,6},{4,0},{6,2},{1,8},{3,10},{5,12},{7,14},{9,13},{11,15},... | collective-permute-start | bytes 344072 | tf_op jit(solution)/shard_map/ppermute | solution.py:552
  4.7 7.4 %collective-permute-start.2 = (f32[32,896]{1,0:T(8,128)S(1)}, f32[32,896]{1,0:T(8,128)S(1)}, u32[]{:S(2)}, u32[]{:S(2)}) collective-permute-start(f32[32,896]{1,0:T(8,128)S(1)} %pack.1.pack_ref.own_ref), channel_id=1, source_target_pairs={{0,12},{2,14},{4,8},{6,10},{9,5},{11,7},{13,1},{15,3},{1,0},{3,2},... | collective-permute-start | bytes 344072 | tf_op jit(solution)/shard_map/ppermute | solution.py:553
  8.0 4.8 %collective-permute-start = (f32[32,896]{1,0:T(8,128)S(1)}, f32[32,896]{1,0:T(8,128)S(1)}, u32[]{:S(2)}, u32[]{:S(2)}) collective-permute-start(f32[32,896]{1,0:T(8,128)S(1)} %pack.1.pack_ref.own_ref), channel_id=1, source_target_pairs={{0,2},{2,0},{4,6},{6,4},{8,10},{10,8},{12,14},{14,12},{1,3},{3,1},... | collective-permute-start | bytes 344072 | tf_op jit(solution)/shard_map/ppermute | solution.py:551
  8.0 5.9 %copy-start.4 = (bf16[2,12,32,128]{3,2,1,0:T(8,128)(2,1)S(1)}, bf16[2,12,32,128]{3,2,1,0:T(8,128)(2,1)}, u32[]{:S(2)}) copy-start(bf16[2,12,32,128]{3,2,1,0:T(8,128)(2,1)} %param.18) | copy-start | bytes 589828
  8.0 5.9 %copy-start.5 = (s32[16,16]{1,0:T(8,128)S(1)}, s32[16,16]{1,0:T(8,128)}, u32[]{:S(2)}) copy-start(s32[16,16]{1,0:T(8,128)} %links_ref.1) | copy-start | bytes 3076
  12.1 1.5 %collective-permute-start.3 = (f32[32,896]{1,0:T(8,128)S(1)}, f32[32,896]{1,0:T(8,128)S(1)}, u32[]{:S(2)}, u32[]{:S(2)}) collective-permute-start(f32[32,896]{1,0:T(8,128)S(1)} %collective-permute-done.1.p1_ref), channel_id=1, source_target_pairs={{0,2},{2,0},{4,6},{6,4},{8,10},{10,8},{12,14},{14,12},{1,3},{3,1},... | collective-permute-start | bytes 344072 | tf_op jit(solution)/shard_map/ppermute | solution.py:602
  12.6 1.3 %collective-permute-start.4 = (f32[32,896]{1,0:T(8,128)S(1)}, f32[32,896]{1,0:T(8,128)S(1)}, u32[]{:S(2)}, u32[]{:S(2)}) collective-permute-start(f32[32,896]{1,0:T(8,128)S(1)} %collective-permute-done.2.p2_ref), channel_id=1, source_target_pairs={{0,2},{2,0},{4,6},{6,4},{8,10},{10,8},{12,14},{14,12},{1,3},{3,1},... | collective-permute-start | bytes 344072 | tf_op jit(solution)/shard_map/ppermute | solution.py:602
  14.0 3.4 %copy-start.1 = (bf16[32,128,128]{2,1,0:T(8,128)(2,1)S(1)}, bf16[32,128,128]{2,1,0:T(8,128)(2,1)}, u32[]{:S(2)}) copy-start(bf16[32,128,128]{2,1,0:T(8,128)(2,1)} %pair_ref.3) | copy-start | bytes 3145732
  15.7 4.2 %collective-permute-start.5 = (f32[32,384]{1,0:T(8,128)S(1)}, f32[32,384]{1,0:T(8,128)S(1)}, u32[]{:S(2)}, u32[]{:S(2)}) collective-permute-start(f32[32,384]{1,0:T(8,128)S(1)} %get-tuple-element.70.e_mine), channel_id=1, source_target_pairs={{0,1},{1,0},{2,3},{3,2},{4,5},{5,4},{6,7},{7,6},{8,9},{9,8},{10,11... | collective-permute-start | bytes 147464 | tf_op jit(solution)/shard_map/ppermute | solution.py:565
  18.7 6.8 %collective-permute-start.7 = (f32[32,1152]{1,0:T(8,128)S(1)}, f32[32,1152]{1,0:T(8,128)S(1)}, u32[]{:S(2)}, u32[]{:S(2)}) collective-permute-start(f32[32,1152]{1,0:T(8,128)S(1)} %get-tuple-element.90.e_mine), channel_id=1, source_target_pairs={{0,1},{1,0},{2,3},{3,2},{4,5},{5,4},{6,7},{7,6},{8,9},{9,8},{10,11... | collective-permute-start | bytes 442376 | tf_op jit(solution)/shard_map/ppermute | solution.py:565
  22.5 13.2 %copy-start = (bf16[2112,384]{1,0:T(8,128)(2,1)S(1)}, bf16[2112,384]{1,0:T(8,128)(2,1)}, u32[]{:S(2)}) copy-start(bf16[2112,384]{1,0:T(8,128)(2,1)} %w_out_ref.1) | copy-start | bytes 4866052
  22.5 13.2 %copy-start.2 = (f32[32,384]{1,0:T(8,128)S(1)}, f32[32,384]{1,0:T(8,128)}, u32[]{:S(2)}) copy-start(f32[32,384]{1,0:T(8,128)} %cot_ref.1) | copy-start | bytes 147460
  22.6 3.0 %collective-permute-start.6 = (f32[64,384]{1,0:T(8,128)S(1)}, f32[64,384]{1,0:T(8,128)S(1)}, u32[]{:S(2)}, u32[]{:S(2)}) collective-permute-start(f32[64,384]{1,0:T(8,128)S(1)} %get-tuple-element.78), channel_id=1, source_target_pairs={{0,2},{2,0},{4,6},{6,4},{8,10},{10,8},{12,14},{14,12},{1,3},{3,1},... | collective-permute-start | bytes 294920 | tf_op jit(solution)/shard_map/ppermute | solution.py:570
  22.6 5.9 %collective-permute-start.10 = (f32[32,1024]{1,0:T(8,128)S(1)}, f32[32,1024]{1,0:T(8,128)S(1)}, u32[]{:S(2)}, u32[]{:S(2)}) collective-permute-start(f32[32,1024]{1,0:T(8,128)S(1)} %get-tuple-element.88.tail_mine), channel_id=1, source_target_pairs={{0,1},{1,0},{2,3},{3,2},{4,5},{5,4},{6,7},{7,6},{8,9},{9,8},{10,11... | collective-permute-start | bytes 393224 | tf_op jit(solution)/shard_map/ppermute | solution.py:565
  25.6 4.2 %collective-permute-start.9 = (f32[32,384]{1,0:T(8,128)S(1)}, f32[32,384]{1,0:T(8,128)S(1)}, u32[]{:S(2)}, u32[]{:S(2)}) collective-permute-start(f32[32,384]{1,0:T(8,128)S(1)} %slice_add_fusion.1), channel_id=1, source_target_pairs={{0,4},{2,6},{4,0},{6,2},{8,12},{10,14},{12,8},{14,10},{1,5},{3,7},... | collective-permute-start | bytes 147464 | tf_op jit(solution)/shard_map/ppermute | solution.py:574
  27.4 5.2 %collective-permute-start.8 = (f32[32,384]{1,0:T(8,128)S(1)}, f32[32,384]{1,0:T(8,128)S(1)}, u32[]{:S(2)}, u32[]{:S(2)}) collective-permute-start(f32[32,384]{1,0:T(8,128)S(1)} %get-tuple-element.84.r0), channel_id=1, source_target_pairs={{0,1},{1,0},{2,3},{3,2},{4,5},{5,4},{6,7},{7,6},{8,9},{9,8},{10,11... | collective-permute-start | bytes 147464 | tf_op jit(solution)/shard_map/ppermute | solution.py:573
  29.7 5.7 %collective-permute-start.11 = (f32[32,384]{1,0:T(8,128)S(1)}, f32[32,384]{1,0:T(8,128)S(1)}, u32[]{:S(2)}, u32[]{:S(2)}) collective-permute-start(f32[32,384]{1,0:T(8,128)S(1)} %add_add_fusion.1.r2), channel_id=1, source_target_pairs={{0,1},{2,3},{4,5},{6,7},{8,0},{10,2},{12,4},{14,6},{9,8},{11,10},{... | collective-permute-start | bytes 147464 | tf_op jit(solution)/shard_map/ppermute | solution.py:577
  30.4 5.3 %collective-permute-start.12 = (f32[32,384]{1,0:T(8,128)S(1)}, f32[32,384]{1,0:T(8,128)S(1)}, u32[]{:S(2)}, u32[]{:S(2)}) collective-permute-start(f32[32,384]{1,0:T(8,128)S(1)} %add_add_fusion.1.r2), channel_id=1, source_target_pairs={{8,1},{10,3},{12,5},{14,7},{1,8},{3,10},{5,12},{7,14},{0,4},{2,6},... | collective-permute-start | bytes 147464 | tf_op jit(solution)/shard_map/ppermute | solution.py:577
  40.1 1.4 %collective-permute-start.13 = (f32[64,512]{1,0:T(8,128)S(1)}, f32[64,512]{1,0:T(8,128)S(1)}, u32[]{:S(2)}, u32[]{:S(2)}) collective-permute-start(f32[64,512]{1,0:T(8,128)S(1)} %get-tuple-element.96), channel_id=1, source_target_pairs={{0,2},{2,0},{4,6},{6,4},{8,10},{10,8},{12,14},{14,12},{1,3},{3,1},... | collective-permute-start | bytes 393224 | tf_op jit(solution)/shard_map/ppermute | solution.py:570
  40.2 2.8 %copy-start.6 = (bf16[128,12]{0,1:T(8,128)(2,1)S(1)}, bf16[128,12]{0,1:T(8,128)(2,1)}, u32[]{:S(2)}) copy-start(bf16[128,12]{0,1:T(8,128)(2,1)} %param.29) | copy-start | bytes 9220
  41.5 6.4 %collective-permute-start.15 = (f32[32,512]{1,0:T(8,128)S(1)}, f32[32,512]{1,0:T(8,128)S(1)}, u32[]{:S(2)}, u32[]{:S(2)}) collective-permute-start(f32[32,512]{1,0:T(8,128)S(1)} %slice_add_fusion), channel_id=1, source_target_pairs={{0,4},{2,6},{4,0},{6,2},{8,12},{10,14},{12,8},{14,10},{1,5},{3,7},... | collective-permute-start | bytes 196616 | tf_op jit(solution)/shard_map/ppermute | solution.py:574
  44.9 5.5 %collective-permute-start.14 = (f32[32,512]{1,0:T(8,128)S(1)}, f32[32,512]{1,0:T(8,128)S(1)}, u32[]{:S(2)}, u32[]{:S(2)}) collective-permute-start(f32[32,512]{1,0:T(8,128)S(1)} %query_zero.1.r0), channel_id=1, source_target_pairs={{0,1},{1,0},{2,3},{3,2},{4,5},{5,4},{6,7},{7,6},{8,9},{9,8},{10,11... | collective-permute-start | bytes 196616 | tf_op jit(solution)/shard_map/ppermute | solution.py:573
  47.9 7.8 %collective-permute-start.16 = (f32[32,512]{1,0:T(8,128)S(1)}, f32[32,512]{1,0:T(8,128)S(1)}, u32[]{:S(2)}, u32[]{:S(2)}) collective-permute-start(f32[32,512]{1,0:T(8,128)S(1)} %add_add_fusion.r2), channel_id=1, source_target_pairs={{0,1},{2,3},{4,5},{6,7},{8,0},{10,2},{12,4},{14,6},{9,8},{11,10},{... | collective-permute-start | bytes 196616 | tf_op jit(solution)/shard_map/ppermute | solution.py:577
  48.7 7.1 %collective-permute-start.17 = (f32[32,512]{1,0:T(8,128)S(1)}, f32[32,512]{1,0:T(8,128)S(1)}, u32[]{:S(2)}, u32[]{:S(2)}) collective-permute-start(f32[32,512]{1,0:T(8,128)S(1)} %add_add_fusion.r2), channel_id=1, source_target_pairs={{8,1},{10,3},{12,5},{14,7},{1,8},{3,10},{5,12},{7,14},{0,4},{2,6},... | collective-permute-start | bytes 196616 | tf_op jit(solution)/shard_map/ppermute | solution.py:577

commit v4 on v3

--- a/solution.py
+++ b/solution.py
@@ -139,9 +139,12 @@
 
 
 def pair_products(pu_ref, pair_ref, d_ref, rows):
-    for i in range(rows):
-        lhs = pu_ref[pl.ds(i, H, stride=rows), :].astype(BF16)
-        d_ref[pl.ds(i, H, stride=rows), :] = mm(lhs, pair_ref[i], NT)
+    for i in range(0, rows, 2):
+        lhs = jnp.concatenate([pu_ref[pl.ds(i, H, stride=rows), :], pu_ref[pl.ds(i + 1, H, stride=rows), :]], axis=0)
+        both = mm(lhs.astype(BF16), pair_ref[i : i + 2].reshape(-1, CZ), NT)
+        keys = both.shape[1] // 2
+        d_ref[pl.ds(i, H, stride=rows), :] = both[:H, :keys]
+        d_ref[pl.ds(i + 1, H, stride=rows), :] = both[H:, keys:]
 
 
 def split3(x):
@@ -352,17 +355,32 @@
     return jnp.concatenate(off + gpt + gptg, axis=1), jnp.concatenate(d_kg + d_vg, axis=1)
 
 
-def frame_sums(prods, first_lane):
-    return mm2(jnp.concatenate(prods, axis=1), lane_matrix(12 * 128, lambda r: first_lane + (r >> 7)))
-
-
-def backward_frames(grads, kv_ref, first_lane):
+def frame_sums(prods, first):
+    def lane(r):
+        q = first + (r >> 7)
+        return q + 2 * ((q * 43) >> 8)
+
+    return mm2(jnp.concatenate(prods, axis=1), lane_matrix(12 * 128, lane))
+
+
+def frame_block(turned, at, rows):
+    return jnp.concatenate([turned[8 * m : 8 * m + 8, at : at + rows] for m in range(4)], axis=1)
+
+
+def store_piece(ref, at, grad, frames):
+    rows = grad.shape[0]
+    for t in range(3):
+        ref[at + rows * t : at + rows * (t + 1), :] = grad[:, 128 * t : 128 * t + 128]
+    ref[at + 3 * rows : at + 3 * rows + 8, :] = frames
+
+
+def backward_frames(grads, kv_ref, first):
     d_kg = [grads[:, 128 * a : 128 * a + 128] for a in range(3)]
     d_vg = [grads[:, 384 + 128 * a : 512 + 128 * a] for a in range(3)]
     k_local = [kv_ref[:, 1280 + 128 * b : 1408 + 128 * b] for b in range(3)]
     v_local = [kv_ref[:, 1664 + 128 * b : 1792 + 128 * b] for b in range(3)]
     prods = [d_kg[a] * k_local[b] + d_vg[a] * v_local[b] for a in range(3) for b in range(3)]
-    return frame_sums(prods + [d_kg[a] + d_vg[a] for a in range(3)], first_lane)
+    return frame_sums(prods + [d_kg[a] + d_vg[a] for a in range(3)], first)
 
 
 def backward_query(dl, kv_ref, own_fr, fcol, q_ref, pts_ref, wq_ref, sc, first_lane, share):
@@ -388,7 +406,7 @@
     core = flag_ref[2]
 
     def get(z, k):
-        return src_ref[pl.ds(pl.multiple_of((2 * z + k) * rows, rows), rows), :]
+        return src_ref[pl.ds(pl.multiple_of((2 * z + k) * rows, 8), rows), :]
 
     mine_a[...] = get(zb, core)
     mine_b[...] = get(1 - zb, core)
@@ -402,10 +420,13 @@
 
 def final_body(flag_ref, r0, r1, r2, r3, r4, one_ref, single_out, frames_out):
     total = add_pieces(flag_ref, r0, r1, r2, r3, r4)
-    single_out[...] = one_ref[...] + total[:, 0:C]
-    turned = jnp.transpose(total[:, C:])
-    for l in range(2):
-        frames_out[:, l, :] = turned[12 * l : 12 * l + 12, :]
+    rows = one_ref.shape[0]
+    for t in range(3):
+        lanes = slice(128 * t, 128 * t + 128)
+        single_out[:, lanes] = one_ref[:, lanes] + total[rows * t : rows * (t + 1), :]
+    for m in range(4):
+        first = 6 * (m % 2)
+        frames_out[first : first + 6, m // 2, :] = total[3 * rows : 3 * rows + 6, rows * m : rows * (m + 1)]
 
 
 def frame_part(ref):
@@ -437,7 +458,7 @@
 def back_zero_body(
     flag_ref, cot_ref, r0, r1, r2, r3, r4, e_mine, e_other, tail_mine, tail_other, pm_ref, kv_ref, keys_ref, own_ref, q_ref, pair_ref,
     w_out_ref, wk_ref, sc_ref, frk_ref,
-    z_ref, mine_a, mine_b, theirs, pts_ref, sum_ref, pu_ref, work_ref, gp_ref, d_ref,
+    z_ref, mine_a, mine_b, theirs, pts_ref, sum_ref, pu_ref, work_ref, pieces_ref, gp_ref, d_ref,
 ):
     rows = own_ref.shape[0]
     total = add_pieces(flag_ref, r0, r1, r2, r3, r4)
@@ -466,8 +487,11 @@
         flag_ref, e, dots, pm_ref[0], kv_ref, frame_part(keys_ref), frame_part(own_ref), 12, q_ref, gp, d_ref, wk_ref,
         sc_ref[0:1, :], z_ref, work_ref,
     )
-    work_ref[:, C:] = backward_frames(grads, kv_ref, 0) + frk_ref[...]
-    send_blocks(flag_ref, work_ref, mine_a, mine_b, theirs, rows)
+    turned = jnp.transpose(backward_frames(grads, kv_ref, 0) + frk_ref[...])
+    for n in range(4):
+        at = n * pieces_ref.shape[0] // 4
+        store_piece(pieces_ref, at, work_ref[rows * n : rows * (n + 1), :], frame_block(turned, rows * n, rows))
+    send_blocks(flag_ref, pieces_ref, mine_a, mine_b, theirs, mine_a.shape[0])
 
 
 def query_zero_body(share, z_ref, kv_ref, own_ref, q_ref, pts_ref, wq_ref, sc_ref, frq_ref, query_out):
@@ -475,8 +499,7 @@
     grad, frames = backward_query(
         z_ref[half:, :], kv_ref, frame_part(own_ref), 12, q_ref, pts_ref, wq_ref, sc_ref[0:1, :], 0, share
     )
-    query_out[:, 0:C] = grad
-    query_out[:, C:] = frames + frq_ref[...]
+    store_piece(query_out, 0, grad, frame_block(jnp.transpose(frames + frq_ref[...]), 0, own_ref.shape[0]))
 
 
 def pair_body(z1_ref, z0_ref, pu1_ref, pu0_ref, wbt_ref, out_ref):
@@ -571,15 +594,17 @@
             query, *rest = late()
             got, query, first_beside = lax.optimization_barrier((got, query, first_beside))
             query_other = lax.ppermute(query, "col", COL_SWAP)
-            half = lax.ppermute(mine_b + got[rows:], "row", Z_SWAP)
+            count = mine_a.shape[0]
+            half = lax.ppermute(mine_b + got[count:], "row", Z_SWAP)
             half, beside = lax.optimization_barrier((half, beside))
-            part = mine_a + got[:rows] + half
+            part = mine_a + got[:count] + half
             sent = [lax.ppermute(part, BOTH, SEND_ONE), lax.ppermute(part, BOTH, SEND_TWO)]
             return [query, query_other, part] + sent, rest, (first_beside, beside)
         query, *rest = late()
-        parts = jnp.concatenate([mine_a, theirs[:rows], mine_b, theirs[rows:]], axis=0)
+        count = mine_a.shape[0]
+        parts = jnp.concatenate([mine_a, theirs[:count], mine_b, theirs[count:]], axis=0)
         summed = lax.all_gather(lax.psum(parts, "row"), "col", axis=0, tiled=True)
-        back = lax.dynamic_slice_in_dim(summed, row * rows, rows, 0)
+        back = lax.dynamic_slice_in_dim(summed, row * count, count, 0)
         zero = jnp.zeros_like(query)
         return [lax.psum(query, "col"), zero, back, zero, zero], rest, (first_beside, beside)
 
@@ -636,12 +661,13 @@
         e0_other,
         tail_other,
     )
+    long = 3 * rows + 8
     z0, mine_a, mine_b, theirs, pts, single_one, pu0 = call(
         back_zero_body, "back_zero", [SMEM] + [VMEM] * 20,
-        [((2 * hr, keys), F32), ((rows, 512), F32), ((rows, 512), F32), ((2 * rows, 512), F32), ((rows, 1152), F32),
+        [((2 * hr, keys), F32), ((long, 128), F32), ((long, 128), F32), ((2 * long, 128), F32), ((rows, 1152), F32),
          ((rows, C), F32), ((hr, CZ), F32)],
         (flags, cotangent, *pieces, e0, e0_other, tail, tail_other, pm, kv0, key_pack, own, q0, pair, w_out, wk, sc, frk),
-        [pltpu.VMEM((keys, 512), F32), pltpu.VMEM((rows, 768), F32), pltpu.VMEM((hr, keys), F32)],
+        [pltpu.VMEM((keys, C), F32), pltpu.VMEM((4 * long, 128), F32), pltpu.VMEM((rows, 768), F32), pltpu.VMEM((hr, keys), F32)],
     )
     (d_pair,) = call(
         pair_body, "pair_grad", [VMEM] * 5, [((rows, keys, CZ), BF16)], (z1, z0, pu1, pu0, w_bias.T)
@@ -649,7 +675,7 @@
     pieces, _, (_, d_pair) = reduce(
         mine_a, mine_b, theirs,
         lambda: call(
-            functools.partial(query_zero_body, share), "query_zero", [VMEM] * 8, [((rows, 512), F32)],
+            functools.partial(query_zero_body, share), "query_zero", [VMEM] * 8, [((long, 128), F32)],
             (z0, kv0, own, q0, pts, wq, sc, frq),
         ),
         (),

time: 57.2 us -> 56.5 us (0.988)
  waiting for transfers between devices: 13 us -> 12.3 us
where the time goes in v4:
time: 56.5 us; the launch traced here: 56.3 us
  starting transfers between devices  22.8 us (40%)
  Pallas kernels  20.3 us (36%)
  waiting for transfers between devices  12.3 us (22%)
  between operations  0.8 us (1%)
    pallas_call x10, Pallas kernels, call(): pl.pallas_call(body, name=name, in_specs=in_specs, out_specs=tuple((VMEM...  20.3 us
    ppermute x2, waiting for transfers between devices, reduce(): lax.ppermute(part, BOTH, SEND_ONE)  7.71 us
    ppermute x3, starting transfers between devices, col_other(): return lax.ppermute(x, 'col', COL_SWAP)  3.98 us
    ppermute x2, starting transfers between devices, reduce(): lax.ppermute(part, BOTH, SEND_TWO)  3.86 us
    ppermute x2, starting transfers between devices, reduce(): half = lax.ppermute(mine_b + got[count:], 'row', Z_SWAP)  3.3 us
    ppermute x1, starting transfers between devices, local(): two = lax.ppermute(pack, BOTH, FETCH_TWO)  3.29 us
    ppermute x2, starting transfers between devices, reduce(): query_other = lax.ppermute(query, 'col', COL_SWAP)  3.23 us
    ppermute x1, starting transfers between devices, local(): one = lax.ppermute(pack, BOTH, FETCH_ONE)  3.09 us
  transfers between devices with their start and end apart: 18, of which 9 were waited for; matrix products, arithmetic and copies ran while one was open for 0% of the time, Pallas kernels for 21%

profile of v4, /device:TPU:0, one launch (start us, length us, event | category | flops | bytes accessed | tf_op | source)
XLA Modules:
  0.0 56.3 jit_solution(7397792734908292890)
XLA Ops:
  0.6 0.0 copy-start.3
  0.6 1.0 %pack.1.pack_ref.own_ref = f32[32,896]{1,0:T(8,128)S(1)} custom-call(f32[2,32,384]{2,1,0:T(8,128)} %single_hbm.1, f32[12,2,32]{2,1,0:T(2,128)} %bitcast.22, s32[1,32]{1,0:T(1,128)} %bitcast.23), custom_call_target="tpu_custom_call" | custom-call | flops 1000000000 | bytes 3000000 | tf_op jit(solution)/shard_map/pack/pallas_call | solution.py:524
  1.6 3.1 %collective-permute-start.1 = (f32[32,896]{1,0:T(8,128)S(1)}, f32[32,896]{1,0:T(8,128)S(1)}, u32[]{:S(2)}, u32[]{:S(2)}) collective-permute-start(f32[32,896]{1,0:T(8,128)S(1)} %pack.1.pack_ref.own_ref), channel_id=1, source_target_pairs={{0,4},{2,6},{4,0},{6,2},{1,8},{3,10},{5,12},{7,14},{9,13},{11,15},... | collective-permute-start | bytes 344072 | tf_op jit(solution)/shard_map/ppermute | solution.py:575
  4.7 3.3 %collective-permute-start.2 = (f32[32,896]{1,0:T(8,128)S(1)}, f32[32,896]{1,0:T(8,128)S(1)}, u32[]{:S(2)}, u32[]{:S(2)}) collective-permute-start(f32[32,896]{1,0:T(8,128)S(1)} %pack.1.pack_ref.own_ref), channel_id=1, source_target_pairs={{0,12},{2,14},{4,8},{6,10},{9,5},{11,7},{13,1},{15,3},{1,0},{3,2},... | collective-permute-start | bytes 344072 | tf_op jit(solution)/shard_map/ppermute | solution.py:576
  8.0 0.0 collective-permute-start
  8.0 0.0 copy-done.3
  8.0 0.0 copy-start.4
  8.0 0.0 copy-start.5
  8.0 3.9 %prep.1 = (bf16[1280,384]{1,0:T(8,128)(2,1)S(1)}, bf16[640,384]{1,0:T(8,128)(2,1)S(1)}, f32[32,768]{1,0:T(8,128)S(1)}, f32[32,1024]{1,0:T(8,128)S(1)}, f32[32,10...) custom-call(f32[12]{0:T(128)S(1)} %copy-done.3, ...), custom_call_target="tpu_custom_call" | custom-call | flops 1000000000 | bytes 3000000 | tf_op jit(solution)/shard_map/prep/pallas_call | solution.py:524
  11.9 0.0 collective-permute-done.1.p1_ref
  11.9 0.0 collective-permute-done.2.p2_ref
  11.9 0.6 collective-permute-start.3
  12.5 0.1 collective-permute-start.4
  12.5 0.1 pad_add_fusion.flag_ref
  12.6 0.0 collective-permute-done.ownx_ref
  12.6 0.8 %collective-permute-done.3.p1x_ref = f32[32,896]{1,0:T(8,128)S(1)} collective-permute-done((f32[32,896]{1,0:T(8,128)S(1)}, f32[32,896]{1,0:T(8,128)S(1)}, u32[]{:S(2)}, u32[]{:S(2)}) %collective-permute-start.3) | collective-permute-done | bytes 114720 | tf_op jit(solution)/shard_map/ppermute | solution.py:627
  13.4 0.4 collective-permute-done.4.p2x_ref
  13.8 0.0 copy-done.4
  13.8 0.0 copy-done.5
  13.8 0.0 copy-start.1
  13.8 1.8 %first.1 = (f32[128,896]{1,0:T(8,128)S(1)}, f32[128,2048]{1,0:T(8,128)S(1)}, bf16[2,384,128]{2,1,0:T(8,128)(2,1)S(1)}, f32[32,384]{1,0:T(8,128)S(1)}) custom-call(s32[3]{0:T(128)S(1)} %pad_add_fusion.flag_ref, f32[32,896]{1,0:T(8,128)S(1)} %pack.1.pack_ref.own_ref, f32[32,896]{1,0:T(8,128)S(1)} %collective-permute-done.ownx_ref, ...), custom_call_target="tpu_custom_call" | custom-call | flops 1000000000 | bytes 3000000 | tf_op jit(solution)/shard_map/first/pallas_call | solution.py:524
  15.6 1.8 %collective-permute-start.5 = (f32[32,384]{1,0:T(8,128)S(1)}, f32[32,384]{1,0:T(8,128)S(1)}, u32[]{:S(2)}, u32[]{:S(2)}) collective-permute-start(f32[32,384]{1,0:T(8,128)S(1)} %get-tuple-element.70.e_mine), channel_id=1, source_target_pairs={{0,1},{1,0},{2,3},{3,2},{4,5},{5,4},{6,7},{7,6},{8,9},{9,8},{10,11... | collective-permute-start | bytes 147464 | tf_op jit(solution)/shard_map/ppermute | solution.py:588
  17.4 0.0 copy-done.1
  17.4 1.3 %second.1 = (f32[128,2048]{1,0:T(8,128)S(1)}, f32[32,1152]{1,0:T(8,128)S(1)}, f32[32,1024]{1,0:T(8,128)S(1)}) custom-call(f32[128,896]{1,0:T(8,128)S(1)} %get-tuple-element.71.keys_ref, bf16[1280,384]{1,0:T(8,128)(2,1)S(1)} %get-tuple-element.67.wk_ref, bf16[2,384,128]{2,1,0:T(8,128)(2,1)S(1)} %get-tuple-element.72.pm_ref, bf16[32,128,128]{2,1,0:T(8,128)(2,1)S(1)} %copy-done.1), custom_call_target="tpu_custom_call" | custom-call | flops 1000000000 | bytes 3000000 | tf_op jit(solution)/shard_map/second/pallas_call | solution.py:524
  18.7 0.3 collective-permute-start.7
  19.0 0.7 %collective-permute-done.5.e_other = f32[32,384]{1,0:T(8,128)S(1)} collective-permute-done((f32[32,384]{1,0:T(8,128)S(1)}, f32[32,384]{1,0:T(8,128)S(1)}, u32[]{:S(2)}, u32[]{:S(2)}) %collective-permute-start.5) | collective-permute-done | bytes 49184 | tf_op jit(solution)/shard_map/ppermute | solution.py:588
  19.7 2.6 %back_one.1 = (f32[768,128]{1,0:T(8,128)S(1)}, f32[32,384]{1,0:T(8,128)S(1)}, f32[32,384]{1,0:T(8,128)S(1)}, f32[64,384]{1,0:T(8,128)S(1)}, f32[32,1152]{1,0:T(8,128)S(1)}, /*index=5*/f32[128,768]{1,0:T(8,128)S(1)}) custom-call(s32[3]{0:T(128)S(1)} %pad_add_fusion.flag_ref, f32[32,384]{1,0:T(8,128)S(1)} %get-tuple-element.70.e_mine, ...), custom_call_target="tpu_custom_call" | custom-call | flops 6000000000 | bytes 18000000 | tf_op jit(solution)/shard_map/back_one/pallas_call | solution.py:524
  22.4 0.0 copy-start
  22.4 0.0 copy-start.2
  22.4 0.1 collective-permute-start.6
  22.5 1.8 %collective-permute-start.10 = (f32[32,1024]{1,0:T(8,128)S(1)}, f32[32,1024]{1,0:T(8,128)S(1)}, u32[]{:S(2)}, u32[]{:S(2)}) collective-permute-start(f32[32,1024]{1,0:T(8,128)S(1)} %get-tuple-element.88.tail_mine), channel_id=1, source_target_pairs={{0,1},{1,0},{2,3},{3,2},{4,5},{5,4},{6,7},{7,6},{8,9},{9,8},{10,11... | collective-permute-start | bytes 393224 | tf_op jit(solution)/shard_map/ppermute | solution.py:588
  24.3 1.2 %query_one.1 = (f32[32,384]{1,0:T(8,128)S(1)}, f32[32,128]{1,0:T(8,128)S(1)}, f32[128,128]{1,0:T(8,128)S(1)}) custom-call(f32[768,128]{1,0:T(8,128)S(1)} %get-tuple-element.79.z_ref.z1_ref, f32[128,2048]{1,0:T(8,128)S(1)} %get-tuple-element.75.kv_ref, f32[32,896]{1,0:T(8,128)S(1)} %pack.1.pack_ref.own_ref, f32[32,1024]{1,0:T(8,128)S(1)} %get-tuple-element.76.q_ref, ...), custom_call_target="tpu_custom_call" | custom-call | flops 10000000 | bytes 30000 | tf_op jit(solution)/shard_map/query_one/pallas_call | solution.py:524
  25.5 0.0 collective-permute-done.6
  25.5 0.0 collective-permute-done.7.e_other
  25.6 1.8 %collective-permute-start.9 = (f32[32,384]{1,0:T(8,128)S(1)}, f32[32,384]{1,0:T(8,128)S(1)}, u32[]{:S(2)}, u32[]{:S(2)}) collective-permute-start(f32[32,384]{1,0:T(8,128)S(1)} %slice_add_fusion.1), channel_id=1, source_target_pairs={{0,4},{2,6},{4,0},{6,2},{8,12},{10,14},{12,8},{14,10},{1,5},{3,7},... | collective-permute-start | bytes 147464 | tf_op jit(solution)/shard_map/ppermute | solution.py:598
  27.4 0.2 collective-permute-start.8
  27.6 0.8 %collective-permute-done.10.tail_other = f32[32,1024]{1,0:T(8,128)S(1)} collective-permute-done((f32[32,1024]{1,0:T(8,128)S(1)}, f32[32,1024]{1,0:T(8,128)S(1)}, u32[]{:S(2)}, u32[]{:S(2)}) %collective-permute-start.10) | collective-permute-done | bytes 131104 | tf_op jit(solution)/shard_map/ppermute | solution.py:588
  28.4 1.3 %collective-permute-done.9 = f32[32,384]{1,0:T(8,128)S(1)} collective-permute-done((f32[32,384]{1,0:T(8,128)S(1)}, f32[32,384]{1,0:T(8,128)S(1)}, u32[]{:S(2)}, u32[]{:S(2)}) %collective-permute-start.9) | collective-permute-done | bytes 49184 | tf_op jit(solution)/shard_map/ppermute | solution.py:598
  29.7 0.6 %collective-permute-start.11 = (f32[32,384]{1,0:T(8,128)S(1)}, f32[32,384]{1,0:T(8,128)S(1)}, u32[]{:S(2)}, u32[]{:S(2)}) collective-permute-start(f32[32,384]{1,0:T(8,128)S(1)} %add_add_fusion.1.r2), channel_id=1, source_target_pairs={{0,1},{2,3},{4,5},{6,7},{8,0},{10,2},{12,4},{14,6},{9,8},{11,10},{... | collective-permute-start | bytes 147464 | tf_op jit(solution)/shard_map/ppermute | solution.py:601
  30.4 2.2 %collective-permute-start.12 = (f32[32,384]{1,0:T(8,128)S(1)}, f32[32,384]{1,0:T(8,128)S(1)}, u32[]{:S(2)}, u32[]{:S(2)}) collective-permute-start(f32[32,384]{1,0:T(8,128)S(1)} %add_add_fusion.1.r2), channel_id=1, source_target_pairs={{8,1},{10,3},{12,5},{14,7},{1,8},{3,10},{5,12},{7,14},{0,4},{2,6},... | collective-permute-start | bytes 147464 | tf_op jit(solution)/shard_map/ppermute | solution.py:601
  32.6 0.0 collective-permute-done.8.r1
  32.6 2.8 %collective-permute-done.11.r3 = f32[32,384]{1,0:T(8,128)S(1)} collective-permute-done((f32[32,384]{1,0:T(8,128)S(1)}, f32[32,384]{1,0:T(8,128)S(1)}, u32[]{:S(2)}, u32[]{:S(2)}) %collective-permute-start.11) | collective-permute-done | bytes 49184 | tf_op jit(solution)/shard_map/ppermute | solution.py:601
  35.4 0.3 collective-permute-done.12.r4
  35.7 0.0 copy-done
  35.7 0.0 copy-done.2
  35.7 4.3 %back_zero.1 = (f32[768,128]{1,0:T(8,128)S(1)}, f32[104,128]{1,0:T(8,128)S(1)}, f32[104,128]{1,0:T(8,128)S(1)}, f32[208,128]{1,0:T(8,128)S(1)}, f32[32,1152]{1,0...) custom-call(s32[3]{0:T(128)S(1)} %pad_add_fusion.flag_ref, f32[32,384]{1,0:T(8,128)S(1)} %copy-done.2, ...), custom_call_target="tpu_custom_call" | custom-call | flops 1000000000 | bytes 3000000 | tf_op jit(solution)/shard_map/back_zero/pallas_call | solution.py:524
  40.1 0.1 collective-permute-start.13
  40.2 0.0 copy-start.6
  40.2 1.0 %query_zero.1.r0 = f32[104,128]{1,0:T(8,128)S(1)} custom-call(f32[768,128]{1,0:T(8,128)S(1)} %get-tuple-element.97.z_ref.z0_ref, f32[128,2048]{1,0:T(8,128)S(1)} %get-tuple-element.93.kv_ref, f32[32,896]{1,0:T(8,128)S(1)} %pack.1.pack_ref.own_ref, f32[32,1024]{1,0:T(8,128)S(1)} %get-tuple-element.94.q_ref, f32[32,1152]{1,0:T(8,128)S(1)} %get-tuple-element.98.pts_ref, ...), custom_call_target="tpu_custom_call" | custom-call | flops 1000000000 | bytes 3000000 | tf_op jit(solution)/shard_map/query_zero/pallas_call | solution.py:524
  41.2 0.3 collective-permute-done.13
  41.5 1.5 %collective-permute-start.15 = (f32[104,128]{1,0:T(8,128)S(1)}, f32[104,128]{1,0:T(8,128)S(1)}, u32[]{:S(2)}, u32[]{:S(2)}) collective-permute-start(f32[104,128]{1,0:T(8,128)S(1)} %slice_add_fusion), channel_id=1, source_target_pairs={{0,4},{2,6},{4,0},{6,2},{8,12},{10,14},{12,8},{14,10},{1,5},{3,7},... | collective-permute-start | bytes 159752 | tf_op jit(solution)/shard_map/ppermute | solution.py:598
  42.9 0.0 copy-done.6
  42.9 1.9 %pair_grad.1 = bf16[32,128,128]{2,1,0:T(8,128)(2,1)} custom-call(f32[768,128]{1,0:T(8,128)S(1)} %get-tuple-element.79.z_ref.z1_ref, f32[768,128]{1,0:T(8,128)S(1)} %get-tuple-element.97.z_ref.z0_ref, f32[384,128]{1,0:T(8,128)S(1)} %get-tuple-element.104.pu1_ref, f32[384,128]{1,0:T(8,128)S(1)} %get-tuple-element.105.pu0_ref, bf16[12,128]{1,0:T(8,128)(2,1)S(1)} %bitcast.15), custom_call_target="tpu_custom_call" | custom-call | flops 1000000000 | bytes 3000000 | tf_op jit(solution)/shard_map/pair_grad/pallas_call | solution.py:524
  44.9 3.0 %collective-permute-start.14 = (f32[104,128]{1,0:T(8,128)S(1)}, f32[104,128]{1,0:T(8,128)S(1)}, u32[]{:S(2)}, u32[]{:S(2)}) collective-permute-start(f32[104,128]{1,0:T(8,128)S(1)} %query_zero.1.r0), channel_id=1, source_target_pairs={{0,1},{1,0},{2,3},{3,2},{4,5},{5,4},{6,7},{7,6},{8,9},{9,8},{10,11... | collective-permute-start | bytes 159752 | tf_op jit(solution)/shard_map/ppermute | solution.py:596
  47.9 0.0 collective-permute-done.15
  47.9 0.6 %collective-permute-start.16 = (f32[104,128]{1,0:T(8,128)S(1)}, f32[104,128]{1,0:T(8,128)S(1)}, u32[]{:S(2)}, u32[]{:S(2)}) collective-permute-start(f32[104,128]{1,0:T(8,128)S(1)} %add_add_fusion.r2), channel_id=1, source_target_pairs={{0,1},{2,3},{4,5},{6,7},{8,0},{10,2},{12,4},{14,6},{9,8},{11,10},{... | collective-permute-start | bytes 159752 | tf_op jit(solution)/shard_map/ppermute | solution.py:601
  48.5 1.6 %collective-permute-start.17 = (f32[104,128]{1,0:T(8,128)S(1)}, f32[104,128]{1,0:T(8,128)S(1)}, u32[]{:S(2)}, u32[]{:S(2)}) collective-permute-start(f32[104,128]{1,0:T(8,128)S(1)} %add_add_fusion.r2), channel_id=1, source_target_pairs={{8,1},{10,3},{12,5},{14,7},{1,8},{3,10},{5,12},{7,14},{0,4},{2,6},... | collective-permute-start | bytes 159752 | tf_op jit(solution)/shard_map/ppermute | solution.py:601
  50.2 0.0 collective-permute-done.14.r1
  50.2 4.9 %collective-permute-done.16.r3 = f32[104,128]{1,0:T(8,128)S(1)} collective-permute-done((f32[104,128]{1,0:T(8,128)S(1)}, f32[104,128]{1,0:T(8,128)S(1)}, u32[]{:S(2)}, u32[]{:S(2)}) %collective-permute-start.16) | collective-permute-done | bytes 53280 | tf_op jit(solution)/shard_map/ppermute | solution.py:601
  55.1 0.0 collective-permute-done.17.r4
  55.1 1.2 %final.1 = (f32[32,384]{1,0:T(8,128)}, f32[12,2,32]{2,1,0:T(2,128)}) custom-call(s32[3]{0:T(128)S(1)} %pad_add_fusion.flag_ref, f32[104,128]{1,0:T(8,128)S(1)} %query_zero.1.r0, f32[104,128]{1,0:T(8,128)S(1)} %collective-permute-done.14.r1, f32[104,128]{1,0:T(8,128)S(1)} %add_add_fusion.r2, f32[104,128]{1,0:T(8,128)S(1)} %collective-permute-done.16.r3, ...), custom_call_target="tpu_custom_call" | custom-call | flops 1000000000 | bytes 3000000 | tf_op jit(solution)/shard_map/final/pallas_call | solution.py:524
  (4 shorter events, 0.0 us)
Async XLA Ops:
  0.6 7.4 %copy-start.3 = (f32[12]{0:T(128)S(1)}, f32[12]{0:T(128)}, u32[]{:S(2)}) copy-start(f32[12]{0:T(128)} %hw_ref.1) | copy-start | bytes 148
  1.6 10.3 %collective-permute-start.1 = (f32[32,896]{1,0:T(8,128)S(1)}, f32[32,896]{1,0:T(8,128)S(1)}, u32[]{:S(2)}, u32[]{:S(2)}) collective-permute-start(f32[32,896]{1,0:T(8,128)S(1)} %pack.1.pack_ref.own_ref), channel_id=1, source_target_pairs={{0,4},{2,6},{4,0},{6,2},{1,8},{3,10},{5,12},{7,14},{9,13},{11,15},... | collective-permute-start | bytes 344072 | tf_op jit(solution)/shard_map/ppermute | solution.py:575
  4.7 7.2 %collective-permute-start.2 = (f32[32,896]{1,0:T(8,128)S(1)}, f32[32,896]{1,0:T(8,128)S(1)}, u32[]{:S(2)}, u32[]{:S(2)}) collective-permute-start(f32[32,896]{1,0:T(8,128)S(1)} %pack.1.pack_ref.own_ref), channel_id=1, source_target_pairs={{0,12},{2,14},{4,8},{6,10},{9,5},{11,7},{13,1},{15,3},{1,0},{3,2},... | collective-permute-start | bytes 344072 | tf_op jit(solution)/shard_map/ppermute | solution.py:576
  8.0 4.6 %collective-permute-start = (f32[32,896]{1,0:T(8,128)S(1)}, f32[32,896]{1,0:T(8,128)S(1)}, u32[]{:S(2)}, u32[]{:S(2)}) collective-permute-start(f32[32,896]{1,0:T(8,128)S(1)} %pack.1.pack_ref.own_ref), channel_id=1, source_target_pairs={{0,2},{2,0},{4,6},{6,4},{8,10},{10,8},{12,14},{14,12},{1,3},{3,1},... | collective-permute-start | bytes 344072 | tf_op jit(solution)/shard_map/ppermute | solution.py:574
  8.0 5.8 %copy-start.4 = (bf16[2,12,32,128]{3,2,1,0:T(8,128)(2,1)S(1)}, bf16[2,12,32,128]{3,2,1,0:T(8,128)(2,1)}, u32[]{:S(2)}) copy-start(bf16[2,12,32,128]{3,2,1,0:T(8,128)(2,1)} %param.18) | copy-start | bytes 589828
  8.0 5.8 %copy-start.5 = (s32[16,16]{1,0:T(8,128)S(1)}, s32[16,16]{1,0:T(8,128)}, u32[]{:S(2)}) copy-start(s32[16,16]{1,0:T(8,128)} %links_ref.1) | copy-start | bytes 3076
  11.9 1.5 %collective-permute-start.3 = (f32[32,896]{1,0:T(8,128)S(1)}, f32[32,896]{1,0:T(8,128)S(1)}, u32[]{:S(2)}, u32[]{:S(2)}) collective-permute-start(f32[32,896]{1,0:T(8,128)S(1)} %collective-permute-done.1.p1_ref), channel_id=1, source_target_pairs={{0,2},{2,0},{4,6},{6,4},{8,10},{10,8},{12,14},{14,12},{1,3},{3,1},... | collective-permute-start | bytes 344072 | tf_op jit(solution)/shard_map/ppermute | solution.py:627
  12.5 1.3 %collective-permute-start.4 = (f32[32,896]{1,0:T(8,128)S(1)}, f32[32,896]{1,0:T(8,128)S(1)}, u32[]{:S(2)}, u32[]{:S(2)}) collective-permute-start(f32[32,896]{1,0:T(8,128)S(1)} %collective-permute-done.2.p2_ref), channel_id=1, source_target_pairs={{0,2},{2,0},{4,6},{6,4},{8,10},{10,8},{12,14},{14,12},{1,3},{3,1},... | collective-permute-start | bytes 344072 | tf_op jit(solution)/shard_map/ppermute | solution.py:627
  13.8 3.6 %copy-start.1 = (bf16[32,128,128]{2,1,0:T(8,128)(2,1)S(1)}, bf16[32,128,128]{2,1,0:T(8,128)(2,1)}, u32[]{:S(2)}) copy-start(bf16[32,128,128]{2,1,0:T(8,128)(2,1)} %pair_ref.3) | copy-start | bytes 3145732
  15.6 4.2 %collective-permute-start.5 = (f32[32,384]{1,0:T(8,128)S(1)}, f32[32,384]{1,0:T(8,128)S(1)}, u32[]{:S(2)}, u32[]{:S(2)}) collective-permute-start(f32[32,384]{1,0:T(8,128)S(1)} %get-tuple-element.70.e_mine), channel_id=1, source_target_pairs={{0,1},{1,0},{2,3},{3,2},{4,5},{5,4},{6,7},{7,6},{8,9},{9,8},{10,11... | collective-permute-start | bytes 147464 | tf_op jit(solution)/shard_map/ppermute | solution.py:588
  18.7 6.8 %collective-permute-start.7 = (f32[32,1152]{1,0:T(8,128)S(1)}, f32[32,1152]{1,0:T(8,128)S(1)}, u32[]{:S(2)}, u32[]{:S(2)}) collective-permute-start(f32[32,1152]{1,0:T(8,128)S(1)} %get-tuple-element.90.e_mine), channel_id=1, source_target_pairs={{0,1},{1,0},{2,3},{3,2},{4,5},{5,4},{6,7},{7,6},{8,9},{9,8},{10,11... | collective-permute-start | bytes 442376 | tf_op jit(solution)/shard_map/ppermute | solution.py:588
  22.4 13.4 %copy-start = (bf16[2112,384]{1,0:T(8,128)(2,1)S(1)}, bf16[2112,384]{1,0:T(8,128)(2,1)}, u32[]{:S(2)}) copy-start(bf16[2112,384]{1,0:T(8,128)(2,1)} %w_out_ref.1) | copy-start | bytes 4866052
  22.4 13.4 %copy-start.2 = (f32[32,384]{1,0:T(8,128)S(1)}, f32[32,384]{1,0:T(8,128)}, u32[]{:S(2)}) copy-start(f32[32,384]{1,0:T(8,128)} %cot_ref.1) | copy-start | bytes 147460
  22.4 3.2 %collective-permute-start.6 = (f32[64,384]{1,0:T(8,128)S(1)}, f32[64,384]{1,0:T(8,128)S(1)}, u32[]{:S(2)}, u32[]{:S(2)}) collective-permute-start(f32[64,384]{1,0:T(8,128)S(1)} %get-tuple-element.78), channel_id=1, source_target_pairs={{0,2},{2,0},{4,6},{6,4},{8,10},{10,8},{12,14},{14,12},{1,3},{3,1},... | collective-permute-start | bytes 294920 | tf_op jit(solution)/shard_map/ppermute | solution.py:593
  22.5 5.9 %collective-permute-start.10 = (f32[32,1024]{1,0:T(8,128)S(1)}, f32[32,1024]{1,0:T(8,128)S(1)}, u32[]{:S(2)}, u32[]{:S(2)}) collective-permute-start(f32[32,1024]{1,0:T(8,128)S(1)} %get-tuple-element.88.tail_mine), channel_id=1, source_target_pairs={{0,1},{1,0},{2,3},{3,2},{4,5},{5,4},{6,7},{7,6},{8,9},{9,8},{10,11... | collective-permute-start | bytes 393224 | tf_op jit(solution)/shard_map/ppermute | solution.py:588
  25.6 4.2 %collective-permute-start.9 = (f32[32,384]{1,0:T(8,128)S(1)}, f32[32,384]{1,0:T(8,128)S(1)}, u32[]{:S(2)}, u32[]{:S(2)}) collective-permute-start(f32[32,384]{1,0:T(8,128)S(1)} %slice_add_fusion.1), channel_id=1, source_target_pairs={{0,4},{2,6},{4,0},{6,2},{8,12},{10,14},{12,8},{14,10},{1,5},{3,7},... | collective-permute-start | bytes 147464 | tf_op jit(solution)/shard_map/ppermute | solution.py:598
  27.4 5.2 %collective-permute-start.8 = (f32[32,384]{1,0:T(8,128)S(1)}, f32[32,384]{1,0:T(8,128)S(1)}, u32[]{:S(2)}, u32[]{:S(2)}) collective-permute-start(f32[32,384]{1,0:T(8,128)S(1)} %get-tuple-element.84.r0), channel_id=1, source_target_pairs={{0,1},{1,0},{2,3},{3,2},{4,5},{5,4},{6,7},{7,6},{8,9},{9,8},{10,11... | collective-permute-start | bytes 147464 | tf_op jit(solution)/shard_map/ppermute | solution.py:596
  29.7 5.7 %collective-permute-start.11 = (f32[32,384]{1,0:T(8,128)S(1)}, f32[32,384]{1,0:T(8,128)S(1)}, u32[]{:S(2)}, u32[]{:S(2)}) collective-permute-start(f32[32,384]{1,0:T(8,128)S(1)} %add_add_fusion.1.r2), channel_id=1, source_target_pairs={{0,1},{2,3},{4,5},{6,7},{8,0},{10,2},{12,4},{14,6},{9,8},{11,10},{... | collective-permute-start | bytes 147464 | tf_op jit(solution)/shard_map/ppermute | solution.py:601
  30.4 5.3 %collective-permute-start.12 = (f32[32,384]{1,0:T(8,128)S(1)}, f32[32,384]{1,0:T(8,128)S(1)}, u32[]{:S(2)}, u32[]{:S(2)}) collective-permute-start(f32[32,384]{1,0:T(8,128)S(1)} %add_add_fusion.1.r2), channel_id=1, source_target_pairs={{8,1},{10,3},{12,5},{14,7},{1,8},{3,10},{5,12},{7,14},{0,4},{2,6},... | collective-permute-start | bytes 147464 | tf_op jit(solution)/shard_map/ppermute | solution.py:601
  40.1 1.4 %collective-permute-start.13 = (f32[208,128]{1,0:T(8,128)S(1)}, f32[208,128]{1,0:T(8,128)S(1)}, u32[]{:S(2)}, u32[]{:S(2)}) collective-permute-start(f32[208,128]{1,0:T(8,128)S(1)} %get-tuple-element.96), channel_id=1, source_target_pairs={{0,2},{2,0},{4,6},{6,4},{8,10},{10,8},{12,14},{14,12},{1,3},{3,1},... | collective-permute-start | bytes 319496 | tf_op jit(solution)/shard_map/ppermute | solution.py:593
  40.2 2.8 %copy-start.6 = (bf16[128,12]{0,1:T(8,128)(2,1)S(1)}, bf16[128,12]{0,1:T(8,128)(2,1)}, u32[]{:S(2)}) copy-start(bf16[128,12]{0,1:T(8,128)(2,1)} %param.29) | copy-start | bytes 9220
  41.5 6.4 %collective-permute-start.15 = (f32[104,128]{1,0:T(8,128)S(1)}, f32[104,128]{1,0:T(8,128)S(1)}, u32[]{:S(2)}, u32[]{:S(2)}) collective-permute-start(f32[104,128]{1,0:T(8,128)S(1)} %slice_add_fusion), channel_id=1, source_target_pairs={{0,4},{2,6},{4,0},{6,2},{8,12},{10,14},{12,8},{14,10},{1,5},{3,7},... | collective-permute-start | bytes 159752 | tf_op jit(solution)/shard_map/ppermute | solution.py:598
  44.9 5.3 %collective-permute-start.14 = (f32[104,128]{1,0:T(8,128)S(1)}, f32[104,128]{1,0:T(8,128)S(1)}, u32[]{:S(2)}, u32[]{:S(2)}) collective-permute-start(f32[104,128]{1,0:T(8,128)S(1)} %query_zero.1.r0), channel_id=1, source_target_pairs={{0,1},{1,0},{2,3},{3,2},{4,5},{5,4},{6,7},{7,6},{8,9},{9,8},{10,11... | collective-permute-start | bytes 159752 | tf_op jit(solution)/shard_map/ppermute | solution.py:596
  47.9 7.1 %collective-permute-start.16 = (f32[104,128]{1,0:T(8,128)S(1)}, f32[104,128]{1,0:T(8,128)S(1)}, u32[]{:S(2)}, u32[]{:S(2)}) collective-permute-start(f32[104,128]{1,0:T(8,128)S(1)} %add_add_fusion.r2), channel_id=1, source_target_pairs={{0,1},{2,3},{4,5},{6,7},{8,0},{10,2},{12,4},{14,6},{9,8},{11,10},{... | collective-permute-start | bytes 159752 | tf_op jit(solution)/shard_map/ppermute | solution.py:601
  48.5 6.5 %collective-permute-start.17 = (f32[104,128]{1,0:T(8,128)S(1)}, f32[104,128]{1,0:T(8,128)S(1)}, u32[]{:S(2)}, u32[]{:S(2)}) collective-permute-start(f32[104,128]{1,0:T(8,128)S(1)} %add_add_fusion.r2), channel_id=1, source_target_pairs={{8,1},{10,3},{12,5},{14,7},{1,8},{3,10},{5,12},{7,14},{0,4},{2,6},... | collective-permute-start | bytes 159752 | tf_op jit(solution)/shard_map/ppermute | solution.py:601

commit v5 on v4

--- a/solution.py
+++ b/solution.py
@@ -177,14 +177,14 @@
 
 
 def prep_body(
-    hw_ref, pack_ref, cot_hbm, w_out_hbm, pair_hbm, wq_hbm, wk_hbm, wv_hbm, wqp_hbm, wkp_hbm, wvp_hbm,
+    pack_ref, cot_hbm, w_out_hbm, pair_hbm, wq_hbm, wk_hbm, wv_hbm, wqp_hbm, wkp_hbm, wvp_hbm, hw_hbm,
     wk_out, wq_out, gp_ref, q1_ref, q0_ref, pu_ref, d_ref, sc_ref,
-    cot_ref, w_out_ref, pair_ref, wq_ref, wk_ref, wv_ref, wqp_ref, wkp_ref, wvp_ref, sems,
+    cot_ref, w_out_ref, pair_ref, wq_ref, wk_ref, wv_ref, wqp_ref, wkp_ref, wvp_ref, hw_ref, sems,
 ):
     rows = pack_ref.shape[0]
     ends = (
         (cot_hbm, cot_ref), (w_out_hbm, w_out_ref), (pair_hbm, pair_ref), (wq_hbm, wq_ref), (wk_hbm, wk_ref),
-        (wv_hbm, wv_ref), (wqp_hbm, wqp_ref), (wkp_hbm, wkp_ref), (wvp_hbm, wvp_ref),
+        (wv_hbm, wv_ref), (wqp_hbm, wqp_ref), (wkp_hbm, wkp_ref), (wvp_hbm, wvp_ref), (hw_hbm, hw_ref),
     )
     copies = [pltpu.make_async_copy(src, dst, sems.at[n]) for n, (src, dst) in enumerate(ends)]
     for copy in copies:
@@ -208,7 +208,7 @@
     lane = iota((8, 128), 1)
     raw = jnp.zeros((8, 128), F32)
     for h in range(H):
-        raw = jnp.where((lane >> 2) == h, hw_ref[h], raw)
+        raw = jnp.where((lane >> 2) == h, hw_ref[:, h : h + 1], raw)
     soft = jnp.maximum(raw, 0.0) + jnp.log(1.0 + jnp.exp(-jnp.abs(raw)))
     sc_ref[...] = soft * POINT_SCALE
     fr = pack_ref[:, FRAME_LANE : FRAME_LANE + 128]
@@ -241,16 +241,14 @@
 
 
 def first_body(
-    flag_ref, own_ref, ownx_ref, p1_ref, p1x_ref, p2_ref, p2x_ref, wk_ref, links_ref, probs_ref, gp_ref, d_ref,
+    fast, own_ref, ownx_ref, p1_ref, p1x_ref, p2_ref, p2x_ref, wk_ref, links_ref, probs_ref, gp_ref, d_ref,
     keys_ref, kv_ref, pm_ref, e_ref,
 ):
     rows = own_ref.shape[0]
-    home = flag_ref[0] == 1
-    zb = flag_ref[1]
-    core = flag_ref[2]
+    home, zb, core = position(fast)
 
     def put(z, k, value):
-        keys_ref[pl.ds(pl.multiple_of((2 * z + k) * rows, rows), rows), :] = value
+        keys_ref[pl.ds(pl.multiple_of(jnp.int32((2 * z + k) * rows), rows), rows), :] = value
 
     put(zb, core, jnp.where(home, own_ref[...], p1_ref[...]))
     put(zb, 1 - core, jnp.where(home, ownx_ref[...], p1x_ref[...]))
@@ -299,7 +297,7 @@
 
 
 def backward(
-    flag_ref, e, dots, probs, kv_ref, key_fr, own_fr, fcol, q_ref, gp, d_ref, wk_ref, sc,
+    e, dots, probs, kv_ref, key_fr, own_fr, fcol, q_ref, gp, d_ref, wk_ref, sc,
     z_ref, keys_out_ref,
 ):
     rows = e.shape[0]
@@ -401,12 +399,18 @@
     return grad, frame_sums(prods, first_lane)
 
 
-def send_blocks(flag_ref, src_ref, mine_a, mine_b, theirs, rows):
-    zb = flag_ref[1]
-    core = flag_ref[2]
+def position(fast):
+    if not fast:
+        return True, 0, 0
+    row = lax.axis_index("row")
+    return row // 4 == lax.axis_index("col"), (row // 2) % 2, row % 2
+
+
+def send_blocks(fast, src_ref, mine_a, mine_b, theirs, rows):
+    _, zb, core = position(fast)
 
     def get(z, k):
-        return src_ref[pl.ds(pl.multiple_of((2 * z + k) * rows, 8), rows), :]
+        return src_ref[pl.ds(pl.multiple_of(jnp.int32((2 * z + k) * rows), 8), rows), :]
 
     mine_a[...] = get(zb, core)
     mine_b[...] = get(1 - zb, core)
@@ -414,12 +418,12 @@
     theirs[rows:, :] = get(1 - zb, 1 - core)
 
 
-def add_pieces(flag_ref, query, query_other, part, one, two):
-    return (query[...] + query_other[...]) + (one[...] + jnp.where(flag_ref[0] == 1, part[...], two[...]))
-
-
-def final_body(flag_ref, r0, r1, r2, r3, r4, one_ref, single_out, frames_out):
-    total = add_pieces(flag_ref, r0, r1, r2, r3, r4)
+def add_pieces(fast, query, query_other, part, one, two):
+    return (query[...] + query_other[...]) + (one[...] + jnp.where(position(fast)[0], part[...], two[...]))
+
+
+def final_body(fast, r0, r1, r2, r3, r4, one_ref, single_out, frames_out):
+    total = add_pieces(fast, r0, r1, r2, r3, r4)
     rows = one_ref.shape[0]
     for t in range(3):
         lanes = slice(128 * t, 128 * t + 128)
@@ -434,15 +438,15 @@
 
 
 def back_one_body(
-    flag_ref, e_mine, e_other, pm_ref, kv_ref, keys_ref, own_ref, q_ref, gp_ref, d_ref, wk_ref, sc_ref,
+    fast, e_mine, e_other, pm_ref, kv_ref, keys_ref, own_ref, q_ref, gp_ref, d_ref, wk_ref, sc_ref,
     z_ref, mine_a, mine_b, theirs, pts_ref, grads_ref, work_ref,
 ):
     e = e_mine[...] + e_other[...]
     pts_ref[...], grads_ref[...] = backward(
-        flag_ref, e, e[:, 128:256], pm_ref[1], kv_ref, frame_part(keys_ref), frame_part(own_ref), 0, q_ref,
+        e, e[:, 128:256], pm_ref[1], kv_ref, frame_part(keys_ref), frame_part(own_ref), 0, q_ref,
         gp_ref[...], d_ref, wk_ref, sc_ref[0:1, :], z_ref, work_ref,
     )
-    send_blocks(flag_ref, work_ref, mine_a, mine_b, theirs, own_ref.shape[0])
+    send_blocks(fast, work_ref, mine_a, mine_b, theirs, own_ref.shape[0])
 
 
 def query_one_body(
@@ -456,12 +460,12 @@
 
 
 def back_zero_body(
-    flag_ref, cot_ref, r0, r1, r2, r3, r4, e_mine, e_other, tail_mine, tail_other, pm_ref, kv_ref, keys_ref, own_ref, q_ref, pair_ref,
+    fast, cot_ref, r0, r1, r2, r3, r4, e_mine, e_other, tail_mine, tail_other, pm_ref, kv_ref, keys_ref, own_ref, q_ref, pair_ref,
     w_out_ref, wk_ref, sc_ref, frk_ref,
     z_ref, mine_a, mine_b, theirs, pts_ref, sum_ref, pu_ref, work_ref, pieces_ref, gp_ref, d_ref,
 ):
     rows = own_ref.shape[0]
-    total = add_pieces(flag_ref, r0, r1, r2, r3, r4)
+    total = add_pieces(fast, r0, r1, r2, r3, r4)
     sum_ref[...] = total
     upstream_parts(cot_ref[...] + total, w_out_ref, gp_ref, pu_ref, rows)
     pair_products(pu_ref, pair_ref, d_ref, rows)
@@ -484,14 +488,14 @@
     )
     dots = dots + mm2(wide, lane_matrix(H * CZ, lambda r: STAT + (r >> 7)))
     pts_ref[...], grads = backward(
-        flag_ref, e, dots, pm_ref[0], kv_ref, frame_part(keys_ref), frame_part(own_ref), 12, q_ref, gp, d_ref, wk_ref,
+        e, dots, pm_ref[0], kv_ref, frame_part(keys_ref), frame_part(own_ref), 12, q_ref, gp, d_ref, wk_ref,
         sc_ref[0:1, :], z_ref, work_ref,
     )
     turned = jnp.transpose(backward_frames(grads, kv_ref, 0) + frk_ref[...])
     for n in range(4):
         at = n * pieces_ref.shape[0] // 4
         store_piece(pieces_ref, at, work_ref[rows * n : rows * (n + 1), :], frame_block(turned, rows * n, rows))
-    send_blocks(flag_ref, pieces_ref, mine_a, mine_b, theirs, mine_a.shape[0])
+    send_blocks(fast, pieces_ref, mine_a, mine_b, theirs, mine_a.shape[0])
 
 
 def query_zero_body(share, z_ref, kv_ref, own_ref, q_ref, pts_ref, wq_ref, sc_ref, frq_ref, query_out):
@@ -516,7 +520,6 @@
 
 
 VMEM = pl.BlockSpec(memory_space=pltpu.VMEM)
-SMEM = pl.BlockSpec(memory_space=pltpu.SMEM)
 HBM = pl.BlockSpec(memory_space=pltpu.HBM)
 
 
@@ -569,14 +572,11 @@
     col = lax.axis_index("col")
     row = lax.axis_index("row")
     if fast:
-        home = (row // 4 == col).astype(jnp.int32)
-        flags = jnp.stack([home, (row // 2) % 2, row % 2])
         ownx = lax.ppermute(pack, "row", CORE_SWAP)
         one = lax.ppermute(pack, BOTH, FETCH_ONE)
         two = lax.ppermute(pack, BOTH, FETCH_TWO)
         own = pack
     else:
-        flags = jnp.array([1, 0, 0], jnp.int32)
         whole = lax.all_gather(pack, "row", axis=0, tiled=True)
         mine = lax.dynamic_slice_in_dim(whole, col * keys, keys, 0)
         quarter = keys // 4
@@ -612,12 +612,13 @@
     hr = H * rows
     loads = (
         cotangent, w_out, pair, w_query.T, w_key.T, w_value.T, w_query_points.T, w_key_points.T, w_value_points.T,
+        head_weights[None],
     )
     wk, wq, gp1, q1, q0, pu1, d1, sc = call(
-        prep_body, "prep", [SMEM, VMEM] + [HBM] * 9,
+        prep_body, "prep", [VMEM] + [HBM] * 10,
         [((1280, C), BF16), ((LANES, C), BF16), ((rows, 768), F32), ((rows, 1024), F32), ((rows, 1024), F32),
          ((hr, CZ), F32), ((hr, keys), F32), ((8, 128), F32)],
-        (head_weights, own, *in_hbm(*loads)),
+        (own, *in_hbm(*loads)),
         [pltpu.VMEM(x.shape, x.dtype) for x in loads] + [pltpu.SemaphoreType.DMA((len(loads),))],
     )
     if fast:
@@ -626,9 +627,9 @@
         )
         blocks = (pack, ownx, one, lax.ppermute(one, "row", CORE_SWAP), two, lax.ppermute(two, "row", CORE_SWAP))
     key_pack, kv1, pm, e1 = call(
-        first_body, "first", [SMEM] + [VMEM] * 11,
+        functools.partial(first_body, fast), "first", [VMEM] * 11,
         [((keys, PACK), F32), ((keys, 2048), F32), ((2, hr, keys), BF16), ((rows, 384), F32)],
-        (flags, *blocks, wk, links, probs, gp1, d1),
+        (*blocks, wk, links, probs, gp1, d1),
     )
     e1_other = col_other(e1)
     kv0, e0, tail = call(
@@ -642,10 +643,10 @@
     share = 1.0 / col_total
     e1_other, e0 = lax.optimization_barrier((e1_other, e0))
     z1, mine_a, mine_b, theirs, pts, grads = call(
-        back_one_body, "back_one", [SMEM] + [VMEM] * 11,
+        functools.partial(back_one_body, fast), "back_one", [VMEM] * 11,
         [((2 * hr, keys), F32), ((rows, C), F32), ((rows, C), F32), ((2 * rows, C), F32), ((rows, 1152), F32),
          ((keys, 768), F32)],
-        (flags, e1, e1_other, pm, kv1, key_pack, own, q1, gp1, d1, wk, sc),
+        (e1, e1_other, pm, kv1, key_pack, own, q1, gp1, d1, wk, sc),
         [pltpu.VMEM((keys, C), F32)],
         6.0,
     )
@@ -663,10 +664,10 @@
     )
     long = 3 * rows + 8
     z0, mine_a, mine_b, theirs, pts, single_one, pu0 = call(
-        back_zero_body, "back_zero", [SMEM] + [VMEM] * 20,
+        functools.partial(back_zero_body, fast), "back_zero", [VMEM] * 20,
         [((2 * hr, keys), F32), ((long, 128), F32), ((long, 128), F32), ((2 * long, 128), F32), ((rows, 1152), F32),
          ((rows, C), F32), ((hr, CZ), F32)],
-        (flags, cotangent, *pieces, e0, e0_other, tail, tail_other, pm, kv0, key_pack, own, q0, pair, w_out, wk, sc, frk),
+        (cotangent, *pieces, e0, e0_other, tail, tail_other, pm, kv0, key_pack, own, q0, pair, w_out, wk, sc, frk),
         [pltpu.VMEM((keys, C), F32), pltpu.VMEM((4 * long, 128), F32), pltpu.VMEM((rows, 768), F32), pltpu.VMEM((hr, keys), F32)],
     )
     (d_pair,) = call(
@@ -682,8 +683,8 @@
         d_pair,
     )
     d_single, d_frames = call(
-        final_body, "final", [SMEM] + [VMEM] * 6, [((rows, C), F32), ((12, 2, rows), F32)],
-        (flags, *pieces, single_one),
+        functools.partial(final_body, fast), "final", [VMEM] * 6, [((rows, C), F32), ((12, 2, rows), F32)],
+        (*pieces, single_one),
     )
     return (d_single, d_frames.transpose(1, 0, 2), d_pair)
 

time: 56.5 us -> 54.3 us (0.961)
  Pallas kernels: 20.3 us -> 17.7 us
    pallas_call x10, Pallas kernels: 20.3 us -> 17.7 us  [call(): pl.pallas_call(body, name=name, in_specs=in_specs, out_specs=tuple((VMEM...]
  transfers between devices with their start and end apart: 18 -> 18, of which waited for: 9 -> 9; matrix products, arithmetic and copies ran while one was open for 0% -> 0% of each run, Pallas kernels for 21% -> 20%
where the time goes in v5:
time: 54.3 us; the launch traced here: 54.1 us
  starting transfers between devices  23.1 us (43%)
  Pallas kernels  17.7 us (33%)
  waiting for transfers between devices  12.4 us (23%)
  between operations  0.79 us (1%)
    pallas_call x10, Pallas kernels, call(): pl.pallas_call(body, name=name, in_specs=in_specs, out_specs=tuple((VMEM...  17.7 us
    ppermute x2, waiting for transfers between devices, reduce(): lax.ppermute(part, BOTH, SEND_ONE)  7.53 us
    ppermute x3, starting transfers between devices, col_other(): return lax.ppermute(x, 'col', COL_SWAP)  4.32 us
    ppermute x2, starting transfers between devices, reduce(): lax.ppermute(part, BOTH, SEND_TWO)  3.97 us
    ppermute x2, starting transfers between devices, reduce(): query_other = lax.ppermute(query, 'col', COL_SWAP)  3.33 us
    ppermute x1, starting transfers between devices, local(): two = lax.ppermute(pack, BOTH, FETCH_TWO)  3.29 us
    ppermute x2, starting transfers between devices, reduce(): half = lax.ppermute(mine_b + got[count:], 'row', Z_SWAP)  3.19 us
    ppermute x1, starting transfers between devices, local(): one = lax.ppermute(pack, BOTH, FETCH_ONE)  3.09 us
  transfers between devices with their start and end apart: 18, of which 9 were waited for; matrix products, arithmetic and copies ran while one was open for 0% of the time, Pallas kernels for 20%

profile of v5, /device:TPU:0, one launch (start us, length us, event | category | flops | bytes accessed | tf_op | source)
XLA Modules:
  0.0 54.1 jit_solution(3258512850439423399)
XLA Ops:
  0.6 1.0 %pack.1.pack_ref.own_ref = f32[32,896]{1,0:T(8,128)S(1)} custom-call(f32[2,32,384]{2,1,0:T(8,128)} %single_hbm.1, f32[12,2,32]{2,1,0:T(2,128)} %bitcast.21, s32[1,32]{1,0:T(1,128)} %bitcast.22), custom_call_target="tpu_custom_call" | custom-call | flops 1000000000 | bytes 3000000 | tf_op jit(solution)/shard_map/pack/pallas_call | solution.py:527
  1.6 3.1 %collective-permute-start.1 = (f32[32,896]{1,0:T(8,128)S(1)}, f32[32,896]{1,0:T(8,128)S(1)}, u32[]{:S(2)}, u32[]{:S(2)}) collective-permute-start(f32[32,896]{1,0:T(8,128)S(1)} %pack.1.pack_ref.own_ref), channel_id=1, source_target_pairs={{0,4},{2,6},{4,0},{6,2},{1,8},{3,10},{5,12},{7,14},{9,13},{11,15},... | collective-permute-start | bytes 344072 | tf_op jit(solution)/shard_map/ppermute | solution.py:576
  4.7 3.3 %collective-permute-start.2 = (f32[32,896]{1,0:T(8,128)S(1)}, f32[32,896]{1,0:T(8,128)S(1)}, u32[]{:S(2)}, u32[]{:S(2)}) collective-permute-start(f32[32,896]{1,0:T(8,128)S(1)} %pack.1.pack_ref.own_ref), channel_id=1, source_target_pairs={{0,12},{2,14},{4,8},{6,10},{9,5},{11,7},{13,1},{15,3},{1,0},{3,2},... | collective-permute-start | bytes 344072 | tf_op jit(solution)/shard_map/ppermute | solution.py:577
  8.0 0.0 collective-permute-start
  8.0 0.0 copy-start.3
  8.0 0.0 copy-start.4
  8.0 3.3 %prep.1 = (bf16[1280,384]{1,0:T(8,128)(2,1)S(1)}, bf16[640,384]{1,0:T(8,128)(2,1)S(1)}, f32[32,768]{1,0:T(8,128)S(1)}, f32[32,1024]{1,0:T(8,128)S(1)}, f32[32,10...) custom-call(f32[32,896]{1,0:T(8,128)S(1)} %pack.1.pack_ref.own_ref, ...), custom_call_target="tpu_custom_call" | custom-call | flops 1000000000 | bytes 3000000 | tf_op jit(solution)/shard_map/prep/pallas_call | solution.py:527
  11.3 0.0 collective-permute-done.1.p1_ref
  11.4 0.0 collective-permute-done.2.p2_ref
  11.4 0.6 %collective-permute-start.3 = (f32[32,896]{1,0:T(8,128)S(1)}, f32[32,896]{1,0:T(8,128)S(1)}, u32[]{:S(2)}, u32[]{:S(2)}) collective-permute-start(f32[32,896]{1,0:T(8,128)S(1)} %collective-permute-done.1.p1_ref), channel_id=1, source_target_pairs={{0,2},{2,0},{4,6},{6,4},{8,10},{10,8},{12,14},{14,12},{1,3},{3,1},... | collective-permute-start | bytes 344072 | tf_op jit(solution)/shard_map/ppermute | solution.py:628
  11.9 0.1 collective-permute-start.4
  12.0 0.0 collective-permute-done.ownx_ref
  12.0 0.9 %collective-permute-done.3.p1x_ref = f32[32,896]{1,0:T(8,128)S(1)} collective-permute-done((f32[32,896]{1,0:T(8,128)S(1)}, f32[32,896]{1,0:T(8,128)S(1)}, u32[]{:S(2)}, u32[]{:S(2)}) %collective-permute-start.3) | collective-permute-done | bytes 114720 | tf_op jit(solution)/shard_map/ppermute | solution.py:628
  12.9 0.4 collective-permute-done.4.p2x_ref
  13.3 0.0 copy-done.3
  13.3 0.0 copy-done.4
  13.3 0.0 copy-start.1
  13.3 1.2 %first.1 = (f32[128,896]{1,0:T(8,128)S(1)}, f32[128,2048]{1,0:T(8,128)S(1)}, bf16[2,384,128]{2,1,0:T(8,128)(2,1)S(1)}, f32[32,384]{1,0:T(8,128)S(1)}) custom-call(f32[32,896]{1,0:T(8,128)S(1)} %pack.1.pack_ref.own_ref, f32[32,896]{1,0:T(8,128)S(1)} %collective-permute-done.ownx_ref, f32[32,896]{1,0:T(8,128)S(1)} %collective-permute-done.1.p1_ref, ...), custom_call_target="tpu_custom_call" | custom-call | flops 1000000000 | bytes 3000000 | tf_op jit(solution)/shard_map/first/pallas_call | solution.py:527
  14.5 2.3 %collective-permute-start.5 = (f32[32,384]{1,0:T(8,128)S(1)}, f32[32,384]{1,0:T(8,128)S(1)}, u32[]{:S(2)}, u32[]{:S(2)}) collective-permute-start(f32[32,384]{1,0:T(8,128)S(1)} %get-tuple-element.70.e_mine), channel_id=1, source_target_pairs={{0,1},{1,0},{2,3},{3,2},{4,5},{5,4},{6,7},{7,6},{8,9},{9,8},{10,11... | collective-permute-start | bytes 147464 | tf_op jit(solution)/shard_map/ppermute | solution.py:588
  16.9 0.0 copy-done.1
  16.9 1.3 %second.1 = (f32[128,2048]{1,0:T(8,128)S(1)}, f32[32,1152]{1,0:T(8,128)S(1)}, f32[32,1024]{1,0:T(8,128)S(1)}) custom-call(f32[128,896]{1,0:T(8,128)S(1)} %get-tuple-element.71.keys_ref, bf16[1280,384]{1,0:T(8,128)(2,1)S(1)} %get-tuple-element.67.wk_ref, bf16[2,384,128]{2,1,0:T(8,128)(2,1)S(1)} %get-tuple-element.72.pm_ref, bf16[32,128,128]{2,1,0:T(8,128)(2,1)S(1)} %copy-done.1), custom_call_target="tpu_custom_call" | custom-call | flops 1000000000 | bytes 3000000 | tf_op jit(solution)/shard_map/second/pallas_call | solution.py:527
  18.2 0.1 collective-permute-start.7
  18.3 0.8 %collective-permute-done.5.e_other = f32[32,384]{1,0:T(8,128)S(1)} collective-permute-done((f32[32,384]{1,0:T(8,128)S(1)}, f32[32,384]{1,0:T(8,128)S(1)}, u32[]{:S(2)}, u32[]{:S(2)}) %collective-permute-start.5) | collective-permute-done | bytes 49184 | tf_op jit(solution)/shard_map/ppermute | solution.py:588
  19.1 2.1 %back_one.1 = (f32[768,128]{1,0:T(8,128)S(1)}, f32[32,384]{1,0:T(8,128)S(1)}, f32[32,384]{1,0:T(8,128)S(1)}, f32[64,384]{1,0:T(8,128)S(1)}, f32[32,1152]{1,0:T(8,128)S(1)}, /*index=5*/f32[128,768]{1,0:T(8,128)S(1)}) custom-call(f32[32,384]{1,0:T(8,128)S(1)} %get-tuple-element.70.e_mine, f32[32,384]{1,0:T(8,128)S(1)} %collective-permute-done.5.e_other, ...), custom_call_target="tpu_custom_call" | custom-call | flops 6000000000 | bytes 18000000 | tf_op jit(solution)/shard_map/back_one/pallas_call | solution.py:527
  21.2 0.0 copy-start
  21.2 0.0 copy-start.2
  21.3 0.1 collective-permute-start.6
  21.3 1.9 %collective-permute-start.10 = (f32[32,1024]{1,0:T(8,128)S(1)}, f32[32,1024]{1,0:T(8,128)S(1)}, u32[]{:S(2)}, u32[]{:S(2)}) collective-permute-start(f32[32,1024]{1,0:T(8,128)S(1)} %get-tuple-element.88.tail_mine), channel_id=1, source_target_pairs={{0,1},{1,0},{2,3},{3,2},{4,5},{5,4},{6,7},{7,6},{8,9},{9,8},{10,11... | collective-permute-start | bytes 393224 | tf_op jit(solution)/shard_map/ppermute | solution.py:588
  23.2 1.2 %query_one.1 = (f32[32,384]{1,0:T(8,128)S(1)}, f32[32,128]{1,0:T(8,128)S(1)}, f32[128,128]{1,0:T(8,128)S(1)}) custom-call(f32[768,128]{1,0:T(8,128)S(1)} %get-tuple-element.79.z_ref.z1_ref, f32[128,2048]{1,0:T(8,128)S(1)} %get-tuple-element.75.kv_ref, f32[32,896]{1,0:T(8,128)S(1)} %pack.1.pack_ref.own_ref, f32[32,1024]{1,0:T(8,128)S(1)} %get-tuple-element.76.q_ref, ...), custom_call_target="tpu_custom_call" | custom-call | flops 10000000 | bytes 30000 | tf_op jit(solution)/shard_map/query_one/pallas_call | solution.py:527
  24.5 0.0 collective-permute-done.6
  24.5 0.0 collective-permute-done.7.e_other
  24.5 1.8 %collective-permute-start.9 = (f32[32,384]{1,0:T(8,128)S(1)}, f32[32,384]{1,0:T(8,128)S(1)}, u32[]{:S(2)}, u32[]{:S(2)}) collective-permute-start(f32[32,384]{1,0:T(8,128)S(1)} %slice_add_fusion.1), channel_id=1, source_target_pairs={{0,4},{2,6},{4,0},{6,2},{8,12},{10,14},{12,8},{14,10},{1,5},{3,7},... | collective-permute-start | bytes 147464 | tf_op jit(solution)/shard_map/ppermute | solution.py:598
  26.3 0.2 collective-permute-start.8
  26.5 0.8 %collective-permute-done.10.tail_other = f32[32,1024]{1,0:T(8,128)S(1)} collective-permute-done((f32[32,1024]{1,0:T(8,128)S(1)}, f32[32,1024]{1,0:T(8,128)S(1)}, u32[]{:S(2)}, u32[]{:S(2)}) %collective-permute-start.10) | collective-permute-done | bytes 131104 | tf_op jit(solution)/shard_map/ppermute | solution.py:588
  27.3 1.3 %collective-permute-done.9 = f32[32,384]{1,0:T(8,128)S(1)} collective-permute-done((f32[32,384]{1,0:T(8,128)S(1)}, f32[32,384]{1,0:T(8,128)S(1)}, u32[]{:S(2)}, u32[]{:S(2)}) %collective-permute-start.9) | collective-permute-done | bytes 49184 | tf_op jit(solution)/shard_map/ppermute | solution.py:598
  28.7 0.7 %collective-permute-start.11 = (f32[32,384]{1,0:T(8,128)S(1)}, f32[32,384]{1,0:T(8,128)S(1)}, u32[]{:S(2)}, u32[]{:S(2)}) collective-permute-start(f32[32,384]{1,0:T(8,128)S(1)} %add_add_fusion.1.r2), channel_id=1, source_target_pairs={{0,1},{2,3},{4,5},{6,7},{8,0},{10,2},{12,4},{14,6},{9,8},{11,10},{... | collective-permute-start | bytes 147464 | tf_op jit(solution)/shard_map/ppermute | solution.py:601
  29.3 2.2 %collective-permute-start.12 = (f32[32,384]{1,0:T(8,128)S(1)}, f32[32,384]{1,0:T(8,128)S(1)}, u32[]{:S(2)}, u32[]{:S(2)}) collective-permute-start(f32[32,384]{1,0:T(8,128)S(1)} %add_add_fusion.1.r2), channel_id=1, source_target_pairs={{8,1},{10,3},{12,5},{14,7},{1,8},{3,10},{5,12},{7,14},{0,4},{2,6},... | collective-permute-start | bytes 147464 | tf_op jit(solution)/shard_map/ppermute | solution.py:601
  31.6 0.0 collective-permute-done.8.r1
  31.6 2.8 %collective-permute-done.11.r3 = f32[32,384]{1,0:T(8,128)S(1)} collective-permute-done((f32[32,384]{1,0:T(8,128)S(1)}, f32[32,384]{1,0:T(8,128)S(1)}, u32[]{:S(2)}, u32[]{:S(2)}) %collective-permute-start.11) | collective-permute-done | bytes 49184 | tf_op jit(solution)/shard_map/ppermute | solution.py:601
  34.3 0.4 collective-permute-done.12.r4
  34.7 0.0 copy-done
  34.7 0.0 copy-done.2
  34.7 3.8 %back_zero.1 = (f32[768,128]{1,0:T(8,128)S(1)}, f32[104,128]{1,0:T(8,128)S(1)}, f32[104,128]{1,0:T(8,128)S(1)}, f32[208,128]{1,0:T(8,128)S(1)}, f32[32,1152]{1,0...) custom-call(f32[32,384]{1,0:T(8,128)S(1)} %copy-done.2, f32[32,384]{1,0:T(8,128)S(1)} %get-tuple-element.84.r0, ...), custom_call_target="tpu_custom_call" | custom-call | flops 1000000000 | bytes 3000000 | tf_op jit(solution)/shard_map/back_zero/pallas_call | solution.py:527
  38.5 0.1 collective-permute-start.13
  38.6 0.0 copy-start.5
  38.6 1.0 %query_zero.1.r0 = f32[104,128]{1,0:T(8,128)S(1)} custom-call(f32[768,128]{1,0:T(8,128)S(1)} %get-tuple-element.97.z_ref.z0_ref, f32[128,2048]{1,0:T(8,128)S(1)} %get-tuple-element.93.kv_ref, f32[32,896]{1,0:T(8,128)S(1)} %pack.1.pack_ref.own_ref, f32[32,1024]{1,0:T(8,128)S(1)} %get-tuple-element.94.q_ref, f32[32,1152]{1,0:T(8,128)S(1)} %get-tuple-element.98.pts_ref, ...), custom_call_target="tpu_custom_call" | custom-call | flops 1000000000 | bytes 3000000 | tf_op jit(solution)/shard_map/query_zero/pallas_call | solution.py:527
  39.6 0.3 collective-permute-done.13
  39.9 1.4 %collective-permute-start.15 = (f32[104,128]{1,0:T(8,128)S(1)}, f32[104,128]{1,0:T(8,128)S(1)}, u32[]{:S(2)}, u32[]{:S(2)}) collective-permute-start(f32[104,128]{1,0:T(8,128)S(1)} %slice_add_fusion), channel_id=1, source_target_pairs={{0,4},{2,6},{4,0},{6,2},{8,12},{10,14},{12,8},{14,10},{1,5},{3,7},... | collective-permute-start | bytes 159752 | tf_op jit(solution)/shard_map/ppermute | solution.py:598
  41.3 0.0 copy-done.5
  41.3 1.9 %pair_grad.1 = bf16[32,128,128]{2,1,0:T(8,128)(2,1)} custom-call(f32[768,128]{1,0:T(8,128)S(1)} %get-tuple-element.79.z_ref.z1_ref, f32[768,128]{1,0:T(8,128)S(1)} %get-tuple-element.97.z_ref.z0_ref, f32[384,128]{1,0:T(8,128)S(1)} %get-tuple-element.104.pu1_ref, f32[384,128]{1,0:T(8,128)S(1)} %get-tuple-element.105.pu0_ref, bf16[12,128]{1,0:T(8,128)(2,1)S(1)} %bitcast.13), custom_call_target="tpu_custom_call" | custom-call | flops 1000000000 | bytes 3000000 | tf_op jit(solution)/shard_map/pair_grad/pallas_call | solution.py:527
  43.2 3.1 %collective-permute-start.14 = (f32[104,128]{1,0:T(8,128)S(1)}, f32[104,128]{1,0:T(8,128)S(1)}, u32[]{:S(2)}, u32[]{:S(2)}) collective-permute-start(f32[104,128]{1,0:T(8,128)S(1)} %query_zero.1.r0), channel_id=1, source_target_pairs={{0,1},{1,0},{2,3},{3,2},{4,5},{5,4},{6,7},{7,6},{8,9},{9,8},{10,11... | collective-permute-start | bytes 159752 | tf_op jit(solution)/shard_map/ppermute | solution.py:596
  46.3 0.0 collective-permute-done.15
  46.4 0.5 collective-permute-start.16
  46.9 1.7 %collective-permute-start.17 = (f32[104,128]{1,0:T(8,128)S(1)}, f32[104,128]{1,0:T(8,128)S(1)}, u32[]{:S(2)}, u32[]{:S(2)}) collective-permute-start(f32[104,128]{1,0:T(8,128)S(1)} %add_add_fusion.r2), channel_id=1, source_target_pairs={{8,1},{10,3},{12,5},{14,7},{1,8},{3,10},{5,12},{7,14},{0,4},{2,6},... | collective-permute-start | bytes 159752 | tf_op jit(solution)/shard_map/ppermute | solution.py:601
  48.6 0.0 collective-permute-done.14.r1
  48.6 4.8 %collective-permute-done.16.r3 = f32[104,128]{1,0:T(8,128)S(1)} collective-permute-done((f32[104,128]{1,0:T(8,128)S(1)}, f32[104,128]{1,0:T(8,128)S(1)}, u32[]{:S(2)}, u32[]{:S(2)}) %collective-permute-start.16) | collective-permute-done | bytes 53280 | tf_op jit(solution)/shard_map/ppermute | solution.py:601
  53.4 0.0 collective-permute-done.17.r4
  53.4 0.7 %final.1 = (f32[32,384]{1,0:T(8,128)}, f32[12,2,32]{2,1,0:T(2,128)}) custom-call(f32[104,128]{1,0:T(8,128)S(1)} %query_zero.1.r0, f32[104,128]{1,0:T(8,128)S(1)} %collective-permute-done.14.r1, f32[104,128]{1,0:T(8,128)S(1)} %add_add_fusion.r2, f32[104,128]{1,0:T(8,128)S(1)} %collective-permute-done.16.r3, f32[104,128]{1,0:T(8,128)S(1)} %collective-permute-done.17.r4, ...), custom_call_target="tpu_custom_call" | custom-call | flops 1000000000 | bytes 3000000 | tf_op jit(solution)/shard_map/final/pallas_call | solution.py:527
  (4 shorter events, 0.0 us)
Async XLA Ops:
  1.6 9.7 %collective-permute-start.1 = (f32[32,896]{1,0:T(8,128)S(1)}, f32[32,896]{1,0:T(8,128)S(1)}, u32[]{:S(2)}, u32[]{:S(2)}) collective-permute-start(f32[32,896]{1,0:T(8,128)S(1)} %pack.1.pack_ref.own_ref), channel_id=1, source_target_pairs={{0,4},{2,6},{4,0},{6,2},{1,8},{3,10},{5,12},{7,14},{9,13},{11,15},... | collective-permute-start | bytes 344072 | tf_op jit(solution)/shard_map/ppermute | solution.py:576
  4.7 6.7 %collective-permute-start.2 = (f32[32,896]{1,0:T(8,128)S(1)}, f32[32,896]{1,0:T(8,128)S(1)}, u32[]{:S(2)}, u32[]{:S(2)}) collective-permute-start(f32[32,896]{1,0:T(8,128)S(1)} %pack.1.pack_ref.own_ref), channel_id=1, source_target_pairs={{0,12},{2,14},{4,8},{6,10},{9,5},{11,7},{13,1},{15,3},{1,0},{3,2},... | collective-permute-start | bytes 344072 | tf_op jit(solution)/shard_map/ppermute | solution.py:577
  8.0 4.0 %collective-permute-start = (f32[32,896]{1,0:T(8,128)S(1)}, f32[32,896]{1,0:T(8,128)S(1)}, u32[]{:S(2)}, u32[]{:S(2)}) collective-permute-start(f32[32,896]{1,0:T(8,128)S(1)} %pack.1.pack_ref.own_ref), channel_id=1, source_target_pairs={{0,2},{2,0},{4,6},{6,4},{8,10},{10,8},{12,14},{14,12},{1,3},{3,1},... | collective-permute-start | bytes 344072 | tf_op jit(solution)/shard_map/ppermute | solution.py:575
  8.0 5.3 %copy-start.3 = (bf16[2,12,32,128]{3,2,1,0:T(8,128)(2,1)S(1)}, bf16[2,12,32,128]{3,2,1,0:T(8,128)(2,1)}, u32[]{:S(2)}) copy-start(bf16[2,12,32,128]{3,2,1,0:T(8,128)(2,1)} %param.18) | copy-start | bytes 589828
  8.0 5.3 %copy-start.4 = (s32[16,16]{1,0:T(8,128)S(1)}, s32[16,16]{1,0:T(8,128)}, u32[]{:S(2)}) copy-start(s32[16,16]{1,0:T(8,128)} %links_ref.1) | copy-start | bytes 3076
  11.4 1.5 %collective-permute-start.3 = (f32[32,896]{1,0:T(8,128)S(1)}, f32[32,896]{1,0:T(8,128)S(1)}, u32[]{:S(2)}, u32[]{:S(2)}) collective-permute-start(f32[32,896]{1,0:T(8,128)S(1)} %collective-permute-done.1.p1_ref), channel_id=1, source_target_pairs={{0,2},{2,0},{4,6},{6,4},{8,10},{10,8},{12,14},{14,12},{1,3},{3,1},... | collective-permute-start | bytes 344072 | tf_op jit(solution)/shard_map/ppermute | solution.py:628
  11.9 1.3 %collective-permute-start.4 = (f32[32,896]{1,0:T(8,128)S(1)}, f32[32,896]{1,0:T(8,128)S(1)}, u32[]{:S(2)}, u32[]{:S(2)}) collective-permute-start(f32[32,896]{1,0:T(8,128)S(1)} %collective-permute-done.2.p2_ref), channel_id=1, source_target_pairs={{0,2},{2,0},{4,6},{6,4},{8,10},{10,8},{12,14},{14,12},{1,3},{3,1},... | collective-permute-start | bytes 344072 | tf_op jit(solution)/shard_map/ppermute | solution.py:628
  13.3 3.6 %copy-start.1 = (bf16[32,128,128]{2,1,0:T(8,128)(2,1)S(1)}, bf16[32,128,128]{2,1,0:T(8,128)(2,1)}, u32[]{:S(2)}) copy-start(bf16[32,128,128]{2,1,0:T(8,128)(2,1)} %pair_ref.3) | copy-start | bytes 3145732
  14.5 4.6 %collective-permute-start.5 = (f32[32,384]{1,0:T(8,128)S(1)}, f32[32,384]{1,0:T(8,128)S(1)}, u32[]{:S(2)}, u32[]{:S(2)}) collective-permute-start(f32[32,384]{1,0:T(8,128)S(1)} %get-tuple-element.70.e_mine), channel_id=1, source_target_pairs={{0,1},{1,0},{2,3},{3,2},{4,5},{5,4},{6,7},{7,6},{8,9},{9,8},{10,11... | collective-permute-start | bytes 147464 | tf_op jit(solution)/shard_map/ppermute | solution.py:588
  18.2 6.3 %collective-permute-start.7 = (f32[32,1152]{1,0:T(8,128)S(1)}, f32[32,1152]{1,0:T(8,128)S(1)}, u32[]{:S(2)}, u32[]{:S(2)}) collective-permute-start(f32[32,1152]{1,0:T(8,128)S(1)} %get-tuple-element.90.e_mine), channel_id=1, source_target_pairs={{0,1},{1,0},{2,3},{3,2},{4,5},{5,4},{6,7},{7,6},{8,9},{9,8},{10,11... | collective-permute-start | bytes 442376 | tf_op jit(solution)/shard_map/ppermute | solution.py:588
  21.2 13.5 %copy-start = (bf16[2112,384]{1,0:T(8,128)(2,1)S(1)}, bf16[2112,384]{1,0:T(8,128)(2,1)}, u32[]{:S(2)}) copy-start(bf16[2112,384]{1,0:T(8,128)(2,1)} %w_out_ref.1) | copy-start | bytes 4866052
  21.2 13.4 %copy-start.2 = (f32[32,384]{1,0:T(8,128)S(1)}, f32[32,384]{1,0:T(8,128)}, u32[]{:S(2)}) copy-start(f32[32,384]{1,0:T(8,128)} %cot_ref.1) | copy-start | bytes 147460
  21.3 3.2 %collective-permute-start.6 = (f32[64,384]{1,0:T(8,128)S(1)}, f32[64,384]{1,0:T(8,128)S(1)}, u32[]{:S(2)}, u32[]{:S(2)}) collective-permute-start(f32[64,384]{1,0:T(8,128)S(1)} %get-tuple-element.78), channel_id=1, source_target_pairs={{0,2},{2,0},{4,6},{6,4},{8,10},{10,8},{12,14},{14,12},{1,3},{3,1},... | collective-permute-start | bytes 294920 | tf_op jit(solution)/shard_map/ppermute | solution.py:593
  21.3 6.0 %collective-permute-start.10 = (f32[32,1024]{1,0:T(8,128)S(1)}, f32[32,1024]{1,0:T(8,128)S(1)}, u32[]{:S(2)}, u32[]{:S(2)}) collective-permute-start(f32[32,1024]{1,0:T(8,128)S(1)} %get-tuple-element.88.tail_mine), channel_id=1, source_target_pairs={{0,1},{1,0},{2,3},{3,2},{4,5},{5,4},{6,7},{7,6},{8,9},{9,8},{10,11... | collective-permute-start | bytes 393224 | tf_op jit(solution)/shard_map/ppermute | solution.py:588
  24.5 4.2 %collective-permute-start.9 = (f32[32,384]{1,0:T(8,128)S(1)}, f32[32,384]{1,0:T(8,128)S(1)}, u32[]{:S(2)}, u32[]{:S(2)}) collective-permute-start(f32[32,384]{1,0:T(8,128)S(1)} %slice_add_fusion.1), channel_id=1, source_target_pairs={{0,4},{2,6},{4,0},{6,2},{8,12},{10,14},{12,8},{14,10},{1,5},{3,7},... | collective-permute-start | bytes 147464 | tf_op jit(solution)/shard_map/ppermute | solution.py:598
  26.3 5.2 %collective-permute-start.8 = (f32[32,384]{1,0:T(8,128)S(1)}, f32[32,384]{1,0:T(8,128)S(1)}, u32[]{:S(2)}, u32[]{:S(2)}) collective-permute-start(f32[32,384]{1,0:T(8,128)S(1)} %get-tuple-element.84.r0), channel_id=1, source_target_pairs={{0,1},{1,0},{2,3},{3,2},{4,5},{5,4},{6,7},{7,6},{8,9},{9,8},{10,11... | collective-permute-start | bytes 147464 | tf_op jit(solution)/shard_map/ppermute | solution.py:596
  28.7 5.6 %collective-permute-start.11 = (f32[32,384]{1,0:T(8,128)S(1)}, f32[32,384]{1,0:T(8,128)S(1)}, u32[]{:S(2)}, u32[]{:S(2)}) collective-permute-start(f32[32,384]{1,0:T(8,128)S(1)} %add_add_fusion.1.r2), channel_id=1, source_target_pairs={{0,1},{2,3},{4,5},{6,7},{8,0},{10,2},{12,4},{14,6},{9,8},{11,10},{... | collective-permute-start | bytes 147464 | tf_op jit(solution)/shard_map/ppermute | solution.py:601
  29.3 5.3 %collective-permute-start.12 = (f32[32,384]{1,0:T(8,128)S(1)}, f32[32,384]{1,0:T(8,128)S(1)}, u32[]{:S(2)}, u32[]{:S(2)}) collective-permute-start(f32[32,384]{1,0:T(8,128)S(1)} %add_add_fusion.1.r2), channel_id=1, source_target_pairs={{8,1},{10,3},{12,5},{14,7},{1,8},{3,10},{5,12},{7,14},{0,4},{2,6},... | collective-permute-start | bytes 147464 | tf_op jit(solution)/shard_map/ppermute | solution.py:601
  38.5 1.4 %collective-permute-start.13 = (f32[208,128]{1,0:T(8,128)S(1)}, f32[208,128]{1,0:T(8,128)S(1)}, u32[]{:S(2)}, u32[]{:S(2)}) collective-permute-start(f32[208,128]{1,0:T(8,128)S(1)} %get-tuple-element.96), channel_id=1, source_target_pairs={{0,2},{2,0},{4,6},{6,4},{8,10},{10,8},{12,14},{14,12},{1,3},{3,1},... | collective-permute-start | bytes 319496 | tf_op jit(solution)/shard_map/ppermute | solution.py:593
  38.6 2.7 %copy-start.5 = (bf16[128,12]{0,1:T(8,128)(2,1)S(1)}, bf16[128,12]{0,1:T(8,128)(2,1)}, u32[]{:S(2)}) copy-start(bf16[128,12]{0,1:T(8,128)(2,1)} %param.29) | copy-start | bytes 9220
  39.9 6.4 %collective-permute-start.15 = (f32[104,128]{1,0:T(8,128)S(1)}, f32[104,128]{1,0:T(8,128)S(1)}, u32[]{:S(2)}, u32[]{:S(2)}) collective-permute-start(f32[104,128]{1,0:T(8,128)S(1)} %slice_add_fusion), channel_id=1, source_target_pairs={{0,4},{2,6},{4,0},{6,2},{8,12},{10,14},{12,8},{14,10},{1,5},{3,7},... | collective-permute-start | bytes 159752 | tf_op jit(solution)/shard_map/ppermute | solution.py:598
  43.2 5.4 %collective-permute-start.14 = (f32[104,128]{1,0:T(8,128)S(1)}, f32[104,128]{1,0:T(8,128)S(1)}, u32[]{:S(2)}, u32[]{:S(2)}) collective-permute-start(f32[104,128]{1,0:T(8,128)S(1)} %query_zero.1.r0), channel_id=1, source_target_pairs={{0,1},{1,0},{2,3},{3,2},{4,5},{5,4},{6,7},{7,6},{8,9},{9,8},{10,11... | collective-permute-start | bytes 159752 | tf_op jit(solution)/shard_map/ppermute | solution.py:596
  46.4 7.0 %collective-permute-start.16 = (f32[104,128]{1,0:T(8,128)S(1)}, f32[104,128]{1,0:T(8,128)S(1)}, u32[]{:S(2)}, u32[]{:S(2)}) collective-permute-start(f32[104,128]{1,0:T(8,128)S(1)} %add_add_fusion.r2), channel_id=1, source_target_pairs={{0,1},{2,3},{4,5},{6,7},{8,0},{10,2},{12,4},{14,6},{9,8},{11,10},{... | collective-permute-start | bytes 159752 | tf_op jit(solution)/shard_map/ppermute | solution.py:601
  46.9 6.5 %collective-permute-start.17 = (f32[104,128]{1,0:T(8,128)S(1)}, f32[104,128]{1,0:T(8,128)S(1)}, u32[]{:S(2)}, u32[]{:S(2)}) collective-permute-start(f32[104,128]{1,0:T(8,128)S(1)} %add_add_fusion.r2), channel_id=1, source_target_pairs={{8,1},{10,3},{12,5},{14,7},{1,8},{3,10},{5,12},{7,14},{0,4},{2,6},... | collective-permute-start | bytes 159752 | tf_op jit(solution)/shard_map/ppermute | solution.py:601

commit v6 on v5

--- a/solution.py
+++ b/solution.py
@@ -588,19 +588,23 @@
             return lax.ppermute(x, "col", COL_SWAP)
         return lax.psum(x, "col") - x
 
-    def reduce(mine_a, mine_b, theirs, late, first_beside, beside):
+    def reduce(mine_a, mine_b, theirs, soon, late, first_beside, beside):
         if fast:
             got = lax.ppermute(theirs, "row", CORE_SWAP)
-            query, *rest = late()
-            got, query, first_beside = lax.optimization_barrier((got, query, first_beside))
+            if soon:
+                query, *rest = late(())
+                got, query = lax.optimization_barrier((got, query))
+            else:
+                got, first_beside = lax.optimization_barrier((got, first_beside))
+                query, *rest = late(got)
             query_other = lax.ppermute(query, "col", COL_SWAP)
             count = mine_a.shape[0]
             half = lax.ppermute(mine_b + got[count:], "row", Z_SWAP)
-            half, beside = lax.optimization_barrier((half, beside))
+            half, beside, query = lax.optimization_barrier((half, beside, query))
             part = mine_a + got[:count] + half
             sent = [lax.ppermute(part, BOTH, SEND_ONE), lax.ppermute(part, BOTH, SEND_TWO)]
             return [query, query_other, part] + sent, rest, (first_beside, beside)
-        query, *rest = late()
+        query, *rest = late(())
         count = mine_a.shape[0]
         parts = jnp.concatenate([mine_a, theirs[:count], mine_b, theirs[count:]], axis=0)
         summed = lax.all_gather(lax.psum(parts, "row"), "col", axis=0, tiled=True)
@@ -651,11 +655,11 @@
         6.0,
     )
     pieces, (frq, frk), (e0_other, tail_other) = reduce(
-        mine_a, mine_b, theirs,
-        lambda: call(
+        mine_a, mine_b, theirs, False,
+        lambda after: call(
             functools.partial(query_one_body, share), "query_one", [VMEM] * 8,
             [((rows, C), F32), ((rows, 128), F32), ((keys, 128), F32)],
-            (z1, kv1, own, q1, pts, grads, wq, sc),
+            (z1, kv1, own, q1, lax.optimization_barrier((pts, after))[0], grads, wq, sc),
             (),
             0.01,
         ),
@@ -674,8 +678,8 @@
         pair_body, "pair_grad", [VMEM] * 5, [((rows, keys, CZ), BF16)], (z1, z0, pu1, pu0, w_bias.T)
     )
     pieces, _, (_, d_pair) = reduce(
-        mine_a, mine_b, theirs,
-        lambda: call(
+        mine_a, mine_b, theirs, True,
+        lambda after: call(
             functools.partial(query_zero_body, share), "query_zero", [VMEM] * 8, [((long, 128), F32)],
             (z0, kv0, own, q0, pts, wq, sc, frq),
         ),

time: 54.3 us -> 53.8 us (level)
  waiting for transfers between devices: 12.4 us -> 11.1 us
  starting transfers between devices: 23.1 us -> 23.9 us
    ppermute x2, waiting for transfers between devices: 1.34 us -> 0.62 us  [reduce(): half = lax.ppermute(mine_b + got[count:], 'row', Z_SWAP)]
    ppermute x2, waiting for transfers between devices: 7.53 us -> 6.84 us  [reduce(): lax.ppermute(part, BOTH, SEND_ONE)]
where the time goes in v6:
time: 53.8 us; the launch traced here: 53.6 us
  starting transfers between devices  23.9 us (44%)
  Pallas kernels  17.7 us (33%)
  waiting for transfers between devices  11.1 us (21%)
  between operations  0.77 us (1%)
    pallas_call x10, Pallas kernels, call(): pl.pallas_call(body, name=name, in_specs=in_specs, out_specs=tuple((VMEM...  17.7 us
    ppermute x2, waiting for transfers between devices, reduce(): lax.ppermute(part, BOTH, SEND_ONE)  6.84 us
    ppermute x3, starting transfers between devices, col_other(): return lax.ppermute(x, 'col', COL_SWAP)  4.32 us
    ppermute x2, starting transfers between devices, reduce(): lax.ppermute(part, BOTH, SEND_TWO)  3.92 us
    ppermute x2, starting transfers between devices, reduce(): query_other = lax.ppermute(query, 'col', COL_SWAP)  3.48 us
    ppermute x2, starting transfers between devices, reduce(): half = lax.ppermute(mine_b + got[count:], 'row', Z_SWAP)  3.34 us
    ppermute x1, starting transfers between devices, local(): two = lax.ppermute(pack, BOTH, FETCH_TWO)  3.29 us
    ppermute x1, starting transfers between devices, local(): one = lax.ppermute(pack, BOTH, FETCH_ONE)  3.09 us
  transfers between devices with their start and end apart: 18, of which 9 were waited for; matrix products, arithmetic and copies ran while one was open for 0% of the time, Pallas kernels for 20%

profile of v6, /device:TPU:0, one launch (start us, length us, event | category | flops | bytes accessed | tf_op | source)
XLA Modules:
  0.0 53.6 jit_solution(15404389170882394896)
XLA Ops:
  0.6 1.0 %pack.1.pack_ref.own_ref = f32[32,896]{1,0:T(8,128)S(1)} custom-call(f32[2,32,384]{2,1,0:T(8,128)} %single_hbm.1, f32[12,2,32]{2,1,0:T(2,128)} %bitcast.21, s32[1,32]{1,0:T(1,128)} %bitcast.22), custom_call_target="tpu_custom_call" | custom-call | flops 1000000000 | bytes 3000000 | tf_op jit(solution)/shard_map/pack/pallas_call | solution.py:527
  1.6 3.1 %collective-permute-start.1 = (f32[32,896]{1,0:T(8,128)S(1)}, f32[32,896]{1,0:T(8,128)S(1)}, u32[]{:S(2)}, u32[]{:S(2)}) collective-permute-start(f32[32,896]{1,0:T(8,128)S(1)} %pack.1.pack_ref.own_ref), channel_id=1, source_target_pairs={{0,4},{2,6},{4,0},{6,2},{1,8},{3,10},{5,12},{7,14},{9,13},{11,15},... | collective-permute-start | bytes 344072 | tf_op jit(solution)/shard_map/ppermute | solution.py:576
  4.7 3.3 %collective-permute-start.2 = (f32[32,896]{1,0:T(8,128)S(1)}, f32[32,896]{1,0:T(8,128)S(1)}, u32[]{:S(2)}, u32[]{:S(2)}) collective-permute-start(f32[32,896]{1,0:T(8,128)S(1)} %pack.1.pack_ref.own_ref), channel_id=1, source_target_pairs={{0,12},{2,14},{4,8},{6,10},{9,5},{11,7},{13,1},{15,3},{1,0},{3,2},... | collective-permute-start | bytes 344072 | tf_op jit(solution)/shard_map/ppermute | solution.py:577
  8.0 0.0 collective-permute-start
  8.0 0.0 copy-start.3
  8.0 0.0 copy-start.4
  8.0 3.3 %prep.1 = (bf16[1280,384]{1,0:T(8,128)(2,1)S(1)}, bf16[640,384]{1,0:T(8,128)(2,1)S(1)}, f32[32,768]{1,0:T(8,128)S(1)}, f32[32,1024]{1,0:T(8,128)S(1)}, f32[32,10...) custom-call(f32[32,896]{1,0:T(8,128)S(1)} %pack.1.pack_ref.own_ref, ...), custom_call_target="tpu_custom_call" | custom-call | flops 1000000000 | bytes 3000000 | tf_op jit(solution)/shard_map/prep/pallas_call | solution.py:527
  11.3 0.0 collective-permute-done.1.p1_ref
  11.4 0.0 collective-permute-done.2.p2_ref
  11.4 0.6 %collective-permute-start.3 = (f32[32,896]{1,0:T(8,128)S(1)}, f32[32,896]{1,0:T(8,128)S(1)}, u32[]{:S(2)}, u32[]{:S(2)}) collective-permute-start(f32[32,896]{1,0:T(8,128)S(1)} %collective-permute-done.1.p1_ref), channel_id=1, source_target_pairs={{0,2},{2,0},{4,6},{6,4},{8,10},{10,8},{12,14},{14,12},{1,3},{3,1},... | collective-permute-start | bytes 344072 | tf_op jit(solution)/shard_map/ppermute | solution.py:632
  11.9 0.1 collective-permute-start.4
  12.0 0.0 collective-permute-done.ownx_ref
  12.0 0.9 %collective-permute-done.3.p1x_ref = f32[32,896]{1,0:T(8,128)S(1)} collective-permute-done((f32[32,896]{1,0:T(8,128)S(1)}, f32[32,896]{1,0:T(8,128)S(1)}, u32[]{:S(2)}, u32[]{:S(2)}) %collective-permute-start.3) | collective-permute-done | bytes 114720 | tf_op jit(solution)/shard_map/ppermute | solution.py:632
  12.9 0.4 collective-permute-done.4.p2x_ref
  13.3 0.0 copy-done.3
  13.3 0.0 copy-done.4
  13.3 0.0 copy-start.1
  13.3 1.2 %first.1 = (f32[128,896]{1,0:T(8,128)S(1)}, f32[128,2048]{1,0:T(8,128)S(1)}, bf16[2,384,128]{2,1,0:T(8,128)(2,1)S(1)}, f32[32,384]{1,0:T(8,128)S(1)}) custom-call(f32[32,896]{1,0:T(8,128)S(1)} %pack.1.pack_ref.own_ref, f32[32,896]{1,0:T(8,128)S(1)} %collective-permute-done.ownx_ref, f32[32,896]{1,0:T(8,128)S(1)} %collective-permute-done.1.p1_ref, ...), custom_call_target="tpu_custom_call" | custom-call | flops 1000000000 | bytes 3000000 | tf_op jit(solution)/shard_map/first/pallas_call | solution.py:527
  14.5 2.3 %collective-permute-start.5 = (f32[32,384]{1,0:T(8,128)S(1)}, f32[32,384]{1,0:T(8,128)S(1)}, u32[]{:S(2)}, u32[]{:S(2)}) collective-permute-start(f32[32,384]{1,0:T(8,128)S(1)} %get-tuple-element.72.e_mine), channel_id=1, source_target_pairs={{0,1},{1,0},{2,3},{3,2},{4,5},{5,4},{6,7},{7,6},{8,9},{9,8},{10,11... | collective-permute-start | bytes 147464 | tf_op jit(solution)/shard_map/ppermute | solution.py:588
  16.9 0.0 copy-done.1
  16.9 1.3 %second.1 = (f32[128,2048]{1,0:T(8,128)S(1)}, f32[32,1152]{1,0:T(8,128)S(1)}, f32[32,1024]{1,0:T(8,128)S(1)}) custom-call(f32[128,896]{1,0:T(8,128)S(1)} %get-tuple-element.73.keys_ref, bf16[1280,384]{1,0:T(8,128)(2,1)S(1)} %get-tuple-element.69.wk_ref, bf16[2,384,128]{2,1,0:T(8,128)(2,1)S(1)} %get-tuple-element.74.pm_ref, bf16[32,128,128]{2,1,0:T(8,128)(2,1)S(1)} %copy-done.1), custom_call_target="tpu_custom_call" | custom-call | flops 1000000000 | bytes 3000000 | tf_op jit(solution)/shard_map/second/pallas_call | solution.py:527
  18.2 0.1 collective-permute-start.7
  18.3 0.8 %collective-permute-done.5.e_other = f32[32,384]{1,0:T(8,128)S(1)} collective-permute-done((f32[32,384]{1,0:T(8,128)S(1)}, f32[32,384]{1,0:T(8,128)S(1)}, u32[]{:S(2)}, u32[]{:S(2)}) %collective-permute-start.5) | collective-permute-done | bytes 49184 | tf_op jit(solution)/shard_map/ppermute | solution.py:588
  19.1 2.1 %back_one.1 = (f32[768,128]{1,0:T(8,128)S(1)}, f32[32,384]{1,0:T(8,128)S(1)}, f32[32,384]{1,0:T(8,128)S(1)}, f32[64,384]{1,0:T(8,128)S(1)}, f32[32,1152]{1,0:T(8,128)S(1)}, /*index=5*/f32[128,768]{1,0:T(8,128)S(1)}) custom-call(f32[32,384]{1,0:T(8,128)S(1)} %get-tuple-element.72.e_mine, f32[32,384]{1,0:T(8,128)S(1)} %collective-permute-done.5.e_other, ...), custom_call_target="tpu_custom_call" | custom-call | flops 6000000000 | bytes 18000000 | tf_op jit(solution)/shard_map/back_one/pallas_call | solution.py:527
  21.2 0.0 copy-start
  21.2 0.0 copy-start.2
  21.3 0.1 collective-permute-start.6
  21.3 1.9 %collective-permute-start.9 = (f32[32,1024]{1,0:T(8,128)S(1)}, f32[32,1024]{1,0:T(8,128)S(1)}, u32[]{:S(2)}, u32[]{:S(2)}) collective-permute-start(f32[32,1024]{1,0:T(8,128)S(1)} %get-tuple-element.83.tail_mine), channel_id=1, source_target_pairs={{0,1},{1,0},{2,3},{3,2},{4,5},{5,4},{6,7},{7,6},{8,9},{9,8},{10,11... | collective-permute-start | bytes 393224 | tf_op jit(solution)/shard_map/ppermute | solution.py:588
  23.2 0.0 collective-permute-done.6
  23.2 0.8 %collective-permute-done.7.e_other = f32[32,1152]{1,0:T(8,128)S(1)} collective-permute-done((f32[32,1152]{1,0:T(8,128)S(1)}, f32[32,1152]{1,0:T(8,128)S(1)}, u32[]{:S(2)}, u32[]{:S(2)}) %collective-permute-start.7) | collective-permute-done | bytes 147488 | tf_op jit(solution)/shard_map/ppermute | solution.py:588
  24.1 1.8 %collective-permute-start.8 = (f32[32,384]{1,0:T(8,128)S(1)}, f32[32,384]{1,0:T(8,128)S(1)}, u32[]{:S(2)}, u32[]{:S(2)}) collective-permute-start(f32[32,384]{1,0:T(8,128)S(1)} %slice_add_fusion.1), channel_id=1, source_target_pairs={{0,4},{2,6},{4,0},{6,2},{8,12},{10,14},{12,8},{14,10},{1,5},{3,7},... | collective-permute-start | bytes 147464 | tf_op jit(solution)/shard_map/ppermute | solution.py:602
  25.9 1.2 %query_one.1 = (f32[32,384]{1,0:T(8,128)S(1)}, f32[32,128]{1,0:T(8,128)S(1)}, f32[128,128]{1,0:T(8,128)S(1)}) custom-call(f32[768,128]{1,0:T(8,128)S(1)} %get-tuple-element.84.z_ref.z1_ref, f32[128,2048]{1,0:T(8,128)S(1)} %get-tuple-element.77.kv_ref, f32[32,896]{1,0:T(8,128)S(1)} %pack.1.pack_ref.own_ref, f32[32,1024]{1,0:T(8,128)S(1)} %get-tuple-element.78.q_ref, ...), custom_call_target="tpu_custom_call" | custom-call | flops 10000000 | bytes 30000 | tf_op jit(solution)/shard_map/query_one/pallas_call | solution.py:527
  27.2 0.5 collective-permute-start.10
  27.6 0.0 collective-permute-done.9.tail_other
  27.6 0.6 %collective-permute-done.8 = f32[32,384]{1,0:T(8,128)S(1)} collective-permute-done((f32[32,384]{1,0:T(8,128)S(1)}, f32[32,384]{1,0:T(8,128)S(1)}, u32[]{:S(2)}, u32[]{:S(2)}) %collective-permute-start.8) | collective-permute-done | bytes 49184 | tf_op jit(solution)/shard_map/ppermute | solution.py:602
  28.2 1.3 %collective-permute-start.11 = (f32[32,384]{1,0:T(8,128)S(1)}, f32[32,384]{1,0:T(8,128)S(1)}, u32[]{:S(2)}, u32[]{:S(2)}) collective-permute-start(f32[32,384]{1,0:T(8,128)S(1)} %add_add_fusion.1.r2), channel_id=1, source_target_pairs={{0,1},{2,3},{4,5},{6,7},{8,0},{10,2},{12,4},{14,6},{9,8},{11,10},{... | collective-permute-start | bytes 147464 | tf_op jit(solution)/shard_map/ppermute | solution.py:605
  29.5 2.1 %collective-permute-start.12 = (f32[32,384]{1,0:T(8,128)S(1)}, f32[32,384]{1,0:T(8,128)S(1)}, u32[]{:S(2)}, u32[]{:S(2)}) collective-permute-start(f32[32,384]{1,0:T(8,128)S(1)} %add_add_fusion.1.r2), channel_id=1, source_target_pairs={{8,1},{10,3},{12,5},{14,7},{1,8},{3,10},{5,12},{7,14},{0,4},{2,6},... | collective-permute-start | bytes 147464 | tf_op jit(solution)/shard_map/ppermute | solution.py:605
  31.6 0.0 collective-permute-done.10.r1
  31.6 2.2 %collective-permute-done.11.r3 = f32[32,384]{1,0:T(8,128)S(1)} collective-permute-done((f32[32,384]{1,0:T(8,128)S(1)}, f32[32,384]{1,0:T(8,128)S(1)}, u32[]{:S(2)}, u32[]{:S(2)}) %collective-permute-start.11) | collective-permute-done | bytes 49184 | tf_op jit(solution)/shard_map/ppermute | solution.py:605
  33.7 0.5 collective-permute-done.12.r4
  34.2 0.0 copy-done
  34.2 0.0 copy-done.2
  34.2 3.8 %back_zero.1 = (f32[768,128]{1,0:T(8,128)S(1)}, f32[104,128]{1,0:T(8,128)S(1)}, f32[104,128]{1,0:T(8,128)S(1)}, f32[208,128]{1,0:T(8,128)S(1)}, f32[32,1152]{1,0...) custom-call(f32[32,384]{1,0:T(8,128)S(1)} %copy-done.2, f32[32,384]{1,0:T(8,128)S(1)} %get-tuple-element.90.r0, ...), custom_call_target="tpu_custom_call" | custom-call | flops 1000000000 | bytes 3000000 | tf_op jit(solution)/shard_map/back_zero/pallas_call | solution.py:527
  38.1 0.1 collective-permute-start.13
  38.1 0.0 copy-start.5
  38.2 1.0 %query_zero.1.r0 = f32[104,128]{1,0:T(8,128)S(1)} custom-call(f32[768,128]{1,0:T(8,128)S(1)} %get-tuple-element.101.z_ref.z0_ref, f32[128,2048]{1,0:T(8,128)S(1)} %get-tuple-element.96.kv_ref, f32[32,896]{1,0:T(8,128)S(1)} %pack.1.pack_ref.own_ref, f32[32,1024]{1,0:T(8,128)S(1)} %get-tuple-element.97.q_ref, f32[32,1152]{1,0:T(8,128)S(1)} %get-tuple-element.102.pts_ref, ...), custom_call_target="tpu_custom_call" | custom-call | flops 1000000000 | bytes 3000000 | tf_op jit(solution)/shard_map/query_zero/pallas_call | solution.py:527
  39.2 0.3 collective-permute-done.13
  39.5 1.5 %collective-permute-start.14 = (f32[104,128]{1,0:T(8,128)S(1)}, f32[104,128]{1,0:T(8,128)S(1)}, u32[]{:S(2)}, u32[]{:S(2)}) collective-permute-start(f32[104,128]{1,0:T(8,128)S(1)} %slice_add_fusion), channel_id=1, source_target_pairs={{0,4},{2,6},{4,0},{6,2},{8,12},{10,14},{12,8},{14,10},{1,5},{3,7},... | collective-permute-start | bytes 159752 | tf_op jit(solution)/shard_map/ppermute | solution.py:602
  41.0 0.0 copy-done.5
  41.0 1.9 %pair_grad.1 = bf16[32,128,128]{2,1,0:T(8,128)(2,1)} custom-call(f32[768,128]{1,0:T(8,128)S(1)} %get-tuple-element.84.z_ref.z1_ref, f32[768,128]{1,0:T(8,128)S(1)} %get-tuple-element.101.z_ref.z0_ref, f32[384,128]{1,0:T(8,128)S(1)} %get-tuple-element.105.pu1_ref, f32[384,128]{1,0:T(8,128)S(1)} %get-tuple-element.106.pu0_ref, bf16[12,128]{1,0:T(8,128)(2,1)S(1)} %bitcast.13), custom_call_target="tpu_custom_call" | custom-call | flops 1000000000 | bytes 3000000 | tf_op jit(solution)/shard_map/pair_grad/pallas_call | solution.py:527
  42.9 3.0 %collective-permute-start.15 = (f32[104,128]{1,0:T(8,128)S(1)}, f32[104,128]{1,0:T(8,128)S(1)}, u32[]{:S(2)}, u32[]{:S(2)}) collective-permute-start(f32[104,128]{1,0:T(8,128)S(1)} %query_zero.1.r0), channel_id=1, source_target_pairs={{0,1},{1,0},{2,3},{3,2},{4,5},{5,4},{6,7},{7,6},{8,9},{9,8},{10,11... | collective-permute-start | bytes 159752 | tf_op jit(solution)/shard_map/ppermute | solution.py:600
  45.9 0.0 collective-permute-done.14
  45.9 0.4 collective-permute-start.16
  46.3 1.9 %collective-permute-start.17 = (f32[104,128]{1,0:T(8,128)S(1)}, f32[104,128]{1,0:T(8,128)S(1)}, u32[]{:S(2)}, u32[]{:S(2)}) collective-permute-start(f32[104,128]{1,0:T(8,128)S(1)} %add_add_fusion.r2), channel_id=1, source_target_pairs={{8,1},{10,3},{12,5},{14,7},{1,8},{3,10},{5,12},{7,14},{0,4},{2,6},... | collective-permute-start | bytes 159752 | tf_op jit(solution)/shard_map/ppermute | solution.py:605
  48.2 0.0 collective-permute-done.15.r1
  48.2 4.7 %collective-permute-done.16.r3 = f32[104,128]{1,0:T(8,128)S(1)} collective-permute-done((f32[104,128]{1,0:T(8,128)S(1)}, f32[104,128]{1,0:T(8,128)S(1)}, u32[]{:S(2)}, u32[]{:S(2)}) %collective-permute-start.16) | collective-permute-done | bytes 53280 | tf_op jit(solution)/shard_map/ppermute | solution.py:605
  52.8 0.0 collective-permute-done.17.r4
  52.8 0.7 %final.1 = (f32[32,384]{1,0:T(8,128)}, f32[12,2,32]{2,1,0:T(2,128)}) custom-call(f32[104,128]{1,0:T(8,128)S(1)} %query_zero.1.r0, f32[104,128]{1,0:T(8,128)S(1)} %collective-permute-done.15.r1, f32[104,128]{1,0:T(8,128)S(1)} %add_add_fusion.r2, f32[104,128]{1,0:T(8,128)S(1)} %collective-permute-done.16.r3, f32[104,128]{1,0:T(8,128)S(1)} %collective-permute-done.17.r4, ...), custom_call_target="tpu_custom_call" | custom-call | flops 1000000000 | bytes 3000000 | tf_op jit(solution)/shard_map/final/pallas_call | solution.py:527
  (4 shorter events, 0.0 us)
Async XLA Ops:
  1.6 9.7 %collective-permute-start.1 = (f32[32,896]{1,0:T(8,128)S(1)}, f32[32,896]{1,0:T(8,128)S(1)}, u32[]{:S(2)}, u32[]{:S(2)}) collective-permute-start(f32[32,896]{1,0:T(8,128)S(1)} %pack.1.pack_ref.own_ref), channel_id=1, source_target_pairs={{0,4},{2,6},{4,0},{6,2},{1,8},{3,10},{5,12},{7,14},{9,13},{11,15},... | collective-permute-start | bytes 344072 | tf_op jit(solution)/shard_map/ppermute | solution.py:576
  4.7 6.7 %collective-permute-start.2 = (f32[32,896]{1,0:T(8,128)S(1)}, f32[32,896]{1,0:T(8,128)S(1)}, u32[]{:S(2)}, u32[]{:S(2)}) collective-permute-start(f32[32,896]{1,0:T(8,128)S(1)} %pack.1.pack_ref.own_ref), channel_id=1, source_target_pairs={{0,12},{2,14},{4,8},{6,10},{9,5},{11,7},{13,1},{15,3},{1,0},{3,2},... | collective-permute-start | bytes 344072 | tf_op jit(solution)/shard_map/ppermute | solution.py:577
  8.0 4.0 %collective-permute-start = (f32[32,896]{1,0:T(8,128)S(1)}, f32[32,896]{1,0:T(8,128)S(1)}, u32[]{:S(2)}, u32[]{:S(2)}) collective-permute-start(f32[32,896]{1,0:T(8,128)S(1)} %pack.1.pack_ref.own_ref), channel_id=1, source_target_pairs={{0,2},{2,0},{4,6},{6,4},{8,10},{10,8},{12,14},{14,12},{1,3},{3,1},... | collective-permute-start | bytes 344072 | tf_op jit(solution)/shard_map/ppermute | solution.py:575
  8.0 5.3 %copy-start.3 = (bf16[2,12,32,128]{3,2,1,0:T(8,128)(2,1)S(1)}, bf16[2,12,32,128]{3,2,1,0:T(8,128)(2,1)}, u32[]{:S(2)}) copy-start(bf16[2,12,32,128]{3,2,1,0:T(8,128)(2,1)} %param.18) | copy-start | bytes 589828
  8.0 5.3 %copy-start.4 = (s32[16,16]{1,0:T(8,128)S(1)}, s32[16,16]{1,0:T(8,128)}, u32[]{:S(2)}) copy-start(s32[16,16]{1,0:T(8,128)} %links_ref.1) | copy-start | bytes 3076
  11.4 1.5 %collective-permute-start.3 = (f32[32,896]{1,0:T(8,128)S(1)}, f32[32,896]{1,0:T(8,128)S(1)}, u32[]{:S(2)}, u32[]{:S(2)}) collective-permute-start(f32[32,896]{1,0:T(8,128)S(1)} %collective-permute-done.1.p1_ref), channel_id=1, source_target_pairs={{0,2},{2,0},{4,6},{6,4},{8,10},{10,8},{12,14},{14,12},{1,3},{3,1},... | collective-permute-start | bytes 344072 | tf_op jit(solution)/shard_map/ppermute | solution.py:632
  11.9 1.3 %collective-permute-start.4 = (f32[32,896]{1,0:T(8,128)S(1)}, f32[32,896]{1,0:T(8,128)S(1)}, u32[]{:S(2)}, u32[]{:S(2)}) collective-permute-start(f32[32,896]{1,0:T(8,128)S(1)} %collective-permute-done.2.p2_ref), channel_id=1, source_target_pairs={{0,2},{2,0},{4,6},{6,4},{8,10},{10,8},{12,14},{14,12},{1,3},{3,1},... | collective-permute-start | bytes 344072 | tf_op jit(solution)/shard_map/ppermute | solution.py:632
  13.3 3.6 %copy-start.1 = (bf16[32,128,128]{2,1,0:T(8,128)(2,1)S(1)}, bf16[32,128,128]{2,1,0:T(8,128)(2,1)}, u32[]{:S(2)}) copy-start(bf16[32,128,128]{2,1,0:T(8,128)(2,1)} %pair_ref.3) | copy-start | bytes 3145732
  14.5 4.6 %collective-permute-start.5 = (f32[32,384]{1,0:T(8,128)S(1)}, f32[32,384]{1,0:T(8,128)S(1)}, u32[]{:S(2)}, u32[]{:S(2)}) collective-permute-start(f32[32,384]{1,0:T(8,128)S(1)} %get-tuple-element.72.e_mine), channel_id=1, source_target_pairs={{0,1},{1,0},{2,3},{3,2},{4,5},{5,4},{6,7},{7,6},{8,9},{9,8},{10,11... | collective-permute-start | bytes 147464 | tf_op jit(solution)/shard_map/ppermute | solution.py:588
  18.2 5.9 %collective-permute-start.7 = (f32[32,1152]{1,0:T(8,128)S(1)}, f32[32,1152]{1,0:T(8,128)S(1)}, u32[]{:S(2)}, u32[]{:S(2)}) collective-permute-start(f32[32,1152]{1,0:T(8,128)S(1)} %get-tuple-element.93.e_mine), channel_id=1, source_target_pairs={{0,1},{1,0},{2,3},{3,2},{4,5},{5,4},{6,7},{7,6},{8,9},{9,8},{10,11... | collective-permute-start | bytes 442376 | tf_op jit(solution)/shard_map/ppermute | solution.py:588
  21.2 13.0 %copy-start = (bf16[2112,384]{1,0:T(8,128)(2,1)S(1)}, bf16[2112,384]{1,0:T(8,128)(2,1)}, u32[]{:S(2)}) copy-start(bf16[2112,384]{1,0:T(8,128)(2,1)} %w_out_ref.1) | copy-start | bytes 4866052
  21.2 13.0 %copy-start.2 = (f32[32,384]{1,0:T(8,128)S(1)}, f32[32,384]{1,0:T(8,128)}, u32[]{:S(2)}) copy-start(f32[32,384]{1,0:T(8,128)} %cot_ref.1) | copy-start | bytes 147460
  21.3 2.0 %collective-permute-start.6 = (f32[64,384]{1,0:T(8,128)S(1)}, f32[64,384]{1,0:T(8,128)S(1)}, u32[]{:S(2)}, u32[]{:S(2)}) collective-permute-start(f32[64,384]{1,0:T(8,128)S(1)} %get-tuple-element.81), channel_id=1, source_target_pairs={{0,2},{2,0},{4,6},{6,4},{8,10},{10,8},{12,14},{14,12},{1,3},{3,1},... | collective-permute-start | bytes 294920 | tf_op jit(solution)/shard_map/ppermute | solution.py:593
  21.3 6.3 %collective-permute-start.9 = (f32[32,1024]{1,0:T(8,128)S(1)}, f32[32,1024]{1,0:T(8,128)S(1)}, u32[]{:S(2)}, u32[]{:S(2)}) collective-permute-start(f32[32,1024]{1,0:T(8,128)S(1)} %get-tuple-element.83.tail_mine), channel_id=1, source_target_pairs={{0,1},{1,0},{2,3},{3,2},{4,5},{5,4},{6,7},{7,6},{8,9},{9,8},{10,11... | collective-permute-start | bytes 393224 | tf_op jit(solution)/shard_map/ppermute | solution.py:588
  24.1 4.2 %collective-permute-start.8 = (f32[32,384]{1,0:T(8,128)S(1)}, f32[32,384]{1,0:T(8,128)S(1)}, u32[]{:S(2)}, u32[]{:S(2)}) collective-permute-start(f32[32,384]{1,0:T(8,128)S(1)} %slice_add_fusion.1), channel_id=1, source_target_pairs={{0,4},{2,6},{4,0},{6,2},{8,12},{10,14},{12,8},{14,10},{1,5},{3,7},... | collective-permute-start | bytes 147464 | tf_op jit(solution)/shard_map/ppermute | solution.py:602
  27.2 4.4 %collective-permute-start.10 = (f32[32,384]{1,0:T(8,128)S(1)}, f32[32,384]{1,0:T(8,128)S(1)}, u32[]{:S(2)}, u32[]{:S(2)}) collective-permute-start(f32[32,384]{1,0:T(8,128)S(1)} %get-tuple-element.90.r0), channel_id=1, source_target_pairs={{0,1},{1,0},{2,3},{3,2},{4,5},{5,4},{6,7},{7,6},{8,9},{9,8},{10,11... | collective-permute-start | bytes 147464 | tf_op jit(solution)/shard_map/ppermute | solution.py:600
  28.2 5.5 %collective-permute-start.11 = (f32[32,384]{1,0:T(8,128)S(1)}, f32[32,384]{1,0:T(8,128)S(1)}, u32[]{:S(2)}, u32[]{:S(2)}) collective-permute-start(f32[32,384]{1,0:T(8,128)S(1)} %add_add_fusion.1.r2), channel_id=1, source_target_pairs={{0,1},{2,3},{4,5},{6,7},{8,0},{10,2},{12,4},{14,6},{9,8},{11,10},{... | collective-permute-start | bytes 147464 | tf_op jit(solution)/shard_map/ppermute | solution.py:605
  29.5 4.7 %collective-permute-start.12 = (f32[32,384]{1,0:T(8,128)S(1)}, f32[32,384]{1,0:T(8,128)S(1)}, u32[]{:S(2)}, u32[]{:S(2)}) collective-permute-start(f32[32,384]{1,0:T(8,128)S(1)} %add_add_fusion.1.r2), channel_id=1, source_target_pairs={{8,1},{10,3},{12,5},{14,7},{1,8},{3,10},{5,12},{7,14},{0,4},{2,6},... | collective-permute-start | bytes 147464 | tf_op jit(solution)/shard_map/ppermute | solution.py:605
  38.1 1.4 %collective-permute-start.13 = (f32[208,128]{1,0:T(8,128)S(1)}, f32[208,128]{1,0:T(8,128)S(1)}, u32[]{:S(2)}, u32[]{:S(2)}) collective-permute-start(f32[208,128]{1,0:T(8,128)S(1)} %get-tuple-element.100), channel_id=1, source_target_pairs={{0,2},{2,0},{4,6},{6,4},{8,10},{10,8},{12,14},{14,12},{1,3},{3,1},... | collective-permute-start | bytes 319496 | tf_op jit(solution)/shard_map/ppermute | solution.py:593
  38.1 2.8 %copy-start.5 = (bf16[128,12]{0,1:T(8,128)(2,1)S(1)}, bf16[128,12]{0,1:T(8,128)(2,1)}, u32[]{:S(2)}) copy-start(bf16[128,12]{0,1:T(8,128)(2,1)} %param.29) | copy-start | bytes 9220
  39.5 6.5 %collective-permute-start.14 = (f32[104,128]{1,0:T(8,128)S(1)}, f32[104,128]{1,0:T(8,128)S(1)}, u32[]{:S(2)}, u32[]{:S(2)}) collective-permute-start(f32[104,128]{1,0:T(8,128)S(1)} %slice_add_fusion), channel_id=1, source_target_pairs={{0,4},{2,6},{4,0},{6,2},{8,12},{10,14},{12,8},{14,10},{1,5},{3,7},... | collective-permute-start | bytes 159752 | tf_op jit(solution)/shard_map/ppermute | solution.py:602
  42.9 5.3 %collective-permute-start.15 = (f32[104,128]{1,0:T(8,128)S(1)}, f32[104,128]{1,0:T(8,128)S(1)}, u32[]{:S(2)}, u32[]{:S(2)}) collective-permute-start(f32[104,128]{1,0:T(8,128)S(1)} %query_zero.1.r0), channel_id=1, source_target_pairs={{0,1},{1,0},{2,3},{3,2},{4,5},{5,4},{6,7},{7,6},{8,9},{9,8},{10,11... | collective-permute-start | bytes 159752 | tf_op jit(solution)/shard_map/ppermute | solution.py:600
  45.9 6.9 %collective-permute-start.16 = (f32[104,128]{1,0:T(8,128)S(1)}, f32[104,128]{1,0:T(8,128)S(1)}, u32[]{:S(2)}, u32[]{:S(2)}) collective-permute-start(f32[104,128]{1,0:T(8,128)S(1)} %add_add_fusion.r2), channel_id=1, source_target_pairs={{0,1},{2,3},{4,5},{6,7},{8,0},{10,2},{12,4},{14,6},{9,8},{11,10},{... | collective-permute-start | bytes 159752 | tf_op jit(solution)/shard_map/ppermute | solution.py:605
  46.3 6.5 %collective-permute-start.17 = (f32[104,128]{1,0:T(8,128)S(1)}, f32[104,128]{1,0:T(8,128)S(1)}, u32[]{:S(2)}, u32[]{:S(2)}) collective-permute-start(f32[104,128]{1,0:T(8,128)S(1)} %add_add_fusion.r2), channel_id=1, source_target_pairs={{8,1},{10,3},{12,5},{14,7},{1,8},{3,10},{5,12},{7,14},{0,4},{2,6},... | collective-permute-start | bytes 159752 | tf_op jit(solution)/shard_map/ppermute | solution.py:605

commit v7 on v6

--- a/solution.py
+++ b/solution.py
@@ -241,7 +241,7 @@
 
 
 def first_body(
-    fast, own_ref, ownx_ref, p1_ref, p1x_ref, p2_ref, p2x_ref, wk_ref, links_ref, probs_ref, gp_ref, d_ref,
+    fast, self_ref, own_ref, ownx_ref, p1_ref, p1x_ref, p2_ref, p2x_ref, wk_ref, links_ref, probs_ref, gp_ref, d_ref,
     keys_ref, kv_ref, pm_ref, e_ref,
 ):
     rows = own_ref.shape[0]
@@ -258,7 +258,7 @@
     keys = fr.shape[0]
     at = CHAIN_LANE - FRAME_LANE
     key_chain = fr[:, at : at + 1]
-    own_chain = own_ref[:, FRAME_LANE : FRAME_LANE + 128][:, at : at + 1]
+    own_chain = self_ref[:, FRAME_LANE : FRAME_LANE + 128][:, at : at + 1]
     key_hot = (iota((keys, NCHAIN), 1).astype(F32) == key_chain).astype(F32).astype(BF16)
     own_hot = (iota((rows, NCHAIN), 1).astype(F32) == own_chain).astype(F32).astype(BF16)
     eye = iota((NCHAIN, NCHAIN), 0) == iota((NCHAIN, NCHAIN), 1)
@@ -631,9 +631,9 @@
         )
         blocks = (pack, ownx, one, lax.ppermute(one, "row", CORE_SWAP), two, lax.ppermute(two, "row", CORE_SWAP))
     key_pack, kv1, pm, e1 = call(
-        functools.partial(first_body, fast), "first", [VMEM] * 11,
+        functools.partial(first_body, fast), "first", [VMEM] * 12,
         [((keys, PACK), F32), ((keys, 2048), F32), ((2, hr, keys), BF16), ((rows, 384), F32)],
-        (*blocks, wk, links, probs, gp1, d1),
+        (own, *blocks, wk, links, probs, gp1, d1),
     )
     e1_other = col_other(e1)
     kv0, e0, tail = call(

time: 53.8 us -> 53.8 us (level)
  no operation moved by 1% of the time
where the time goes in v7:
time: 53.8 us; the launch traced here: 53.6 us
  starting transfers between devices  23.9 us (44%)
  Pallas kernels  17.7 us (33%)
  waiting for transfers between devices  11.2 us (21%)
  between operations  0.77 us (1%)
    pallas_call x10, Pallas kernels, call(): pl.pallas_call(body, name=name, in_specs=in_specs, out_specs=tuple((VMEM...  17.7 us
    ppermute x2, waiting for transfers between devices, reduce(): lax.ppermute(part, BOTH, SEND_ONE)  6.85 us
    ppermute x3, starting transfers between devices, col_other(): return lax.ppermute(x, 'col', COL_SWAP)  4.32 us
    ppermute x2, starting transfers between devices, reduce(): lax.ppermute(part, BOTH, SEND_TWO)  3.92 us
    ppermute x2, starting transfers between devices, reduce(): query_other = lax.ppermute(query, 'col', COL_SWAP)  3.48 us
    ppermute x2, starting transfers between devices, reduce(): half = lax.ppermute(mine_b + got[count:], 'row', Z_SWAP)  3.34 us
    ppermute x1, starting transfers between devices, local(): two = lax.ppermute(pack, BOTH, FETCH_TWO)  3.29 us
    ppermute x1, starting transfers between devices, local(): one = lax.ppermute(pack, BOTH, FETCH_ONE)  3.09 us
  transfers between devices with their start and end apart: 18, of which 9 were waited for; matrix products, arithmetic and copies ran while one was open for 0% of the time, Pallas kernels for 20%

profile of v7, /device:TPU:0, one launch (start us, length us, event | category | flops | bytes accessed | tf_op | source)
XLA Modules:
  0.0 53.6 jit_solution(14183756345160362278)
XLA Ops:
  0.6 1.0 %pack.1.pack_ref.self_ref.own_ref = f32[32,896]{1,0:T(8,128)S(1)} custom-call(f32[2,32,384]{2,1,0:T(8,128)} %single_hbm.1, f32[12,2,32]{2,1,0:T(2,128)} %bitcast.21, s32[1,32]{1,0:T(1,128)} %bitcast.22), custom_call_target="tpu_custom_call" | custom-call | flops 1000000000 | bytes 3000000 | tf_op jit(solution)/shard_map/pack/pallas_call | solution.py:527
  1.6 3.1 %collective-permute-start.1 = (f32[32,896]{1,0:T(8,128)S(1)}, f32[32,896]{1,0:T(8,128)S(1)}, u32[]{:S(2)}, u32[]{:S(2)}) collective-permute-start(f32[32,896]{1,0:T(8,128)S(1)} %pack.1.pack_ref.self_ref.own_ref), channel_id=1, source_target_pairs={{0,4},{2,6},{4,0},{6,2},{1,8},{3,10},{5,12},{7,14},{9,13},{11,15},... | collective-permute-start | bytes 344072 | tf_op jit(solution)/shard_map/ppermute | solution.py:576
  4.7 3.3 %collective-permute-start.2 = (f32[32,896]{1,0:T(8,128)S(1)}, f32[32,896]{1,0:T(8,128)S(1)}, u32[]{:S(2)}, u32[]{:S(2)}) collective-permute-start(f32[32,896]{1,0:T(8,128)S(1)} %pack.1.pack_ref.self_ref.own_ref), channel_id=1, source_target_pairs={{0,12},{2,14},{4,8},{6,10},{9,5},{11,7},{13,1},{15,3},{1,0},{3,2},... | collective-permute-start | bytes 344072 | tf_op jit(solution)/shard_map/ppermute | solution.py:577
  8.0 0.0 collective-permute-start
  8.0 0.0 copy-start.3
  8.0 0.0 copy-start.4
  8.0 3.3 %prep.1 = (bf16[1280,384]{1,0:T(8,128)(2,1)S(1)}, bf16[640,384]{1,0:T(8,128)(2,1)S(1)}, f32[32,768]{1,0:T(8,128)S(1)}, f32[32,1024]{1,0:T(8,128)S(1)}, f32[32,10...) custom-call(f32[32,896]{1,0:T(8,128)S(1)} %pack.1.pack_ref.self_ref.own_ref, ...), custom_call_target="tpu_custom_call" | custom-call | flops 1000000000 | bytes 3000000 | tf_op jit(solution)/shard_map/prep/pallas_call | solution.py:527
  11.3 0.0 collective-permute-done.1.p1_ref
  11.4 0.0 collective-permute-done.2.p2_ref
  11.4 0.6 %collective-permute-start.3 = (f32[32,896]{1,0:T(8,128)S(1)}, f32[32,896]{1,0:T(8,128)S(1)}, u32[]{:S(2)}, u32[]{:S(2)}) collective-permute-start(f32[32,896]{1,0:T(8,128)S(1)} %collective-permute-done.1.p1_ref), channel_id=1, source_target_pairs={{0,2},{2,0},{4,6},{6,4},{8,10},{10,8},{12,14},{14,12},{1,3},{3,1},... | collective-permute-start | bytes 344072 | tf_op jit(solution)/shard_map/ppermute | solution.py:632
  11.9 0.1 collective-permute-start.4
  12.0 0.0 collective-permute-done.ownx_ref
  12.0 0.9 %collective-permute-done.3.p1x_ref = f32[32,896]{1,0:T(8,128)S(1)} collective-permute-done((f32[32,896]{1,0:T(8,128)S(1)}, f32[32,896]{1,0:T(8,128)S(1)}, u32[]{:S(2)}, u32[]{:S(2)}) %collective-permute-start.3) | collective-permute-done | bytes 114720 | tf_op jit(solution)/shard_map/ppermute | solution.py:632
  12.9 0.4 collective-permute-done.4.p2x_ref
  13.3 0.0 copy-done.3
  13.3 0.0 copy-done.4
  13.3 0.0 copy-start.1
  13.3 1.3 %first.1 = (f32[128,896]{1,0:T(8,128)S(1)}, f32[128,2048]{1,0:T(8,128)S(1)}, bf16[2,384,128]{2,1,0:T(8,128)(2,1)S(1)}, f32[32,384]{1,0:T(8,128)S(1)}) custom-call(f32[32,896]{1,0:T(8,128)S(1)} %pack.1.pack_ref.self_ref.own_ref, f32[32,896]{1,0:T(8,128)S(1)} %pack.1.pack_ref.self_ref.own_ref, f32[32,896]{1,0:T(8,128)S(1)} %collective-permute-done.ownx_ref, ...), custom_call_target="tpu_custom_call" | custom-call | flops 1000000000 | bytes 3000000 | tf_op jit(solution)/shard_map/first/pallas_call | solution.py:527
  14.5 2.3 %collective-permute-start.5 = (f32[32,384]{1,0:T(8,128)S(1)}, f32[32,384]{1,0:T(8,128)S(1)}, u32[]{:S(2)}, u32[]{:S(2)}) collective-permute-start(f32[32,384]{1,0:T(8,128)S(1)} %get-tuple-element.72.e_mine), channel_id=1, source_target_pairs={{0,1},{1,0},{2,3},{3,2},{4,5},{5,4},{6,7},{7,6},{8,9},{9,8},{10,11... | collective-permute-start | bytes 147464 | tf_op jit(solution)/shard_map/ppermute | solution.py:588
  16.9 0.0 copy-done.1
  16.9 1.3 %second.1 = (f32[128,2048]{1,0:T(8,128)S(1)}, f32[32,1152]{1,0:T(8,128)S(1)}, f32[32,1024]{1,0:T(8,128)S(1)}) custom-call(f32[128,896]{1,0:T(8,128)S(1)} %get-tuple-element.73.keys_ref, bf16[1280,384]{1,0:T(8,128)(2,1)S(1)} %get-tuple-element.69.wk_ref, bf16[2,384,128]{2,1,0:T(8,128)(2,1)S(1)} %get-tuple-element.74.pm_ref, bf16[32,128,128]{2,1,0:T(8,128)(2,1)S(1)} %copy-done.1), custom_call_target="tpu_custom_call" | custom-call | flops 1000000000 | bytes 3000000 | tf_op jit(solution)/shard_map/second/pallas_call | solution.py:527
  18.2 0.1 collective-permute-start.7
  18.3 0.8 %collective-permute-done.5.e_other = f32[32,384]{1,0:T(8,128)S(1)} collective-permute-done((f32[32,384]{1,0:T(8,128)S(1)}, f32[32,384]{1,0:T(8,128)S(1)}, u32[]{:S(2)}, u32[]{:S(2)}) %collective-permute-start.5) | collective-permute-done | bytes 49184 | tf_op jit(solution)/shard_map/ppermute | solution.py:588
  19.1 2.1 %back_one.1 = (f32[768,128]{1,0:T(8,128)S(1)}, f32[32,384]{1,0:T(8,128)S(1)}, f32[32,384]{1,0:T(8,128)S(1)}, f32[64,384]{1,0:T(8,128)S(1)}, f32[32,1152]{1,0:T(8,128)S(1)}, /*index=5*/f32[128,768]{1,0:T(8,128)S(1)}) custom-call(f32[32,384]{1,0:T(8,128)S(1)} %get-tuple-element.72.e_mine, f32[32,384]{1,0:T(8,128)S(1)} %collective-permute-done.5.e_other, ...), custom_call_target="tpu_custom_call" | custom-call | flops 6000000000 | bytes 18000000 | tf_op jit(solution)/shard_map/back_one/pallas_call | solution.py:527
  21.2 0.0 copy-start
  21.2 0.0 copy-start.2
  21.2 0.1 collective-permute-start.6
  21.3 1.9 %collective-permute-start.9 = (f32[32,1024]{1,0:T(8,128)S(1)}, f32[32,1024]{1,0:T(8,128)S(1)}, u32[]{:S(2)}, u32[]{:S(2)}) collective-permute-start(f32[32,1024]{1,0:T(8,128)S(1)} %get-tuple-element.83.tail_mine), channel_id=1, source_target_pairs={{0,1},{1,0},{2,3},{3,2},{4,5},{5,4},{6,7},{7,6},{8,9},{9,8},{10,11... | collective-permute-start | bytes 393224 | tf_op jit(solution)/shard_map/ppermute | solution.py:588
  23.2 0.0 collective-permute-done.6
  23.2 0.8 %collective-permute-done.7.e_other = f32[32,1152]{1,0:T(8,128)S(1)} collective-permute-done((f32[32,1152]{1,0:T(8,128)S(1)}, f32[32,1152]{1,0:T(8,128)S(1)}, u32[]{:S(2)}, u32[]{:S(2)}) %collective-permute-start.7) | collective-permute-done | bytes 147488 | tf_op jit(solution)/shard_map/ppermute | solution.py:588
  24.1 1.8 %collective-permute-start.8 = (f32[32,384]{1,0:T(8,128)S(1)}, f32[32,384]{1,0:T(8,128)S(1)}, u32[]{:S(2)}, u32[]{:S(2)}) collective-permute-start(f32[32,384]{1,0:T(8,128)S(1)} %slice_add_fusion.1), channel_id=1, source_target_pairs={{0,4},{2,6},{4,0},{6,2},{8,12},{10,14},{12,8},{14,10},{1,5},{3,7},... | collective-permute-start | bytes 147464 | tf_op jit(solution)/shard_map/ppermute | solution.py:602
  25.9 1.2 %query_one.1 = (f32[32,384]{1,0:T(8,128)S(1)}, f32[32,128]{1,0:T(8,128)S(1)}, f32[128,128]{1,0:T(8,128)S(1)}) custom-call(f32[768,128]{1,0:T(8,128)S(1)} %get-tuple-element.84.z_ref.z1_ref, f32[128,2048]{1,0:T(8,128)S(1)} %get-tuple-element.77.kv_ref, f32[32,896]{1,0:T(8,128)S(1)} %pack.1.pack_ref.self_ref.own_ref, f32[32,1024]{1,0:T(8,128)S(1)} %get-tuple-element.78.q_ref, ...), custom_call_target="tpu_custom_call" | custom-call | flops 10000000 | bytes 30000 | tf_op jit(solution)/shard_map/query_one/pallas_call | solution.py:527
  27.2 0.5 collective-permute-start.10
  27.6 0.0 collective-permute-done.9.tail_other
  27.6 0.6 %collective-permute-done.8 = f32[32,384]{1,0:T(8,128)S(1)} collective-permute-done((f32[32,384]{1,0:T(8,128)S(1)}, f32[32,384]{1,0:T(8,128)S(1)}, u32[]{:S(2)}, u32[]{:S(2)}) %collective-permute-start.8) | collective-permute-done | bytes 49184 | tf_op jit(solution)/shard_map/ppermute | solution.py:602
  28.2 1.3 %collective-permute-start.11 = (f32[32,384]{1,0:T(8,128)S(1)}, f32[32,384]{1,0:T(8,128)S(1)}, u32[]{:S(2)}, u32[]{:S(2)}) collective-permute-start(f32[32,384]{1,0:T(8,128)S(1)} %add_add_fusion.1.r2), channel_id=1, source_target_pairs={{0,1},{2,3},{4,5},{6,7},{8,0},{10,2},{12,4},{14,6},{9,8},{11,10},{... | collective-permute-start | bytes 147464 | tf_op jit(solution)/shard_map/ppermute | solution.py:605
  29.5 2.1 %collective-permute-start.12 = (f32[32,384]{1,0:T(8,128)S(1)}, f32[32,384]{1,0:T(8,128)S(1)}, u32[]{:S(2)}, u32[]{:S(2)}) collective-permute-start(f32[32,384]{1,0:T(8,128)S(1)} %add_add_fusion.1.r2), channel_id=1, source_target_pairs={{8,1},{10,3},{12,5},{14,7},{1,8},{3,10},{5,12},{7,14},{0,4},{2,6},... | collective-permute-start | bytes 147464 | tf_op jit(solution)/shard_map/ppermute | solution.py:605
  31.6 0.0 collective-permute-done.10.r1
  31.6 2.2 %collective-permute-done.11.r3 = f32[32,384]{1,0:T(8,128)S(1)} collective-permute-done((f32[32,384]{1,0:T(8,128)S(1)}, f32[32,384]{1,0:T(8,128)S(1)}, u32[]{:S(2)}, u32[]{:S(2)}) %collective-permute-start.11) | collective-permute-done | bytes 49184 | tf_op jit(solution)/shard_map/ppermute | solution.py:605
  33.8 0.5 collective-permute-done.12.r4
  34.2 0.0 copy-done
  34.2 0.0 copy-done.2
  34.2 3.8 %back_zero.1 = (f32[768,128]{1,0:T(8,128)S(1)}, f32[104,128]{1,0:T(8,128)S(1)}, f32[104,128]{1,0:T(8,128)S(1)}, f32[208,128]{1,0:T(8,128)S(1)}, f32[32,1152]{1,0...) custom-call(f32[32,384]{1,0:T(8,128)S(1)} %copy-done.2, f32[32,384]{1,0:T(8,128)S(1)} %get-tuple-element.90.r0, ...), custom_call_target="tpu_custom_call" | custom-call | flops 1000000000 | bytes 3000000 | tf_op jit(solution)/shard_map/back_zero/pallas_call | solution.py:527
  38.1 0.1 collective-permute-start.13
  38.1 0.0 copy-start.5
  38.2 1.0 %query_zero.1.r0 = f32[104,128]{1,0:T(8,128)S(1)} custom-call(f32[768,128]{1,0:T(8,128)S(1)} %get-tuple-element.101.z_ref.z0_ref, f32[128,2048]{1,0:T(8,128)S(1)} %get-tuple-element.96.kv_ref, f32[32,896]{1,0:T(8,128)S(1)} %pack.1.pack_ref.self_ref.own_ref, f32[32,1024]{1,0:T(8,128)S(1)} %get-tuple-element.97.q_ref, ...), custom_call_target="tpu_custom_call" | custom-call | flops 1000000000 | bytes 3000000 | tf_op jit(solution)/shard_map/query_zero/pallas_call | solution.py:527
  39.2 0.3 collective-permute-done.13
  39.5 1.5 %collective-permute-start.14 = (f32[104,128]{1,0:T(8,128)S(1)}, f32[104,128]{1,0:T(8,128)S(1)}, u32[]{:S(2)}, u32[]{:S(2)}) collective-permute-start(f32[104,128]{1,0:T(8,128)S(1)} %slice_add_fusion), channel_id=1, source_target_pairs={{0,4},{2,6},{4,0},{6,2},{8,12},{10,14},{12,8},{14,10},{1,5},{3,7},... | collective-permute-start | bytes 159752 | tf_op jit(solution)/shard_map/ppermute | solution.py:602
  41.0 0.0 copy-done.5
  41.0 1.9 %pair_grad.1 = bf16[32,128,128]{2,1,0:T(8,128)(2,1)} custom-call(f32[768,128]{1,0:T(8,128)S(1)} %get-tuple-element.84.z_ref.z1_ref, f32[768,128]{1,0:T(8,128)S(1)} %get-tuple-element.101.z_ref.z0_ref, f32[384,128]{1,0:T(8,128)S(1)} %get-tuple-element.105.pu1_ref, f32[384,128]{1,0:T(8,128)S(1)} %get-tuple-element.106.pu0_ref, bf16[12,128]{1,0:T(8,128)(2,1)S(1)} %bitcast.13), custom_call_target="tpu_custom_call" | custom-call | flops 1000000000 | bytes 3000000 | tf_op jit(solution)/shard_map/pair_grad/pallas_call | solution.py:527
  42.9 3.0 %collective-permute-start.15 = (f32[104,128]{1,0:T(8,128)S(1)}, f32[104,128]{1,0:T(8,128)S(1)}, u32[]{:S(2)}, u32[]{:S(2)}) collective-permute-start(f32[104,128]{1,0:T(8,128)S(1)} %query_zero.1.r0), channel_id=1, source_target_pairs={{0,1},{1,0},{2,3},{3,2},{4,5},{5,4},{6,7},{7,6},{8,9},{9,8},{10,11... | collective-permute-start | bytes 159752 | tf_op jit(solution)/shard_map/ppermute | solution.py:600
  45.9 0.0 collective-permute-done.14
  45.9 0.4 collective-permute-start.16
  46.3 1.9 %collective-permute-start.17 = (f32[104,128]{1,0:T(8,128)S(1)}, f32[104,128]{1,0:T(8,128)S(1)}, u32[]{:S(2)}, u32[]{:S(2)}) collective-permute-start(f32[104,128]{1,0:T(8,128)S(1)} %add_add_fusion.r2), channel_id=1, source_target_pairs={{8,1},{10,3},{12,5},{14,7},{1,8},{3,10},{5,12},{7,14},{0,4},{2,6},... | collective-permute-start | bytes 159752 | tf_op jit(solution)/shard_map/ppermute | solution.py:605
  48.2 0.0 collective-permute-done.15.r1
  48.2 4.7 %collective-permute-done.16.r3 = f32[104,128]{1,0:T(8,128)S(1)} collective-permute-done((f32[104,128]{1,0:T(8,128)S(1)}, f32[104,128]{1,0:T(8,128)S(1)}, u32[]{:S(2)}, u32[]{:S(2)}) %collective-permute-start.16) | collective-permute-done | bytes 53280 | tf_op jit(solution)/shard_map/ppermute | solution.py:605
  52.8 0.0 collective-permute-done.17.r4
  52.8 0.7 %final.1 = (f32[32,384]{1,0:T(8,128)}, f32[12,2,32]{2,1,0:T(2,128)}) custom-call(f32[104,128]{1,0:T(8,128)S(1)} %query_zero.1.r0, f32[104,128]{1,0:T(8,128)S(1)} %collective-permute-done.15.r1, f32[104,128]{1,0:T(8,128)S(1)} %add_add_fusion.r2, f32[104,128]{1,0:T(8,128)S(1)} %collective-permute-done.16.r3, f32[104,128]{1,0:T(8,128)S(1)} %collective-permute-done.17.r4, ...), custom_call_target="tpu_custom_call" | custom-call | flops 1000000000 | bytes 3000000 | tf_op jit(solution)/shard_map/final/pallas_call | solution.py:527
  (4 shorter events, 0.0 us)
Async XLA Ops:
  1.6 9.7 %collective-permute-start.1 = (f32[32,896]{1,0:T(8,128)S(1)}, f32[32,896]{1,0:T(8,128)S(1)}, u32[]{:S(2)}, u32[]{:S(2)}) collective-permute-start(f32[32,896]{1,0:T(8,128)S(1)} %pack.1.pack_ref.self_ref.own_ref), channel_id=1, source_target_pairs={{0,4},{2,6},{4,0},{6,2},{1,8},{3,10},{5,12},{7,14},{9,13},{11,15},... | collective-permute-start | bytes 344072 | tf_op jit(solution)/shard_map/ppermute | solution.py:576
  4.7 6.7 %collective-permute-start.2 = (f32[32,896]{1,0:T(8,128)S(1)}, f32[32,896]{1,0:T(8,128)S(1)}, u32[]{:S(2)}, u32[]{:S(2)}) collective-permute-start(f32[32,896]{1,0:T(8,128)S(1)} %pack.1.pack_ref.self_ref.own_ref), channel_id=1, source_target_pairs={{0,12},{2,14},{4,8},{6,10},{9,5},{11,7},{13,1},{15,3},{1,0},{3,2},... | collective-permute-start | bytes 344072 | tf_op jit(solution)/shard_map/ppermute | solution.py:577
  8.0 4.0 %collective-permute-start = (f32[32,896]{1,0:T(8,128)S(1)}, f32[32,896]{1,0:T(8,128)S(1)}, u32[]{:S(2)}, u32[]{:S(2)}) collective-permute-start(f32[32,896]{1,0:T(8,128)S(1)} %pack.1.pack_ref.self_ref.own_ref), channel_id=1, source_target_pairs={{0,2},{2,0},{4,6},{6,4},{8,10},{10,8},{12,14},{14,12},{1,3},{3,1},... | collective-permute-start | bytes 344072 | tf_op jit(solution)/shard_map/ppermute | solution.py:575
  8.0 5.3 %copy-start.3 = (bf16[2,12,32,128]{3,2,1,0:T(8,128)(2,1)S(1)}, bf16[2,12,32,128]{3,2,1,0:T(8,128)(2,1)}, u32[]{:S(2)}) copy-start(bf16[2,12,32,128]{3,2,1,0:T(8,128)(2,1)} %param.18) | copy-start | bytes 589828
  8.0 5.3 %copy-start.4 = (s32[16,16]{1,0:T(8,128)S(1)}, s32[16,16]{1,0:T(8,128)}, u32[]{:S(2)}) copy-start(s32[16,16]{1,0:T(8,128)} %links_ref.1) | copy-start | bytes 3076
  11.4 1.5 %collective-permute-start.3 = (f32[32,896]{1,0:T(8,128)S(1)}, f32[32,896]{1,0:T(8,128)S(1)}, u32[]{:S(2)}, u32[]{:S(2)}) collective-permute-start(f32[32,896]{1,0:T(8,128)S(1)} %collective-permute-done.1.p1_ref), channel_id=1, source_target_pairs={{0,2},{2,0},{4,6},{6,4},{8,10},{10,8},{12,14},{14,12},{1,3},{3,1},... | collective-permute-start | bytes 344072 | tf_op jit(solution)/shard_map/ppermute | solution.py:632
  11.9 1.3 %collective-permute-start.4 = (f32[32,896]{1,0:T(8,128)S(1)}, f32[32,896]{1,0:T(8,128)S(1)}, u32[]{:S(2)}, u32[]{:S(2)}) collective-permute-start(f32[32,896]{1,0:T(8,128)S(1)} %collective-permute-done.2.p2_ref), channel_id=1, source_target_pairs={{0,2},{2,0},{4,6},{6,4},{8,10},{10,8},{12,14},{14,12},{1,3},{3,1},... | collective-permute-start | bytes 344072 | tf_op jit(solution)/shard_map/ppermute | solution.py:632
  13.3 3.6 %copy-start.1 = (bf16[32,128,128]{2,1,0:T(8,128)(2,1)S(1)}, bf16[32,128,128]{2,1,0:T(8,128)(2,1)}, u32[]{:S(2)}) copy-start(bf16[32,128,128]{2,1,0:T(8,128)(2,1)} %pair_ref.3) | copy-start | bytes 3145732
  14.5 4.6 %collective-permute-start.5 = (f32[32,384]{1,0:T(8,128)S(1)}, f32[32,384]{1,0:T(8,128)S(1)}, u32[]{:S(2)}, u32[]{:S(2)}) collective-permute-start(f32[32,384]{1,0:T(8,128)S(1)} %get-tuple-element.72.e_mine), channel_id=1, source_target_pairs={{0,1},{1,0},{2,3},{3,2},{4,5},{5,4},{6,7},{7,6},{8,9},{9,8},{10,11... | collective-permute-start | bytes 147464 | tf_op jit(solution)/shard_map/ppermute | solution.py:588
  18.2 5.9 %collective-permute-start.7 = (f32[32,1152]{1,0:T(8,128)S(1)}, f32[32,1152]{1,0:T(8,128)S(1)}, u32[]{:S(2)}, u32[]{:S(2)}) collective-permute-start(f32[32,1152]{1,0:T(8,128)S(1)} %get-tuple-element.93.e_mine), channel_id=1, source_target_pairs={{0,1},{1,0},{2,3},{3,2},{4,5},{5,4},{6,7},{7,6},{8,9},{9,8},{10,11... | collective-permute-start | bytes 442376 | tf_op jit(solution)/shard_map/ppermute | solution.py:588
  21.2 13.0 %copy-start = (bf16[2112,384]{1,0:T(8,128)(2,1)S(1)}, bf16[2112,384]{1,0:T(8,128)(2,1)}, u32[]{:S(2)}) copy-start(bf16[2112,384]{1,0:T(8,128)(2,1)} %w_out_ref.1) | copy-start | bytes 4866052
  21.2 13.0 %copy-start.2 = (f32[32,384]{1,0:T(8,128)S(1)}, f32[32,384]{1,0:T(8,128)}, u32[]{:S(2)}) copy-start(f32[32,384]{1,0:T(8,128)} %cot_ref.1) | copy-start | bytes 147460
  21.2 2.0 %collective-permute-start.6 = (f32[64,384]{1,0:T(8,128)S(1)}, f32[64,384]{1,0:T(8,128)S(1)}, u32[]{:S(2)}, u32[]{:S(2)}) collective-permute-start(f32[64,384]{1,0:T(8,128)S(1)} %get-tuple-element.81), channel_id=1, source_target_pairs={{0,2},{2,0},{4,6},{6,4},{8,10},{10,8},{12,14},{14,12},{1,3},{3,1},... | collective-permute-start | bytes 294920 | tf_op jit(solution)/shard_map/ppermute | solution.py:593
  21.3 6.3 %collective-permute-start.9 = (f32[32,1024]{1,0:T(8,128)S(1)}, f32[32,1024]{1,0:T(8,128)S(1)}, u32[]{:S(2)}, u32[]{:S(2)}) collective-permute-start(f32[32,1024]{1,0:T(8,128)S(1)} %get-tuple-element.83.tail_mine), channel_id=1, source_target_pairs={{0,1},{1,0},{2,3},{3,2},{4,5},{5,4},{6,7},{7,6},{8,9},{9,8},{10,11... | collective-permute-start | bytes 393224 | tf_op jit(solution)/shard_map/ppermute | solution.py:588
  24.1 4.2 %collective-permute-start.8 = (f32[32,384]{1,0:T(8,128)S(1)}, f32[32,384]{1,0:T(8,128)S(1)}, u32[]{:S(2)}, u32[]{:S(2)}) collective-permute-start(f32[32,384]{1,0:T(8,128)S(1)} %slice_add_fusion.1), channel_id=1, source_target_pairs={{0,4},{2,6},{4,0},{6,2},{8,12},{10,14},{12,8},{14,10},{1,5},{3,7},... | collective-permute-start | bytes 147464 | tf_op jit(solution)/shard_map/ppermute | solution.py:602
  27.2 4.4 %collective-permute-start.10 = (f32[32,384]{1,0:T(8,128)S(1)}, f32[32,384]{1,0:T(8,128)S(1)}, u32[]{:S(2)}, u32[]{:S(2)}) collective-permute-start(f32[32,384]{1,0:T(8,128)S(1)} %get-tuple-element.90.r0), channel_id=1, source_target_pairs={{0,1},{1,0},{2,3},{3,2},{4,5},{5,4},{6,7},{7,6},{8,9},{9,8},{10,11... | collective-permute-start | bytes 147464 | tf_op jit(solution)/shard_map/ppermute | solution.py:600
  28.2 5.5 %collective-permute-start.11 = (f32[32,384]{1,0:T(8,128)S(1)}, f32[32,384]{1,0:T(8,128)S(1)}, u32[]{:S(2)}, u32[]{:S(2)}) collective-permute-start(f32[32,384]{1,0:T(8,128)S(1)} %add_add_fusion.1.r2), channel_id=1, source_target_pairs={{0,1},{2,3},{4,5},{6,7},{8,0},{10,2},{12,4},{14,6},{9,8},{11,10},{... | collective-permute-start | bytes 147464 | tf_op jit(solution)/shard_map/ppermute | solution.py:605
  29.5 4.7 %collective-permute-start.12 = (f32[32,384]{1,0:T(8,128)S(1)}, f32[32,384]{1,0:T(8,128)S(1)}, u32[]{:S(2)}, u32[]{:S(2)}) collective-permute-start(f32[32,384]{1,0:T(8,128)S(1)} %add_add_fusion.1.r2), channel_id=1, source_target_pairs={{8,1},{10,3},{12,5},{14,7},{1,8},{3,10},{5,12},{7,14},{0,4},{2,6},... | collective-permute-start | bytes 147464 | tf_op jit(solution)/shard_map/ppermute | solution.py:605
  38.1 1.4 %collective-permute-start.13 = (f32[208,128]{1,0:T(8,128)S(1)}, f32[208,128]{1,0:T(8,128)S(1)}, u32[]{:S(2)}, u32[]{:S(2)}) collective-permute-start(f32[208,128]{1,0:T(8,128)S(1)} %get-tuple-element.100), channel_id=1, source_target_pairs={{0,2},{2,0},{4,6},{6,4},{8,10},{10,8},{12,14},{14,12},{1,3},{3,1},... | collective-permute-start | bytes 319496 | tf_op jit(solution)/shard_map/ppermute | solution.py:593
  38.1 2.8 %copy-start.5 = (bf16[128,12]{0,1:T(8,128)(2,1)S(1)}, bf16[128,12]{0,1:T(8,128)(2,1)}, u32[]{:S(2)}) copy-start(bf16[128,12]{0,1:T(8,128)(2,1)} %param.29) | copy-start | bytes 9220
  39.5 6.5 %collective-permute-start.14 = (f32[104,128]{1,0:T(8,128)S(1)}, f32[104,128]{1,0:T(8,128)S(1)}, u32[]{:S(2)}, u32[]{:S(2)}) collective-permute-start(f32[104,128]{1,0:T(8,128)S(1)} %slice_add_fusion), channel_id=1, source_target_pairs={{0,4},{2,6},{4,0},{6,2},{8,12},{10,14},{12,8},{14,10},{1,5},{3,7},... | collective-permute-start | bytes 159752 | tf_op jit(solution)/shard_map/ppermute | solution.py:602
  42.9 5.3 %collective-permute-start.15 = (f32[104,128]{1,0:T(8,128)S(1)}, f32[104,128]{1,0:T(8,128)S(1)}, u32[]{:S(2)}, u32[]{:S(2)}) collective-permute-start(f32[104,128]{1,0:T(8,128)S(1)} %query_zero.1.r0), channel_id=1, source_target_pairs={{0,1},{1,0},{2,3},{3,2},{4,5},{5,4},{6,7},{7,6},{8,9},{9,8},{10,11... | collective-permute-start | bytes 159752 | tf_op jit(solution)/shard_map/ppermute | solution.py:600
  45.9 6.9 %collective-permute-start.16 = (f32[104,128]{1,0:T(8,128)S(1)}, f32[104,128]{1,0:T(8,128)S(1)}, u32[]{:S(2)}, u32[]{:S(2)}) collective-permute-start(f32[104,128]{1,0:T(8,128)S(1)} %add_add_fusion.r2), channel_id=1, source_target_pairs={{0,1},{2,3},{4,5},{6,7},{8,0},{10,2},{12,4},{14,6},{9,8},{11,10},{... | collective-permute-start | bytes 159752 | tf_op jit(solution)/shard_map/ppermute | solution.py:605
  46.3 6.5 %collective-permute-start.17 = (f32[104,128]{1,0:T(8,128)S(1)}, f32[104,128]{1,0:T(8,128)S(1)}, u32[]{:S(2)}, u32[]{:S(2)}) collective-permute-start(f32[104,128]{1,0:T(8,128)S(1)} %add_add_fusion.r2), channel_id=1, source_target_pairs={{8,1},{10,3},{12,5},{14,7},{1,8},{3,10},{5,12},{7,14},{0,4},{2,6},... | collective-permute-start | bytes 159752 | tf_op jit(solution)/shard_map/ppermute | solution.py:605

commit v8 on v7

--- a/solution.py
+++ b/solution.py
@@ -139,12 +139,13 @@
 
 
 def pair_products(pu_ref, pair_ref, d_ref, rows):
-    for i in range(0, rows, 2):
-        lhs = jnp.concatenate([pu_ref[pl.ds(i, H, stride=rows), :], pu_ref[pl.ds(i + 1, H, stride=rows), :]], axis=0)
-        both = mm(lhs.astype(BF16), pair_ref[i : i + 2].reshape(-1, CZ), NT)
-        keys = both.shape[1] // 2
-        d_ref[pl.ds(i, H, stride=rows), :] = both[:H, :keys]
-        d_ref[pl.ds(i + 1, H, stride=rows), :] = both[H:, keys:]
+    step = 4
+    for i in range(0, rows, step):
+        lhs = jnp.concatenate([pu_ref[pl.ds(i + n, H, stride=rows), :] for n in range(step)], axis=0)
+        both = mm(lhs.astype(BF16), pair_ref[i : i + step].reshape(-1, CZ), NT)
+        keys = both.shape[1] // step
+        for n in range(step):
+            d_ref[pl.ds(i + n, H, stride=rows), :] = both[H * n : H * (n + 1), keys * n : keys * (n + 1)]
 
 
 def split3(x):
@@ -242,7 +243,7 @@
 
 def first_body(
     fast, self_ref, own_ref, ownx_ref, p1_ref, p1x_ref, p2_ref, p2x_ref, wk_ref, links_ref, probs_ref, gp_ref, d_ref,
-    keys_ref, kv_ref, pm_ref, e_ref,
+    keys_ref, kv_ref, pm_ref, mask_ref, e_ref,
 ):
     rows = own_ref.shape[0]
     home, zb, core = position(fast)
@@ -264,11 +265,10 @@
     eye = iota((NCHAIN, NCHAIN), 0) == iota((NCHAIN, NCHAIN), 1)
     allowed = jnp.where(eye, 1.0, links_ref[...].astype(F32)).astype(BF16)
     mask = mm(mm(own_hot, allowed).astype(BF16), key_hot, NT)
-    mask_all = jnp.concatenate([mask] * H, axis=0)
-    for l in range(2):
-        pm_ref[l] = (probs_ref[l].astype(F32) * mask_all).astype(BF16)
+    mask_ref[...] = mask
+    pm_ref[...] = (probs_ref[1].astype(F32) * jnp.concatenate([mask] * H, axis=0)).astype(BF16)
     project_keys(keys_ref[:, 0:C], fr, 0, wk_ref, kv_ref)
-    probs = pm_ref[1]
+    probs = pm_ref[...]
     sums = value_sums(probs, kv_ref, rows)
     weighted = mm2(probs.astype(F32) * d_ref[...], jnp.ones((keys, 128), BF16))
     lane = iota((rows, 128), 1)
@@ -278,11 +278,14 @@
     e_ref[:, 256:384] = block(sums, 2)
 
 
-def second_body(keys_ref, wk_ref, pm_ref, pair_ref, kv_ref, e_ref, tail_ref, p32_ref, op_ref):
+def second_body(
+    keys_ref, wk_ref, probs_ref, mask_ref, pair_ref, kv_ref, pm_ref, e_ref, tail_ref, p32_ref, op_ref
+):
     rows = pair_ref.shape[0]
     fr = keys_ref[:, FRAME_LANE : FRAME_LANE + 128]
     project_keys(keys_ref[:, C : 2 * C], fr, 12, wk_ref, kv_ref)
-    probs = pm_ref[0]
+    probs = (probs_ref[0].astype(F32) * jnp.concatenate([mask_ref[...]] * H, axis=0)).astype(BF16)
+    pm_ref[...] = probs
     sums = value_sums(probs, kv_ref, rows)
     for a in range(3):
         e_ref[:, 128 * a : 128 * a + 128] = block(sums, a)
@@ -443,7 +446,7 @@
 ):
     e = e_mine[...] + e_other[...]
     pts_ref[...], grads_ref[...] = backward(
-        e, e[:, 128:256], pm_ref[1], kv_ref, frame_part(keys_ref), frame_part(own_ref), 0, q_ref,
+        e, e[:, 128:256], pm_ref[...], kv_ref, frame_part(keys_ref), frame_part(own_ref), 0, q_ref,
         gp_ref[...], d_ref, wk_ref, sc_ref[0:1, :], z_ref, work_ref,
     )
     send_blocks(fast, work_ref, mine_a, mine_b, theirs, own_ref.shape[0])
@@ -488,7 +491,7 @@
     )
     dots = dots + mm2(wide, lane_matrix(H * CZ, lambda r: STAT + (r >> 7)))
     pts_ref[...], grads = backward(
-        e, dots, pm_ref[0], kv_ref, frame_part(keys_ref), frame_part(own_ref), 12, q_ref, gp, d_ref, wk_ref,
+        e, dots, pm_ref[...], kv_ref, frame_part(keys_ref), frame_part(own_ref), 12, q_ref, gp, d_ref, wk_ref,
         sc_ref[0:1, :], z_ref, work_ref,
     )
     turned = jnp.transpose(backward_frames(grads, kv_ref, 0) + frk_ref[...])
@@ -630,16 +633,16 @@
             (one, two, wk, wq, gp1, q1, q0, pu1, d1, sc)
         )
         blocks = (pack, ownx, one, lax.ppermute(one, "row", CORE_SWAP), two, lax.ppermute(two, "row", CORE_SWAP))
-    key_pack, kv1, pm, e1 = call(
+    key_pack, kv1, pm1, mask, e1 = call(
         functools.partial(first_body, fast), "first", [VMEM] * 12,
-        [((keys, PACK), F32), ((keys, 2048), F32), ((2, hr, keys), BF16), ((rows, 384), F32)],
+        [((keys, PACK), F32), ((keys, 2048), F32), ((hr, keys), BF16), ((rows, keys), F32), ((rows, 384), F32)],
         (own, *blocks, wk, links, probs, gp1, d1),
     )
     e1_other = col_other(e1)
-    kv0, e0, tail = call(
-        second_body, "second", [VMEM] * 4,
-        [((keys, 2048), F32), ((rows, 640 + EARLY * CZ), F32), ((rows, (H - EARLY) * CZ), F32)],
-        (key_pack, wk, pm, pair),
+    kv0, pm0, e0, tail = call(
+        second_body, "second", [VMEM] * 5,
+        [((keys, 2048), F32), ((hr, keys), BF16), ((rows, 640 + EARLY * CZ), F32), ((rows, (H - EARLY) * CZ), F32)],
+        (key_pack, wk, probs, mask, pair),
         [pltpu.VMEM((hr, keys), F32), pltpu.VMEM((hr, CZ), F32)],
     )
     e0_other = col_other(e0)
@@ -650,7 +653,7 @@
         functools.partial(back_one_body, fast), "back_one", [VMEM] * 11,
         [((2 * hr, keys), F32), ((rows, C), F32), ((rows, C), F32), ((2 * rows, C), F32), ((rows, 1152), F32),
          ((keys, 768), F32)],
-        (e1, e1_other, pm, kv1, key_pack, own, q1, gp1, d1, wk, sc),
+        (e1, e1_other, pm1, kv1, key_pack, own, q1, gp1, d1, wk, sc),
         [pltpu.VMEM((keys, C), F32)],
         6.0,
     )
@@ -671,7 +674,7 @@
         functools.partial(back_zero_body, fast), "back_zero", [VMEM] * 20,
         [((2 * hr, keys), F32), ((long, 128), F32), ((long, 128), F32), ((2 * long, 128), F32), ((rows, 1152), F32),
          ((rows, C), F32), ((hr, CZ), F32)],
-        (cotangent, *pieces, e0, e0_other, tail, tail_other, pm, kv0, key_pack, own, q0, pair, w_out, wk, sc, frk),
+        (cotangent, *pieces, e0, e0_other, tail, tail_other, pm0, kv0, key_pack, own, q0, pair, w_out, wk, sc, frk),
         [pltpu.VMEM((keys, C), F32), pltpu.VMEM((4 * long, 128), F32), pltpu.VMEM((rows, 768), F32), pltpu.VMEM((hr, keys), F32)],
     )
     (d_pair,) = call(

time: 53.8 us -> 53.7 us (level)
  no operation moved by 1% of the time
where the time goes in v8:
time: 53.7 us; the launch traced here: 53.5 us
  starting transfers between devices  23.9 us (45%)
  Pallas kernels  17.6 us (33%)
  waiting for transfers between devices  11.1 us (21%)
  between operations  0.77 us (1%)
    pallas_call x10, Pallas kernels, call(): pl.pallas_call(body, name=name, in_specs=in_specs, out_specs=tuple((VMEM...  17.6 us
    ppermute x2, waiting for transfers between devices, reduce(): lax.ppermute(part, BOTH, SEND_ONE)  6.84 us
    ppermute x3, starting transfers between devices, col_other(): return lax.ppermute(x, 'col', COL_SWAP)  4.32 us
    ppermute x2, starting transfers between devices, reduce(): lax.ppermute(part, BOTH, SEND_TWO)  3.93 us
    ppermute x2, starting transfers between devices, reduce(): query_other = lax.ppermute(query, 'col', COL_SWAP)  3.48 us
    ppermute x2, starting transfers between devices, reduce(): half = lax.ppermute(mine_b + got[count:], 'row', Z_SWAP)  3.35 us
    ppermute x1, starting transfers between devices, local(): two = lax.ppermute(pack, BOTH, FETCH_TWO)  3.29 us
    ppermute x1, starting transfers between devices, local(): one = lax.ppermute(pack, BOTH, FETCH_ONE)  3.09 us
  transfers between devices with their start and end apart: 18, of which 9 were waited for; matrix products, arithmetic and copies ran while one was open for 0% of the time, Pallas kernels for 20%

profile of v8, /device:TPU:0, one launch (start us, length us, event | category | flops | bytes accessed | tf_op | source)
XLA Modules:
  0.0 53.5 jit_solution(4158075140186281139)
XLA Ops:
  0.6 1.0 %pack.1.pack_ref.self_ref.own_ref = f32[32,896]{1,0:T(8,128)S(1)} custom-call(f32[2,32,384]{2,1,0:T(8,128)} %single_hbm.1, f32[12,2,32]{2,1,0:T(2,128)} %bitcast.22, s32[1,32]{1,0:T(1,128)} %bitcast.23), custom_call_target="tpu_custom_call" | custom-call | flops 1000000000 | bytes 3000000 | tf_op jit(solution)/shard_map/pack/pallas_call | solution.py:530
  1.6 3.1 %collective-permute-start.1 = (f32[32,896]{1,0:T(8,128)S(1)}, f32[32,896]{1,0:T(8,128)S(1)}, u32[]{:S(2)}, u32[]{:S(2)}) collective-permute-start(f32[32,896]{1,0:T(8,128)S(1)} %pack.1.pack_ref.self_ref.own_ref), channel_id=1, source_target_pairs={{0,4},{2,6},{4,0},{6,2},{1,8},{3,10},{5,12},{7,14},{9,13},{11,15},... | collective-permute-start | bytes 344072 | tf_op jit(solution)/shard_map/ppermute | solution.py:579
  4.7 3.3 %collective-permute-start.2 = (f32[32,896]{1,0:T(8,128)S(1)}, f32[32,896]{1,0:T(8,128)S(1)}, u32[]{:S(2)}, u32[]{:S(2)}) collective-permute-start(f32[32,896]{1,0:T(8,128)S(1)} %pack.1.pack_ref.self_ref.own_ref), channel_id=1, source_target_pairs={{0,12},{2,14},{4,8},{6,10},{9,5},{11,7},{13,1},{15,3},{1,0},{3,2},... | collective-permute-start | bytes 344072 | tf_op jit(solution)/shard_map/ppermute | solution.py:580
  8.0 0.0 collective-permute-start
  8.0 0.0 copy-start.3
  8.0 0.0 copy-start.4
  8.0 3.3 %prep.1 = (bf16[1280,384]{1,0:T(8,128)(2,1)S(1)}, bf16[640,384]{1,0:T(8,128)(2,1)S(1)}, f32[32,768]{1,0:T(8,128)S(1)}, f32[32,1024]{1,0:T(8,128)S(1)}, f32[32,10...) custom-call(f32[32,896]{1,0:T(8,128)S(1)} %pack.1.pack_ref.self_ref.own_ref, ...), custom_call_target="tpu_custom_call" | custom-call | flops 1000000000 | bytes 3000000 | tf_op jit(solution)/shard_map/prep/pallas_call | solution.py:530
  11.4 0.0 collective-permute-done.1.p1_ref
  11.4 0.0 collective-permute-done.2.p2_ref
  11.4 0.6 %collective-permute-start.3 = (f32[32,896]{1,0:T(8,128)S(1)}, f32[32,896]{1,0:T(8,128)S(1)}, u32[]{:S(2)}, u32[]{:S(2)}) collective-permute-start(f32[32,896]{1,0:T(8,128)S(1)} %collective-permute-done.1.p1_ref), channel_id=1, source_target_pairs={{0,2},{2,0},{4,6},{6,4},{8,10},{10,8},{12,14},{14,12},{1,3},{3,1},... | collective-permute-start | bytes 344072 | tf_op jit(solution)/shard_map/ppermute | solution.py:635
  11.9 0.1 collective-permute-start.4
  12.0 0.0 collective-permute-done.ownx_ref
  12.0 0.9 %collective-permute-done.3.p1x_ref = f32[32,896]{1,0:T(8,128)S(1)} collective-permute-done((f32[32,896]{1,0:T(8,128)S(1)}, f32[32,896]{1,0:T(8,128)S(1)}, u32[]{:S(2)}, u32[]{:S(2)}) %collective-permute-start.3) | collective-permute-done | bytes 114720 | tf_op jit(solution)/shard_map/ppermute | solution.py:635
  12.9 0.4 collective-permute-done.4.p2x_ref
  13.3 0.0 copy-done.3
  13.3 0.0 copy-done.4
  13.3 0.0 copy-start.1
  13.3 1.2 %first.1 = (f32[128,896]{1,0:T(8,128)S(1)}, f32[128,2048]{1,0:T(8,128)S(1)}, bf16[384,128]{1,0:T(8,128)(2,1)S(1)}, f32[32,128]{1,0:T(8,128)S(1)}, f32[32,384]{1,0:T(8,128)S(1)}) custom-call(f32[32,896]{1,0:T(8,128)S(1)} %pack.1.pack_ref.self_ref.own_ref, f32[32,896]{1,0:T(8,128)S(1)} %pack.1.pack_ref.self_ref.own_ref, ...), custom_call_target="tpu_custom_call" | custom-call | flops 1000000000 | bytes 3000000 | tf_op jit(solution)/shard_map/first/pallas_call | solution.py:530
  14.5 2.3 %collective-permute-start.5 = (f32[32,384]{1,0:T(8,128)S(1)}, f32[32,384]{1,0:T(8,128)S(1)}, u32[]{:S(2)}, u32[]{:S(2)}) collective-permute-start(f32[32,384]{1,0:T(8,128)S(1)} %get-tuple-element.74.e_mine), channel_id=1, source_target_pairs={{0,1},{1,0},{2,3},{3,2},{4,5},{5,4},{6,7},{7,6},{8,9},{9,8},{10,11... | collective-permute-start | bytes 147464 | tf_op jit(solution)/shard_map/ppermute | solution.py:591
  16.8 0.0 copy-done.1
  16.8 1.3 %second.1 = (f32[128,2048]{1,0:T(8,128)S(1)}, bf16[384,128]{1,0:T(8,128)(2,1)S(1)}, f32[32,1152]{1,0:T(8,128)S(1)}, f32[32,1024]{1,0:T(8,128)S(1)}) custom-call(f32[128,896]{1,0:T(8,128)S(1)} %get-tuple-element.75.keys_ref, bf16[1280,384]{1,0:T(8,128)(2,1)S(1)} %get-tuple-element.71.wk_ref, bf16[2,384,128]{2,1,0:T(8,128)(2,1)S(1)} %bitcast.13, ...), custom_call_target="tpu_custom_call" | custom-call | flops 1000000000 | bytes 3000000 | tf_op jit(solution)/shard_map/second/pallas_call | solution.py:530
  18.2 0.1 collective-permute-start.7
  18.3 0.8 %collective-permute-done.5.e_other = f32[32,384]{1,0:T(8,128)S(1)} collective-permute-done((f32[32,384]{1,0:T(8,128)S(1)}, f32[32,384]{1,0:T(8,128)S(1)}, u32[]{:S(2)}, u32[]{:S(2)}) %collective-permute-start.5) | collective-permute-done | bytes 49184 | tf_op jit(solution)/shard_map/ppermute | solution.py:591
  19.1 2.1 %back_one.1 = (f32[768,128]{1,0:T(8,128)S(1)}, f32[32,384]{1,0:T(8,128)S(1)}, f32[32,384]{1,0:T(8,128)S(1)}, f32[64,384]{1,0:T(8,128)S(1)}, f32[32,1152]{1,0:T(8,128)S(1)}, /*index=5*/f32[128,768]{1,0:T(8,128)S(1)}) custom-call(f32[32,384]{1,0:T(8,128)S(1)} %get-tuple-element.74.e_mine, f32[32,384]{1,0:T(8,128)S(1)} %collective-permute-done.5.e_other, ...), custom_call_target="tpu_custom_call" | custom-call | flops 6000000000 | bytes 18000000 | tf_op jit(solution)/shard_map/back_one/pallas_call | solution.py:530
  21.2 0.0 copy-start
  21.2 0.0 copy-start.2
  21.2 0.1 collective-permute-start.6
  21.3 1.9 %collective-permute-start.9 = (f32[32,1024]{1,0:T(8,128)S(1)}, f32[32,1024]{1,0:T(8,128)S(1)}, u32[]{:S(2)}, u32[]{:S(2)}) collective-permute-start(f32[32,1024]{1,0:T(8,128)S(1)} %get-tuple-element.86.tail_mine), channel_id=1, source_target_pairs={{0,1},{1,0},{2,3},{3,2},{4,5},{5,4},{6,7},{7,6},{8,9},{9,8},{10,11... | collective-permute-start | bytes 393224 | tf_op jit(solution)/shard_map/ppermute | solution.py:591
  23.2 0.0 collective-permute-done.6
  23.2 0.8 %collective-permute-done.7.e_other = f32[32,1152]{1,0:T(8,128)S(1)} collective-permute-done((f32[32,1152]{1,0:T(8,128)S(1)}, f32[32,1152]{1,0:T(8,128)S(1)}, u32[]{:S(2)}, u32[]{:S(2)}) %collective-permute-start.7) | collective-permute-done | bytes 147488 | tf_op jit(solution)/shard_map/ppermute | solution.py:591
  24.1 1.8 %collective-permute-start.8 = (f32[32,384]{1,0:T(8,128)S(1)}, f32[32,384]{1,0:T(8,128)S(1)}, u32[]{:S(2)}, u32[]{:S(2)}) collective-permute-start(f32[32,384]{1,0:T(8,128)S(1)} %slice_add_fusion.1), channel_id=1, source_target_pairs={{0,4},{2,6},{4,0},{6,2},{8,12},{10,14},{12,8},{14,10},{1,5},{3,7},... | collective-permute-start | bytes 147464 | tf_op jit(solution)/shard_map/ppermute | solution.py:605
  25.9 1.2 %query_one.1 = (f32[32,384]{1,0:T(8,128)S(1)}, f32[32,128]{1,0:T(8,128)S(1)}, f32[128,128]{1,0:T(8,128)S(1)}) custom-call(f32[768,128]{1,0:T(8,128)S(1)} %get-tuple-element.87.z_ref.z1_ref, f32[128,2048]{1,0:T(8,128)S(1)} %get-tuple-element.80.kv_ref, f32[32,896]{1,0:T(8,128)S(1)} %pack.1.pack_ref.self_ref.own_ref, f32[32,1024]{1,0:T(8,128)S(1)} %get-tuple-element.81.q_ref, ...), custom_call_target="tpu_custom_call" | custom-call | flops 10000000 | bytes 30000 | tf_op jit(solution)/shard_map/query_one/pallas_call | solution.py:530
  27.1 0.5 collective-permute-start.10
  27.6 0.0 collective-permute-done.9.tail_other
  27.6 0.6 %collective-permute-done.8 = f32[32,384]{1,0:T(8,128)S(1)} collective-permute-done((f32[32,384]{1,0:T(8,128)S(1)}, f32[32,384]{1,0:T(8,128)S(1)}, u32[]{:S(2)}, u32[]{:S(2)}) %collective-permute-start.8) | collective-permute-done | bytes 49184 | tf_op jit(solution)/shard_map/ppermute | solution.py:605
  28.2 1.3 %collective-permute-start.11 = (f32[32,384]{1,0:T(8,128)S(1)}, f32[32,384]{1,0:T(8,128)S(1)}, u32[]{:S(2)}, u32[]{:S(2)}) collective-permute-start(f32[32,384]{1,0:T(8,128)S(1)} %add_add_fusion.1.r2), channel_id=1, source_target_pairs={{0,1},{2,3},{4,5},{6,7},{8,0},{10,2},{12,4},{14,6},{9,8},{11,10},{... | collective-permute-start | bytes 147464 | tf_op jit(solution)/shard_map/ppermute | solution.py:608
  29.5 2.1 %collective-permute-start.12 = (f32[32,384]{1,0:T(8,128)S(1)}, f32[32,384]{1,0:T(8,128)S(1)}, u32[]{:S(2)}, u32[]{:S(2)}) collective-permute-start(f32[32,384]{1,0:T(8,128)S(1)} %add_add_fusion.1.r2), channel_id=1, source_target_pairs={{8,1},{10,3},{12,5},{14,7},{1,8},{3,10},{5,12},{7,14},{0,4},{2,6},... | collective-permute-start | bytes 147464 | tf_op jit(solution)/shard_map/ppermute | solution.py:608
  31.5 0.0 collective-permute-done.10.r1
  31.6 2.2 %collective-permute-done.11.r3 = f32[32,384]{1,0:T(8,128)S(1)} collective-permute-done((f32[32,384]{1,0:T(8,128)S(1)}, f32[32,384]{1,0:T(8,128)S(1)}, u32[]{:S(2)}, u32[]{:S(2)}) %collective-permute-start.11) | collective-permute-done | bytes 49184 | tf_op jit(solution)/shard_map/ppermute | solution.py:608
  33.7 0.5 collective-permute-done.12.r4
  34.2 0.0 copy-done
  34.2 0.0 copy-done.2
  34.2 3.8 %back_zero.1 = (f32[768,128]{1,0:T(8,128)S(1)}, f32[104,128]{1,0:T(8,128)S(1)}, f32[104,128]{1,0:T(8,128)S(1)}, f32[208,128]{1,0:T(8,128)S(1)}, f32[32,1152]{1,0...) custom-call(f32[32,384]{1,0:T(8,128)S(1)} %copy-done.2, f32[32,384]{1,0:T(8,128)S(1)} %get-tuple-element.93.r0, ...), custom_call_target="tpu_custom_call" | custom-call | flops 1000000000 | bytes 3000000 | tf_op jit(solution)/shard_map/back_zero/pallas_call | solution.py:530
  38.0 0.1 collective-permute-start.13
  38.1 0.0 copy-start.5
  38.1 1.0 %query_zero.1.r0 = f32[104,128]{1,0:T(8,128)S(1)} custom-call(f32[768,128]{1,0:T(8,128)S(1)} %get-tuple-element.105.z_ref.z0_ref, f32[128,2048]{1,0:T(8,128)S(1)} %get-tuple-element.100.kv_ref, f32[32,896]{1,0:T(8,128)S(1)} %pack.1.pack_ref.self_ref.own_ref, f32[32,1024]{1,0:T(8,128)S(1)} %get-tuple-element.101.q_ref, ...), custom_call_target="tpu_custom_call" | custom-call | flops 1000000000 | bytes 3000000 | tf_op jit(solution)/shard_map/query_zero/pallas_call | solution.py:530
  39.1 0.3 collective-permute-done.13
  39.4 1.5 %collective-permute-start.14 = (f32[104,128]{1,0:T(8,128)S(1)}, f32[104,128]{1,0:T(8,128)S(1)}, u32[]{:S(2)}, u32[]{:S(2)}) collective-permute-start(f32[104,128]{1,0:T(8,128)S(1)} %slice_add_fusion), channel_id=1, source_target_pairs={{0,4},{2,6},{4,0},{6,2},{8,12},{10,14},{12,8},{14,10},{1,5},{3,7},... | collective-permute-start | bytes 159752 | tf_op jit(solution)/shard_map/ppermute | solution.py:605
  40.9 0.0 copy-done.5
  40.9 1.9 %pair_grad.1 = bf16[32,128,128]{2,1,0:T(8,128)(2,1)} custom-call(f32[768,128]{1,0:T(8,128)S(1)} %get-tuple-element.87.z_ref.z1_ref, f32[768,128]{1,0:T(8,128)S(1)} %get-tuple-element.105.z_ref.z0_ref, f32[384,128]{1,0:T(8,128)S(1)} %get-tuple-element.109.pu1_ref, f32[384,128]{1,0:T(8,128)S(1)} %get-tuple-element.110.pu0_ref, bf16[12,128]{1,0:T(8,128)(2,1)S(1)} %bitcast.14), custom_call_target="tpu_custom_call" | custom-call | flops 1000000000 | bytes 3000000 | tf_op jit(solution)/shard_map/pair_grad/pallas_call | solution.py:530
  42.8 3.0 %collective-permute-start.15 = (f32[104,128]{1,0:T(8,128)S(1)}, f32[104,128]{1,0:T(8,128)S(1)}, u32[]{:S(2)}, u32[]{:S(2)}) collective-permute-start(f32[104,128]{1,0:T(8,128)S(1)} %query_zero.1.r0), channel_id=1, source_target_pairs={{0,1},{1,0},{2,3},{3,2},{4,5},{5,4},{6,7},{7,6},{8,9},{9,8},{10,11... | collective-permute-start | bytes 159752 | tf_op jit(solution)/shard_map/ppermute | solution.py:603
  45.8 0.0 collective-permute-done.14
  45.9 0.4 collective-permute-start.16
  46.2 1.9 %collective-permute-start.17 = (f32[104,128]{1,0:T(8,128)S(1)}, f32[104,128]{1,0:T(8,128)S(1)}, u32[]{:S(2)}, u32[]{:S(2)}) collective-permute-start(f32[104,128]{1,0:T(8,128)S(1)} %add_add_fusion.r2), channel_id=1, source_target_pairs={{8,1},{10,3},{12,5},{14,7},{1,8},{3,10},{5,12},{7,14},{0,4},{2,6},... | collective-permute-start | bytes 159752 | tf_op jit(solution)/shard_map/ppermute | solution.py:608
  48.1 0.0 collective-permute-done.15.r1
  48.1 4.7 %collective-permute-done.16.r3 = f32[104,128]{1,0:T(8,128)S(1)} collective-permute-done((f32[104,128]{1,0:T(8,128)S(1)}, f32[104,128]{1,0:T(8,128)S(1)}, u32[]{:S(2)}, u32[]{:S(2)}) %collective-permute-start.16) | collective-permute-done | bytes 53280 | tf_op jit(solution)/shard_map/ppermute | solution.py:608
  52.8 0.0 collective-permute-done.17.r4
  52.8 0.7 %final.1 = (f32[32,384]{1,0:T(8,128)}, f32[12,2,32]{2,1,0:T(2,128)}) custom-call(f32[104,128]{1,0:T(8,128)S(1)} %query_zero.1.r0, f32[104,128]{1,0:T(8,128)S(1)} %collective-permute-done.15.r1, f32[104,128]{1,0:T(8,128)S(1)} %add_add_fusion.r2, f32[104,128]{1,0:T(8,128)S(1)} %collective-permute-done.16.r3, f32[104,128]{1,0:T(8,128)S(1)} %collective-permute-done.17.r4, ...), custom_call_target="tpu_custom_call" | custom-call | flops 1000000000 | bytes 3000000 | tf_op jit(solution)/shard_map/final/pallas_call | solution.py:530
  (4 shorter events, 0.0 us)
Async XLA Ops:
  1.6 9.7 %collective-permute-start.1 = (f32[32,896]{1,0:T(8,128)S(1)}, f32[32,896]{1,0:T(8,128)S(1)}, u32[]{:S(2)}, u32[]{:S(2)}) collective-permute-start(f32[32,896]{1,0:T(8,128)S(1)} %pack.1.pack_ref.self_ref.own_ref), channel_id=1, source_target_pairs={{0,4},{2,6},{4,0},{6,2},{1,8},{3,10},{5,12},{7,14},{9,13},{11,15},... | collective-permute-start | bytes 344072 | tf_op jit(solution)/shard_map/ppermute | solution.py:579
  4.7 6.7 %collective-permute-start.2 = (f32[32,896]{1,0:T(8,128)S(1)}, f32[32,896]{1,0:T(8,128)S(1)}, u32[]{:S(2)}, u32[]{:S(2)}) collective-permute-start(f32[32,896]{1,0:T(8,128)S(1)} %pack.1.pack_ref.self_ref.own_ref), channel_id=1, source_target_pairs={{0,12},{2,14},{4,8},{6,10},{9,5},{11,7},{13,1},{15,3},{1,0},{3,2},... | collective-permute-start | bytes 344072 | tf_op jit(solution)/shard_map/ppermute | solution.py:580
  8.0 4.0 %collective-permute-start = (f32[32,896]{1,0:T(8,128)S(1)}, f32[32,896]{1,0:T(8,128)S(1)}, u32[]{:S(2)}, u32[]{:S(2)}) collective-permute-start(f32[32,896]{1,0:T(8,128)S(1)} %pack.1.pack_ref.self_ref.own_ref), channel_id=1, source_target_pairs={{0,2},{2,0},{4,6},{6,4},{8,10},{10,8},{12,14},{14,12},{1,3},{3,1},... | collective-permute-start | bytes 344072 | tf_op jit(solution)/shard_map/ppermute | solution.py:578
  8.0 5.3 %copy-start.3 = (bf16[2,12,32,128]{3,2,1,0:T(8,128)(2,1)S(1)}, bf16[2,12,32,128]{3,2,1,0:T(8,128)(2,1)}, u32[]{:S(2)}) copy-start(bf16[2,12,32,128]{3,2,1,0:T(8,128)(2,1)} %param.18) | copy-start | bytes 589828
  8.0 5.3 %copy-start.4 = (s32[16,16]{1,0:T(8,128)S(1)}, s32[16,16]{1,0:T(8,128)}, u32[]{:S(2)}) copy-start(s32[16,16]{1,0:T(8,128)} %links_ref.1) | copy-start | bytes 3076
  11.4 1.5 %collective-permute-start.3 = (f32[32,896]{1,0:T(8,128)S(1)}, f32[32,896]{1,0:T(8,128)S(1)}, u32[]{:S(2)}, u32[]{:S(2)}) collective-permute-start(f32[32,896]{1,0:T(8,128)S(1)} %collective-permute-done.1.p1_ref), channel_id=1, source_target_pairs={{0,2},{2,0},{4,6},{6,4},{8,10},{10,8},{12,14},{14,12},{1,3},{3,1},... | collective-permute-start | bytes 344072 | tf_op jit(solution)/shard_map/ppermute | solution.py:635
  11.9 1.3 %collective-permute-start.4 = (f32[32,896]{1,0:T(8,128)S(1)}, f32[32,896]{1,0:T(8,128)S(1)}, u32[]{:S(2)}, u32[]{:S(2)}) collective-permute-start(f32[32,896]{1,0:T(8,128)S(1)} %collective-permute-done.2.p2_ref), channel_id=1, source_target_pairs={{0,2},{2,0},{4,6},{6,4},{8,10},{10,8},{12,14},{14,12},{1,3},{3,1},... | collective-permute-start | bytes 344072 | tf_op jit(solution)/shard_map/ppermute | solution.py:635
  13.3 3.6 %copy-start.1 = (bf16[32,128,128]{2,1,0:T(8,128)(2,1)S(1)}, bf16[32,128,128]{2,1,0:T(8,128)(2,1)}, u32[]{:S(2)}) copy-start(bf16[32,128,128]{2,1,0:T(8,128)(2,1)} %pair_ref.3) | copy-start | bytes 3145732
  14.5 4.6 %collective-permute-start.5 = (f32[32,384]{1,0:T(8,128)S(1)}, f32[32,384]{1,0:T(8,128)S(1)}, u32[]{:S(2)}, u32[]{:S(2)}) collective-permute-start(f32[32,384]{1,0:T(8,128)S(1)} %get-tuple-element.74.e_mine), channel_id=1, source_target_pairs={{0,1},{1,0},{2,3},{3,2},{4,5},{5,4},{6,7},{7,6},{8,9},{9,8},{10,11... | collective-permute-start | bytes 147464 | tf_op jit(solution)/shard_map/ppermute | solution.py:591
  18.2 5.9 %collective-permute-start.7 = (f32[32,1152]{1,0:T(8,128)S(1)}, f32[32,1152]{1,0:T(8,128)S(1)}, u32[]{:S(2)}, u32[]{:S(2)}) collective-permute-start(f32[32,1152]{1,0:T(8,128)S(1)} %get-tuple-element.96.e_mine), channel_id=1, source_target_pairs={{0,1},{1,0},{2,3},{3,2},{4,5},{5,4},{6,7},{7,6},{8,9},{9,8},{10,11... | collective-permute-start | bytes 442376 | tf_op jit(solution)/shard_map/ppermute | solution.py:591
  21.2 13.0 %copy-start = (bf16[2112,384]{1,0:T(8,128)(2,1)S(1)}, bf16[2112,384]{1,0:T(8,128)(2,1)}, u32[]{:S(2)}) copy-start(bf16[2112,384]{1,0:T(8,128)(2,1)} %w_out_ref.1) | copy-start | bytes 4866052
  21.2 13.0 %copy-start.2 = (f32[32,384]{1,0:T(8,128)S(1)}, f32[32,384]{1,0:T(8,128)}, u32[]{:S(2)}) copy-start(f32[32,384]{1,0:T(8,128)} %cot_ref.1) | copy-start | bytes 147460
  21.2 2.0 %collective-permute-start.6 = (f32[64,384]{1,0:T(8,128)S(1)}, f32[64,384]{1,0:T(8,128)S(1)}, u32[]{:S(2)}, u32[]{:S(2)}) collective-permute-start(f32[64,384]{1,0:T(8,128)S(1)} %get-tuple-element.84), channel_id=1, source_target_pairs={{0,2},{2,0},{4,6},{6,4},{8,10},{10,8},{12,14},{14,12},{1,3},{3,1},... | collective-permute-start | bytes 294920 | tf_op jit(solution)/shard_map/ppermute | solution.py:596
  21.3 6.3 %collective-permute-start.9 = (f32[32,1024]{1,0:T(8,128)S(1)}, f32[32,1024]{1,0:T(8,128)S(1)}, u32[]{:S(2)}, u32[]{:S(2)}) collective-permute-start(f32[32,1024]{1,0:T(8,128)S(1)} %get-tuple-element.86.tail_mine), channel_id=1, source_target_pairs={{0,1},{1,0},{2,3},{3,2},{4,5},{5,4},{6,7},{7,6},{8,9},{9,8},{10,11... | collective-permute-start | bytes 393224 | tf_op jit(solution)/shard_map/ppermute | solution.py:591
  24.1 4.2 %collective-permute-start.8 = (f32[32,384]{1,0:T(8,128)S(1)}, f32[32,384]{1,0:T(8,128)S(1)}, u32[]{:S(2)}, u32[]{:S(2)}) collective-permute-start(f32[32,384]{1,0:T(8,128)S(1)} %slice_add_fusion.1), channel_id=1, source_target_pairs={{0,4},{2,6},{4,0},{6,2},{8,12},{10,14},{12,8},{14,10},{1,5},{3,7},... | collective-permute-start | bytes 147464 | tf_op jit(solution)/shard_map/ppermute | solution.py:605
  27.1 4.4 %collective-permute-start.10 = (f32[32,384]{1,0:T(8,128)S(1)}, f32[32,384]{1,0:T(8,128)S(1)}, u32[]{:S(2)}, u32[]{:S(2)}) collective-permute-start(f32[32,384]{1,0:T(8,128)S(1)} %get-tuple-element.93.r0), channel_id=1, source_target_pairs={{0,1},{1,0},{2,3},{3,2},{4,5},{5,4},{6,7},{7,6},{8,9},{9,8},{10,11... | collective-permute-start | bytes 147464 | tf_op jit(solution)/shard_map/ppermute | solution.py:603
  28.2 5.5 %collective-permute-start.11 = (f32[32,384]{1,0:T(8,128)S(1)}, f32[32,384]{1,0:T(8,128)S(1)}, u32[]{:S(2)}, u32[]{:S(2)}) collective-permute-start(f32[32,384]{1,0:T(8,128)S(1)} %add_add_fusion.1.r2), channel_id=1, source_target_pairs={{0,1},{2,3},{4,5},{6,7},{8,0},{10,2},{12,4},{14,6},{9,8},{11,10},{... | collective-permute-start | bytes 147464 | tf_op jit(solution)/shard_map/ppermute | solution.py:608
  29.5 4.7 %collective-permute-start.12 = (f32[32,384]{1,0:T(8,128)S(1)}, f32[32,384]{1,0:T(8,128)S(1)}, u32[]{:S(2)}, u32[]{:S(2)}) collective-permute-start(f32[32,384]{1,0:T(8,128)S(1)} %add_add_fusion.1.r2), channel_id=1, source_target_pairs={{8,1},{10,3},{12,5},{14,7},{1,8},{3,10},{5,12},{7,14},{0,4},{2,6},... | collective-permute-start | bytes 147464 | tf_op jit(solution)/shard_map/ppermute | solution.py:608
  38.0 1.4 %collective-permute-start.13 = (f32[208,128]{1,0:T(8,128)S(1)}, f32[208,128]{1,0:T(8,128)S(1)}, u32[]{:S(2)}, u32[]{:S(2)}) collective-permute-start(f32[208,128]{1,0:T(8,128)S(1)} %get-tuple-element.104), channel_id=1, source_target_pairs={{0,2},{2,0},{4,6},{6,4},{8,10},{10,8},{12,14},{14,12},{1,3},{3,1},... | collective-permute-start | bytes 319496 | tf_op jit(solution)/shard_map/ppermute | solution.py:596
  38.1 2.8 %copy-start.5 = (bf16[128,12]{0,1:T(8,128)(2,1)S(1)}, bf16[128,12]{0,1:T(8,128)(2,1)}, u32[]{:S(2)}) copy-start(bf16[128,12]{0,1:T(8,128)(2,1)} %param.29) | copy-start | bytes 9220
  39.4 6.5 %collective-permute-start.14 = (f32[104,128]{1,0:T(8,128)S(1)}, f32[104,128]{1,0:T(8,128)S(1)}, u32[]{:S(2)}, u32[]{:S(2)}) collective-permute-start(f32[104,128]{1,0:T(8,128)S(1)} %slice_add_fusion), channel_id=1, source_target_pairs={{0,4},{2,6},{4,0},{6,2},{8,12},{10,14},{12,8},{14,10},{1,5},{3,7},... | collective-permute-start | bytes 159752 | tf_op jit(solution)/shard_map/ppermute | solution.py:605
  42.8 5.3 %collective-permute-start.15 = (f32[104,128]{1,0:T(8,128)S(1)}, f32[104,128]{1,0:T(8,128)S(1)}, u32[]{:S(2)}, u32[]{:S(2)}) collective-permute-start(f32[104,128]{1,0:T(8,128)S(1)} %query_zero.1.r0), channel_id=1, source_target_pairs={{0,1},{1,0},{2,3},{3,2},{4,5},{5,4},{6,7},{7,6},{8,9},{9,8},{10,11... | collective-permute-start | bytes 159752 | tf_op jit(solution)/shard_map/ppermute | solution.py:603
  45.9 6.9 %collective-permute-start.16 = (f32[104,128]{1,0:T(8,128)S(1)}, f32[104,128]{1,0:T(8,128)S(1)}, u32[]{:S(2)}, u32[]{:S(2)}) collective-permute-start(f32[104,128]{1,0:T(8,128)S(1)} %add_add_fusion.r2), channel_id=1, source_target_pairs={{0,1},{2,3},{4,5},{6,7},{8,0},{10,2},{12,4},{14,6},{9,8},{11,10},{... | collective-permute-start | bytes 159752 | tf_op jit(solution)/shard_map/ppermute | solution.py:608
  46.2 6.5 %collective-permute-start.17 = (f32[104,128]{1,0:T(8,128)S(1)}, f32[104,128]{1,0:T(8,128)S(1)}, u32[]{:S(2)}, u32[]{:S(2)}) collective-permute-start(f32[104,128]{1,0:T(8,128)S(1)} %add_add_fusion.r2), channel_id=1, source_target_pairs={{8,1},{10,3},{12,5},{14,7},{1,8},{3,10},{5,12},{7,14},{0,4},{2,6},... | collective-permute-start | bytes 159752 | tf_op jit(solution)/shard_map/ppermute | solution.py:608
